TPU v7x, 32 devices: a whole 2x2x4 slice. The times are simulated.
32 devices in a mesh: parts: 2 (over y), space: 4 (over z), section: 2 (over x), chan: 2 (over core).
Axes of the slice: x: 2, y: 2, z: 4, core: 2. Of those that a mesh axis runs over, the one named last changes fastest.
Arguments:
- section_inputs: bfloat16 [2, 6, 8, 16, 16, 128], P('section', 'parts', 'space'), parts along dimension 1, may hold values from -6 to 6
- cotangent: bfloat16 [6, 8, 16, 16, 128], P('parts', 'space'), parts along dimension 0, may hold values from -6 to 6
- phase_labels: int32 [6, 8, 16, 16], P('parts', 'space'), parts along dimension 0, may hold values from 0 to 2
- expand_weight: bfloat16 [2, 128, 256], P('section', None, 'chan'), may hold values from -0.5 to 0.5
- phase_code: float32 [2, 3, 256], P('section', None, 'chan'), may hold values from -6 to 6
- kernel: bfloat16 [2, 27, 32, 8, 8], P('section', None, 'chan'), may hold values from -0.4375 to 0.4375
- reduce_weight: bfloat16 [2, 256, 128], P('section', 'chan'), may hold values from -0.375 to 0.375
Outputs:
- input_grads: bfloat16 [2, 6, 8, 16, 16, 128], P('section', 'parts', 'space'), parts along dimension 1
- expand_grad: float32 [4, 128, 256], P(('parts', 'section'), None, 'chan'), parts along dimension 0
- kernel_grad: float32 [4, 27, 32, 8, 8], P(('parts', 'section'), None, 'chan'), parts along dimension 0
- reduce_grad: float32 [4, 256, 128], P(('parts', 'section'), 'chan'), parts along dimension 0
There are 2 independent parts, one for each index of `parts`. A program takes and returns all parts, laid end to end along the dimension named above; an argument that names none is the same for every part. Nothing has to cross between parts.
All inputs are finite; a program needn't handle non-finite values.
Results may differ from a plain program's by a relative error of at most 0.015.
Values may be sent and summed in bfloat16 or wider, within the bound.
No kernel may reach another device: no remote copies, remote signals or barrier semaphores. Data moves between devices by JAX's collectives and lax.ppermute only.
A program may use at most 192 MiB of HBM per device.

v0:
```python
import math

import jax
import jax.numpy as jnp
from jax import lax
from jax.sharding import PartitionSpec as P


def with_halo(value, sides, width):
    for axis, dim in sides:
        size, length = (lax.axis_size(axis), value.shape[dim])
        up = [(i, (i + 1) % size) for i in range(size)]
        down = [(j, i) for i, j in up]
        last = lax.slice_in_dim(value, length - width, length, axis=dim)
        leading = lax.slice_in_dim(value, 0, width, axis=dim)
        before = lax.ppermute(last, axis, up)
        after = lax.ppermute(leading, axis, down)
        value = jnp.concatenate([before, value, after], axis=dim)
    return value


def shifted(block, axis, distance):
    devices = range(lax.axis_size(axis))
    route = [((i - distance) % len(devices), i) for i in devices]
    return lax.ppermute(block, axis, route)


def shifted_2(value, axis, steps):
    count = lax.axis_size(axis)
    leading, last = (max(0, -steps), min(count, count - steps))
    return lax.ppermute(value, axis, [(source, source + steps) for source in range(leading, last)])


def silu_slope(value):
    sigma = jax.nn.sigmoid(value)
    return sigma * (1.0 + value * (1.0 - sigma))


def wrap_pad(field):
    field = jnp.concatenate([field[:, -1:], field, field[:, :1]], axis=1)
    return jnp.concatenate([field[:, :, -1:], field, field[:, :, :1]], axis=2)


def tap_views(padded, slab_depth, direction):
    grid_wide = padded.shape[1] - 2
    grid_deep = padded.shape[2] - 2
    view_list = []
    for step_x in (-1, 0, 1):
        for step_y in (-1, 0, 1):
            for step_z in (-1, 0, 1):
                start_x = 1 + direction * step_x
                start_y = 1 + direction * step_y
                start_z = 1 + direction * step_z
                view_list.append(
                    padded[
                        start_x : start_x + slab_depth,
                        start_y : start_y + grid_wide,
                        start_z : start_z + grid_deep,
                    ]
                )
    return view_list


def block_kernel(kernel_local):
    taps, local_groups, group_width, _ = kernel_local.shape
    width = local_groups * group_width
    block_width = min(128, width)
    block_count = width // block_width
    per_block = block_width // group_width
    shaped = kernel_local.reshape(taps, block_count, per_block, group_width, group_width)
    identity = jnp.eye(per_block, dtype=kernel_local.dtype)
    full = jnp.einsum("tngio,gh->tngiho", shaped, identity)
    return full.reshape(taps, block_count, block_width, block_width)


def block_forward(rows, blocks):
    cell_count, width = rows.shape
    block_count, block_width = (blocks.shape[0], blocks.shape[1])
    split_rows = rows.reshape(cell_count, block_count, block_width)
    return jnp.einsum(
        "cnk,nkl->cnl", split_rows, blocks, preferred_element_type=jnp.float32
    ).reshape(cell_count, width)


def block_backward(rows, blocks):
    cell_count, width = rows.shape
    block_count, block_width = (blocks.shape[0], blocks.shape[1])
    split_rows = rows.reshape(cell_count, block_count, block_width)
    return jnp.einsum(
        "cnl,nkl->cnk", split_rows, blocks, preferred_element_type=jnp.float32
    ).reshape(cell_count, width)


def block_outer(left, right, block_count, block_width):
    cell_count = left.shape[0]
    left_split = left.reshape(cell_count, block_count, block_width)
    right_split = right.reshape(cell_count, block_count, block_width)
    return jnp.einsum("cnk,cnl->nkl", left_split, right_split, preferred_element_type=jnp.float32)


def block_extract(block_grads, local_groups, group_width):
    taps, block_count, block_width, _ = block_grads.shape
    per_block = block_width // group_width
    shaped = block_grads.reshape(taps, block_count, per_block, group_width, per_block, group_width)
    identity = jnp.eye(per_block, dtype=jnp.float32)
    picked = jnp.einsum("tngiho,gh->tngio", shaped, identity)
    return picked.reshape(taps, local_groups, group_width, group_width)


def phase_rows(flat_tags, code_table, cell_count):
    code_rows = jnp.zeros((cell_count, code_table.shape[1]), jnp.float32)
    for phase_id in range(code_table.shape[0]):
        code_rows = jnp.where(flat_tags == phase_id, code_table[phase_id][None, :], code_rows)
    return code_rows


def conv_forward_parts(padded_hidden, slab_depth, cell_count, local_width, blocks):
    hidden_list = [
        view.reshape(cell_count, local_width) for view in tap_views(padded_hidden, slab_depth, 1)
    ]
    conv_out = jnp.zeros((cell_count, local_width), jnp.float32)
    for tap_id in range(27):
        conv_out = conv_out + block_forward(hidden_list[tap_id], blocks[tap_id])
    return (hidden_list, conv_out)


def kernel_terms(hidden_list, grad_conv, blocks, local_groups, group_width):
    block_count, block_width = (blocks.shape[1], blocks.shape[2])
    stacked = jnp.stack(
        [
            block_outer(hidden_list[tap_id], grad_conv, block_count, block_width)
            for tap_id in range(27)
        ]
    )
    return block_extract(stacked, local_groups, group_width)


def block_groups(slab_in, slab_tags, upstream, weights_in, code_table, kernel_local, weights_out):
    slab_depth, grid_wide, grid_deep, trunk_width = slab_in.shape
    local_width = weights_in.shape[1]
    local_groups = kernel_local.shape[1]
    group_width = kernel_local.shape[2]
    chan_rank = lax.axis_index("chan")
    cell_count = slab_depth * grid_wide * grid_deep
    share_rows = cell_count // lax.axis_size("chan")
    slab_shape = (slab_depth, grid_wide, grid_deep, local_width)
    blocks = block_kernel(kernel_local)
    flat_in = slab_in.reshape(cell_count, trunk_width)
    code_rows = phase_rows(slab_tags.reshape(cell_count, 1), code_table, cell_count)
    pre_act = jnp.dot(flat_in, weights_in, preferred_element_type=jnp.float32) + code_rows
    hidden = jax.nn.silu(pre_act).astype(jnp.bfloat16).reshape(slab_shape)
    hidden_rims = with_halo(hidden, (("space", 0),), 1)
    hidden_list, conv_out = conv_forward_parts(
        wrap_pad(hidden_rims), slab_depth, cell_count, local_width, blocks
    )
    mixed_out = jax.nn.silu(conv_out).astype(jnp.bfloat16)
    flat_up = upstream.reshape(cell_count, trunk_width)
    grad_mixed = lax.dot_general(
        flat_up, weights_out, (((1,), (1,)), ((), ())), preferred_element_type=jnp.float32
    )
    reduce_term = jnp.dot(mixed_out.T, flat_up, preferred_element_type=jnp.float32)
    grad_conv = (grad_mixed * silu_slope(conv_out)).astype(jnp.bfloat16)
    kernel_term = kernel_terms(hidden_list, grad_conv, blocks, local_groups, group_width)
    padded = jnp.zeros((slab_depth + 2, grid_wide + 2, grid_deep + 2, local_width), jnp.float32)
    tap_id = 0
    for step_x in (-1, 0, 1):
        for step_y in (-1, 0, 1):
            for step_z in (-1, 0, 1):
                spread_term = block_backward(grad_conv, blocks[tap_id]).reshape(slab_shape)
                padded = padded.at[
                    1 + step_x : 1 + step_x + slab_depth,
                    1 + step_y : 1 + step_y + grid_wide,
                    1 + step_z : 1 + step_z + grid_deep,
                ].add(spread_term)
                tap_id = tap_id + 1
    folded = (
        padded[:, 1 : grid_wide + 1]
        .at[:, 0]
        .add(padded[:, grid_wide + 1])
        .at[:, grid_wide - 1]
        .add(padded[:, 0])
    )
    folded = (
        folded[:, :, 1 : grid_deep + 1]
        .at[:, :, 0]
        .add(folded[:, :, grid_deep + 1])
        .at[:, :, grid_deep - 1]
        .add(folded[:, :, 0])
    )
    from_above = shifted(folded[0].astype(jnp.bfloat16), "space", -1).astype(jnp.float32)
    from_below = shifted(folded[slab_depth + 1].astype(jnp.bfloat16), "space", 1).astype(
        jnp.float32
    )
    interior = folded[1 : slab_depth + 1]
    interior = interior.at[slab_depth - 1].add(from_above).at[0].add(from_below)
    grad_hidden = interior.reshape(cell_count, local_width)
    grad_pre = (grad_hidden * silu_slope(pre_act)).astype(jnp.bfloat16)
    expand_term = jnp.dot(flat_in.T, grad_pre, preferred_element_type=jnp.float32)
    branch_share = lax.psum_scatter(
        lax.dot_general(
            grad_pre, weights_in, (((1,), (1,)), ((), ())), preferred_element_type=jnp.float32
        ).astype(jnp.bfloat16),
        "chan",
        scatter_dimension=0,
        tiled=True,
    ).astype(jnp.float32)
    own_rows = lax.dynamic_slice_in_dim(flat_up, chan_rank * share_rows, share_rows, 0)
    out_share = (own_rows.astype(jnp.float32) + branch_share).astype(jnp.bfloat16)
    out_full = lax.all_gather(out_share, "chan", axis=0, tiled=True)
    return (
        out_full.reshape(slab_depth, grid_wide, grid_deep, trunk_width),
        expand_term,
        kernel_term,
        reduce_term,
    )


def on_device(
    section_inputs, cotangent, phase_labels, expand_weight, phase_code, kernel, reduce_weight
):
    micro_count = section_inputs.shape[1]
    slab_depth = section_inputs.shape[2]
    grid_wide = section_inputs.shape[3]
    grid_deep = section_inputs.shape[4]
    trunk_width = section_inputs.shape[5]
    sections = lax.axis_size("section")
    section_rank = lax.axis_index("section")
    weights_in, code_table, kernel_used, weights_out = (
        expand_weight[0],
        phase_code[0],
        kernel[0],
        reduce_weight[0],
    )
    inputs_here = section_inputs[0]
    output_buf = jnp.zeros(
        (micro_count, slab_depth, grid_wide, grid_deep, trunk_width), jnp.bfloat16
    )
    expand_acc = jnp.zeros((trunk_width, weights_in.shape[1]), jnp.float32)
    kernel_acc = jnp.zeros(kernel_used.shape, jnp.float32)
    reduce_acc = jnp.zeros((weights_out.shape[0], trunk_width), jnp.float32)
    incoming = jnp.zeros((slab_depth, grid_wide, grid_deep, trunk_width), jnp.bfloat16)
    for moment in range(micro_count + sections - 1):
        batch_id = moment - (sections - 1 - section_rank)
        active_now = (batch_id >= 0) & (batch_id < micro_count)
        chosen = jnp.clip(batch_id, 0, micro_count - 1)
        slab_in = lax.dynamic_index_in_dim(inputs_here, chosen, 0, keepdims=False)
        slab_tags = lax.dynamic_index_in_dim(phase_labels, chosen, 0, keepdims=False)
        given = lax.dynamic_index_in_dim(cotangent, chosen, 0, keepdims=False)
        upstream = jnp.where(section_rank == sections - 1, given, incoming)
        result, expand_term, kernel_term, reduce_term = block_groups(
            slab_in, slab_tags, upstream, weights_in, code_table, kernel_used, weights_out
        )
        expand_acc = expand_acc + jnp.where(active_now, expand_term, 0.0)
        kernel_acc = kernel_acc + jnp.where(active_now, kernel_term, 0.0)
        reduce_acc = reduce_acc + jnp.where(active_now, reduce_term, 0.0)
        current = lax.dynamic_index_in_dim(output_buf, chosen, 0, keepdims=False)
        output_buf = lax.dynamic_update_index_in_dim(
            output_buf, jnp.where(active_now, result, current), chosen, 0
        )
        incoming = shifted_2(result, "section", -1)
    totals = (
        lax.psum(expand_acc.astype(jnp.bfloat16), "space").astype(jnp.float32),
        lax.psum(kernel_acc.astype(jnp.bfloat16), "space").astype(jnp.float32),
        lax.psum(reduce_acc.astype(jnp.bfloat16), "space").astype(jnp.float32),
    )
    norm_scale = 1.0 / math.sqrt(
        micro_count * slab_depth * lax.axis_size("space") * grid_wide * grid_deep
    )
    return (
        output_buf[None],
        (totals[0] * norm_scale)[None],
        (totals[1] * norm_scale)[None],
        (totals[2] * norm_scale)[None],
    )


def solution(mesh):
    placed = (
        P("section", "parts", "space", None, None, None),
        P("parts", "space", None, None, None),
        P("parts", "space", None, None),
        P("section", None, "chan"),
        P("section", None, "chan"),
        P("section", None, "chan", None, None),
        P("section", "chan", None),
    )
    return jax.shard_map(
        on_device,
        mesh=mesh,
        in_specs=placed,
        out_specs=(
            P("section", "parts", "space", None, None, None),
            P(("parts", "section"), None, "chan"),
            P(("parts", "section"), None, "chan", None, None),
            P(("parts", "section"), "chan", None),
        ),
        check_vma=False,
    )
```

profile of v0, /device:TPU:0, one launch (start us, length us, event | category | flops | bytes accessed | tf_op | source)
XLA Modules:
  0.0 994.7 jit_solution(11868415606705595782)
XLA Ops:
  12.6 3.0 collective-permute-start.15
  16.4 2.0 collective-permute-start.16
  25.3 2.3 collective-permute-start.1
  29.4 2.5 multiply_bitcast_fusion
  31.9 2.1 fusion.552
  34.0 3.5 fusion.551
  82.5 2.1 collective-permute-start.11
  125.4 1.8 copy.265
  132.5 1.8 copy.261
  152.1 3.5 dynamic-slice_add_fusion.3
  155.6 3.0 scatter-add.449
  192.7 3.8 collective-permute-start.6
  237.1 2.2 collective-permute-start.3
  256.8 1.8 fusion.605
  266.2 1.8 fusion.617
  332.0 11.8 %fusion.6 = f32[16,1,27,8,8]{2,1,4,3,0:T(1,128)} fusion(bf16[27,16,8,16,8]{3,2,4,1,0:T(8,128)(2,1)S(1)} %bitcast.3926, pred[16,16,1,1,1]{1,0,2,3,4:T(8,128)(4,1)S(1)} %fusion.441), kind=kOutput, calls=%fused_computation.6 | convolution fusion | flops 884736 | bytes 995584 | tf_op jit(solution)/shard_map/tngiho,gh->tngio/dot_general | solution.py:106
  351.5 1.8 convolution_bitcast_fusion.189
  470.4 2.0 fusion.125
  473.3 1.9 all_gather.12
  476.8 5.9 collective-permute-done.4
  506.5 1.8 copy.299
  538.4 3.5 dynamic-slice_add_fusion.2
  541.9 3.0 scatter-add.504
  606.2 2.9 copy-done.1
  616.3 14.8 %fusion.4 = f32[16,1,27,8,8]{2,1,4,3,0:T(1,128)} fusion(bf16[27,16,8,16,8]{3,2,4,1,0:T(8,128)(2,1)} %bitcast.3927, pred[16,16,1,1,1]{1,0,2,3,4:T(8,128)(4,1)S(1)} %fusion.441), kind=kOutput, calls=%fused_computation.4 | convolution fusion | flops 884736 | bytes 995584 | tf_op jit(solution)/shard_map/tngiho,gh->tngio/dot_general | solution.py:106
  633.7 1.9 all_gather.13
  637.4 5.6 collective-permute-done.9
  678.5 1.8 copy.325
  682.1 1.8 copy.323
  700.6 3.5 dynamic-slice_add_fusion.1
  704.2 3.0 scatter-add.559
  740.8 3.6 collective-permute-start.12
  769.1 12.2 %fusion.2 = f32[16,1,27,8,8]{2,1,4,3,0:T(1,128)} fusion(bf16[27,16,8,16,8]{3,2,4,1,0:T(8,128)(2,1)S(1)} %bitcast.3928, pred[16,16,1,1,1]{1,0,2,3,4:T(8,128)(4,1)S(1)} %fusion.441), kind=kOutput, calls=%fused_computation.2 | convolution fusion | flops 884736 | bytes 995584 | tf_op jit(solution)/shard_map/tngiho,gh->tngio/dot_general | solution.py:106
  788.1 2.7 convolution_select_fusion.1
  792.6 3.9 reduce-scatter.9.cloned.1.call-done
  797.4 1.9 all_gather.14
  801.4 5.4 collective-permute-done.14
  860.1 3.5 dynamic-slice_add_fusion
  863.6 3.0 scatter-add.614
  889.9 2.3 convolution_select_fusion
  915.8 12.0 %fusion = f32[16,1,27,8,8]{2,1,4,3,0:T(1,128)} fusion(bf16[27,16,8,16,8]{3,2,4,1,0:T(8,128)(2,1)S(1)} %bitcast.3929, pred[16,16,1,1,1]{1,0,2,3,4:T(8,128)(4,1)S(1)} %fusion.441), kind=kOutput, calls=%fused_computation | convolution fusion | flops 884736 | bytes 995584 | tf_op jit(solution)/shard_map/tngiho,gh->tngio/dot_general | solution.py:106
  928.3 3.8 collective-permute-start.17
  932.1 2.2 fusion.142
  934.3 2.3 fusion.152
  940.5 34.9 %all-reduce.7.cloned.1.call-done = (bf16[128,128]{1,0:T(8,128)(2,1)}, bf16[27,16,8,8]{0,3,2,1:T(8,128)(2,1)}, bf16[128,128]{1,0:T(8,128)(2,1)}) async-done(((bf16[128,128]{1,0:T(8,128)(2,1)}, bf16[27,16,8,8]{0,3,2,1:T(8,128)(2,1)}, bf16[128,128]{1,0:T(8,128)(2,1)}), (bf16[128,128]{1,0:T(8,128)(2,1)}, bf16[27,16,8,8]{0,3,2,1:T(8,128)(2,1)}, bf16[128,128]{1,0:T(8,128)(2,1)})) %all-reduce.7.cloned.1.call-update) | async-done | bytes 120848 | tf_op jit(solution)/shard_map/psum | solution.py:262
  978.1 1.8 multiply_bitcast_fusion.1
  979.9 4.5 reduce-scatter.11.cloned.1.call-done
  985.3 1.9 all_gather.15
  (1444 shorter events, 768.3 us)
Async XLA Ops:
  7.2 465.2 %reduce-scatter.5.cloned.1.call-start = ((), (), s32[]{:S(2)}) async-start(), calls=%async_computation.4 | async-start | bytes 196608 | tf_op jit(solution)/shard_map/reduce_scatter | solution.py:199
  12.6 180.1 %collective-permute-start.15 = (bf16[1,16,16,128]{3,2,1,0:T(8,128)(2,1)}, bf16[1,16,16,128]{3,2,1,0:T(8,128)(2,1)}, u32[]{:S(2)}, u32[]{:S(2)}) collective-permute-start(bf16[1,16,16,128]{3,2,1,0:T(8,128)(2,1)} %bitcast.484), channel_id=1, source_target_pairs={{0,4},{4,8},{8,12},{12,0},{1,5},{5,9},{9,13},{13,1},{2,6},{6,10},{... | collective-permute-start | bytes 196616 | tf_op jit(solution)/shard_map/ppermute | solution.py:16
  16.4 180.1 %collective-permute-start.16 = (bf16[1,16,16,128]{3,2,1,0:T(8,128)(2,1)}, bf16[1,16,16,128]{3,2,1,0:T(8,128)(2,1)}, u32[]{:S(2)}, u32[]{:S(2)}) collective-permute-start(bf16[1,16,16,128]{3,2,1,0:T(8,128)(2,1)} %bitcast.486), channel_id=1, source_target_pairs={{4,0},{8,4},{12,8},{0,12},{5,1},{9,5},{13,9},{1,13},{6,2},{10,6},{... | collective-permute-start | bytes 196616 | tf_op jit(solution)/shard_map/ppermute | solution.py:17
  21.0 188.5 %collective-permute-start.10 = (bf16[1,16,16,128]{3,2,1,0:T(8,128)(2,1)}, bf16[1,16,16,128]{3,2,1,0:T(8,128)(2,1)}, u32[]{:S(2)}, u32[]{:S(2)}) collective-permute-start(bf16[1,16,16,128]{3,2,1,0:T(8,128)(2,1)} %bitcast.327), channel_id=1, source_target_pairs={{0,4},{4,8},{8,12},{12,0},{1,5},{5,9},{9,13},{13,1},{2,6},{6,10},{... | collective-permute-start | bytes 196616 | tf_op jit(solution)/shard_map/ppermute | solution.py:16
  23.0 59.5 %collective-permute-start = (bf16[1,16,16,128]{3,2,1,0:T(8,128)(2,1)}, bf16[1,16,16,128]{3,2,1,0:T(8,128)(2,1)}, u32[]{:S(2)}, u32[]{:S(2)}) collective-permute-start(bf16[1,16,16,128]{3,2,1,0:T(8,128)(2,1)} %bitcast.11), channel_id=1, source_target_pairs={{0,4},{4,8},{8,12},{12,0},{1,5},{5,9},{9,13},{13,1},{2,6},{6,10},{... | collective-permute-start | bytes 196616 | tf_op jit(solution)/shard_map/ppermute | solution.py:16
  25.3 59.2 %collective-permute-start.1 = (bf16[1,16,16,128]{3,2,1,0:T(8,128)(2,1)}, bf16[1,16,16,128]{3,2,1,0:T(8,128)(2,1)}, u32[]{:S(2)}, u32[]{:S(2)}) collective-permute-start(bf16[1,16,16,128]{3,2,1,0:T(8,128)(2,1)} %bitcast.13), channel_id=1, source_target_pairs={{4,0},{8,4},{12,8},{0,12},{5,1},{9,5},{13,9},{1,13},{6,2},{10,6},{... | collective-permute-start | bytes 196616 | tf_op jit(solution)/shard_map/ppermute | solution.py:17
  82.5 127.0 %collective-permute-start.11 = (bf16[1,16,16,128]{3,2,1,0:T(8,128)(2,1)}, bf16[1,16,16,128]{3,2,1,0:T(8,128)(2,1)}, u32[]{:S(2)}, u32[]{:S(2)}) collective-permute-start(bf16[1,16,16,128]{3,2,1,0:T(8,128)(2,1)} %bitcast.4299), channel_id=1, source_target_pairs={{4,0},{8,4},{12,8},{0,12},{5,1},{9,5},{13,9},{1,13},{6,2},{10,6},{... | collective-permute-start | bytes 196616 | tf_op jit(solution)/shard_map/ppermute | solution.py:17
  84.5 138.5 %collective-permute-start.5 = (bf16[1,16,16,128]{3,2,1,0:T(8,128)(2,1)}, bf16[1,16,16,128]{3,2,1,0:T(8,128)(2,1)}, u32[]{:S(2)}, u32[]{:S(2)}) collective-permute-start(bf16[1,16,16,128]{3,2,1,0:T(8,128)(2,1)} %bitcast.4298), channel_id=1, source_target_pairs={{0,4},{4,8},{8,12},{12,0},{1,5},{5,9},{9,13},{13,1},{2,6},{6,10},{... | collective-permute-start | bytes 196616 | tf_op jit(solution)/shard_map/ppermute | solution.py:16
  192.7 30.3 %collective-permute-start.6 = (bf16[1,16,16,128]{3,2,1,0:T(8,128)(2,1)}, bf16[1,16,16,128]{3,2,1,0:T(8,128)(2,1)S(1)}, u32[]{:S(2)}, u32[]{:S(2)}) collective-permute-start(bf16[1,16,16,128]{3,2,1,0:T(8,128)(2,1)} %bitcast.4297), channel_id=1, source_target_pairs={{4,0},{8,4},{12,8},{0,12},{5,1},{9,5},{13,9},{1,13},{6,2},{10,6},{... | collective-permute-start | bytes 196616 | tf_op jit(solution)/shard_map/ppermute | solution.py:17
  199.2 61.4 %copy-start.88 = (bf16[2,16,16,128]{3,2,1,0:T(8,128)(2,1)}, bf16[2,16,16,128]{3,2,1,0:T(8,128)(2,1)S(1)}, u32[]{:S(2)}) copy-start(bf16[2,16,16,128]{3,2,1,0:T(8,128)(2,1)S(1)} %get-tuple-element.1621) | copy-start | bytes 393220
  199.2 63.3 %copy-start.83 = (bf16[2,16,16,128]{3,2,1,0:T(8,128)(2,1)}, bf16[2,16,16,128]{3,2,1,0:T(8,128)(2,1)S(1)}, u32[]{:S(2)}) copy-start(bf16[2,16,16,128]{3,2,1,0:T(8,128)(2,1)S(1)} %get-tuple-element.1620) | copy-start | bytes 393220
  199.2 65.1 %copy-start.79 = (bf16[2,16,16,128]{3,2,1,0:T(8,128)(2,1)}, bf16[2,16,16,128]{3,2,1,0:T(8,128)(2,1)S(1)}, u32[]{:S(2)}) copy-start(bf16[2,16,16,128]{3,2,1,0:T(8,128)(2,1)S(1)} %get-tuple-element.1619) | copy-start | bytes 393220
  201.6 58.1 %copy-start.91 = (bf16[2,16,16,128]{3,2,1,0:T(8,128)(2,1)}, bf16[2,16,16,128]{3,2,1,0:T(8,128)(2,1)S(1)}, u32[]{:S(2)}) copy-start(bf16[2,16,16,128]{3,2,1,0:T(8,128)(2,1)S(1)} %get-tuple-element.1631) | copy-start | bytes 393220
  201.6 59.9 %copy-start.90 = (bf16[2,16,16,128]{3,2,1,0:T(8,128)(2,1)}, bf16[2,16,16,128]{3,2,1,0:T(8,128)(2,1)S(1)}, u32[]{:S(2)}) copy-start(bf16[2,16,16,128]{3,2,1,0:T(8,128)(2,1)S(1)} %get-tuple-element.1630) | copy-start | bytes 393220
  201.6 61.7 %copy-start.89 = (bf16[2,16,16,128]{3,2,1,0:T(8,128)(2,1)}, bf16[2,16,16,128]{3,2,1,0:T(8,128)(2,1)S(1)}, u32[]{:S(2)}) copy-start(bf16[2,16,16,128]{3,2,1,0:T(8,128)(2,1)S(1)} %get-tuple-element.1629) | copy-start | bytes 393220
  201.7 63.6 %copy-start.86 = (bf16[2,16,16,128]{3,2,1,0:T(8,128)(2,1)}, bf16[2,16,16,128]{3,2,1,0:T(8,128)(2,1)S(1)}, u32[]{:S(2)}) copy-start(bf16[2,16,16,128]{3,2,1,0:T(8,128)(2,1)S(1)} %get-tuple-element.1628) | copy-start | bytes 393220
  203.7 54.9 %copy-start.93 = (bf16[2,16,16,128]{3,2,1,0:T(8,128)(2,1)}, bf16[2,16,16,128]{3,2,1,0:T(8,128)(2,1)S(1)}, u32[]{:S(2)}) copy-start(bf16[2,16,16,128]{3,2,1,0:T(8,128)(2,1)S(1)} %get-tuple-element.1695) | copy-start | bytes 393220
  203.7 55.1 %copy-start.92 = (bf16[2,16,16,128]{3,2,1,0:T(8,128)(2,1)}, bf16[2,16,16,128]{3,2,1,0:T(8,128)(2,1)S(1)}, u32[]{:S(2)}) copy-start(bf16[2,16,16,128]{3,2,1,0:T(8,128)(2,1)S(1)} %get-tuple-element.1794) | copy-start | bytes 393220
  237.1 109.5 %collective-permute-start.2 = (bf16[16,16,128]{2,1,0:T(8,128)(2,1)}, bf16[16,16,128]{2,1,0:T(8,128)(2,1)}, u32[]{:S(2)}, u32[]{:S(2)}) collective-permute-start(bf16[16,16,128]{2,1,0:T(8,128)(2,1)} %get-tuple-element.1737), channel_id=1, source_target_pairs={{4,0},{8,4},{12,8},{0,12},{5,1},{9,5},{13,9},{1,13},{6,2},{10,6},{... | collective-permute-start | bytes 196616 | tf_op jit(solution)/shard_map/ppermute | solution.py:25
  237.1 110.4 %collective-permute-start.3 = (bf16[16,16,128]{2,1,0:T(8,128)(2,1)}, bf16[16,16,128]{2,1,0:T(8,128)(2,1)}, u32[]{:S(2)}, u32[]{:S(2)}) collective-permute-start(bf16[16,16,128]{2,1,0:T(8,128)(2,1)} %get-tuple-element.1736), channel_id=1, source_target_pairs={{12,0},{0,4},{4,8},{8,12},{13,1},{1,5},{5,9},{9,13},{14,2},{2,6},{... | collective-permute-start | bytes 196616 | tf_op jit(solution)/shard_map/ppermute | solution.py:25
  258.8 45.9 %copy-start.70 = (bf16[2,16,16,128]{3,2,1,0:T(8,128)(2,1)S(1)}, bf16[2,16,16,128]{3,2,1,0:T(8,128)(2,1)}, u32[]{:S(2)}) copy-start(bf16[2,16,16,128]{3,2,1,0:T(8,128)(2,1)} %copy-done.69) | copy-start | bytes 393220
  332.0 47.0 %copy-start.124 = (bf16[2,16,16,128]{3,2,1,0:T(8,128)(2,1)S(1)}, bf16[2,16,16,128]{3,2,1,0:T(8,128)(2,1)}, u32[]{:S(2)}) copy-start(bf16[2,16,16,128]{3,2,1,0:T(8,128)(2,1)} %copy-done.123) | copy-start | bytes 393220
  343.8 44.8 %copy-start.107 = (bf16[2,16,16,128]{3,2,1,0:T(8,128)(2,1)S(1)}, bf16[2,16,16,128]{3,2,1,0:T(8,128)(2,1)}, u32[]{:S(2)}) copy-start(bf16[2,16,16,128]{3,2,1,0:T(8,128)(2,1)} %copy-done.106) | copy-start | bytes 393220
  343.8 52.2 %copy-start.109 = (bf16[2,16,16,128]{3,2,1,0:T(8,128)(2,1)S(1)}, bf16[2,16,16,128]{3,2,1,0:T(8,128)(2,1)}, u32[]{:S(2)}) copy-start(bf16[2,16,16,128]{3,2,1,0:T(8,128)(2,1)} %copy-done.108) | copy-start | bytes 393220
  351.1 281.7 %reduce-scatter.7.cloned.1.call-start = ((), (), s32[]{:S(2)}) async-start(), calls=%async_computation.5 | async-start | bytes 196608 | tf_op jit(solution)/shard_map/reduce_scatter | solution.py:199
  380.5 82.6 %copy-start.84 = (bf16[2,16,16,128]{3,2,1,0:T(8,128)(2,1)S(1)}, bf16[2,16,16,128]{3,2,1,0:T(8,128)(2,1)}, u32[]{:S(2)}) copy-start(bf16[2,16,16,128]{3,2,1,0:T(8,128)(2,1)} %copy-done.83) | copy-start | bytes 393220
  383.8 83.5 %copy-start.80 = (bf16[2,16,16,128]{3,2,1,0:T(8,128)(2,1)S(1)}, bf16[2,16,16,128]{3,2,1,0:T(8,128)(2,1)}, u32[]{:S(2)}) copy-start(bf16[2,16,16,128]{3,2,1,0:T(8,128)(2,1)} %copy-done.79) | copy-start | bytes 393220
  386.2 83.4 %copy-start.87 = (bf16[2,16,16,128]{3,2,1,0:T(8,128)(2,1)S(1)}, bf16[2,16,16,128]{3,2,1,0:T(8,128)(2,1)}, u32[]{:S(2)}) copy-start(bf16[2,16,16,128]{3,2,1,0:T(8,128)(2,1)} %copy-done.86) | copy-start | bytes 393220
  400.0 83.6 %copy-start.35 = (f32[128,512]{1,0:T(8,128)S(1)}, f32[128,512]{1,0:T(8,128)}, u32[]{:S(2)}) copy-start(f32[128,512]{1,0:T(8,128)} %fusion.590) | copy-start | bytes 786436
  400.0 83.6 %copy-start.37 = (f32[128,512]{1,0:T(8,128)S(1)}, f32[128,512]{1,0:T(8,128)}, u32[]{:S(2)}) copy-start(f32[128,512]{1,0:T(8,128)} %fusion.596) | copy-start | bytes 786436
  400.0 83.6 %copy-start.39 = (f32[128,512]{1,0:T(8,128)S(1)}, f32[128,512]{1,0:T(8,128)}, u32[]{:S(2)}) copy-start(f32[128,512]{1,0:T(8,128)} %fusion.588) | copy-start | bytes 786436
  400.0 83.6 %copy-start.41 = (f32[128,512]{1,0:T(8,128)S(1)}, f32[128,512]{1,0:T(8,128)}, u32[]{:S(2)}) copy-start(f32[128,512]{1,0:T(8,128)} %fusion.589) | copy-start | bytes 786436
  400.0 83.6 %copy-start.43 = (f32[128,512]{1,0:T(8,128)S(1)}, f32[128,512]{1,0:T(8,128)}, u32[]{:S(2)}) copy-start(f32[128,512]{1,0:T(8,128)} %fusion.591) | copy-start | bytes 786436
  400.1 83.6 %copy-start.45 = (f32[128,512]{1,0:T(8,128)S(1)}, f32[128,512]{1,0:T(8,128)}, u32[]{:S(2)}) copy-start(f32[128,512]{1,0:T(8,128)} %fusion.592) | copy-start | bytes 786436
  400.1 83.6 %copy-start.47 = (f32[128,512]{1,0:T(8,128)S(1)}, f32[128,512]{1,0:T(8,128)}, u32[]{:S(2)}) copy-start(f32[128,512]{1,0:T(8,128)} %fusion.594) | copy-start | bytes 786436
  475.2 7.4 collective-permute-start.4
  578.6 31.3 %collective-permute-start.7 = (bf16[16,16,128]{2,1,0:T(8,128)(2,1)}, bf16[16,16,128]{2,1,0:T(8,128)(2,1)}, u32[]{:S(2)}, u32[]{:S(2)}) collective-permute-start(bf16[16,16,128]{2,1,0:T(8,128)(2,1)} %get-tuple-element.1731), channel_id=1, source_target_pairs={{4,0},{8,4},{12,8},{0,12},{5,1},{9,5},{13,9},{1,13},{6,2},{10,6},{... | collective-permute-start | bytes 196616 | tf_op jit(solution)/shard_map/ppermute | solution.py:25
  580.4 31.0 %collective-permute-start.8 = (bf16[16,16,128]{2,1,0:T(8,128)(2,1)}, bf16[16,16,128]{2,1,0:T(8,128)(2,1)}, u32[]{:S(2)}, u32[]{:S(2)}) collective-permute-start(bf16[16,16,128]{2,1,0:T(8,128)(2,1)} %get-tuple-element.1730), channel_id=1, source_target_pairs={{12,0},{0,4},{4,8},{8,12},{13,1},{1,5},{5,9},{9,13},{14,2},{2,6},{... | collective-permute-start | bytes 196616 | tf_op jit(solution)/shard_map/ppermute | solution.py:25
  616.0 180.5 %reduce-scatter.9.cloned.1.call-start = ((), (), s32[]{:S(2)}) async-start(), calls=%async_computation.6 | async-start | bytes 196608 | tf_op jit(solution)/shard_map/reduce_scatter | solution.py:199
  635.6 7.4 collective-permute-start.9
  740.8 41.2 %collective-permute-start.12 = (bf16[16,16,128]{2,1,0:T(8,128)(2,1)}, bf16[16,16,128]{2,1,0:T(8,128)(2,1)}, u32[]{:S(2)}, u32[]{:S(2)}) collective-permute-start(bf16[16,16,128]{2,1,0:T(8,128)(2,1)} %get-tuple-element.1725), channel_id=1, source_target_pairs={{4,0},{8,4},{12,8},{0,12},{5,1},{9,5},{13,9},{1,13},{6,2},{10,6},{... | collective-permute-start | bytes 196616 | tf_op jit(solution)/shard_map/ppermute | solution.py:25
  744.4 39.1 %collective-permute-start.13 = (bf16[16,16,128]{2,1,0:T(8,128)(2,1)}, bf16[16,16,128]{2,1,0:T(8,128)(2,1)}, u32[]{:S(2)}, u32[]{:S(2)}) collective-permute-start(bf16[16,16,128]{2,1,0:T(8,128)(2,1)} %get-tuple-element.1724), channel_id=1, source_target_pairs={{12,0},{0,4},{4,8},{8,12},{13,1},{1,5},{5,9},{9,13},{14,2},{2,6},{... | collective-permute-start | bytes 196616 | tf_op jit(solution)/shard_map/ppermute | solution.py:25
  788.1 187.3 %all-reduce.7.cloned.1.call-start = ((), (), s32[]{:S(2)}) async-start(), calls=%async_computation.8 | async-start | bytes 655360 | tf_op jit(solution)/shard_map/psum | solution.py:262
  799.3 7.5 collective-permute-start.14
  927.8 56.7 %copy-start.62 = (bf16[2,16,16,128]{3,2,1,0:T(8,128)(2,1)S(1)}, bf16[2,16,16,128]{3,2,1,0:T(8,128)(2,1)}, u32[]{:S(2)}) copy-start(bf16[2,16,16,128]{3,2,1,0:T(8,128)(2,1)} %copy-done.61) | copy-start | bytes 393220
  928.3 8.3 collective-permute-start.17
  932.0 6.1 collective-permute-start.18
  939.5 44.9 %reduce-scatter.11.cloned.1.call-start = ((), (), s32[]{:S(2)}) async-start(), calls=%async_computation.7 | async-start | bytes 196608 | tf_op jit(solution)/shard_map/reduce_scatter | solution.py:199
  (229 other events, 3836.2 us)
Sparse Core Ops, SparseCore 0:
  351.2 7.1 reduce-scatter.4
  616.1 8.0 reduce-scatter.6
  788.2 8.2 reduce-scatter.8
  939.6 35.6 all-reduce.6
  977.4 6.9 reduce-scatter.10
where the time goes:
time: 1010 us; the launch traced here: 995 us
  local copies, waits for them, and re-layouts  428 us (42%)
  matrix products  310 us (31%)
  other arithmetic  135 us (13%)
  waiting for transfers between devices  61.7 us (6%)
  starting transfers between devices  32 us (3%)
  between operations  20.8 us (2%)
    dot_general x104, local copies, waits for them, and re-layouts, block_outer(): jnp.einsum('cnk,cnl->nkl', left_split, right_split, preferred_element_typ...  154 us
    transpose x108, local copies, waits for them, and re-layouts, block_backward(): jnp.einsum('cnl,nkl->cnk', split_rows, blocks, preferred_element_type=jnp...  129 us
    dot_general x108, matrix products, block_outer(): jnp.einsum('cnk,cnl->nkl', left_split, right_split, preferred_element_typ...  92.1 us
    dot_general x108, matrix products, block_backward(): jnp.einsum('cnl,nkl->cnk', split_rows, blocks, preferred_element_type=jnp...  84.6 us
    add x72, other arithmetic, block_groups(): padded = padded.at[1 + step_x:1 + step_x + slab_depth, 1 + step_y:1 + ste...  66.4 us
    scatter-add x76, local copies, waits for them, and re-layouts, block_groups(): padded = padded.at[1 + step_x:1 + step_x + slab_depth, 1 + step_y:1 + ste...  60.4 us
    dot_general x108, matrix products, block_forward(): jnp.einsum('cnk,nkl->cnl', split_rows, blocks, preferred_element_type=jnp...  57.7 us
    dot_general x4, matrix products, block_extract(): picked = jnp.einsum('tngiho,gh->tngio', shaped, identity)  50.6 us
  transfers between devices with their start and end apart: 24, of which 7 were waited for; matrix products, arithmetic and copies ran while one was open for 52% of the time, Pallas kernels for 0%

commit v1 on v0

v1 whole, which is shorter than its diff:
```python
import functools
import math

import jax
import jax.numpy as jnp
from jax import lax
from jax.experimental import pallas as pl
from jax.experimental.pallas import tpu as pltpu
from jax.sharding import PartitionSpec as P

BF = jnp.bfloat16
F32 = jnp.float32
LANES = 128


def gate(v):
    return 0.5 + 0.5 * jnp.tanh(0.5 * v)


def slope(v, q):
    return q * (1.0 + v * (1.0 - q))


def nt_dot(a, b):
    return lax.dot_general(a, b, (((1,), (1,)), ((), ())), preferred_element_type=F32)


def store_shifts(ref, plane, value, wide, deep):
    cells = wide * deep
    cube = value.reshape(wide, deep, LANES)
    for j, turn in enumerate((1, 0, deep - 1)):
        moved = cube if turn == 0 else pltpu.roll(cube, turn, axis=1)
        flat = moved.reshape(cells, LANES).astype(BF)
        lanes = slice(j * LANES, (j + 1) * LANES)
        ref[plane, deep : deep + cells, lanes] = flat
        ref[plane, 0:deep, lanes] = flat[cells - deep :]
        ref[plane, deep + cells : cells + 2 * deep, lanes] = flat[:deep]


def views(ref, plane, cells, deep):
    return [
        ref[plane + dx, (1 + dy) * deep : (1 + dy) * deep + cells, :]
        for dx in (-1, 0, 1)
        for dy in (-1, 0, 1)
    ]


def conv_plane(ref, plane, weights, cells, deep):
    rows = jnp.concatenate(views(ref, plane, cells, deep), axis=1)
    return jnp.dot(rows, weights[...], preferred_element_type=F32)


def pack_kernel(micro, cells, wide, x_ref, ct_ref, lab_ref, *outs):
    c = lax.axis_index("chan")
    for m in range(micro):
        a_ref, b_ref = outs[2 * m], outs[2 * m + 1]
        x = x_ref[m, c]
        lab = lab_ref[m, c]
        a_ref[0:cells] = x
        a_ref[cells : cells + wide] = lab
        a_ref[cells + wide : 2 * cells + wide] = ct_ref[m, c]
        b_ref[0:cells] = x
        b_ref[cells : cells + wide] = lab


def weights_kernel(taps, width, kf_ref, kb_ref, f_ref, b_ref):
    groups = LANES // width
    g = lax.broadcasted_iota(jnp.int32, (groups, width, LANES), 0)
    lane = lax.broadcasted_iota(jnp.int32, (groups, width, LANES), 2)
    keep = g == lane // width
    for src, dst in ((kf_ref, f_ref), (kb_ref, b_ref)):
        for t in range(taps):
            one = src[t * width : (t + 1) * width, :]
            full = jnp.where(keep, jnp.broadcast_to(one[None], keep.shape), 0.0)
            dst[t * LANES : (t + 1) * LANES, :] = full.reshape(LANES, LANES).astype(BF)


def forward_kernel(
    wide,
    deep,
    x_ref,
    lab_ref,
    a_ref,
    b_ref,
    a2_ref,
    b2_ref,
    ct_ref,
    w_ref,
    code_ref,
    rw_ref,
    kf_ref,
    kb_ref,
    hid_ref,
    spre_ref,
    sconv_ref,
    mixed_ref,
    base_ref,
    other_ref,
    hs_ref,
    gs_ref,
    br_ref,
):
    c = lax.axis_index("chan")
    cells = wide * deep
    low, high = 1 - c, c
    codes = [jnp.broadcast_to(code_ref[i : i + 1, :], (deep, LANES)) for i in range(3)]

    def hidden_of(x, lab, plane, own):
        pre = jnp.dot(x, w_ref[...], preferred_element_type=F32)
        lab = lab.astype(F32)
        adds = []
        for y in range(wide):
            tag = jnp.broadcast_to(lab[:, y : y + 1], (deep, LANES))
            adds.append(jnp.where(tag < 0.5, codes[0], jnp.where(tag < 1.5, codes[1], codes[2])))
        pre = pre + jnp.concatenate(adds, axis=0)
        q = gate(pre)
        h = pre * q
        if own is not None:
            hid_ref[own] = h.astype(BF)
            spre_ref[own] = slope(pre, q)
        store_shifts(hs_ref, plane, h, wide, deep)

    hidden_of(x_ref[0, 0], lab_ref[0, 0], 2, 0)
    hidden_of(x_ref[0, 1], lab_ref[0, 1], 3, 1)
    for ref, plane in (
        (a_ref, 4 - 3 * c),
        (b_ref, 5 * c),
        (a2_ref, 1 + 3 * c),
        (b2_ref, 5 - 5 * c),
    ):
        hidden_of(ref[0:cells], ref[cells : cells + wide], plane, None)

    for p in range(4):
        conv = conv_plane(hs_ref, p + 1, kf_ref, cells, deep)
        q = gate(conv)
        sconv_ref[p] = slope(conv, q)
        if p in (1, 2):
            mixed_ref[p - 1] = (conv * q).astype(BF)

    ups = (
        (ct_ref[0, 0], 1),
        (ct_ref[0, 1], 2),
        (a_ref[cells + wide : 2 * cells + wide], 3 - 3 * c),
        (a2_ref[cells + wide : 2 * cells + wide], 3 * c),
    )
    for up, plane in ups:
        grad = nt_dot(up, rw_ref[...]) * sconv_ref[plane]
        store_shifts(gs_ref, plane, grad.astype(BF).astype(F32), wide, deep)
    for p in (0, 1):
        grad_hidden = conv_plane(gs_ref, p + 1, kb_ref, cells, deep)
        grad_pre = (grad_hidden * spre_ref[p]).astype(BF)
        br_ref[p] = nt_dot(grad_pre, w_ref[...])
    base_ref[...] = ct_ref[0, c].astype(F32) + br_ref[c]
    other_ref[...] = br_ref[1 - c].astype(BF)


def backward_kernel(
    full,
    wide,
    deep,
    taps,
    width,
    x_ref,
    ct_ref,
    cta_ref,
    cta2_ref,
    st_ref,
    st2_ref,
    dg_ref,
    dg2_ref,
    hid_ref,
    spre_ref,
    sconv_ref,
    mixed_ref,
    w_ref,
    rw_ref,
    kb_ref,
    *rest,
):
    c = lax.axis_index("chan")
    cells = wide * deep
    if full:
        exp_in, red_in, kg_in, part_ref, up_ref, exp_ref, red_ref, kg_ref, gs_ref = rest
    else:
        base_ref, other_ref, gs_ref, up_ref, br_ref = rest
    last = lax.axis_index("section") == lax.axis_size("section") - 1

    @pl.when(last)
    def _():
        up_ref[0] = ct_ref[0, 0]
        up_ref[1] = ct_ref[0, 1]

    @pl.when(jnp.logical_not(last))
    def _():
        up_ref[c] = st_ref[...]
        up_ref[1 - c] = st2_ref[...]

    tail = slice(cells + wide, 2 * cells + wide)
    halo = jnp.where(last, cta_ref[tail], dg_ref[...])
    halo2 = jnp.where(last, cta2_ref[tail], dg2_ref[...])
    ups = ((up_ref[0], 1), (up_ref[1], 2), (halo, 3 - 3 * c), (halo2, 3 * c))
    for up, plane in ups:
        grad = nt_dot(up, rw_ref[...]) * sconv_ref[plane]
        store_shifts(gs_ref, plane, grad.astype(BF).astype(F32), wide, deep)
    if full:
        ups2 = up_ref[...].reshape(2 * cells, LANES)
        red = lax.dot_general(
            mixed_ref[...].reshape(2 * cells, LANES),
            ups2,
            (((0,), (0,)), ((), ())),
            preferred_element_type=F32,
        )
        red_ref[...] = red_in[...] + red
        groups = LANES // width
        g = lax.broadcasted_iota(jnp.int32, (groups, width, LANES), 0)
        lane = lax.broadcasted_iota(jnp.int32, (groups, width, LANES), 2)
        keep = g == lane // width
        turned = [hid_ref[p].T for p in (0, 1)]
        left = jnp.concatenate(turned, axis=1)
        for dx in (-1, 0, 1):
            for dy in (-1, 0, 1):
                rows = slice((1 + dy) * deep, (1 + dy) * deep + cells)
                right = jnp.concatenate([gs_ref[1 + dx, rows, :], gs_ref[2 + dx, rows, :]], axis=0)
                dense = jnp.dot(left, right, preferred_element_type=F32)
                for j in range(3):
                    tap = 9 * (dx + 1) + 3 * (dy + 1) + j
                    block = dense[:, j * LANES : (j + 1) * LANES].reshape(groups, width, LANES)
                    thin = jnp.sum(jnp.where(keep, block, 0.0), axis=0)
                    at = slice((taps - 1 - tap) * width, (taps - tap) * width)
                    kg_ref[at] = kg_in[at] + thin
    grads = []
    for p in (0, 1):
        grad_hidden = conv_plane(gs_ref, p + 1, kb_ref, cells, deep)
        grad_pre = (grad_hidden * spre_ref[p]).astype(BF)
        branch = nt_dot(grad_pre, w_ref[...])
        if full:
            part_ref[p] = branch.astype(BF)
            grads.append(grad_pre)
        else:
            br_ref[p] = branch
    if full:
        exp_ref[...] = exp_in[...] + lax.dot_general(
            x_ref[0].reshape(2 * cells, LANES),
            jnp.concatenate(grads, axis=0),
            (((0,), (0,)), ((), ())),
            preferred_element_type=F32,
        )
    else:
        base_ref[...] = up_ref[c].astype(F32) + br_ref[c]
        other_ref[...] = br_ref[1 - c].astype(BF)


def finish_kernel(micro, count, scale, *refs):
    ins, outs = refs[: 3 * micro + count], refs[3 * micro + count : -1]
    buf = refs[-1]
    for m in range(micro):
        up, mine, other = ins[3 * m : 3 * m + 3]
        both = mine[...].astype(F32) + other[...].astype(F32)
        outs[0][m] = (up[...].astype(F32) + both).astype(BF)
    rank = lax.axis_index("space")
    for d in range(count):
        buf[lax.rem(rank + count - d, count)] = ins[3 * micro + d][...]
    total = buf[0].astype(F32)
    for d in range(1, count):
        total = total + buf[d].astype(F32)
    total = total * scale
    outs[1][...] = total[0:LANES]
    outs[2][...] = total[LANES : 2 * LANES]
    outs[3][...] = total[2 * LANES :]


def sds(shape, dtype):
    return jax.ShapeDtypeStruct(shape, dtype)


def params():
    return pltpu.CompilerParams(vmem_limit_bytes=40 * 2**20)


def cost(flops, nbytes):
    return pl.CostEstimate(flops=flops, bytes_accessed=nbytes, transcendentals=0)


def whole(shape):
    return pl.BlockSpec(shape, lambda i: (0,) * len(shape))


def picked(shape, m):
    return pl.BlockSpec((1,) + shape, lambda i: (m,) + (0,) * len(shape))


def on_device(
    section_inputs, cotangent, phase_labels, expand_weight, phase_code, kernel, reduce_weight
):
    _, micro, depth, wide, deep, trunk = section_inputs.shape
    cells = wide * deep
    taps, groups, width = kernel.shape[1], kernel.shape[2], kernel.shape[3]
    assert depth == 2 and lax.axis_size("chan") == 2
    assert trunk == LANES and groups * width == LANES
    spaces, sections = lax.axis_size("space"), lax.axis_size("section")
    scale = 1.0 / math.sqrt(micro * depth * spaces * cells)

    x = section_inputs[0].reshape(micro, depth, cells, trunk)
    ct = cotangent.reshape(micro, depth, cells, trunk)
    lab = jnp.swapaxes(phase_labels, 2, 3).astype(BF)
    lab = jnp.pad(lab, ((0, 0), (0, 0), (0, 0), (0, LANES - wide)))
    w, rw = expand_weight[0], reduce_weight[0]
    code = jnp.pad(phase_code[0], ((0, 8 - phase_code.shape[1]), (0, 0)))
    kern = kernel[0].astype(F32)
    kf = kern.transpose(0, 2, 1, 3).reshape(taps * width, LANES)
    kb = kern[::-1].transpose(0, 3, 1, 2).reshape(taps * width, LANES)

    away = [(k, c, (k + 2 * c - 1) % spaces) for k in range(spaces) for c in (0, 1)]
    back = [(k, c, (k - 2 * c + 1) % spaces) for k in range(spaces) for c in (0, 1)]
    route_a = [(2 * k + c, 2 * t + c) for k, c, t in away]
    route_b = [(2 * k + c, 2 * t + c) for k, c, t in back]
    route_d = [
        ((k * sections + s) * 2 + c, (t * sections + s - 1) * 2 + c)
        for k, c, t in away
        for s in range(1, sections)
    ]
    route_s = [(s, s - 1) for s in range(1, sections)]

    def swap(v):
        return lax.ppermute(v, "chan", [(0, 1), (1, 0)])

    packed = pl.pallas_call(
        functools.partial(pack_kernel, micro, cells, wide),
        out_shape=[
            sds((n, LANES), BF)
            for _ in range(micro)
            for n in (2 * cells + wide, cells + wide)
        ],
        name="pack",
        cost_estimate=cost(0, 4 * 2**20),
        compiler_params=params(),
    )(x, ct, lab)
    halos = []
    for m in range(micro):
        a = lax.ppermute(packed[2 * m], ("space", "chan"), route_a)
        b = lax.ppermute(packed[2 * m + 1], ("space", "chan"), route_b)
        halos.append((a, b, swap(a), swap(b)))

    dense_f, dense_b = pl.pallas_call(
        functools.partial(weights_kernel, taps, width),
        out_shape=[sds((taps * LANES, LANES), BF)] * 2,
        name="weights",
        cost_estimate=cost(0, 2 * 2**20),
        compiler_params=params(),
    )(kf, kb)

    plane2, plane4 = (2, cells, LANES), (4, cells, LANES)
    pad_rows = cells + 2 * deep
    shape_a, shape_b = (2 * cells + wide, LANES), (cells + wide, LANES)
    square, tall = (LANES, LANES), (taps * LANES, LANES)
    saved, handed = [], []
    for m in range(micro):
        a, b, a2, b2 = halos[m]
        hid, spre, sconv, mixed, base, other = pl.pallas_call(
            functools.partial(forward_kernel, wide, deep),
            grid=(1,),
            in_specs=[
                picked(plane2, m),
                picked((2, deep, LANES), m),
                whole(shape_a),
                whole(shape_b),
                whole(shape_a),
                whole(shape_b),
                picked(plane2, m),
                whole(square),
                whole((8, LANES)),
                whole(square),
                whole(tall),
                whole(tall),
            ],
            out_specs=[
                whole(plane2),
                whole(plane2),
                whole(plane4),
                whole(plane2),
                whole((cells, LANES)),
                whole((cells, LANES)),
            ],
            out_shape=[
                sds(plane2, BF),
                sds(plane2, F32),
                sds(plane4, F32),
                sds(plane2, BF),
                sds((cells, LANES), F32),
                sds((cells, LANES), BF),
            ],
            scratch_shapes=[
                pltpu.VMEM((6, pad_rows, 3 * LANES), BF),
                pltpu.VMEM((4, pad_rows, 3 * LANES), BF),
                pltpu.VMEM(plane2, F32),
            ],
            name="forward",
            cost_estimate=cost(2 * 10**9, 5 * 2**20),
            compiler_params=params(),
        )(x, lab, a, b, a2, b2, ct, w, code, rw, dense_f, dense_b)
        saved.append((hid, spre, sconv, mixed))
        handed.append((base, other))

    def hand_over(base, other):
        out = (base + swap(other).astype(F32)).astype(BF)
        st = lax.ppermute(out, "section", route_s)
        dg = lax.ppermute(out, ("space", "section", "chan"), route_d)
        return st, swap(st), dg, swap(dg)

    def back_pass(full, m, ups, sums):
        hid, spre, sconv, mixed = saved[m]
        a, _, a2, _ = halos[m]
        st, st2, dg, dg2 = ups
        flat = (cells, LANES)
        in_specs = [
            picked(plane2, m),
            picked(plane2, m),
            whole(shape_a),
            whole(shape_a),
            whole(flat),
            whole(flat),
            whole(flat),
            whole(flat),
            whole(plane2),
            whole(plane2),
            whole(plane4),
            whole(plane2),
            whole(square),
            whole(square),
            whole(tall),
        ]
        scratch = [pltpu.VMEM((4, pad_rows, 3 * LANES), BF)]
        sum_shapes = [square, square, (taps * width, LANES)]
        if full:
            out_shape = [sds(plane2, BF), sds(plane2, BF)] + [sds(s, F32) for s in sum_shapes]
            in_specs = in_specs + [whole(s) for s in sum_shapes]
        else:
            out_shape = [sds(flat, F32), sds(flat, BF)]
            scratch = scratch + [pltpu.VMEM(plane2, BF), pltpu.VMEM(plane2, F32)]
        return pl.pallas_call(
            functools.partial(backward_kernel, full, wide, deep, taps, width),
            grid=(1,),
            in_specs=in_specs,
            out_specs=[whole(s.shape) for s in out_shape],
            out_shape=out_shape,
            scratch_shapes=scratch,
            name="backward" if full else "backward_light",
            cost_estimate=cost(2 * 10**9, 5 * 2**20),
            compiler_params=params(),
        )(x, ct, a, a2, st, st2, dg, dg2, hid, spre, sconv, mixed, w, rw, dense_b, *sums)

    rank = lax.axis_index("section")
    ups = [hand_over(*handed[m]) for m in range(micro)]
    for stage in range(1, sections - 1):
        fresh = [hand_over(*back_pass(False, m, ups[m], ())) for m in range(micro)]
        mine = rank == sections - 2 - stage
        ups = [
            tuple(jnp.where(mine, n, o) for n, o in zip(fresh[m], ups[m])) for m in range(micro)
        ]
    sums = [jnp.zeros(s, F32) for s in (square, square, (taps * width, LANES))]
    pieces = []
    for m in range(micro):
        part, up, *sums = back_pass(True, m, ups[m], sums)
        pieces += [up, part, swap(part)]

    grads = jnp.concatenate([s.astype(BF) for s in sums], axis=0)
    if spaces <= 4:
        copies = [grads] + [
            lax.ppermute(grads, "space", [(k, (k + d) % spaces) for k in range(spaces)])
            for d in range(1, spaces)
        ]
    else:
        copies = [lax.psum(grads, "space")]
    rows = grads.shape[0]
    out, exp_g, red_g, kg = pl.pallas_call(
        functools.partial(finish_kernel, micro, len(copies), scale),
        out_shape=[
            sds((micro,) + plane2, BF),
            sds(square, F32),
            sds(square, F32),
            sds((taps * width, LANES), F32),
        ],
        scratch_shapes=[pltpu.VMEM((len(copies), rows, LANES), BF)],
        name="finish",
        cost_estimate=cost(10**6, 4 * 2**20),
        compiler_params=params(),
    )(*pieces, *copies)
    kg = kg.reshape(taps, width, groups, width).transpose(0, 2, 1, 3)
    return (
        out.reshape(section_inputs.shape),
        exp_g[None],
        kg[None],
        red_g[None],
    )


def solution(mesh):
    placed = (
        P("section", "parts", "space", None, None, None),
        P("parts", "space", None, None, None),
        P("parts", "space", None, None),
        P("section", None, "chan"),
        P("section", None, "chan"),
        P("section", None, "chan", None, None),
        P("section", "chan", None),
    )
    return jax.shard_map(
        on_device,
        mesh=mesh,
        in_specs=placed,
        out_specs=(
            P("section", "parts", "space", None, None, None),
            P(("parts", "section"), None, "chan"),
            P(("parts", "section"), None, "chan", None, None),
            P(("parts", "section"), "chan", None),
        ),
        check_vma=False,
    )
```

time: 1010 us -> 85.6 us (0.08); the launches traced: 995 us -> 85.1 us
  local copies, waits for them, and re-layouts: 428 us -> 15.9 us
  matrix products: 310 us -> 0 us
  other arithmetic: 135 us -> 1.12 us
  waiting for transfers between devices: 61.7 us -> 16.5 us
  Pallas kernels: 0 us -> 21.3 us
  between operations: 20.8 us -> 1.01 us
    dot_general x348 -> x0, matrix products: 310 us -> none  [the longest x108 92.1 us: block_outer(): jnp.einsum('cnk,cnl->nkl', left_split, right_split, preferred_element_typ...]
    dot_general x104 -> x0, local copies, waits for them, and re-layouts: 154 us -> none  [block_outer(): jnp.einsum('cnk,cnl->nkl', left_split, right_split, preferred_element_typ...]
    transpose x108 -> x2, local copies, waits for them, and re-layouts: 129 us -> 5.25 us  [the longest x1 2.63 us: on_device(): kf = kern.transpose(0, 2, 1, 3).reshape(taps * width, LANES)]
    add x81 -> x0, other arithmetic: 69.6 us -> none  [the longest x72 66.4 us: block_groups(): padded = padded.at[1 + step_x:1 + step_x + slab_depth, 1 + step_y:1 + ste...]
    scatter-add x84 -> x0, local copies, waits for them, and re-layouts: 62 us -> none  [the longest x76 60.4 us: block_groups(): padded = padded.at[1 + step_x:1 + step_x + slab_depth, 1 + step_y:1 + ste...]
    another operation x38 -> x1, local copies, waits for them, and re-layouts: 42.2 us -> 0.01 us
    psum x1 -> x0, waiting for transfers between devices: 34.9 us -> none  [on_device(): lax.psum(expand_acc.astype(jnp.bfloat16), 'space').astype(jnp.float32)]
    slice x38 -> x0, local copies, waits for them, and re-layouts: 24.4 us -> none  [the longest x12 6.57 us: tap_views(): padded[start_x:start_x + slab_depth, start_y:start_y + grid_wide, start_z...]
  transfers between devices with their start and end apart: 24 -> 33, of which waited for: 7 -> 8; matrix products, arithmetic and copies ran while one was open for 52% -> 13% of each run, Pallas kernels for 0% -> 21%
where the time goes in v1:
time: 85.6 us; the launch traced here: 85.1 us
  starting transfers between devices  29.3 us (34%)
  Pallas kernels  21.3 us (25%)
  waiting for transfers between devices  16.5 us (19%)
  local copies, waits for them, and re-layouts  15.9 us (19%)
  other arithmetic  1.12 us (1%)
  between operations  1.01 us (1%)
    pallas_call x3, Pallas kernels, on_device(): pl.pallas_call(functools.partial(forward_kernel, wide, deep), grid=(1,),...  12.8 us
    ppermute x3, starting transfers between devices, on_device(): a = lax.ppermute(packed[2 * m], ('space', 'chan'), route_a)  10.9 us
    ppermute x3, waiting for transfers between devices, on_device(): lax.ppermute(grads, 'space', [(k, (k + d) % spaces) for k in range(spaces)])  10.1 us
    pallas_call x3, Pallas kernels, back_pass(): pl.pallas_call(functools.partial(backward_kernel, full, wide, deep, taps,...  7.27 us
    ppermute x18, starting transfers between devices, swap(): return lax.ppermute(v, 'chan', [(0, 1), (1, 0)])  5.75 us
    unnamed x17, local copies, waits for them, and re-layouts  4.97 us
    ppermute x3, starting transfers between devices, on_device(): lax.ppermute(grads, 'space', [(k, (k + d) % spaces) for k in range(spaces)])  4.14 us
    ppermute x3, starting transfers between devices, hand_over(): st = lax.ppermute(out, 'section', route_s)  3.88 us
  transfers between devices with their start and end apart: 33, of which 8 were waited for; matrix products, arithmetic and copies ran while one was open for 13% of the time, Pallas kernels for 21%

profile of v1, /device:TPU:0, one launch (start us, length us, event | category | flops | bytes accessed | tf_op | source)
XLA Modules:
  0.0 85.1 jit_solution(2863747507115224177)
XLA Ops:
  0.6 0.9 %copy.15 = s32[3,2,16,16]{2,3,1,0:T(8,128)S(1)} copy(s32[3,2,16,16]{3,2,1,0:T(8,128)} %param.9) | data formatting | bytes 12288 | tf_op args[2]
  1.6 1.0 %copy-done = bf16[1,3,2,16,16,128]{5,4,3,2,1,0:T(8,128)(2,1)S(1)} copy-done((bf16[1,3,2,16,16,128]{5,4,3,2,1,0:T(8,128)(2,1)S(1)}, bf16[1,3,2,16,16,128]{5,4,3,2,1,0:T(8,128)(2,1)}, u32[]{:S(2)}) %copy-start) | copy-done | bytes 393240
  2.6 1.0 %copy-done.2 = bf16[3,2,16,16,128]{4,3,2,1,0:T(8,128)(2,1)S(1)} copy-done((bf16[3,2,16,16,128]{4,3,2,1,0:T(8,128)(2,1)S(1)}, bf16[3,2,16,16,128]{4,3,2,1,0:T(8,128)(2,1)}, u32[]{:S(2)}) %copy-start.2) | copy-done | bytes 393240
  3.6 5.1 %collective-permute-start = (bf16[528,128]{1,0:T(8,128)(2,1)S(1)}, bf16[528,128]{1,0:T(8,128)(2,1)S(1)}, u32[]{:S(2)}, u32[]{:S(2)}) collective-permute-start(bf16[528,128]{1,0:T(8,128)(2,1)S(1)} %get-tuple-element.49), channel_id=1, source_target_pairs={{0,12},{1,5},{4,0},{5,9},{8,4},{9,13},{12,8},{13,1},{2,14},{3,7},{... | collective-permute-start | bytes 405512 | tf_op jit(solution)/shard_map/ppermute | solution.py:340
  8.7 3.9 %collective-permute-start.10 = (bf16[528,128]{1,0:T(8,128)(2,1)S(1)}, bf16[528,128]{1,0:T(8,128)(2,1)S(1)}, u32[]{:S(2)}, u32[]{:S(2)}) collective-permute-start(bf16[528,128]{1,0:T(8,128)(2,1)S(1)} %get-tuple-element.61), channel_id=1, source_target_pairs={{0,12},{1,5},{4,0},{5,9},{8,4},{9,13},{12,8},{13,1},{2,14},{3,7},{... | collective-permute-start | bytes 405512 | tf_op jit(solution)/shard_map/ppermute | solution.py:340
  12.6 2.0 %collective-permute-start.20 = (bf16[528,128]{1,0:T(8,128)(2,1)S(1)}, bf16[528,128]{1,0:T(8,128)(2,1)S(1)}, u32[]{:S(2)}, u32[]{:S(2)}) collective-permute-start(bf16[528,128]{1,0:T(8,128)(2,1)S(1)} %get-tuple-element.74), channel_id=1, source_target_pairs={{0,12},{1,5},{4,0},{5,9},{8,4},{9,13},{12,8},{13,1},{2,14},{3,7},{... | collective-permute-start | bytes 405512 | tf_op jit(solution)/shard_map/ppermute | solution.py:340
  14.6 1.1 %collective-permute-done.2.b_ref = bf16[272,128]{1,0:T(8,128)(2,1)S(1)} collective-permute-done((bf16[272,128]{1,0:T(8,128)(2,1)S(1)}, bf16[272,128]{1,0:T(8,128)(2,1)S(1)}, u32[]{:S(2)}, u32[]{:S(2)}) %collective-permute-start.2) | collective-permute-done | bytes 69664 | tf_op jit(solution)/shard_map/ppermute | solution.py:341
  15.6 0.7 collective-permute-start.22
  16.3 0.8 collective-permute-done.12.b_ref
  17.2 0.5 collective-permute-start.1
  17.7 1.0 %bitcast_convert_fusion = (f32[27,16,8,8]{0,3,2,1:T(8,128)S(1)}, f32[27,8,16,8]{0,3,1,2:T(8,128)S(1)}) fusion(bf16[1,27,16,8,8]{1,4,3,2,0:T(8,128)(2,1)} %param.12), kind=kLoop, calls=%fused_computation | loop fusion | flops 27648 | bytes 276480 | tf_op jit(solution)/shard_map/convert_element_type | solution.py:309
  18.7 2.6 %copy.16 = f32[27,8,16,8]{3,2,1,0:T(8,128)} copy(f32[27,8,16,8]{0,3,1,2:T(8,128)S(1)} %get-tuple-element.99) | data formatting | bytes 221184 | tf_op jit(solution)/shard_map/transpose | solution.py:310
  21.4 2.3 %reshape.26.kf_ref = f32[216,128]{1,0:T(8,128)S(1)} reshape(f32[27,8,16,8]{3,2,1,0:T(8,128)} %copy.16) | data formatting | bytes 221184 | tf_op jit(solution)/shard_map/reshape | solution.py:310
  23.6 0.2 rev.3
  23.9 2.6 %copy.17 = f32[27,8,16,8]{3,2,1,0:T(8,128)} copy(f32[27,8,16,8]{0,1,3,2:T(8,128)S(1)} %bitcast.54) | data formatting | bytes 221184 | tf_op jit(solution)/shard_map/transpose | solution.py:311
  26.5 2.3 %reshape.27.kb_ref = f32[216,128]{1,0:T(8,128)S(1)} reshape(f32[27,8,16,8]{3,2,1,0:T(8,128)} %copy.17) | data formatting | bytes 221184 | tf_op jit(solution)/shard_map/reshape | solution.py:311
  28.7 0.2 weights.1
  29.0 0.5 collective-permute-start.23
  29.6 0.4 collective-permute-start.21
  30.1 4.2 %forward.3 = (bf16[2,256,128]{2,1,0:T(8,128)(2,1)S(1)}, f32[2,256,128]{2,1,0:T(8,128)S(1)}, f32[4,256,128]{2,1,0:T(8,128)S(1)}, bf16[2,256,128]{2,1,0:T(8,128)(2...) custom-call(bf16[3,2,256,128]{3,2,1,0:T(8,128)(2,1)S(1)} %bitcast.28, ...), custom_call_target="tpu_custom_call" | custom-call | flops 2000000000 | bytes 5242880 | tf_op jit(solution)/shard_map/forward/pallas_call | solution.py:359
  34.4 4.4 %forward.4 = (bf16[2,256,128]{2,1,0:T(8,128)(2,1)S(1)}, f32[2,256,128]{2,1,0:T(8,128)S(1)}, f32[4,256,128]{2,1,0:T(8,128)S(1)}, bf16[2,256,128]{2,1,0:T(8,128)(2...) custom-call(bf16[3,2,256,128]{3,2,1,0:T(8,128)(2,1)S(1)} %bitcast.29, ...), custom_call_target="tpu_custom_call" | custom-call | flops 2000000000 | bytes 5242880 | tf_op jit(solution)/shard_map/forward/pallas_call | solution.py:359
  38.8 0.5 collective-permute-start.14
  39.3 4.2 %forward.5 = (bf16[2,256,128]{2,1,0:T(8,128)(2,1)S(1)}, f32[2,256,128]{2,1,0:T(8,128)S(1)}, f32[4,256,128]{2,1,0:T(8,128)S(1)}, bf16[2,256,128]{2,1,0:T(8,128)(2...) custom-call(bf16[3,2,256,128]{3,2,1,0:T(8,128)(2,1)S(1)} %bitcast.30, ...), custom_call_target="tpu_custom_call" | custom-call | flops 2000000000 | bytes 5242880 | tf_op jit(solution)/shard_map/forward/pallas_call | solution.py:359
  43.7 1.3 %collective-permute-start.5 = (bf16[256,128]{1,0:T(8,128)(2,1)S(1)}, bf16[256,128]{1,0:T(8,128)(2,1)S(1)}, u32[]{:S(2)}, u32[]{:S(2)}) collective-permute-start(bf16[256,128]{1,0:T(8,128)(2,1)S(1)} %add_convert_fusion.2), channel_id=1, source_target_pairs={{2,0},{3,1},{6,4},{7,5},{10,8},{11,9},{14,12},{15,13},{18,16},{19,... | collective-permute-start | bytes 196616 | tf_op jit(solution)/shard_map/ppermute | solution.py:406
  45.0 1.3 %collective-permute-start.7 = (bf16[256,128]{1,0:T(8,128)(2,1)S(1)}, bf16[256,128]{1,0:T(8,128)(2,1)S(1)}, u32[]{:S(2)}, u32[]{:S(2)}) collective-permute-start(bf16[256,128]{1,0:T(8,128)(2,1)S(1)} %add_convert_fusion.2), channel_id=1, source_target_pairs={{2,12},{3,5},{6,0},{7,9},{10,4},{11,13},{14,8},{15,1},{18,28},{19,... | collective-permute-start | bytes 196616 | tf_op jit(solution)/shard_map/ppermute | solution.py:407
  46.3 1.3 %collective-permute-start.15 = (bf16[256,128]{1,0:T(8,128)(2,1)S(1)}, bf16[256,128]{1,0:T(8,128)(2,1)S(1)}, u32[]{:S(2)}, u32[]{:S(2)}) collective-permute-start(bf16[256,128]{1,0:T(8,128)(2,1)S(1)} %add_convert_fusion.1), channel_id=1, source_target_pairs={{2,0},{3,1},{6,4},{7,5},{10,8},{11,9},{14,12},{15,13},{18,16},{19,... | collective-permute-start | bytes 196616 | tf_op jit(solution)/shard_map/ppermute | solution.py:406
  47.6 1.3 %collective-permute-start.17 = (bf16[256,128]{1,0:T(8,128)(2,1)S(1)}, bf16[256,128]{1,0:T(8,128)(2,1)S(1)}, u32[]{:S(2)}, u32[]{:S(2)}) collective-permute-start(bf16[256,128]{1,0:T(8,128)(2,1)S(1)} %add_convert_fusion.1), channel_id=1, source_target_pairs={{2,12},{3,5},{6,0},{7,9},{10,4},{11,13},{14,8},{15,1},{18,28},{19,... | collective-permute-start | bytes 196616 | tf_op jit(solution)/shard_map/ppermute | solution.py:407
  49.0 1.3 %collective-permute-start.25 = (bf16[256,128]{1,0:T(8,128)(2,1)S(1)}, bf16[256,128]{1,0:T(8,128)(2,1)S(1)}, u32[]{:S(2)}, u32[]{:S(2)}) collective-permute-start(bf16[256,128]{1,0:T(8,128)(2,1)S(1)} %add_convert_fusion), channel_id=1, source_target_pairs={{2,0},{3,1},{6,4},{7,5},{10,8},{11,9},{14,12},{15,13},{18,16},{19,... | collective-permute-start | bytes 196616 | tf_op jit(solution)/shard_map/ppermute | solution.py:406
  50.3 1.3 %collective-permute-start.27 = (bf16[256,128]{1,0:T(8,128)(2,1)S(1)}, bf16[256,128]{1,0:T(8,128)(2,1)S(1)}, u32[]{:S(2)}, u32[]{:S(2)}) collective-permute-start(bf16[256,128]{1,0:T(8,128)(2,1)S(1)} %add_convert_fusion), channel_id=1, source_target_pairs={{2,12},{3,5},{6,0},{7,9},{10,4},{11,13},{14,8},{15,1},{18,28},{19,... | collective-permute-start | bytes 196616 | tf_op jit(solution)/shard_map/ppermute | solution.py:407
  51.6 0.6 collective-permute-done.7.dg_ref
  52.1 1.3 %collective-permute-start.6 = (bf16[256,128]{1,0:T(8,128)(2,1)S(1)}, bf16[256,128]{1,0:T(8,128)(2,1)S(1)}, u32[]{:S(2)}, u32[]{:S(2)}) collective-permute-start(bf16[256,128]{1,0:T(8,128)(2,1)S(1)} %collective-permute-done.5.st_ref), channel_id=1, source_target_pairs={{0,1},{1,0},{2,3},{3,2},{4,5},{5,4},{6,7},{7,6},{8,9},{9,8},{10,11... | collective-permute-start | bytes 196616 | tf_op jit(solution)/shard_map/ppermute | solution.py:325
  53.4 2.2 %collective-permute-done.15.st_ref = bf16[256,128]{1,0:T(8,128)(2,1)S(1)} collective-permute-done((bf16[256,128]{1,0:T(8,128)(2,1)S(1)}, bf16[256,128]{1,0:T(8,128)(2,1)S(1)}, u32[]{:S(2)}, u32[]{:S(2)}) %collective-permute-start.15) | collective-permute-done | bytes 65568 | tf_op jit(solution)/shard_map/ppermute | solution.py:406
  55.6 0.5 collective-permute-start.16
  56.1 1.7 %collective-permute-done.25.st_ref = bf16[256,128]{1,0:T(8,128)(2,1)S(1)} collective-permute-done((bf16[256,128]{1,0:T(8,128)(2,1)S(1)}, bf16[256,128]{1,0:T(8,128)(2,1)S(1)}, u32[]{:S(2)}, u32[]{:S(2)}) %collective-permute-start.25) | collective-permute-done | bytes 65568 | tf_op jit(solution)/shard_map/ppermute | solution.py:406
  57.8 0.9 %collective-permute-start.26 = (bf16[256,128]{1,0:T(8,128)(2,1)S(1)}, bf16[256,128]{1,0:T(8,128)(2,1)S(1)}, u32[]{:S(2)}, u32[]{:S(2)}) collective-permute-start(bf16[256,128]{1,0:T(8,128)(2,1)S(1)} %collective-permute-done.25.st_ref), channel_id=1, source_target_pairs={{0,1},{1,0},{2,3},{3,2},{4,5},{5,4},{6,7},{7,6},{8,9},{9,8},{10,11... | collective-permute-start | bytes 196616 | tf_op jit(solution)/shard_map/ppermute | solution.py:325
  58.8 2.4 %backward.3 = (bf16[2,256,128]{2,1,0:T(8,128)(2,1)S(1)}, bf16[2,256,128]{2,1,0:T(8,128)(2,1)S(1)}, f32[128,128]{1,0:T(8,128)S(1)}, f32[128,128]{1,0:T(8,128)S(1)}, f32[216,128]{1,0:T(8,128)S(1)}) custom-call(bf16[3,2,256,128]{3,2,1,0:T(8,128)(2,1)S(1)} %bitcast.31, bf16[3,2,256,128]{3,2,1,0:T(8,128)(2,1)S(1)} %bitcast.38, ...), custom_call_target="tpu_custom_call" | custom-call | flops 2000000000 | bytes 5242880 | tf_op jit(solution)/shard_map/backward/pallas_call | solution.py:440
  61.1 2.4 %backward.4 = (bf16[2,256,128]{2,1,0:T(8,128)(2,1)S(1)}, bf16[2,256,128]{2,1,0:T(8,128)(2,1)S(1)}, f32[128,128]{1,0:T(8,128)S(1)}, f32[128,128]{1,0:T(8,128)S(1)}, f32[216,128]{1,0:T(8,128)S(1)}) custom-call(bf16[3,2,256,128]{3,2,1,0:T(8,128)(2,1)S(1)} %bitcast.32, bf16[3,2,256,128]{3,2,1,0:T(8,128)(2,1)S(1)} %bitcast.39, ...), custom_call_target="tpu_custom_call" | custom-call | flops 2000000000 | bytes 5242880 | tf_op jit(solution)/shard_map/backward/pallas_call | solution.py:440
  63.5 2.6 %backward.5 = (bf16[2,256,128]{2,1,0:T(8,128)(2,1)S(1)}, bf16[2,256,128]{2,1,0:T(8,128)(2,1)S(1)}, f32[128,128]{1,0:T(8,128)S(1)}, f32[128,128]{1,0:T(8,128)S(1)}, f32[216,128]{1,0:T(8,128)S(1)}) custom-call(bf16[3,2,256,128]{3,2,1,0:T(8,128)(2,1)S(1)} %bitcast.33, bf16[3,2,256,128]{3,2,1,0:T(8,128)(2,1)S(1)} %bitcast.40, ...), custom_call_target="tpu_custom_call" | custom-call | flops 2000000000 | bytes 5242880 | tf_op jit(solution)/shard_map/backward/pallas_call | solution.py:440
  66.2 0.4 collective-permute-start.30
  66.8 0.3 collective-permute-start.19
  67.3 3.2 %collective-permute-start.31 = (bf16[472,128]{1,0:T(8,128)(2,1)S(1)}, bf16[472,128]{1,0:T(8,128)(2,1)S(1)}, u32[]{:S(2)}, u32[]{:S(2)}) collective-permute-start(bf16[472,128]{1,0:T(8,128)(2,1)S(1)} %pad_maximum_fusion.refs_9_), channel_id=1, source_target_pairs={{0,8},{4,12},{8,0},{12,4},{1,9},{5,13},{9,1},{13,5},{2,10},{6,14},... | collective-permute-start | bytes 362504 | tf_op jit(solution)/shard_map/ppermute | solution.py:469
  70.5 3.7 %collective-permute-done.30.refs_10_ = bf16[472,128]{1,0:T(8,128)(2,1)S(1)} collective-permute-done((bf16[472,128]{1,0:T(8,128)(2,1)S(1)}, bf16[472,128]{1,0:T(8,128)(2,1)S(1)}, u32[]{:S(2)}, u32[]{:S(2)}) %collective-permute-start.30) | collective-permute-done | bytes 120864 | tf_op jit(solution)/shard_map/ppermute | solution.py:469
  74.2 0.5 collective-permute-start.32
  74.6 4.3 %collective-permute-done.31.refs_11_ = bf16[472,128]{1,0:T(8,128)(2,1)S(1)} collective-permute-done((bf16[472,128]{1,0:T(8,128)(2,1)S(1)}, bf16[472,128]{1,0:T(8,128)(2,1)S(1)}, u32[]{:S(2)}, u32[]{:S(2)}) %collective-permute-start.31) | collective-permute-done | bytes 120864 | tf_op jit(solution)/shard_map/ppermute | solution.py:469
  79.0 2.1 %collective-permute-done.32.refs_12_ = bf16[472,128]{1,0:T(8,128)(2,1)S(1)} collective-permute-done((bf16[472,128]{1,0:T(8,128)(2,1)S(1)}, bf16[472,128]{1,0:T(8,128)(2,1)S(1)}, u32[]{:S(2)}, u32[]{:S(2)}) %collective-permute-start.32) | collective-permute-done | bytes 120864 | tf_op jit(solution)/shard_map/ppermute | solution.py:469
  81.1 1.0 %finish.1 = (bf16[3,2,256,128]{3,2,1,0:T(8,128)(2,1)}, f32[128,128]{1,0:T(8,128)}, f32[128,128]{1,0:T(8,128)}, f32[216,128]{1,0:T(8,128)S(1)}) custom-call(bf16[2,256,128]{2,1,0:T(8,128)(2,1)S(1)} %get-tuple-element.59.refs_0_, bf16[2,256,128]{2,1,0:T(8,128)(2,1)S(1)} %get-tuple-element.60.refs_1_, bf16[2,256,128]{2,1,0:T(8,128)(2,1)S(1)} %collective-permute-done.9.refs_2_, ...), custom_call_target="tpu_custom_call" | custom-call | flops 1000000 | bytes 4194304 | tf_op jit(solution)/shard_map/finish/pallas_call | solution.py:475
  82.1 0.9 %reshape.29 = f32[27,8,16,8]{3,2,1,0:T(8,128)S(1)} reshape(f32[216,128]{1,0:T(8,128)S(1)} %get-tuple-element.92) | data formatting | bytes 221184 | tf_op jit(solution)/shard_map/reshape | solution.py:488
  83.0 2.1 %copy.18 = f32[1,27,16,8,8]{1,4,3,2,0:T(8,128)} copy(f32[1,27,16,8,8]{4,2,3,1,0:T(8,128)S(1)} %bitcast.53) | data formatting | bytes 221184
  (63 shorter events, 1.1 us)
Async XLA Ops:
  0.6 18.1 %copy-start.6 = (f32[1,3,128]{2,0,1:T(1,128)S(1)}, f32[1,3,128]{2,0,1:T(1,128)}, u32[]{:S(2)}) copy-start(f32[1,3,128]{2,0,1:T(1,128)} %param.11) | copy-start | bytes 4612
  1.6 1.0 %copy-start = (bf16[1,3,2,16,16,128]{5,4,3,2,1,0:T(8,128)(2,1)S(1)}, bf16[1,3,2,16,16,128]{5,4,3,2,1,0:T(8,128)(2,1)}, u32[]{:S(2)}) copy-start(bf16[1,3,2,16,16,128]{5,4,3,2,1,0:T(8,128)(2,1)} %param.7) | copy-start | bytes 1179652
  2.6 1.0 %copy-start.2 = (bf16[3,2,16,16,128]{4,3,2,1,0:T(8,128)(2,1)S(1)}, bf16[3,2,16,16,128]{4,3,2,1,0:T(8,128)(2,1)}, u32[]{:S(2)}) copy-start(bf16[3,2,16,16,128]{4,3,2,1,0:T(8,128)(2,1)} %param.8) | copy-start | bytes 1179652
  3.6 13.6 %collective-permute-start = (bf16[528,128]{1,0:T(8,128)(2,1)S(1)}, bf16[528,128]{1,0:T(8,128)(2,1)S(1)}, u32[]{:S(2)}, u32[]{:S(2)}) collective-permute-start(bf16[528,128]{1,0:T(8,128)(2,1)S(1)} %get-tuple-element.49), channel_id=1, source_target_pairs={{0,12},{1,5},{4,0},{5,9},{8,4},{9,13},{12,8},{13,1},{2,14},{3,7},{... | collective-permute-start | bytes 405512 | tf_op jit(solution)/shard_map/ppermute | solution.py:340
  8.7 6.9 %collective-permute-start.2 = (bf16[272,128]{1,0:T(8,128)(2,1)S(1)}, bf16[272,128]{1,0:T(8,128)(2,1)S(1)}, u32[]{:S(2)}, u32[]{:S(2)}) collective-permute-start(bf16[272,128]{1,0:T(8,128)(2,1)S(1)} %get-tuple-element.50), channel_id=1, source_target_pairs={{0,4},{1,13},{4,8},{5,1},{8,12},{9,5},{12,0},{13,9},{2,6},{3,15},{... | collective-permute-start | bytes 208904 | tf_op jit(solution)/shard_map/ppermute | solution.py:341
  8.7 8.4 %collective-permute-start.12 = (bf16[272,128]{1,0:T(8,128)(2,1)S(1)}, bf16[272,128]{1,0:T(8,128)(2,1)S(1)}, u32[]{:S(2)}, u32[]{:S(2)}) collective-permute-start(bf16[272,128]{1,0:T(8,128)(2,1)S(1)} %get-tuple-element.62), channel_id=1, source_target_pairs={{0,4},{1,13},{4,8},{5,1},{8,12},{9,5},{12,0},{13,9},{2,6},{3,15},{... | collective-permute-start | bytes 208904 | tf_op jit(solution)/shard_map/ppermute | solution.py:341
  8.7 20.3 %collective-permute-start.10 = (bf16[528,128]{1,0:T(8,128)(2,1)S(1)}, bf16[528,128]{1,0:T(8,128)(2,1)S(1)}, u32[]{:S(2)}, u32[]{:S(2)}) collective-permute-start(bf16[528,128]{1,0:T(8,128)(2,1)S(1)} %get-tuple-element.61), channel_id=1, source_target_pairs={{0,12},{1,5},{4,0},{5,9},{8,4},{9,13},{12,8},{13,1},{2,14},{3,7},{... | collective-permute-start | bytes 405512 | tf_op jit(solution)/shard_map/ppermute | solution.py:340
  12.6 16.9 %collective-permute-start.20 = (bf16[528,128]{1,0:T(8,128)(2,1)S(1)}, bf16[528,128]{1,0:T(8,128)(2,1)S(1)}, u32[]{:S(2)}, u32[]{:S(2)}) collective-permute-start(bf16[528,128]{1,0:T(8,128)(2,1)S(1)} %get-tuple-element.74), channel_id=1, source_target_pairs={{0,12},{1,5},{4,0},{5,9},{8,4},{9,13},{12,8},{13,1},{2,14},{3,7},{... | collective-permute-start | bytes 405512 | tf_op jit(solution)/shard_map/ppermute | solution.py:340
  15.6 13.3 %collective-permute-start.22 = (bf16[272,128]{1,0:T(8,128)(2,1)S(1)}, bf16[272,128]{1,0:T(8,128)(2,1)S(1)}, u32[]{:S(2)}, u32[]{:S(2)}) collective-permute-start(bf16[272,128]{1,0:T(8,128)(2,1)S(1)} %get-tuple-element.75), channel_id=1, source_target_pairs={{0,4},{1,13},{4,8},{5,1},{8,12},{9,5},{12,0},{13,9},{2,6},{3,15},{... | collective-permute-start | bytes 208904 | tf_op jit(solution)/shard_map/ppermute | solution.py:341
  17.2 12.4 %collective-permute-start.3 = (bf16[272,128]{1,0:T(8,128)(2,1)S(1)}, bf16[272,128]{1,0:T(8,128)(2,1)S(1)}, u32[]{:S(2)}, u32[]{:S(2)}) collective-permute-start(bf16[272,128]{1,0:T(8,128)(2,1)S(1)} %collective-permute-done.2.b_ref), channel_id=1, source_target_pairs={{0,1},{1,0},{2,3},{3,2},{4,5},{5,4},{6,7},{7,6},{8,9},{9,8},{10,11... | collective-permute-start | bytes 208904 | tf_op jit(solution)/shard_map/ppermute | solution.py:325
  17.2 12.9 %collective-permute-start.1 = (bf16[528,128]{1,0:T(8,128)(2,1)S(1)}, bf16[528,128]{1,0:T(8,128)(2,1)S(1)}, u32[]{:S(2)}, u32[]{:S(2)}) collective-permute-start(bf16[528,128]{1,0:T(8,128)(2,1)S(1)} %collective-permute-done.a_ref.cta_ref), channel_id=1, source_target_pairs={{0,1},{1,0},{2,3},{3,2},{4,5},{5,4},{6,7},{7,6},{8,9},{9,8},{10,11... | collective-permute-start | bytes 405512 | tf_op jit(solution)/shard_map/ppermute | solution.py:325
  23.8 6.2 %copy-start.1 = (bf16[1,3,2,16,16,128]{5,4,3,2,1,0:T(8,128)(2,1)S(1)}, bf16[1,3,2,16,16,128]{5,4,3,2,1,0:T(8,128)(2,1)}, u32[]{:S(2)}) copy-start(bf16[1,3,2,16,16,128]{5,4,3,2,1,0:T(8,128)(2,1)} %param.7) | copy-start | bytes 1179652
  23.8 6.2 %copy-start.3 = (bf16[3,2,16,16,128]{4,3,2,1,0:T(8,128)(2,1)S(1)}, bf16[3,2,16,16,128]{4,3,2,1,0:T(8,128)(2,1)}, u32[]{:S(2)}) copy-start(bf16[3,2,16,16,128]{4,3,2,1,0:T(8,128)(2,1)} %param.8) | copy-start | bytes 1179652
  23.8 6.2 %copy-start.4 = (bf16[1,128,128]{2,1,0:T(8,128)(2,1)S(1)}, bf16[1,128,128]{2,1,0:T(8,128)(2,1)}, u32[]{:S(2)}) copy-start(bf16[1,128,128]{2,1,0:T(8,128)(2,1)} %param.10) | copy-start | bytes 98308
  23.8 6.2 %copy-start.5 = (bf16[1,128,128]{2,1,0:T(8,128)(2,1)S(1)}, bf16[1,128,128]{2,1,0:T(8,128)(2,1)}, u32[]{:S(2)}) copy-start(bf16[1,128,128]{2,1,0:T(8,128)(2,1)} %param.13) | copy-start | bytes 98308
  28.9 5.5 %collective-permute-start.13 = (bf16[272,128]{1,0:T(8,128)(2,1)S(1)}, bf16[272,128]{1,0:T(8,128)(2,1)S(1)}, u32[]{:S(2)}, u32[]{:S(2)}) collective-permute-start(bf16[272,128]{1,0:T(8,128)(2,1)S(1)} %collective-permute-done.12.b_ref), channel_id=1, source_target_pairs={{0,1},{1,0},{2,3},{3,2},{4,5},{5,4},{6,7},{7,6},{8,9},{9,8},{10,11... | collective-permute-start | bytes 208904 | tf_op jit(solution)/shard_map/ppermute | solution.py:325
  29.0 10.3 %collective-permute-start.23 = (bf16[272,128]{1,0:T(8,128)(2,1)S(1)}, bf16[272,128]{1,0:T(8,128)(2,1)S(1)}, u32[]{:S(2)}, u32[]{:S(2)}) collective-permute-start(bf16[272,128]{1,0:T(8,128)(2,1)S(1)} %collective-permute-done.22.b_ref), channel_id=1, source_target_pairs={{0,1},{1,0},{2,3},{3,2},{4,5},{5,4},{6,7},{7,6},{8,9},{9,8},{10,11... | collective-permute-start | bytes 208904 | tf_op jit(solution)/shard_map/ppermute | solution.py:325
  29.5 4.9 %collective-permute-start.11 = (bf16[528,128]{1,0:T(8,128)(2,1)S(1)}, bf16[528,128]{1,0:T(8,128)(2,1)S(1)}, u32[]{:S(2)}, u32[]{:S(2)}) collective-permute-start(bf16[528,128]{1,0:T(8,128)(2,1)S(1)} %collective-permute-done.10.a_ref.cta_ref), channel_id=1, source_target_pairs={{0,1},{1,0},{2,3},{3,2},{4,5},{5,4},{6,7},{7,6},{8,9},{9,8},{10,11... | collective-permute-start | bytes 405512 | tf_op jit(solution)/shard_map/ppermute | solution.py:325
  29.6 9.7 %collective-permute-start.21 = (bf16[528,128]{1,0:T(8,128)(2,1)S(1)}, bf16[528,128]{1,0:T(8,128)(2,1)S(1)}, u32[]{:S(2)}, u32[]{:S(2)}) collective-permute-start(bf16[528,128]{1,0:T(8,128)(2,1)S(1)} %collective-permute-done.20.a_ref.cta_ref), channel_id=1, source_target_pairs={{0,1},{1,0},{2,3},{3,2},{4,5},{5,4},{6,7},{7,6},{8,9},{9,8},{10,11... | collective-permute-start | bytes 405512 | tf_op jit(solution)/shard_map/ppermute | solution.py:325
  34.3 9.4 %collective-permute-start.4 = (bf16[256,128]{1,0:T(8,128)(2,1)S(1)}, bf16[256,128]{1,0:T(8,128)(2,1)S(1)}, u32[]{:S(2)}, u32[]{:S(2)}) collective-permute-start(bf16[256,128]{1,0:T(8,128)(2,1)S(1)} %get-tuple-element.54), channel_id=1, source_target_pairs={{0,1},{1,0},{2,3},{3,2},{4,5},{5,4},{6,7},{7,6},{8,9},{9,8},{10,11... | collective-permute-start | bytes 196616 | tf_op jit(solution)/shard_map/ppermute | solution.py:325
  38.8 7.5 %collective-permute-start.14 = (bf16[256,128]{1,0:T(8,128)(2,1)S(1)}, bf16[256,128]{1,0:T(8,128)(2,1)S(1)}, u32[]{:S(2)}, u32[]{:S(2)}) collective-permute-start(bf16[256,128]{1,0:T(8,128)(2,1)S(1)} %get-tuple-element.64), channel_id=1, source_target_pairs={{0,1},{1,0},{2,3},{3,2},{4,5},{5,4},{6,7},{7,6},{8,9},{9,8},{10,11... | collective-permute-start | bytes 196616 | tf_op jit(solution)/shard_map/ppermute | solution.py:325
  43.5 5.4 %collective-permute-start.24 = (bf16[256,128]{1,0:T(8,128)(2,1)S(1)}, bf16[256,128]{1,0:T(8,128)(2,1)S(1)}, u32[]{:S(2)}, u32[]{:S(2)}) collective-permute-start(bf16[256,128]{1,0:T(8,128)(2,1)S(1)} %get-tuple-element.77), channel_id=1, source_target_pairs={{0,1},{1,0},{2,3},{3,2},{4,5},{5,4},{6,7},{7,6},{8,9},{9,8},{10,11... | collective-permute-start | bytes 196616 | tf_op jit(solution)/shard_map/ppermute | solution.py:325
  43.7 6.6 %collective-permute-start.5 = (bf16[256,128]{1,0:T(8,128)(2,1)S(1)}, bf16[256,128]{1,0:T(8,128)(2,1)S(1)}, u32[]{:S(2)}, u32[]{:S(2)}) collective-permute-start(bf16[256,128]{1,0:T(8,128)(2,1)S(1)} %add_convert_fusion.2), channel_id=1, source_target_pairs={{2,0},{3,1},{6,4},{7,5},{10,8},{11,9},{14,12},{15,13},{18,16},{19,... | collective-permute-start | bytes 196616 | tf_op jit(solution)/shard_map/ppermute | solution.py:406
  45.0 7.1 %collective-permute-start.7 = (bf16[256,128]{1,0:T(8,128)(2,1)S(1)}, bf16[256,128]{1,0:T(8,128)(2,1)S(1)}, u32[]{:S(2)}, u32[]{:S(2)}) collective-permute-start(bf16[256,128]{1,0:T(8,128)(2,1)S(1)} %add_convert_fusion.2), channel_id=1, source_target_pairs={{2,12},{3,5},{6,0},{7,9},{10,4},{11,13},{14,8},{15,1},{18,28},{19,... | collective-permute-start | bytes 196616 | tf_op jit(solution)/shard_map/ppermute | solution.py:407
  46.3 9.2 %collective-permute-start.15 = (bf16[256,128]{1,0:T(8,128)(2,1)S(1)}, bf16[256,128]{1,0:T(8,128)(2,1)S(1)}, u32[]{:S(2)}, u32[]{:S(2)}) collective-permute-start(bf16[256,128]{1,0:T(8,128)(2,1)S(1)} %add_convert_fusion.1), channel_id=1, source_target_pairs={{2,0},{3,1},{6,4},{7,5},{10,8},{11,9},{14,12},{15,13},{18,16},{19,... | collective-permute-start | bytes 196616 | tf_op jit(solution)/shard_map/ppermute | solution.py:406
  47.6 8.0 %collective-permute-start.17 = (bf16[256,128]{1,0:T(8,128)(2,1)S(1)}, bf16[256,128]{1,0:T(8,128)(2,1)S(1)}, u32[]{:S(2)}, u32[]{:S(2)}) collective-permute-start(bf16[256,128]{1,0:T(8,128)(2,1)S(1)} %add_convert_fusion.1), channel_id=1, source_target_pairs={{2,12},{3,5},{6,0},{7,9},{10,4},{11,13},{14,8},{15,1},{18,28},{19,... | collective-permute-start | bytes 196616 | tf_op jit(solution)/shard_map/ppermute | solution.py:407
  49.0 8.8 %collective-permute-start.25 = (bf16[256,128]{1,0:T(8,128)(2,1)S(1)}, bf16[256,128]{1,0:T(8,128)(2,1)S(1)}, u32[]{:S(2)}, u32[]{:S(2)}) collective-permute-start(bf16[256,128]{1,0:T(8,128)(2,1)S(1)} %add_convert_fusion), channel_id=1, source_target_pairs={{2,0},{3,1},{6,4},{7,5},{10,8},{11,9},{14,12},{15,13},{18,16},{19,... | collective-permute-start | bytes 196616 | tf_op jit(solution)/shard_map/ppermute | solution.py:406
  50.3 7.5 %collective-permute-start.27 = (bf16[256,128]{1,0:T(8,128)(2,1)S(1)}, bf16[256,128]{1,0:T(8,128)(2,1)S(1)}, u32[]{:S(2)}, u32[]{:S(2)}) collective-permute-start(bf16[256,128]{1,0:T(8,128)(2,1)S(1)} %add_convert_fusion), channel_id=1, source_target_pairs={{2,12},{3,5},{6,0},{7,9},{10,4},{11,13},{14,8},{15,1},{18,28},{19,... | collective-permute-start | bytes 196616 | tf_op jit(solution)/shard_map/ppermute | solution.py:407
  52.1 6.6 %collective-permute-start.6 = (bf16[256,128]{1,0:T(8,128)(2,1)S(1)}, bf16[256,128]{1,0:T(8,128)(2,1)S(1)}, u32[]{:S(2)}, u32[]{:S(2)}) collective-permute-start(bf16[256,128]{1,0:T(8,128)(2,1)S(1)} %collective-permute-done.5.st_ref), channel_id=1, source_target_pairs={{0,1},{1,0},{2,3},{3,2},{4,5},{5,4},{6,7},{7,6},{8,9},{9,8},{10,11... | collective-permute-start | bytes 196616 | tf_op jit(solution)/shard_map/ppermute | solution.py:325
  55.6 3.1 %collective-permute-start.8 = (bf16[256,128]{1,0:T(8,128)(2,1)S(1)}, bf16[256,128]{1,0:T(8,128)(2,1)S(1)}, u32[]{:S(2)}, u32[]{:S(2)}) collective-permute-start(bf16[256,128]{1,0:T(8,128)(2,1)S(1)} %collective-permute-done.7.dg_ref), channel_id=1, source_target_pairs={{0,1},{1,0},{2,3},{3,2},{4,5},{5,4},{6,7},{7,6},{8,9},{9,8},{10,11... | collective-permute-start | bytes 196616 | tf_op jit(solution)/shard_map/ppermute | solution.py:325
  55.6 5.5 %collective-permute-start.16 = (bf16[256,128]{1,0:T(8,128)(2,1)S(1)}, bf16[256,128]{1,0:T(8,128)(2,1)S(1)}, u32[]{:S(2)}, u32[]{:S(2)}) collective-permute-start(bf16[256,128]{1,0:T(8,128)(2,1)S(1)} %collective-permute-done.15.st_ref), channel_id=1, source_target_pairs={{0,1},{1,0},{2,3},{3,2},{4,5},{5,4},{6,7},{7,6},{8,9},{9,8},{10,11... | collective-permute-start | bytes 196616 | tf_op jit(solution)/shard_map/ppermute | solution.py:325
  57.8 3.3 %collective-permute-start.18 = (bf16[256,128]{1,0:T(8,128)(2,1)S(1)}, bf16[256,128]{1,0:T(8,128)(2,1)S(1)}, u32[]{:S(2)}, u32[]{:S(2)}) collective-permute-start(bf16[256,128]{1,0:T(8,128)(2,1)S(1)} %collective-permute-done.17.dg_ref), channel_id=1, source_target_pairs={{0,1},{1,0},{2,3},{3,2},{4,5},{5,4},{6,7},{7,6},{8,9},{9,8},{10,11... | collective-permute-start | bytes 196616 | tf_op jit(solution)/shard_map/ppermute | solution.py:325
  57.8 5.7 %collective-permute-start.26 = (bf16[256,128]{1,0:T(8,128)(2,1)S(1)}, bf16[256,128]{1,0:T(8,128)(2,1)S(1)}, u32[]{:S(2)}, u32[]{:S(2)}) collective-permute-start(bf16[256,128]{1,0:T(8,128)(2,1)S(1)} %collective-permute-done.25.st_ref), channel_id=1, source_target_pairs={{0,1},{1,0},{2,3},{3,2},{4,5},{5,4},{6,7},{7,6},{8,9},{9,8},{10,11... | collective-permute-start | bytes 196616 | tf_op jit(solution)/shard_map/ppermute | solution.py:325
  58.7 4.8 %collective-permute-start.28 = (bf16[256,128]{1,0:T(8,128)(2,1)S(1)}, bf16[256,128]{1,0:T(8,128)(2,1)S(1)}, u32[]{:S(2)}, u32[]{:S(2)}) collective-permute-start(bf16[256,128]{1,0:T(8,128)(2,1)S(1)} %collective-permute-done.27.dg_ref), channel_id=1, source_target_pairs={{0,1},{1,0},{2,3},{3,2},{4,5},{5,4},{6,7},{7,6},{8,9},{9,8},{10,11... | collective-permute-start | bytes 196616 | tf_op jit(solution)/shard_map/ppermute | solution.py:325
  66.2 8.0 %collective-permute-start.30 = (bf16[472,128]{1,0:T(8,128)(2,1)S(1)}, bf16[472,128]{1,0:T(8,128)(2,1)S(1)}, u32[]{:S(2)}, u32[]{:S(2)}) collective-permute-start(bf16[472,128]{1,0:T(8,128)(2,1)S(1)} %pad_maximum_fusion.refs_9_), channel_id=1, source_target_pairs={{0,4},{4,8},{8,12},{12,0},{1,5},{5,9},{9,13},{13,1},{2,6},{6,10},{... | collective-permute-start | bytes 362504 | tf_op jit(solution)/shard_map/ppermute | solution.py:469
  66.6 14.5 %collective-permute-start.9 = (bf16[2,256,128]{2,1,0:T(8,128)(2,1)S(1)}, bf16[2,256,128]{2,1,0:T(8,128)(2,1)S(1)}, u32[]{:S(2)}, u32[]{:S(2)}) collective-permute-start(bf16[2,256,128]{2,1,0:T(8,128)(2,1)S(1)} %get-tuple-element.60.refs_1_), channel_id=1, source_target_pairs={{0,1},{1,0},{2,3},{3,2},{4,5},{5,4},{6,7},{7,6},{8,9},{9,8},{10,11... | collective-permute-start | bytes 393224 | tf_op jit(solution)/shard_map/ppermute | solution.py:325
  66.8 14.3 %collective-permute-start.19 = (bf16[2,256,128]{2,1,0:T(8,128)(2,1)S(1)}, bf16[2,256,128]{2,1,0:T(8,128)(2,1)S(1)}, u32[]{:S(2)}, u32[]{:S(2)}) collective-permute-start(bf16[2,256,128]{2,1,0:T(8,128)(2,1)S(1)} %get-tuple-element.73.refs_4_), channel_id=1, source_target_pairs={{0,1},{1,0},{2,3},{3,2},{4,5},{5,4},{6,7},{7,6},{8,9},{9,8},{10,11... | collective-permute-start | bytes 393224 | tf_op jit(solution)/shard_map/ppermute | solution.py:325
  67.1 14.0 %collective-permute-start.29 = (bf16[2,256,128]{2,1,0:T(8,128)(2,1)S(1)}, bf16[2,256,128]{2,1,0:T(8,128)(2,1)S(1)}, u32[]{:S(2)}, u32[]{:S(2)}) collective-permute-start(bf16[2,256,128]{2,1,0:T(8,128)(2,1)S(1)} %get-tuple-element.86.refs_7_), channel_id=1, source_target_pairs={{0,1},{1,0},{2,3},{3,2},{4,5},{5,4},{6,7},{7,6},{8,9},{9,8},{10,11... | collective-permute-start | bytes 393224 | tf_op jit(solution)/shard_map/ppermute | solution.py:325
  67.3 11.7 %collective-permute-start.31 = (bf16[472,128]{1,0:T(8,128)(2,1)S(1)}, bf16[472,128]{1,0:T(8,128)(2,1)S(1)}, u32[]{:S(2)}, u32[]{:S(2)}) collective-permute-start(bf16[472,128]{1,0:T(8,128)(2,1)S(1)} %pad_maximum_fusion.refs_9_), channel_id=1, source_target_pairs={{0,8},{4,12},{8,0},{12,4},{1,9},{5,13},{9,1},{13,5},{2,10},{6,14},... | collective-permute-start | bytes 362504 | tf_op jit(solution)/shard_map/ppermute | solution.py:469
  74.2 6.9 %collective-permute-start.32 = (bf16[472,128]{1,0:T(8,128)(2,1)S(1)}, bf16[472,128]{1,0:T(8,128)(2,1)S(1)}, u32[]{:S(2)}, u32[]{:S(2)}) collective-permute-start(bf16[472,128]{1,0:T(8,128)(2,1)S(1)} %pad_maximum_fusion.refs_9_), channel_id=1, source_target_pairs={{0,12},{4,0},{8,4},{12,8},{1,13},{5,1},{9,5},{13,9},{2,14},{6,2},{... | collective-permute-start | bytes 362504 | tf_op jit(solution)/shard_map/ppermute | solution.py:469

commit v2 on v1

--- a/solution.py
+++ b/solution.py
@@ -50,29 +50,63 @@
     return jnp.dot(rows, weights[...], preferred_element_type=F32)
 
 
-def pack_kernel(micro, cells, wide, x_ref, ct_ref, lab_ref, *outs):
+def pack_kernel(micro, cells, wide, x_ref, ct_ref, lab_ref, *rest):
+    outs, own_ref, sem = rest[: 2 * micro], rest[2 * micro], rest[2 * micro + 1]
     c = lax.axis_index("chan")
+    copies = []
     for m in range(micro):
         a_ref, b_ref = outs[2 * m], outs[2 * m + 1]
-        x = x_ref[m, c]
-        lab = lab_ref[m, c]
-        a_ref[0:cells] = x
-        a_ref[cells : cells + wide] = lab
-        a_ref[cells + wide : 2 * cells + wide] = ct_ref[m, c]
-        b_ref[0:cells] = x
-        b_ref[cells : cells + wide] = lab
-
-
-def weights_kernel(taps, width, kf_ref, kb_ref, f_ref, b_ref):
+        moves = (
+            (x_ref.at[m, c], a_ref.at[0:cells]),
+            (x_ref.at[m, c], b_ref.at[0:cells]),
+            (ct_ref.at[m, c], a_ref.at[cells + wide : 2 * cells + wide]),
+        )
+        for n, (src, dst) in enumerate(moves):
+            copy = pltpu.make_async_copy(src, dst, sem.at[3 * m + n])
+            copy.start()
+            copies.append(copy)
+    deep = lab_ref.shape[3]
+    row = lax.broadcasted_iota(jnp.int32, (LANES, LANES), 0)
+    lane = lax.broadcasted_iota(jnp.int32, (LANES, LANES), 1)
+    eye = jnp.where(row == lane, 1.0, 0.0)[:deep, :deep].astype(BF)
+    for m in range(micro):
+        for p in range(2):
+            own_ref[m, p] = jnp.zeros((deep, LANES), BF)
+            turned = nt_dot(eye, lab_ref[m, p].astype(F32).astype(BF))
+            own_ref[m, p, :, 0:wide] = turned.astype(BF)
+        lab = own_ref[m, c]
+        outs[2 * m][cells : cells + wide] = lab
+        outs[2 * m + 1][cells : cells + wide] = lab
+    for copy in copies:
+        copy.wait()
+
+
+def diagonal_mask(width):
     groups = LANES // width
     g = lax.broadcasted_iota(jnp.int32, (groups, width, LANES), 0)
     lane = lax.broadcasted_iota(jnp.int32, (groups, width, LANES), 2)
-    keep = g == lane // width
-    for src, dst in ((kf_ref, f_ref), (kb_ref, b_ref)):
+    return g == lane // width
+
+
+def weights_kernel(taps, width, k_ref, f_ref, b_ref, flat_ref, thin_ref):
+    groups = LANES // width
+    keep = diagonal_mask(width)
+    flat_ref[:, 0:taps] = k_ref[...].astype(F32).reshape(groups * width * width, taps)
+    for i in range(width):
+        rows = [
+            flat_ref[(g * width + i) * width : (g * width + i + 1) * width, :]
+            for g in range(groups)
+        ]
+        turned = jnp.concatenate(rows, axis=0).T
+        thin_ref[0, pl.ds(i, taps, stride=width), :] = turned[:taps]
+        turned = flat_ref[pl.ds(i, LANES, stride=width), :].T
+        thin_ref[1, pl.ds(i, taps, stride=width), :] = turned[:taps]
+    for n, dst in enumerate((f_ref, b_ref)):
         for t in range(taps):
-            one = src[t * width : (t + 1) * width, :]
+            one = thin_ref[n, t * width : (t + 1) * width, :]
             full = jnp.where(keep, jnp.broadcast_to(one[None], keep.shape), 0.0)
-            dst[t * LANES : (t + 1) * LANES, :] = full.reshape(LANES, LANES).astype(BF)
+            at = t if n == 0 else taps - 1 - t
+            dst[at * LANES : (at + 1) * LANES, :] = full.reshape(LANES, LANES).astype(BF)
 
 
 def forward_kernel(
@@ -212,9 +246,7 @@
         )
         red_ref[...] = red_in[...] + red
         groups = LANES // width
-        g = lax.broadcasted_iota(jnp.int32, (groups, width, LANES), 0)
-        lane = lax.broadcasted_iota(jnp.int32, (groups, width, LANES), 2)
-        keep = g == lane // width
+        keep = diagonal_mask(width)
         turned = [hid_ref[p].T for p in (0, 1)]
         left = jnp.concatenate(turned, axis=1)
         for dx in (-1, 0, 1):
@@ -250,23 +282,29 @@
         other_ref[...] = br_ref[1 - c].astype(BF)
 
 
-def finish_kernel(micro, count, scale, *refs):
-    ins, outs = refs[: 3 * micro + count], refs[3 * micro + count : -1]
-    buf = refs[-1]
+def emit_kernel(micro, *refs):
+    ins, out_ref = refs[:-1], refs[-1]
     for m in range(micro):
         up, mine, other = ins[3 * m : 3 * m + 3]
         both = mine[...].astype(F32) + other[...].astype(F32)
-        outs[0][m] = (up[...].astype(F32) + both).astype(BF)
+        out_ref[m] = (up[...].astype(F32) + both).astype(BF)
+
+
+def finish_kernel(count, scale, taps, width, *refs):
+    ins, outs, buf, thin_ref = refs[:count], refs[count:-2], refs[-2], refs[-1]
     rank = lax.axis_index("space")
     for d in range(count):
-        buf[lax.rem(rank + count - d, count)] = ins[3 * micro + d][...]
+        buf[lax.rem(rank + count - d, count)] = ins[d][...]
     total = buf[0].astype(F32)
     for d in range(1, count):
         total = total + buf[d].astype(F32)
     total = total * scale
-    outs[1][...] = total[0:LANES]
-    outs[2][...] = total[LANES : 2 * LANES]
-    outs[3][...] = total[2 * LANES :]
+    outs[0][...] = total[0:LANES]
+    outs[1][...] = total[LANES : 2 * LANES]
+    thin_ref[0 : taps * width] = total[2 * LANES :]
+    for i in range(width):
+        turned = thin_ref[pl.ds(i, LANES, stride=width), :].T
+        outs[2][:, i] = turned[:, :taps].reshape(LANES // width, width, taps)
 
 
 def sds(shape, dtype):
@@ -302,60 +340,77 @@
 
     x = section_inputs[0].reshape(micro, depth, cells, trunk)
     ct = cotangent.reshape(micro, depth, cells, trunk)
-    lab = jnp.swapaxes(phase_labels, 2, 3).astype(BF)
-    lab = jnp.pad(lab, ((0, 0), (0, 0), (0, 0), (0, LANES - wide)))
     w, rw = expand_weight[0], reduce_weight[0]
     code = jnp.pad(phase_code[0], ((0, 8 - phase_code.shape[1]), (0, 0)))
-    kern = kernel[0].astype(F32)
-    kf = kern.transpose(0, 2, 1, 3).reshape(taps * width, LANES)
-    kb = kern[::-1].transpose(0, 3, 1, 2).reshape(taps * width, LANES)
+    kern = kernel[0].transpose(1, 2, 3, 0)
 
     away = [(k, c, (k + 2 * c - 1) % spaces) for k in range(spaces) for c in (0, 1)]
     back = [(k, c, (k - 2 * c + 1) % spaces) for k in range(spaces) for c in (0, 1)]
     route_a = [(2 * k + c, 2 * t + c) for k, c, t in away]
     route_b = [(2 * k + c, 2 * t + c) for k, c, t in back]
     route_d = [
-        ((k * sections + s) * 2 + c, (t * sections + s - 1) * 2 + c)
+        ((k * sections + s) * 2 + c, (t * sections + (s - 1) % sections) * 2 + c)
         for k, c, t in away
-        for s in range(1, sections)
+        for s in range(sections)
     ]
-    route_s = [(s, s - 1) for s in range(1, sections)]
+    route_s = [(s, (s - 1) % sections) for s in range(sections)]
 
     def swap(v):
         return lax.ppermute(v, "chan", [(0, 1), (1, 0)])
 
-    packed = pl.pallas_call(
+    rows_a, rows_b = 2 * cells + wide, cells + wide
+    hbm = pl.BlockSpec(memory_space=pl.ANY)
+    vmem = pl.BlockSpec(memory_space=pltpu.VMEM)
+    *packed, lab = pl.pallas_call(
         functools.partial(pack_kernel, micro, cells, wide),
-        out_shape=[
-            sds((n, LANES), BF)
-            for _ in range(micro)
-            for n in (2 * cells + wide, cells + wide)
-        ],
+        in_specs=[hbm, hbm, vmem],
+        out_specs=[vmem] * (2 * micro + 1),
+        out_shape=[sds((n, LANES), BF) for _ in range(micro) for n in (rows_a, rows_b)]
+        + [sds((micro, depth, deep, LANES), BF)],
+        scratch_shapes=[pltpu.SemaphoreType.DMA((3 * micro,))],
         name="pack",
         cost_estimate=cost(0, 4 * 2**20),
         compiler_params=params(),
-    )(x, ct, lab)
+    )(x, ct, phase_labels)
+    dense_f, dense_b = pl.pallas_call(
+        functools.partial(weights_kernel, taps, width),
+        out_shape=[sds((taps * LANES, LANES), BF)] * 2,
+        scratch_shapes=[
+            pltpu.VMEM((LANES * width, LANES), F32),
+            pltpu.VMEM((2, taps * width, LANES), F32),
+        ],
+        name="weights",
+        cost_estimate=cost(0, 2 * 2**20),
+        compiler_params=params(),
+    )(kern)
     halos = []
     for m in range(micro):
         a = lax.ppermute(packed[2 * m], ("space", "chan"), route_a)
         b = lax.ppermute(packed[2 * m + 1], ("space", "chan"), route_b)
+        if m == 0:
+            a, b, dense_f, dense_b = lax.optimization_barrier((a, b, dense_f, dense_b))
         halos.append((a, b, swap(a), swap(b)))
-
-    dense_f, dense_b = pl.pallas_call(
-        functools.partial(weights_kernel, taps, width),
-        out_shape=[sds((taps * LANES, LANES), BF)] * 2,
-        name="weights",
-        cost_estimate=cost(0, 2 * 2**20),
-        compiler_params=params(),
-    )(kf, kb)
 
     plane2, plane4 = (2, cells, LANES), (4, cells, LANES)
     pad_rows = cells + 2 * deep
     shape_a, shape_b = (2 * cells + wide, LANES), (cells + wide, LANES)
     square, tall = (LANES, LANES), (taps * LANES, LANES)
-    saved, handed = [], []
+    saved, ups, waiting = [], [], []
+
+    def joined(base, other):
+        return (base + swap(other).astype(F32)).astype(BF)
+
+    def send_on(out):
+        st = lax.ppermute(out, "section", route_s)
+        dg = lax.ppermute(out, ("space", "section", "chan"), route_d)
+        return st, swap(st), dg, swap(dg)
+
     for m in range(micro):
         a, b, a2, b2 = halos[m]
+        if m >= 2:
+            out = joined(*waiting.pop(0))
+            out, code = lax.optimization_barrier((out, code))
+            ups.append(send_on(out))
         hid, spre, sconv, mixed, base, other = pl.pallas_call(
             functools.partial(forward_kernel, wide, deep),
             grid=(1,),
@@ -399,13 +454,8 @@
             compiler_params=params(),
         )(x, lab, a, b, a2, b2, ct, w, code, rw, dense_f, dense_b)
         saved.append((hid, spre, sconv, mixed))
-        handed.append((base, other))
-
-    def hand_over(base, other):
-        out = (base + swap(other).astype(F32)).astype(BF)
-        st = lax.ppermute(out, "section", route_s)
-        dg = lax.ppermute(out, ("space", "section", "chan"), route_d)
-        return st, swap(st), dg, swap(dg)
+        waiting.append((base, other))
+    ups += [send_on(joined(*pair)) for pair in waiting]
 
     def back_pass(full, m, ups, sums):
         hid, spre, sconv, mixed = saved[m]
@@ -450,9 +500,8 @@
         )(x, ct, a, a2, st, st2, dg, dg2, hid, spre, sconv, mixed, w, rw, dense_b, *sums)
 
     rank = lax.axis_index("section")
-    ups = [hand_over(*handed[m]) for m in range(micro)]
     for stage in range(1, sections - 1):
-        fresh = [hand_over(*back_pass(False, m, ups[m], ())) for m in range(micro)]
+        fresh = [send_on(joined(*back_pass(False, m, ups[m], ()))) for m in range(micro)]
         mine = rank == sections - 2 - stage
         ups = [
             tuple(jnp.where(mine, n, o) for n, o in zip(fresh[m], ups[m])) for m in range(micro)
@@ -471,21 +520,29 @@
         ]
     else:
         copies = [lax.psum(grads, "space")]
-    rows = grads.shape[0]
-    out, exp_g, red_g, kg = pl.pallas_call(
-        functools.partial(finish_kernel, micro, len(copies), scale),
+    out = pl.pallas_call(
+        functools.partial(emit_kernel, micro),
+        out_shape=sds((micro,) + plane2, BF),
+        name="emit",
+        cost_estimate=cost(10**6, 4 * 2**20),
+        compiler_params=params(),
+    )(*pieces)
+    exp_g, red_g, kg = pl.pallas_call(
+        functools.partial(finish_kernel, len(copies), scale, taps, width),
         out_shape=[
-            sds((micro,) + plane2, BF),
             sds(square, F32),
             sds(square, F32),
-            sds((taps * width, LANES), F32),
+            sds((groups, width, width, taps), F32),
         ],
-        scratch_shapes=[pltpu.VMEM((len(copies), rows, LANES), BF)],
+        scratch_shapes=[
+            pltpu.VMEM((len(copies),) + grads.shape, BF),
+            pltpu.VMEM((LANES * width, LANES), F32),
+        ],
         name="finish",
         cost_estimate=cost(10**6, 4 * 2**20),
         compiler_params=params(),
-    )(*pieces, *copies)
-    kg = kg.reshape(taps, width, groups, width).transpose(0, 2, 1, 3)
+    )(*copies)
+    kg = kg.transpose(3, 0, 1, 2)
     return (
         out.reshape(section_inputs.shape),
         exp_g[None],

time: 85.6 us -> 75.6 us (0.88)
  local copies, waits for them, and re-layouts: 15.9 us -> 3.78 us
  Pallas kernels: 21.3 us -> 23.2 us
  starting transfers between devices: 29.3 us -> 30.6 us
  other arithmetic: 1.12 us -> 0.09 us
    reshape x3 -> x0, local copies, waits for them, and re-layouts: 5.44 us -> none  [the longest x1 2.25 us: on_device(): kf = kern.transpose(0, 2, 1, 3).reshape(taps * width, LANES)]
    transpose x2 -> x0, local copies, waits for them, and re-layouts: 5.25 us -> none  [the longest x1 2.63 us: on_device(): kf = kern.transpose(0, 2, 1, 3).reshape(taps * width, LANES)]
    ppermute x3, waiting for transfers between devices: 1.89 us -> 6.35 us  [on_device(): b = lax.ppermute(packed[2 * m + 1], ('space', 'chan'), route_b)]
    ppermute x6, starting transfers between devices: 7.75 us -> 10 us  [the longest x3 5.33 us: send_on(): dg = lax.ppermute(out, ('space', 'section', 'chan'), route_d)]
    ppermute x6, waiting for transfers between devices: 4.43 us -> 2.3 us  [the longest x3 1.19 us: send_on(): st = lax.ppermute(out, 'section', route_s)]
    ppermute x3, waiting for transfers between devices: 10.1 us -> 8.01 us  [on_device(): lax.ppermute(grads, 'space', [(k, (k + d) % spaces) for k in range(spaces)])]
    pallas_call x2 -> x3, Pallas kernels: 1.08 us -> 2.96 us  [the longest x1 1.09 us: on_device(): pl.pallas_call(functools.partial(finish_kernel, len(copies), scale, taps,...]
    ppermute x18, starting transfers between devices: 5.75 us -> 4.26 us  [swap(): return lax.ppermute(v, 'chan', [(0, 1), (1, 0)])]
  transfers between devices with their start and end apart: 33 -> 33, of which waited for: 8 -> 7; matrix products, arithmetic and copies ran while one was open for 13% -> 0% of each run, Pallas kernels for 21% -> 25%
where the time goes in v2:
time: 75.6 us; the launch traced here: 75.3 us
  starting transfers between devices  30.6 us (40%)
  Pallas kernels  23.2 us (31%)
  waiting for transfers between devices  16.7 us (22%)
  local copies, waits for them, and re-layouts  3.78 us (5%)
  between operations  0.9 us (1%)
    pallas_call x3, Pallas kernels, on_device(): pl.pallas_call(functools.partial(forward_kernel, wide, deep), grid=(1,),...  12.6 us
    ppermute x3, starting transfers between devices, on_device(): a = lax.ppermute(packed[2 * m], ('space', 'chan'), route_a)  10.9 us
    ppermute x3, waiting for transfers between devices, on_device(): lax.ppermute(grads, 'space', [(k, (k + d) % spaces) for k in range(spaces)])  8.01 us
    pallas_call x3, Pallas kernels, back_pass(): pl.pallas_call(functools.partial(backward_kernel, full, wide, deep, taps,...  7.12 us
    ppermute x3, waiting for transfers between devices, on_device(): b = lax.ppermute(packed[2 * m + 1], ('space', 'chan'), route_b)  6.35 us
    ppermute x3, starting transfers between devices, send_on(): dg = lax.ppermute(out, ('space', 'section', 'chan'), route_d)  5.33 us
    ppermute x3, starting transfers between devices, on_device(): lax.ppermute(grads, 'space', [(k, (k + d) % spaces) for k in range(spaces)])  5.17 us
    ppermute x3, starting transfers between devices, send_on(): st = lax.ppermute(out, 'section', route_s)  4.67 us
  transfers between devices with their start and end apart: 33, of which 7 were waited for; matrix products, arithmetic and copies ran while one was open for 0% of the time, Pallas kernels for 25%

profile of v2, /device:TPU:0, one launch (start us, length us, event | category | flops | bytes accessed | tf_op | source)
XLA Modules:
  0.0 75.3 jit_solution(7973481446613870193)
XLA Ops:
  0.6 1.0 %copy-done = bf16[1,3,2,16,16,128]{5,4,3,2,1,0:T(8,128)(2,1)S(1)} copy-done((bf16[1,3,2,16,16,128]{5,4,3,2,1,0:T(8,128)(2,1)S(1)}, bf16[1,3,2,16,16,128]{5,4,3,2,1,0:T(8,128)(2,1)}, u32[]{:S(2)}) %copy-start) | copy-done | bytes 393240
  1.6 1.0 %copy-done.2 = bf16[3,2,16,16,128]{4,3,2,1,0:T(8,128)(2,1)S(1)} copy-done((bf16[3,2,16,16,128]{4,3,2,1,0:T(8,128)(2,1)S(1)}, bf16[3,2,16,16,128]{4,3,2,1,0:T(8,128)(2,1)}, u32[]{:S(2)}) %copy-start.2) | copy-done | bytes 393240
  2.6 0.8 %copy-done.5 = s32[3,2,16,16]{3,2,1,0:T(8,128)S(1)} copy-done((s32[3,2,16,16]{3,2,1,0:T(8,128)S(1)}, s32[3,2,16,16]{3,2,1,0:T(8,128)}, u32[]{:S(2)}) %copy-start.5) | copy-done | bytes 6168
  3.4 1.0 %pack.1 = (bf16[528,128]{1,0:T(8,128)(2,1)S(1)}, bf16[272,128]{1,0:T(8,128)(2,1)S(1)}, bf16[528,128]{1,0:T(8,128)(2,1)S(1)}, bf16[272,128]{1,0:T(8,128)(2,1)S(1)...) custom-call(bf16[3,2,256,128]{3,2,1,0:T(8,128)(2,1)S(1)} %bitcast.16, ...), custom_call_target="tpu_custom_call" | custom-call | bytes 4194304 | tf_op jit(solution)/shard_map/pack/pallas_call | solution.py:364
  4.4 5.1 %collective-permute-start = (bf16[528,128]{1,0:T(8,128)(2,1)S(1)}, bf16[528,128]{1,0:T(8,128)(2,1)S(1)}, u32[]{:S(2)}, u32[]{:S(2)}) collective-permute-start(bf16[528,128]{1,0:T(8,128)(2,1)S(1)} %get-tuple-element.55), channel_id=1, source_target_pairs={{0,12},{1,5},{4,0},{5,9},{8,4},{9,13},{12,8},{13,1},{2,14},{3,7},{... | collective-permute-start | bytes 405512 | tf_op jit(solution)/shard_map/ppermute | solution.py:388
  9.5 3.9 %collective-permute-start.10 = (bf16[528,128]{1,0:T(8,128)(2,1)S(1)}, bf16[528,128]{1,0:T(8,128)(2,1)S(1)}, u32[]{:S(2)}, u32[]{:S(2)}) collective-permute-start(bf16[528,128]{1,0:T(8,128)(2,1)S(1)} %get-tuple-element.73), channel_id=1, source_target_pairs={{0,12},{1,5},{4,0},{5,9},{8,4},{9,13},{12,8},{13,1},{2,14},{3,7},{... | collective-permute-start | bytes 405512 | tf_op jit(solution)/shard_map/ppermute | solution.py:388
  13.4 2.0 %collective-permute-start.20 = (bf16[528,128]{1,0:T(8,128)(2,1)S(1)}, bf16[528,128]{1,0:T(8,128)(2,1)S(1)}, u32[]{:S(2)}, u32[]{:S(2)}) collective-permute-start(bf16[528,128]{1,0:T(8,128)(2,1)S(1)} %get-tuple-element.86), channel_id=1, source_target_pairs={{0,12},{1,5},{4,0},{5,9},{8,4},{9,13},{12,8},{13,1},{2,14},{3,7},{... | collective-permute-start | bytes 405512 | tf_op jit(solution)/shard_map/ppermute | solution.py:388
  15.4 0.9 %copy-done.4 = bf16[1,27,16,8,8]{1,4,3,2,0:T(8,128)(2,1)S(1)} copy-done((bf16[1,27,16,8,8]{1,4,3,2,0:T(8,128)(2,1)S(1)}, bf16[1,27,16,8,8]{1,4,3,2,0:T(8,128)(2,1)}, u32[]{:S(2)}) %copy-start.4) | copy-done | bytes 55320
  16.3 0.5 weights.1
  16.9 0.0 copy-start.8
  16.9 0.1 collective-permute-start.2
  16.9 0.3 collective-permute-start.22
  17.2 0.8 %collective-permute-done.12.b_ref = bf16[272,128]{1,0:T(8,128)(2,1)S(1)} collective-permute-done((bf16[272,128]{1,0:T(8,128)(2,1)S(1)}, bf16[272,128]{1,0:T(8,128)(2,1)S(1)}, u32[]{:S(2)}, u32[]{:S(2)}) %collective-permute-start.12) | collective-permute-done | bytes 69664 | tf_op jit(solution)/shard_map/ppermute | solution.py:389
  18.0 0.1 collective-permute-start.3
  18.2 5.5 %collective-permute-done.22.b_ref = bf16[272,128]{1,0:T(8,128)(2,1)S(1)} collective-permute-done((bf16[272,128]{1,0:T(8,128)(2,1)S(1)}, bf16[272,128]{1,0:T(8,128)(2,1)S(1)}, u32[]{:S(2)}, u32[]{:S(2)}) %collective-permute-start.22) | collective-permute-done | bytes 69664 | tf_op jit(solution)/shard_map/ppermute | solution.py:389
  23.7 0.5 collective-permute-start.23
  24.2 0.1 collective-permute-start.11
  24.3 0.4 collective-permute-start.21
  24.8 4.2 %forward.3 = (bf16[2,256,128]{2,1,0:T(8,128)(2,1)S(1)}, f32[2,256,128]{2,1,0:T(8,128)S(1)}, f32[4,256,128]{2,1,0:T(8,128)S(1)}, bf16[2,256,128]{2,1,0:T(8,128)(2...) custom-call(bf16[3,2,256,128]{3,2,1,0:T(8,128)(2,1)S(1)} %bitcast.17, ...), custom_call_target="tpu_custom_call" | custom-call | flops 2000000000 | bytes 5242880 | tf_op jit(solution)/shard_map/forward/pallas_call | solution.py:414
  29.0 0.1 collective-permute-start.4
  29.1 4.2 %forward.4 = (bf16[2,256,128]{2,1,0:T(8,128)(2,1)S(1)}, f32[2,256,128]{2,1,0:T(8,128)S(1)}, f32[4,256,128]{2,1,0:T(8,128)S(1)}, bf16[2,256,128]{2,1,0:T(8,128)(2...) custom-call(bf16[3,2,256,128]{3,2,1,0:T(8,128)(2,1)S(1)} %bitcast.18, ...), custom_call_target="tpu_custom_call" | custom-call | flops 2000000000 | bytes 5242880 | tf_op jit(solution)/shard_map/forward/pallas_call | solution.py:414
  33.3 0.5 collective-permute-start.14
  33.9 1.6 %collective-permute-start.5 = (bf16[256,128]{1,0:T(8,128)(2,1)S(1)}, bf16[256,128]{1,0:T(8,128)(2,1)S(1)}, u32[]{:S(2)}, u32[]{:S(2)}) collective-permute-start(bf16[256,128]{1,0:T(8,128)(2,1)S(1)} %add_convert_fusion.2), channel_id=1, source_target_pairs={{0,2},{2,0},{1,3},{3,1},{4,6},{6,4},{5,7},{7,5},{8,10},{10,8},{9,1... | collective-permute-start | bytes 196616 | tf_op jit(solution)/shard_map/ppermute | solution.py:404
  35.4 1.6 %collective-permute-start.7 = (bf16[256,128]{1,0:T(8,128)(2,1)S(1)}, bf16[256,128]{1,0:T(8,128)(2,1)S(1)}, u32[]{:S(2)}, u32[]{:S(2)}) collective-permute-start(bf16[256,128]{1,0:T(8,128)(2,1)S(1)} %add_convert_fusion.2), channel_id=1, source_target_pairs={{0,14},{2,12},{1,7},{3,5},{4,2},{6,0},{5,11},{7,9},{8,6},{10,4},{9... | collective-permute-start | bytes 196616 | tf_op jit(solution)/shard_map/ppermute | solution.py:405
  37.1 4.2 %forward.5 = (bf16[2,256,128]{2,1,0:T(8,128)(2,1)S(1)}, f32[2,256,128]{2,1,0:T(8,128)S(1)}, f32[4,256,128]{2,1,0:T(8,128)S(1)}, bf16[2,256,128]{2,1,0:T(8,128)(2...) custom-call(bf16[3,2,256,128]{3,2,1,0:T(8,128)(2,1)S(1)} %bitcast.19, ...), custom_call_target="tpu_custom_call" | custom-call | flops 2000000000 | bytes 5242880 | tf_op jit(solution)/shard_map/forward/pallas_call | solution.py:414
  41.3 0.1 collective-permute-start.24
  41.4 1.6 %collective-permute-start.15 = (bf16[256,128]{1,0:T(8,128)(2,1)S(1)}, bf16[256,128]{1,0:T(8,128)(2,1)S(1)}, u32[]{:S(2)}, u32[]{:S(2)}) collective-permute-start(bf16[256,128]{1,0:T(8,128)(2,1)S(1)} %add_convert_fusion.1), channel_id=1, source_target_pairs={{0,2},{2,0},{1,3},{3,1},{4,6},{6,4},{5,7},{7,5},{8,10},{10,8},{9,1... | collective-permute-start | bytes 196616 | tf_op jit(solution)/shard_map/ppermute | solution.py:404
  43.0 1.6 %collective-permute-start.17 = (bf16[256,128]{1,0:T(8,128)(2,1)S(1)}, bf16[256,128]{1,0:T(8,128)(2,1)S(1)}, u32[]{:S(2)}, u32[]{:S(2)}) collective-permute-start(bf16[256,128]{1,0:T(8,128)(2,1)S(1)} %add_convert_fusion.1), channel_id=1, source_target_pairs={{0,14},{2,12},{1,7},{3,5},{4,2},{6,0},{5,11},{7,9},{8,6},{10,4},{9... | collective-permute-start | bytes 196616 | tf_op jit(solution)/shard_map/ppermute | solution.py:405
  44.6 1.6 %collective-permute-start.25 = (bf16[256,128]{1,0:T(8,128)(2,1)S(1)}, bf16[256,128]{1,0:T(8,128)(2,1)S(1)}, u32[]{:S(2)}, u32[]{:S(2)}) collective-permute-start(bf16[256,128]{1,0:T(8,128)(2,1)S(1)} %add_convert_fusion), channel_id=1, source_target_pairs={{0,2},{2,0},{1,3},{3,1},{4,6},{6,4},{5,7},{7,5},{8,10},{10,8},{9,1... | collective-permute-start | bytes 196616 | tf_op jit(solution)/shard_map/ppermute | solution.py:404
  46.2 2.1 %collective-permute-start.27 = (bf16[256,128]{1,0:T(8,128)(2,1)S(1)}, bf16[256,128]{1,0:T(8,128)(2,1)S(1)}, u32[]{:S(2)}, u32[]{:S(2)}) collective-permute-start(bf16[256,128]{1,0:T(8,128)(2,1)S(1)} %add_convert_fusion), channel_id=1, source_target_pairs={{0,14},{2,12},{1,7},{3,5},{4,2},{6,0},{5,11},{7,9},{8,6},{10,4},{9... | collective-permute-start | bytes 196616 | tf_op jit(solution)/shard_map/ppermute | solution.py:405
  48.3 0.8 %collective-permute-start.16 = (bf16[256,128]{1,0:T(8,128)(2,1)S(1)}, bf16[256,128]{1,0:T(8,128)(2,1)S(1)}, u32[]{:S(2)}, u32[]{:S(2)}) collective-permute-start(bf16[256,128]{1,0:T(8,128)(2,1)S(1)} %collective-permute-done.15.st_ref), channel_id=1, source_target_pairs={{0,1},{1,0},{2,3},{3,2},{4,5},{5,4},{6,7},{7,6},{8,9},{9,8},{10,11... | collective-permute-start | bytes 196616 | tf_op jit(solution)/shard_map/ppermute | solution.py:359
  49.0 1.2 %collective-permute-done.25.st_ref = bf16[256,128]{1,0:T(8,128)(2,1)S(1)} collective-permute-done((bf16[256,128]{1,0:T(8,128)(2,1)S(1)}, bf16[256,128]{1,0:T(8,128)(2,1)S(1)}, u32[]{:S(2)}, u32[]{:S(2)}) %collective-permute-start.25) | collective-permute-done | bytes 65568 | tf_op jit(solution)/shard_map/ppermute | solution.py:404
  50.2 1.1 %collective-permute-done.27.dg_ref = bf16[256,128]{1,0:T(8,128)(2,1)S(1)} collective-permute-done((bf16[256,128]{1,0:T(8,128)(2,1)S(1)}, bf16[256,128]{1,0:T(8,128)(2,1)S(1)}, u32[]{:S(2)}, u32[]{:S(2)}) %collective-permute-start.27) | collective-permute-done | bytes 65568 | tf_op jit(solution)/shard_map/ppermute | solution.py:405
  51.3 0.9 %collective-permute-start.28 = (bf16[256,128]{1,0:T(8,128)(2,1)S(1)}, bf16[256,128]{1,0:T(8,128)(2,1)S(1)}, u32[]{:S(2)}, u32[]{:S(2)}) collective-permute-start(bf16[256,128]{1,0:T(8,128)(2,1)S(1)} %collective-permute-done.27.dg_ref), channel_id=1, source_target_pairs={{0,1},{1,0},{2,3},{3,2},{4,5},{5,4},{6,7},{7,6},{8,9},{9,8},{10,11... | collective-permute-start | bytes 196616 | tf_op jit(solution)/shard_map/ppermute | solution.py:359
  52.2 2.4 %backward.3 = (bf16[2,256,128]{2,1,0:T(8,128)(2,1)S(1)}, bf16[2,256,128]{2,1,0:T(8,128)(2,1)S(1)}, f32[128,128]{1,0:T(8,128)S(1)}, f32[128,128]{1,0:T(8,128)S(1)}, f32[216,128]{1,0:T(8,128)S(1)}) custom-call(bf16[3,2,256,128]{3,2,1,0:T(8,128)(2,1)S(1)} %bitcast.20, bf16[3,2,256,128]{3,2,1,0:T(8,128)(2,1)S(1)} %bitcast.27, ...), custom_call_target="tpu_custom_call" | custom-call | flops 2000000000 | bytes 5242880 | tf_op jit(solution)/shard_map/backward/pallas_call | solution.py:490
  54.6 2.4 %backward.4 = (bf16[2,256,128]{2,1,0:T(8,128)(2,1)S(1)}, bf16[2,256,128]{2,1,0:T(8,128)(2,1)S(1)}, f32[128,128]{1,0:T(8,128)S(1)}, f32[128,128]{1,0:T(8,128)S(1)}, f32[216,128]{1,0:T(8,128)S(1)}) custom-call(bf16[3,2,256,128]{3,2,1,0:T(8,128)(2,1)S(1)} %bitcast.21, bf16[3,2,256,128]{3,2,1,0:T(8,128)(2,1)S(1)} %bitcast.28, ...), custom_call_target="tpu_custom_call" | custom-call | flops 2000000000 | bytes 5242880 | tf_op jit(solution)/shard_map/backward/pallas_call | solution.py:490
  57.0 2.4 %backward.5 = (bf16[2,256,128]{2,1,0:T(8,128)(2,1)S(1)}, bf16[2,256,128]{2,1,0:T(8,128)(2,1)S(1)}, f32[128,128]{1,0:T(8,128)S(1)}, f32[128,128]{1,0:T(8,128)S(1)}, f32[216,128]{1,0:T(8,128)S(1)}) custom-call(bf16[3,2,256,128]{3,2,1,0:T(8,128)(2,1)S(1)} %bitcast.22, bf16[3,2,256,128]{3,2,1,0:T(8,128)(2,1)S(1)} %bitcast.29, ...), custom_call_target="tpu_custom_call" | custom-call | flops 2000000000 | bytes 5242880 | tf_op jit(solution)/shard_map/backward/pallas_call | solution.py:490
  59.5 0.1 collective-permute-start.30
  59.5 0.1 collective-permute-start.9
  59.6 0.5 collective-permute-start.19
  60.1 0.1 collective-permute-start.29
  60.2 3.7 %collective-permute-start.31 = (bf16[472,128]{1,0:T(8,128)(2,1)S(1)}, bf16[472,128]{1,0:T(8,128)(2,1)S(1)}, u32[]{:S(2)}, u32[]{:S(2)}) collective-permute-start(bf16[472,128]{1,0:T(8,128)(2,1)S(1)} %pad_maximum_fusion.refs_0_), channel_id=1, source_target_pairs={{0,8},{4,12},{8,0},{12,4},{1,9},{5,13},{9,1},{13,5},{2,10},{6,14},... | collective-permute-start | bytes 362504 | tf_op jit(solution)/shard_map/ppermute | solution.py:518
  63.9 3.7 %collective-permute-done.30.refs_1_ = bf16[472,128]{1,0:T(8,128)(2,1)S(1)} collective-permute-done((bf16[472,128]{1,0:T(8,128)(2,1)S(1)}, bf16[472,128]{1,0:T(8,128)(2,1)S(1)}, u32[]{:S(2)}, u32[]{:S(2)}) %collective-permute-start.30) | collective-permute-done | bytes 120864 | tf_op jit(solution)/shard_map/ppermute | solution.py:518
  67.6 1.4 %collective-permute-start.32 = (bf16[472,128]{1,0:T(8,128)(2,1)S(1)}, bf16[472,128]{1,0:T(8,128)(2,1)S(1)}, u32[]{:S(2)}, u32[]{:S(2)}) collective-permute-start(bf16[472,128]{1,0:T(8,128)(2,1)S(1)} %pad_maximum_fusion.refs_0_), channel_id=1, source_target_pairs={{0,12},{4,0},{8,4},{12,8},{1,13},{5,1},{9,5},{13,9},{2,14},{6,2},{... | collective-permute-start | bytes 362504 | tf_op jit(solution)/shard_map/ppermute | solution.py:518
  69.0 2.8 %collective-permute-done.31.refs_2_ = bf16[472,128]{1,0:T(8,128)(2,1)S(1)} collective-permute-done((bf16[472,128]{1,0:T(8,128)(2,1)S(1)}, bf16[472,128]{1,0:T(8,128)(2,1)S(1)}, u32[]{:S(2)}, u32[]{:S(2)}) %collective-permute-start.31) | collective-permute-done | bytes 120864 | tf_op jit(solution)/shard_map/ppermute | solution.py:518
  71.8 1.5 %collective-permute-done.32.refs_3_ = bf16[472,128]{1,0:T(8,128)(2,1)S(1)} collective-permute-done((bf16[472,128]{1,0:T(8,128)(2,1)S(1)}, bf16[472,128]{1,0:T(8,128)(2,1)S(1)}, u32[]{:S(2)}, u32[]{:S(2)}) %collective-permute-start.32) | collective-permute-done | bytes 120864 | tf_op jit(solution)/shard_map/ppermute | solution.py:518
  73.3 1.1 %finish.1 = (f32[128,128]{1,0:T(8,128)}, f32[128,128]{1,0:T(8,128)}, f32[16,8,8,27]{3,2,1,0:T(8,128)}) custom-call(bf16[472,128]{1,0:T(8,128)(2,1)S(1)} %pad_maximum_fusion.refs_0_, bf16[472,128]{1,0:T(8,128)(2,1)S(1)} %collective-permute-done.30.refs_1_, bf16[472,128]{1,0:T(8,128)(2,1)S(1)} %collective-permute-done.31.refs_2_, ...), custom_call_target="tpu_custom_call" | custom-call | flops 1000000 | bytes 4194304 | tf_op jit(solution)/shard_map/finish/pallas_call | solution.py:530
  74.4 0.9 %emit.1 = bf16[3,2,256,128]{3,2,1,0:T(8,128)(2,1)} custom-call(bf16[2,256,128]{2,1,0:T(8,128)(2,1)S(1)} %get-tuple-element.71.refs_0_, bf16[2,256,128]{2,1,0:T(8,128)(2,1)S(1)} %get-tuple-element.72.refs_1_, bf16[2,256,128]{2,1,0:T(8,128)(2,1)S(1)} %collective-permute-done.9.refs_2_, bf16[2,256,128]{2,1,0:T(8,128)(2,1)S(1)} %get-tuple-element.84.refs_3_, ...), custom_call_target="tpu_custom_call" | custom-call | flops 1000000 | bytes 4194304 | tf_op jit(solution)/shard_map/emit/pallas_call | solution.py:523
  (57 shorter events, 0.2 us)
Async XLA Ops:
  0.6 1.0 %copy-start = (bf16[1,3,2,16,16,128]{5,4,3,2,1,0:T(8,128)(2,1)S(1)}, bf16[1,3,2,16,16,128]{5,4,3,2,1,0:T(8,128)(2,1)}, u32[]{:S(2)}) copy-start(bf16[1,3,2,16,16,128]{5,4,3,2,1,0:T(8,128)(2,1)} %param.7) | copy-start | bytes 1179652
  1.6 1.0 %copy-start.2 = (bf16[3,2,16,16,128]{4,3,2,1,0:T(8,128)(2,1)S(1)}, bf16[3,2,16,16,128]{4,3,2,1,0:T(8,128)(2,1)}, u32[]{:S(2)}) copy-start(bf16[3,2,16,16,128]{4,3,2,1,0:T(8,128)(2,1)} %param.8) | copy-start | bytes 1179652
  2.6 0.8 %copy-start.5 = (s32[3,2,16,16]{3,2,1,0:T(8,128)S(1)}, s32[3,2,16,16]{3,2,1,0:T(8,128)}, u32[]{:S(2)}) copy-start(s32[3,2,16,16]{3,2,1,0:T(8,128)} %lab_ref.1) | copy-start | bytes 18436
  3.4 21.3 %copy-start.1 = (bf16[1,3,2,16,16,128]{5,4,3,2,1,0:T(8,128)(2,1)S(1)}, bf16[1,3,2,16,16,128]{5,4,3,2,1,0:T(8,128)(2,1)}, u32[]{:S(2)}) copy-start(bf16[1,3,2,16,16,128]{5,4,3,2,1,0:T(8,128)(2,1)} %param.7) | copy-start | bytes 1179652
  3.4 21.3 %copy-start.3 = (bf16[3,2,16,16,128]{4,3,2,1,0:T(8,128)(2,1)S(1)}, bf16[3,2,16,16,128]{4,3,2,1,0:T(8,128)(2,1)}, u32[]{:S(2)}) copy-start(bf16[3,2,16,16,128]{4,3,2,1,0:T(8,128)(2,1)} %param.8) | copy-start | bytes 1179652
  4.4 12.4 %collective-permute-start = (bf16[528,128]{1,0:T(8,128)(2,1)S(1)}, bf16[528,128]{1,0:T(8,128)(2,1)S(1)}, u32[]{:S(2)}, u32[]{:S(2)}) collective-permute-start(bf16[528,128]{1,0:T(8,128)(2,1)S(1)} %get-tuple-element.55), channel_id=1, source_target_pairs={{0,12},{1,5},{4,0},{5,9},{8,4},{9,13},{12,8},{13,1},{2,14},{3,7},{... | collective-permute-start | bytes 405512 | tf_op jit(solution)/shard_map/ppermute | solution.py:388
  9.5 7.3 %collective-permute-start.1 = (bf16[272,128]{1,0:T(8,128)(2,1)S(1)}, bf16[272,128]{1,0:T(8,128)(2,1)S(1)}, u32[]{:S(2)}, u32[]{:S(2)}) collective-permute-start(bf16[272,128]{1,0:T(8,128)(2,1)S(1)} %get-tuple-element.56), channel_id=1, source_target_pairs={{0,4},{1,13},{4,8},{5,1},{8,12},{9,5},{12,0},{13,9},{2,6},{3,15},{... | collective-permute-start | bytes 208904 | tf_op jit(solution)/shard_map/ppermute | solution.py:389
  9.5 8.5 %collective-permute-start.12 = (bf16[272,128]{1,0:T(8,128)(2,1)S(1)}, bf16[272,128]{1,0:T(8,128)(2,1)S(1)}, u32[]{:S(2)}, u32[]{:S(2)}) collective-permute-start(bf16[272,128]{1,0:T(8,128)(2,1)S(1)} %get-tuple-element.74), channel_id=1, source_target_pairs={{0,4},{1,13},{4,8},{5,1},{8,12},{9,5},{12,0},{13,9},{2,6},{3,15},{... | collective-permute-start | bytes 208904 | tf_op jit(solution)/shard_map/ppermute | solution.py:389
  9.5 14.2 %collective-permute-start.10 = (bf16[528,128]{1,0:T(8,128)(2,1)S(1)}, bf16[528,128]{1,0:T(8,128)(2,1)S(1)}, u32[]{:S(2)}, u32[]{:S(2)}) collective-permute-start(bf16[528,128]{1,0:T(8,128)(2,1)S(1)} %get-tuple-element.73), channel_id=1, source_target_pairs={{0,12},{1,5},{4,0},{5,9},{8,4},{9,13},{12,8},{13,1},{2,14},{3,7},{... | collective-permute-start | bytes 405512 | tf_op jit(solution)/shard_map/ppermute | solution.py:388
  13.4 10.8 %collective-permute-start.20 = (bf16[528,128]{1,0:T(8,128)(2,1)S(1)}, bf16[528,128]{1,0:T(8,128)(2,1)S(1)}, u32[]{:S(2)}, u32[]{:S(2)}) collective-permute-start(bf16[528,128]{1,0:T(8,128)(2,1)S(1)} %get-tuple-element.86), channel_id=1, source_target_pairs={{0,12},{1,5},{4,0},{5,9},{8,4},{9,13},{12,8},{13,1},{2,14},{3,7},{... | collective-permute-start | bytes 405512 | tf_op jit(solution)/shard_map/ppermute | solution.py:388
  15.4 0.9 %copy-start.4 = (bf16[1,27,16,8,8]{1,4,3,2,0:T(8,128)(2,1)S(1)}, bf16[1,27,16,8,8]{1,4,3,2,0:T(8,128)(2,1)}, u32[]{:S(2)}) copy-start(bf16[1,27,16,8,8]{1,4,3,2,0:T(8,128)(2,1)} %param.12) | copy-start | bytes 165892
  16.3 8.4 %copy-start.6 = (bf16[1,128,128]{2,1,0:T(8,128)(2,1)S(1)}, bf16[1,128,128]{2,1,0:T(8,128)(2,1)}, u32[]{:S(2)}) copy-start(bf16[1,128,128]{2,1,0:T(8,128)(2,1)} %param.10) | copy-start | bytes 98308
  16.3 8.4 %copy-start.7 = (bf16[1,128,128]{2,1,0:T(8,128)(2,1)S(1)}, bf16[1,128,128]{2,1,0:T(8,128)(2,1)}, u32[]{:S(2)}) copy-start(bf16[1,128,128]{2,1,0:T(8,128)(2,1)} %param.13) | copy-start | bytes 98308
  16.9 1.3 %copy-start.8 = (f32[1,3,128]{2,0,1:T(1,128)S(1)}, f32[1,3,128]{2,0,1:T(1,128)}, u32[]{:S(2)}) copy-start(f32[1,3,128]{2,0,1:T(1,128)} %param.11) | copy-start | bytes 4612
  16.9 7.9 %collective-permute-start.2 = (bf16[528,128]{1,0:T(8,128)(2,1)S(1)}, bf16[528,128]{1,0:T(8,128)(2,1)S(1)}, u32[]{:S(2)}, u32[]{:S(2)}) collective-permute-start(bf16[528,128]{1,0:T(8,128)(2,1)S(1)} %collective-permute-done.a_ref.cta_ref), channel_id=1, source_target_pairs={{0,1},{1,0},{2,3},{3,2},{4,5},{5,4},{6,7},{7,6},{8,9},{9,8},{10,11... | collective-permute-start | bytes 405512 | tf_op jit(solution)/shard_map/ppermute | solution.py:359
  16.9 6.8 %collective-permute-start.22 = (bf16[272,128]{1,0:T(8,128)(2,1)S(1)}, bf16[272,128]{1,0:T(8,128)(2,1)S(1)}, u32[]{:S(2)}, u32[]{:S(2)}) collective-permute-start(bf16[272,128]{1,0:T(8,128)(2,1)S(1)} %get-tuple-element.87), channel_id=1, source_target_pairs={{0,4},{1,13},{4,8},{5,1},{8,12},{9,5},{12,0},{13,9},{2,6},{3,15},{... | collective-permute-start | bytes 208904 | tf_op jit(solution)/shard_map/ppermute | solution.py:389
  18.0 6.3 %collective-permute-start.3 = (bf16[272,128]{1,0:T(8,128)(2,1)S(1)}, bf16[272,128]{1,0:T(8,128)(2,1)S(1)}, u32[]{:S(2)}, u32[]{:S(2)}) collective-permute-start(bf16[272,128]{1,0:T(8,128)(2,1)S(1)} %collective-permute-done.1.b_ref), channel_id=1, source_target_pairs={{0,1},{1,0},{2,3},{3,2},{4,5},{5,4},{6,7},{7,6},{8,9},{9,8},{10,11... | collective-permute-start | bytes 208904 | tf_op jit(solution)/shard_map/ppermute | solution.py:359
  23.7 5.4 %collective-permute-start.13 = (bf16[272,128]{1,0:T(8,128)(2,1)S(1)}, bf16[272,128]{1,0:T(8,128)(2,1)S(1)}, u32[]{:S(2)}, u32[]{:S(2)}) collective-permute-start(bf16[272,128]{1,0:T(8,128)(2,1)S(1)} %collective-permute-done.12.b_ref), channel_id=1, source_target_pairs={{0,1},{1,0},{2,3},{3,2},{4,5},{5,4},{6,7},{7,6},{8,9},{9,8},{10,11... | collective-permute-start | bytes 208904 | tf_op jit(solution)/shard_map/ppermute | solution.py:359
  23.7 13.4 %collective-permute-start.23 = (bf16[272,128]{1,0:T(8,128)(2,1)S(1)}, bf16[272,128]{1,0:T(8,128)(2,1)S(1)}, u32[]{:S(2)}, u32[]{:S(2)}) collective-permute-start(bf16[272,128]{1,0:T(8,128)(2,1)S(1)} %collective-permute-done.22.b_ref), channel_id=1, source_target_pairs={{0,1},{1,0},{2,3},{3,2},{4,5},{5,4},{6,7},{7,6},{8,9},{9,8},{10,11... | collective-permute-start | bytes 208904 | tf_op jit(solution)/shard_map/ppermute | solution.py:359
  24.2 4.9 %collective-permute-start.11 = (bf16[528,128]{1,0:T(8,128)(2,1)S(1)}, bf16[528,128]{1,0:T(8,128)(2,1)S(1)}, u32[]{:S(2)}, u32[]{:S(2)}) collective-permute-start(bf16[528,128]{1,0:T(8,128)(2,1)S(1)} %collective-permute-done.10.a_ref.cta_ref), channel_id=1, source_target_pairs={{0,1},{1,0},{2,3},{3,2},{4,5},{5,4},{6,7},{7,6},{8,9},{9,8},{10,11... | collective-permute-start | bytes 405512 | tf_op jit(solution)/shard_map/ppermute | solution.py:359
  24.3 12.8 %collective-permute-start.21 = (bf16[528,128]{1,0:T(8,128)(2,1)S(1)}, bf16[528,128]{1,0:T(8,128)(2,1)S(1)}, u32[]{:S(2)}, u32[]{:S(2)}) collective-permute-start(bf16[528,128]{1,0:T(8,128)(2,1)S(1)} %collective-permute-done.20.a_ref.cta_ref), channel_id=1, source_target_pairs={{0,1},{1,0},{2,3},{3,2},{4,5},{5,4},{6,7},{7,6},{8,9},{9,8},{10,11... | collective-permute-start | bytes 405512 | tf_op jit(solution)/shard_map/ppermute | solution.py:359
  29.0 4.9 %collective-permute-start.4 = (bf16[256,128]{1,0:T(8,128)(2,1)S(1)}, bf16[256,128]{1,0:T(8,128)(2,1)S(1)}, u32[]{:S(2)}, u32[]{:S(2)}) collective-permute-start(bf16[256,128]{1,0:T(8,128)(2,1)S(1)} %get-tuple-element.65), channel_id=1, source_target_pairs={{0,1},{1,0},{2,3},{3,2},{4,5},{5,4},{6,7},{7,6},{8,9},{9,8},{10,11... | collective-permute-start | bytes 196616 | tf_op jit(solution)/shard_map/ppermute | solution.py:359
  33.3 8.0 %collective-permute-start.14 = (bf16[256,128]{1,0:T(8,128)(2,1)S(1)}, bf16[256,128]{1,0:T(8,128)(2,1)S(1)}, u32[]{:S(2)}, u32[]{:S(2)}) collective-permute-start(bf16[256,128]{1,0:T(8,128)(2,1)S(1)} %get-tuple-element.76), channel_id=1, source_target_pairs={{0,1},{1,0},{2,3},{3,2},{4,5},{5,4},{6,7},{7,6},{8,9},{9,8},{10,11... | collective-permute-start | bytes 196616 | tf_op jit(solution)/shard_map/ppermute | solution.py:359
  33.9 10.7 %collective-permute-start.5 = (bf16[256,128]{1,0:T(8,128)(2,1)S(1)}, bf16[256,128]{1,0:T(8,128)(2,1)S(1)}, u32[]{:S(2)}, u32[]{:S(2)}) collective-permute-start(bf16[256,128]{1,0:T(8,128)(2,1)S(1)} %add_convert_fusion.2), channel_id=1, source_target_pairs={{0,2},{2,0},{1,3},{3,1},{4,6},{6,4},{5,7},{7,5},{8,10},{10,8},{9,1... | collective-permute-start | bytes 196616 | tf_op jit(solution)/shard_map/ppermute | solution.py:404
  35.4 10.8 %collective-permute-start.7 = (bf16[256,128]{1,0:T(8,128)(2,1)S(1)}, bf16[256,128]{1,0:T(8,128)(2,1)S(1)}, u32[]{:S(2)}, u32[]{:S(2)}) collective-permute-start(bf16[256,128]{1,0:T(8,128)(2,1)S(1)} %add_convert_fusion.2), channel_id=1, source_target_pairs={{0,14},{2,12},{1,7},{3,5},{4,2},{6,0},{5,11},{7,9},{8,6},{10,4},{9... | collective-permute-start | bytes 196616 | tf_op jit(solution)/shard_map/ppermute | solution.py:405
  41.3 3.3 %collective-permute-start.24 = (bf16[256,128]{1,0:T(8,128)(2,1)S(1)}, bf16[256,128]{1,0:T(8,128)(2,1)S(1)}, u32[]{:S(2)}, u32[]{:S(2)}) collective-permute-start(bf16[256,128]{1,0:T(8,128)(2,1)S(1)} %get-tuple-element.90), channel_id=1, source_target_pairs={{0,1},{1,0},{2,3},{3,2},{4,5},{5,4},{6,7},{7,6},{8,9},{9,8},{10,11... | collective-permute-start | bytes 196616 | tf_op jit(solution)/shard_map/ppermute | solution.py:359
  41.4 6.8 %collective-permute-start.15 = (bf16[256,128]{1,0:T(8,128)(2,1)S(1)}, bf16[256,128]{1,0:T(8,128)(2,1)S(1)}, u32[]{:S(2)}, u32[]{:S(2)}) collective-permute-start(bf16[256,128]{1,0:T(8,128)(2,1)S(1)} %add_convert_fusion.1), channel_id=1, source_target_pairs={{0,2},{2,0},{1,3},{3,1},{4,6},{6,4},{5,7},{7,5},{8,10},{10,8},{9,1... | collective-permute-start | bytes 196616 | tf_op jit(solution)/shard_map/ppermute | solution.py:404
  43.0 5.3 %collective-permute-start.17 = (bf16[256,128]{1,0:T(8,128)(2,1)S(1)}, bf16[256,128]{1,0:T(8,128)(2,1)S(1)}, u32[]{:S(2)}, u32[]{:S(2)}) collective-permute-start(bf16[256,128]{1,0:T(8,128)(2,1)S(1)} %add_convert_fusion.1), channel_id=1, source_target_pairs={{0,14},{2,12},{1,7},{3,5},{4,2},{6,0},{5,11},{7,9},{8,6},{10,4},{9... | collective-permute-start | bytes 196616 | tf_op jit(solution)/shard_map/ppermute | solution.py:405
  44.6 4.5 %collective-permute-start.6 = (bf16[256,128]{1,0:T(8,128)(2,1)S(1)}, bf16[256,128]{1,0:T(8,128)(2,1)S(1)}, u32[]{:S(2)}, u32[]{:S(2)}) collective-permute-start(bf16[256,128]{1,0:T(8,128)(2,1)S(1)} %collective-permute-done.5.st_ref), channel_id=1, source_target_pairs={{0,1},{1,0},{2,3},{3,2},{4,5},{5,4},{6,7},{7,6},{8,9},{9,8},{10,11... | collective-permute-start | bytes 196616 | tf_op jit(solution)/shard_map/ppermute | solution.py:359
  44.6 5.6 %collective-permute-start.25 = (bf16[256,128]{1,0:T(8,128)(2,1)S(1)}, bf16[256,128]{1,0:T(8,128)(2,1)S(1)}, u32[]{:S(2)}, u32[]{:S(2)}) collective-permute-start(bf16[256,128]{1,0:T(8,128)(2,1)S(1)} %add_convert_fusion), channel_id=1, source_target_pairs={{0,2},{2,0},{1,3},{3,1},{4,6},{6,4},{5,7},{7,5},{8,10},{10,8},{9,1... | collective-permute-start | bytes 196616 | tf_op jit(solution)/shard_map/ppermute | solution.py:404
  46.2 5.2 %collective-permute-start.27 = (bf16[256,128]{1,0:T(8,128)(2,1)S(1)}, bf16[256,128]{1,0:T(8,128)(2,1)S(1)}, u32[]{:S(2)}, u32[]{:S(2)}) collective-permute-start(bf16[256,128]{1,0:T(8,128)(2,1)S(1)} %add_convert_fusion), channel_id=1, source_target_pairs={{0,14},{2,12},{1,7},{3,5},{4,2},{6,0},{5,11},{7,9},{8,6},{10,4},{9... | collective-permute-start | bytes 196616 | tf_op jit(solution)/shard_map/ppermute | solution.py:405
  48.2 4.0 %collective-permute-start.8 = (bf16[256,128]{1,0:T(8,128)(2,1)S(1)}, bf16[256,128]{1,0:T(8,128)(2,1)S(1)}, u32[]{:S(2)}, u32[]{:S(2)}) collective-permute-start(bf16[256,128]{1,0:T(8,128)(2,1)S(1)} %collective-permute-done.7.dg_ref), channel_id=1, source_target_pairs={{0,1},{1,0},{2,3},{3,2},{4,5},{5,4},{6,7},{7,6},{8,9},{9,8},{10,11... | collective-permute-start | bytes 196616 | tf_op jit(solution)/shard_map/ppermute | solution.py:359
  48.3 6.4 %collective-permute-start.16 = (bf16[256,128]{1,0:T(8,128)(2,1)S(1)}, bf16[256,128]{1,0:T(8,128)(2,1)S(1)}, u32[]{:S(2)}, u32[]{:S(2)}) collective-permute-start(bf16[256,128]{1,0:T(8,128)(2,1)S(1)} %collective-permute-done.15.st_ref), channel_id=1, source_target_pairs={{0,1},{1,0},{2,3},{3,2},{4,5},{5,4},{6,7},{7,6},{8,9},{9,8},{10,11... | collective-permute-start | bytes 196616 | tf_op jit(solution)/shard_map/ppermute | solution.py:359
  49.0 5.6 %collective-permute-start.18 = (bf16[256,128]{1,0:T(8,128)(2,1)S(1)}, bf16[256,128]{1,0:T(8,128)(2,1)S(1)}, u32[]{:S(2)}, u32[]{:S(2)}) collective-permute-start(bf16[256,128]{1,0:T(8,128)(2,1)S(1)} %collective-permute-done.17.dg_ref), channel_id=1, source_target_pairs={{0,1},{1,0},{2,3},{3,2},{4,5},{5,4},{6,7},{7,6},{8,9},{9,8},{10,11... | collective-permute-start | bytes 196616 | tf_op jit(solution)/shard_map/ppermute | solution.py:359
  50.2 6.8 %collective-permute-start.26 = (bf16[256,128]{1,0:T(8,128)(2,1)S(1)}, bf16[256,128]{1,0:T(8,128)(2,1)S(1)}, u32[]{:S(2)}, u32[]{:S(2)}) collective-permute-start(bf16[256,128]{1,0:T(8,128)(2,1)S(1)} %collective-permute-done.25.st_ref), channel_id=1, source_target_pairs={{0,1},{1,0},{2,3},{3,2},{4,5},{5,4},{6,7},{7,6},{8,9},{9,8},{10,11... | collective-permute-start | bytes 196616 | tf_op jit(solution)/shard_map/ppermute | solution.py:359
  51.3 5.7 %collective-permute-start.28 = (bf16[256,128]{1,0:T(8,128)(2,1)S(1)}, bf16[256,128]{1,0:T(8,128)(2,1)S(1)}, u32[]{:S(2)}, u32[]{:S(2)}) collective-permute-start(bf16[256,128]{1,0:T(8,128)(2,1)S(1)} %collective-permute-done.27.dg_ref), channel_id=1, source_target_pairs={{0,1},{1,0},{2,3},{3,2},{4,5},{5,4},{6,7},{7,6},{8,9},{9,8},{10,11... | collective-permute-start | bytes 196616 | tf_op jit(solution)/shard_map/ppermute | solution.py:359
  59.5 8.1 %collective-permute-start.30 = (bf16[472,128]{1,0:T(8,128)(2,1)S(1)}, bf16[472,128]{1,0:T(8,128)(2,1)S(1)}, u32[]{:S(2)}, u32[]{:S(2)}) collective-permute-start(bf16[472,128]{1,0:T(8,128)(2,1)S(1)} %pad_maximum_fusion.refs_0_), channel_id=1, source_target_pairs={{0,4},{4,8},{8,12},{12,0},{1,5},{5,9},{9,13},{13,1},{2,6},{6,10},{... | collective-permute-start | bytes 362504 | tf_op jit(solution)/shard_map/ppermute | solution.py:518
  59.5 14.9 %collective-permute-start.9 = (bf16[2,256,128]{2,1,0:T(8,128)(2,1)S(1)}, bf16[2,256,128]{2,1,0:T(8,128)(2,1)S(1)}, u32[]{:S(2)}, u32[]{:S(2)}) collective-permute-start(bf16[2,256,128]{2,1,0:T(8,128)(2,1)S(1)} %get-tuple-element.72.refs_1_), channel_id=1, source_target_pairs={{0,1},{1,0},{2,3},{3,2},{4,5},{5,4},{6,7},{7,6},{8,9},{9,8},{10,11... | collective-permute-start | bytes 393224 | tf_op jit(solution)/shard_map/ppermute | solution.py:359
  59.6 14.8 %collective-permute-start.19 = (bf16[2,256,128]{2,1,0:T(8,128)(2,1)S(1)}, bf16[2,256,128]{2,1,0:T(8,128)(2,1)S(1)}, u32[]{:S(2)}, u32[]{:S(2)}) collective-permute-start(bf16[2,256,128]{2,1,0:T(8,128)(2,1)S(1)} %get-tuple-element.85.refs_4_), channel_id=1, source_target_pairs={{0,1},{1,0},{2,3},{3,2},{4,5},{5,4},{6,7},{7,6},{8,9},{9,8},{10,11... | collective-permute-start | bytes 393224 | tf_op jit(solution)/shard_map/ppermute | solution.py:359
  60.1 14.3 %collective-permute-start.29 = (bf16[2,256,128]{2,1,0:T(8,128)(2,1)S(1)}, bf16[2,256,128]{2,1,0:T(8,128)(2,1)S(1)}, u32[]{:S(2)}, u32[]{:S(2)}) collective-permute-start(bf16[2,256,128]{2,1,0:T(8,128)(2,1)S(1)} %get-tuple-element.99.refs_7_), channel_id=1, source_target_pairs={{0,1},{1,0},{2,3},{3,2},{4,5},{5,4},{6,7},{7,6},{8,9},{9,8},{10,11... | collective-permute-start | bytes 393224 | tf_op jit(solution)/shard_map/ppermute | solution.py:359
  60.2 11.6 %collective-permute-start.31 = (bf16[472,128]{1,0:T(8,128)(2,1)S(1)}, bf16[472,128]{1,0:T(8,128)(2,1)S(1)}, u32[]{:S(2)}, u32[]{:S(2)}) collective-permute-start(bf16[472,128]{1,0:T(8,128)(2,1)S(1)} %pad_maximum_fusion.refs_0_), channel_id=1, source_target_pairs={{0,8},{4,12},{8,0},{12,4},{1,9},{5,13},{9,1},{13,5},{2,10},{6,14},... | collective-permute-start | bytes 362504 | tf_op jit(solution)/shard_map/ppermute | solution.py:518
  67.6 5.8 %collective-permute-start.32 = (bf16[472,128]{1,0:T(8,128)(2,1)S(1)}, bf16[472,128]{1,0:T(8,128)(2,1)S(1)}, u32[]{:S(2)}, u32[]{:S(2)}) collective-permute-start(bf16[472,128]{1,0:T(8,128)(2,1)S(1)} %pad_maximum_fusion.refs_0_), channel_id=1, source_target_pairs={{0,12},{4,0},{8,4},{12,8},{1,13},{5,1},{9,5},{13,9},{2,14},{6,2},{... | collective-permute-start | bytes 362504 | tf_op jit(solution)/shard_map/ppermute | solution.py:518

commit v3 on v2

v3 whole, which is shorter than its diff:
```python
import functools
import math

import jax
import jax.numpy as jnp
from jax import lax
from jax.experimental import pallas as pl
from jax.experimental.pallas import tpu as pltpu
from jax.sharding import PartitionSpec as P

BF = jnp.bfloat16
F32 = jnp.float32
LANES = 128


def gate(v):
    return 0.5 + 0.5 * jnp.tanh(0.5 * v)


def slope(v, q):
    return q * (1.0 + v * (1.0 - q))


def nt_dot(a, b):
    return lax.dot_general(a, b, (((1,), (1,)), ((), ())), preferred_element_type=F32)


def store_shifts(ref, plane, value, wide, deep):
    cells = wide * deep
    cube = value.reshape(wide, deep, LANES)
    for j, turn in enumerate((1, 0, deep - 1)):
        moved = cube if turn == 0 else pltpu.roll(cube, turn, axis=1)
        flat = moved.reshape(cells, LANES).astype(BF)
        lanes = slice(j * LANES, (j + 1) * LANES)
        ref[plane, deep : deep + cells, lanes] = flat
        ref[plane, 0:deep, lanes] = flat[cells - deep :]
        ref[plane, deep + cells : cells + 2 * deep, lanes] = flat[:deep]


def pair_rows(planes, first, cells, deep):
    parts = []
    for at in range(first - 1, first + 3):
        ref, plane = planes[at]
        for dy in range(3):
            parts.append(ref[plane, dy * deep : dy * deep + cells, :])
    return jnp.concatenate(parts, axis=1)


def conv_pairs(planes, firsts, weights, cells, deep):
    rows = [pair_rows(planes, first, cells, deep) for first in firsts]
    rows = rows[0] if len(rows) == 1 else jnp.concatenate(rows, axis=0)
    both = jnp.dot(rows, weights[...], preferred_element_type=F32)
    outs = []
    for n in range(len(firsts)):
        for o in range(2):
            outs.append(both[n * cells : (n + 1) * cells, o * LANES : (o + 1) * LANES])
    return outs


def pack_kernel(groups, cells, wide, x_ref, ct_ref, tag_ref, *rest):
    micro = sum(len(group) for group in groups)
    outs, (own_ref, lab_ref, sem) = rest[: 2 * len(groups)], rest[2 * len(groups) :]
    spots = []
    for n, group in enumerate(groups):
        for i in range(len(group)):
            at = i * (cells + wide)
            a_ref = outs[2 * n].at[pl.ds(at + i * cells, 2 * cells + wide)]
            spots.append((a_ref, outs[2 * n + 1].at[pl.ds(at, cells + wide)]))
    tags = pltpu.make_async_copy(tag_ref, lab_ref, sem.at[3 * micro])
    tags.start()
    c = lax.axis_index("chan")
    copies = []
    for m in range(micro):
        a_ref, b_ref = spots[m]
        moves = (
            (x_ref.at[m, c], a_ref.at[0:cells]),
            (x_ref.at[m, c], b_ref.at[0:cells]),
            (ct_ref.at[m, c], a_ref.at[cells + wide : 2 * cells + wide]),
        )
        for n, (src, dst) in enumerate(moves):
            copy = pltpu.make_async_copy(src, dst, sem.at[3 * m + n])
            copy.start()
            copies.append(copy)
    deep = lab_ref.shape[3]
    tags.wait()
    row = lax.broadcasted_iota(jnp.int32, (LANES, LANES), 0)
    lane = lax.broadcasted_iota(jnp.int32, (LANES, LANES), 1)
    eye = jnp.where(row == lane, 1.0, 0.0)[:deep, :deep].astype(BF)
    for m in range(micro):
        for p in range(2):
            own_ref[m, p] = jnp.zeros((deep, LANES), BF)
            turned = nt_dot(eye, lab_ref[m, p].astype(F32).astype(BF))
            own_ref[m, p, :, 0:wide] = turned.astype(BF)
        lab = own_ref[m, c]
        spots[m][0][cells : cells + wide] = lab
        spots[m][1][cells : cells + wide] = lab
    for copy in copies:
        copy.wait()


def diagonal_mask(width):
    groups = LANES // width
    g = lax.broadcasted_iota(jnp.int32, (groups, width, LANES), 0)
    lane = lax.broadcasted_iota(jnp.int32, (groups, width, LANES), 2)
    return g == lane // width


def weights_kernel(taps, width, k_ref, f_ref, b_ref, flat_ref, thin_ref):
    groups = LANES // width
    keep = diagonal_mask(width)
    flat_ref[:, 0:taps] = k_ref[...].astype(F32).reshape(groups * width * width, taps)
    for i in range(width):
        rows = [
            flat_ref[(g * width + i) * width : (g * width + i + 1) * width, :]
            for g in range(groups)
        ]
        turned = jnp.concatenate(rows, axis=0).T
        thin_ref[0, pl.ds(i, taps, stride=width), :] = turned[:taps]
        turned = flat_ref[pl.ds(i, LANES, stride=width), :].T
        thin_ref[1, pl.ds(i, taps, stride=width), :] = turned[:taps]
    third = taps // 3 * LANES
    zero = jnp.zeros((third, LANES), BF)
    for n, dst in enumerate((f_ref, b_ref)):
        dst[0:third, LANES:] = zero
        dst[3 * third :, 0:LANES] = zero
        for t in range(taps):
            one = thin_ref[n, t * width : (t + 1) * width, :]
            full = jnp.where(keep, jnp.broadcast_to(one[None], keep.shape), 0.0)
            full = full.reshape(LANES, LANES).astype(BF)
            at = (t if n == 0 else taps - 1 - t) * LANES
            dst[at : at + LANES, 0:LANES] = full
            dst[third + at : third + at + LANES, LANES:] = full


def hidden_rows(x, lab, w, codes, wide, deep):
    pre = jnp.dot(x, w, preferred_element_type=F32)
    lab = lab.astype(F32)
    adds = []
    for y in range(wide):
        tag = jnp.broadcast_to(lab[:, y : y + 1], (deep, LANES))
        adds.append(jnp.where(tag < 0.5, codes[0], jnp.where(tag < 1.5, codes[1], codes[2])))
    return pre + jnp.concatenate(adds, axis=0)


def code_rows(code_ref, deep):
    return [jnp.broadcast_to(code_ref[i : i + 1, :], (deep, LANES)) for i in range(3)]


def own_kernel(
    micro, wide, deep, x_ref, ct_ref, lab_ref, w_ref, rw_ref, code_ref, *outs
):
    for src, dst in zip((x_ref, ct_ref, w_ref, rw_ref, code_ref), outs[3 * micro :]):
        dst[...] = src[...]
    codes = code_rows(code_ref, deep)
    for m in range(micro):
        hs_ref, hid_ref, spre_ref = outs[3 * m : 3 * m + 3]
        for p in range(2):
            pre = hidden_rows(x_ref[m, p], lab_ref[m, p], w_ref[...], codes, wide, deep)
            q = gate(pre)
            h = pre * q
            hid_ref[p] = h.astype(BF)
            spre_ref[p] = slope(pre, q)
            store_shifts(hs_ref, p, h, wide, deep)


def forward_kernel(
    slot,
    wide,
    deep,
    own_ref,
    a_ref,
    b_ref,
    a2_ref,
    b2_ref,
    w_ref,
    code_ref,
    kf_ref,
    sconv_ref,
    mixed_ref,
    hs_ref,
):
    c = lax.axis_index("chan")
    cells = wide * deep
    codes = code_rows(code_ref, deep)
    a_ref, a2_ref = [v.at[pl.ds(slot * (2 * cells + wide), 2 * cells + wide)] for v in (a_ref, a2_ref)]
    b_ref, b2_ref = [v.at[pl.ds(slot * (cells + wide), cells + wide)] for v in (b_ref, b2_ref)]
    for ref, plane in ((a_ref, 2 - c), (b_ref, 3 * c), (a2_ref, 1 + c), (b2_ref, 3 - 3 * c)):
        lab = ref[cells : cells + wide]
        pre = hidden_rows(ref[0:cells], lab, w_ref[...], codes, wide, deep)
        store_shifts(hs_ref, plane, pre * gate(pre), wide, deep)
    planes = [(hs_ref, 0), (hs_ref, 1), (own_ref, 0), (own_ref, 1), (hs_ref, 2), (hs_ref, 3)]
    for p, conv in enumerate(conv_pairs(planes, (1, 3), kf_ref, cells, deep)):
        q = gate(conv)
        sconv_ref[p] = slope(conv, q)
        if p in (1, 2):
            mixed_ref[p - 1] = (conv * q).astype(BF)


def backward_kernel(
    mode,
    m,
    slot,
    wide,
    deep,
    taps,
    width,
    x_ref,
    ct_ref,
    cta_ref,
    cta2_ref,
    w_ref,
    rw_ref,
    kb_ref,
    spre_ref,
    sconv_ref,
    *rest,
):
    c = lax.axis_index("chan")
    cells = wide * deep
    tail = pl.ds(slot * (2 * cells + wide) + cells + wide, cells)
    full = mode == "full"
    if mode == "first":
        base_ref, other_ref, gs_ref, br_ref = rest
        up_ref = ct_ref.at[m]
        halo, halo2 = cta_ref[tail], cta2_ref[tail]
    else:
        st_ref, st2_ref, dg_ref, dg2_ref, *rest = rest
        if full:
            hid_ref, mixed_ref, exp_in, red_in, kg_in, *rest = rest
            part_ref, up_ref, exp_ref, red_ref, kg_ref, gs_ref = rest
        else:
            base_ref, other_ref, gs_ref, br_ref, up_ref = rest
        last = lax.axis_index("section") == lax.axis_size("section") - 1

        @pl.when(last)
        def _():
            up_ref[0] = ct_ref[m, 0]
            up_ref[1] = ct_ref[m, 1]

        @pl.when(jnp.logical_not(last))
        def _():
            up_ref[c] = st_ref[...]
            up_ref[1 - c] = st2_ref[...]

        halo = jnp.where(last, cta_ref[tail], dg_ref[...])
        halo2 = jnp.where(last, cta2_ref[tail], dg2_ref[...])
    ups = ((up_ref[0], 1), (up_ref[1], 2), (halo, 3 - 3 * c), (halo2, 3 * c))
    for up, plane in ups:
        grad = nt_dot(up, rw_ref[...]) * sconv_ref[plane]
        store_shifts(gs_ref, plane, grad.astype(BF).astype(F32), wide, deep)
    if full:
        ups2 = up_ref[...].reshape(2 * cells, LANES)
        red = lax.dot_general(
            mixed_ref[...].reshape(2 * cells, LANES),
            ups2,
            (((0,), (0,)), ((), ())),
            preferred_element_type=F32,
        )
        red_ref[...] = red_in[...] + red
        groups = LANES // width
        keep = diagonal_mask(width)
        turned = [hid_ref[p].T for p in (0, 1)]
        left = jnp.concatenate(turned, axis=1)
        for dx in (-1, 0, 1):
            for dy in (-1, 0, 1):
                rows = slice((1 + dy) * deep, (1 + dy) * deep + cells)
                right = jnp.concatenate([gs_ref[1 + dx, rows, :], gs_ref[2 + dx, rows, :]], axis=0)
                dense = jnp.dot(left, right, preferred_element_type=F32)
                for j in range(3):
                    tap = 9 * (dx + 1) + 3 * (dy + 1) + j
                    block = dense[:, j * LANES : (j + 1) * LANES].reshape(groups, width, LANES)
                    thin = jnp.sum(jnp.where(keep, block, 0.0), axis=0)
                    at = slice((taps - 1 - tap) * width, (taps - tap) * width)
                    kg_ref[at] = kg_in[at] + thin
    planes = [(gs_ref, p) for p in range(4)]
    grads = []
    for p, grad_hidden in enumerate(conv_pairs(planes, (1,), kb_ref, cells, deep)):
        grad_pre = (grad_hidden * spre_ref[p]).astype(BF)
        branch = nt_dot(grad_pre, w_ref[...])
        if full:
            part_ref[p] = branch.astype(BF)
            grads.append(grad_pre)
        else:
            br_ref[p] = branch
    if full:
        exp_ref[...] = exp_in[...] + lax.dot_general(
            x_ref[m].reshape(2 * cells, LANES),
            jnp.concatenate(grads, axis=0),
            (((0,), (0,)), ((), ())),
            preferred_element_type=F32,
        )
    else:
        base_ref[...] = up_ref[c].astype(F32) + br_ref[c]
        other_ref[...] = br_ref[1 - c].astype(BF)


def emit_kernel(micro, *refs):
    ins, out_ref = refs[:-1], refs[-1]
    for m in range(micro):
        up, mine, other = ins[3 * m : 3 * m + 3]
        both = mine[...].astype(F32) + other[...].astype(F32)
        out_ref[m] = (up[...].astype(F32) + both).astype(BF)


def finish_kernel(count, scale, taps, width, *refs):
    ins, outs, thin_ref = refs[:count], refs[count:-1], refs[-1]
    total = ins[0][...].astype(F32)
    for ref in ins[1:]:
        total = total + ref[...].astype(F32)
    total = total * scale
    outs[0][...] = total[0:LANES]
    outs[1][...] = total[LANES : 2 * LANES]
    thin_ref[0 : taps * width] = total[2 * LANES :]
    for i in range(width):
        turned = thin_ref[pl.ds(i, LANES, stride=width), :].T
        outs[2][:, i] = turned[:, :taps].reshape(LANES // width, width, taps)


def GROUPS(micro):
    return [list(range(micro))]


def sds(shape, dtype):
    return jax.ShapeDtypeStruct(shape, dtype)


def params(mebibytes):
    return pltpu.CompilerParams(vmem_limit_bytes=mebibytes * 2**20)


def call(kernel, name, out_shape, args, scratch=(), in_specs=None, room=16):
    vmem = pl.BlockSpec(memory_space=pltpu.VMEM)
    outs = [vmem] * len(out_shape)
    return pl.pallas_call(
        kernel,
        in_specs=[vmem] * len(args) if in_specs is None else in_specs,
        out_specs=outs,
        out_shape=out_shape,
        scratch_shapes=list(scratch),
        name=name,
        cost_estimate=pl.CostEstimate(flops=1000, bytes_accessed=1000, transcendentals=0),
        compiler_params=params(room),
    )(*args)


def on_device(
    section_inputs, cotangent, phase_labels, expand_weight, phase_code, kernel, reduce_weight
):
    _, micro, depth, wide, deep, trunk = section_inputs.shape
    cells = wide * deep
    taps, groups, width = kernel.shape[1], kernel.shape[2], kernel.shape[3]
    assert depth == 2 and lax.axis_size("chan") == 2
    assert trunk == LANES and groups * width == LANES
    spaces, sections = lax.axis_size("space"), lax.axis_size("section")
    scale = 1.0 / math.sqrt(micro * depth * spaces * cells)

    x = section_inputs[0].reshape(micro, depth, cells, trunk)
    ct = cotangent.reshape(micro, depth, cells, trunk)
    w, rw = expand_weight[0], reduce_weight[0]
    code = jnp.pad(phase_code[0], ((0, 8 - phase_code.shape[1]), (0, 0)))
    kern = kernel[0].transpose(1, 2, 3, 0)

    away = [(k, c, (k + 2 * c - 1) % spaces) for k in range(spaces) for c in (0, 1)]
    back = [(k, c, (k - 2 * c + 1) % spaces) for k in range(spaces) for c in (0, 1)]
    route_a = [(2 * k + c, 2 * t + c) for k, c, t in away]
    route_b = [(2 * k + c, 2 * t + c) for k, c, t in back]
    route_d = [
        ((k * sections + s) * 2 + c, (t * sections + (s - 1) % sections) * 2 + c)
        for k, c, t in away
        for s in range(sections)
    ]
    route_s = [(s, (s - 1) % sections) for s in range(sections)]

    def swap(v):
        return lax.ppermute(v, "chan", [(0, 1), (1, 0)])

    groups_m = GROUPS(micro)
    rows_a, rows_b = 2 * cells + wide, cells + wide
    hbm = pl.BlockSpec(memory_space=pltpu.HBM)
    *packed, lab = call(
        functools.partial(pack_kernel, groups_m, cells, wide),
        "pack",
        [sds((len(g) * n, LANES), BF) for g in groups_m for n in (rows_a, rows_b)]
        + [sds((micro, depth, deep, LANES), BF)],
        (x, ct, phase_labels),
        [
            pltpu.VMEM(phase_labels.shape, jnp.int32),
            pltpu.SemaphoreType.DMA((3 * micro + 1,)),
        ],
        [hbm, hbm, hbm],
        60,
    )
    plane2, plane4, flat = (2, cells, LANES), (4, cells, LANES), (cells, LANES)
    pad_rows = cells + 2 * deep
    square, thin = (LANES, LANES), (taps * width, LANES)
    dense_f, dense_b = call(
        functools.partial(weights_kernel, taps, width),
        "weights",
        [sds((4 * taps // 3 * LANES, 2 * LANES), BF)] * 2,
        (kern,),
        [pltpu.VMEM((LANES * width, LANES), F32), pltpu.VMEM((2,) + thin, F32)],
    )
    *owned, x, ct, w, rw, code = call(
        functools.partial(own_kernel, micro, wide, deep),
        "own",
        [sds((2, pad_rows, 3 * LANES), BF), sds(plane2, BF), sds(plane2, F32)] * micro
        + [sds(v.shape, v.dtype) for v in (x, ct, w, rw, code)],
        (x, ct, lab, w, rw, code),
    )
    halos, slots = [], []
    for n, group in enumerate(groups_m):
        a = lax.ppermute(packed[2 * n], ("space", "chan"), route_a)
        b = lax.ppermute(packed[2 * n + 1], ("space", "chan"), route_b)
        if n == 0:
            a, b, dense_f, dense_b, *owned = lax.optimization_barrier(
                (a, b, dense_f, dense_b, *owned)
            )
        halos += [(a, b, swap(a), swap(b))] * len(group)
        slots += list(range(len(group)))

    def joined(base, other):
        return (base + swap(other).astype(F32)).astype(BF)

    def send_on(out):
        st = lax.ppermute(out, "section", route_s)
        dg = lax.ppermute(out, ("space", "section", "chan"), route_d)
        return st, swap(st), dg, swap(dg)

    def back_pass(mode, m, extra, extra_out=()):
        outs = [sds(flat, F32), sds(flat, BF)] if mode != "full" else [sds(plane2, BF)] * 2
        scratch = [pltpu.VMEM((4, pad_rows, 3 * LANES), BF)]
        if mode != "full":
            scratch.append(pltpu.VMEM(plane2, F32))
        if mode == "light":
            scratch.append(pltpu.VMEM(plane2, BF))
        return call(
            functools.partial(backward_kernel, mode, m, slots[m], wide, deep, taps, width),
            "backward_" + mode,
            outs + list(extra_out),
            (x, ct, halos[m][0], halos[m][2], w, rw, dense_b, spre[m], sconv[m], *extra),
            scratch,
        )

    sconv, mixed, ups = [], [], []
    spre = [owned[3 * m + 2] for m in range(micro)]
    pending = None
    for m in range(micro):
        a, b, a2, b2 = halos[m]
        con, mix = call(
            functools.partial(forward_kernel, slots[m], wide, deep),
            "forward",
            [sds(plane4, F32), sds(plane2, BF)],
            (owned[3 * m], a, b, a2, b2, w, code, dense_f),
            [pltpu.VMEM((4, pad_rows, 3 * LANES), BF)],
        )
        sconv.append(con)
        mixed.append(mix)
        if pending is not None:
            out, sconv[m] = lax.optimization_barrier((joined(*pending), sconv[m]))
            ups.append(send_on(out))
        pending = back_pass("first", m, ())
    ups.append(send_on(joined(*pending)))

    rank = lax.axis_index("section")
    for stage in range(1, sections - 1):
        fresh = [send_on(joined(*back_pass("light", m, ups[m]))) for m in range(micro)]
        mine = rank == sections - 2 - stage
        ups = [
            tuple(jnp.where(mine, n, o) for n, o in zip(fresh[m], ups[m])) for m in range(micro)
        ]
    sum_shapes = [sds(s, F32) for s in (square, square, thin)]
    sums = [jnp.zeros(s.shape, F32) for s in sum_shapes]
    pieces = []
    for m in range(micro):
        extra = (*ups[m], owned[3 * m + 1], mixed[m], *sums)
        part, up, *sums = back_pass("full", m, extra, sum_shapes)
        pieces += [up, part, swap(part)]

    grads = jnp.concatenate([s.astype(BF) for s in sums], axis=0)
    if spaces == 4:
        near = [(k, k ^ 1) for k in range(spaces)]
        far = [(k, k ^ 3) for k in range(spaces)]
        grads = grads + lax.ppermute(grads, "space", near)
        copies = [grads, lax.ppermute(grads, "space", far)]
    else:
        copies = [lax.psum(grads, "space")]
    (out,) = call(
        functools.partial(emit_kernel, micro), "emit", [sds((micro,) + plane2, BF)], pieces
    )
    *copies, out = lax.optimization_barrier((*copies, out))
    exp_g, red_g, kg = call(
        functools.partial(finish_kernel, len(copies), scale, taps, width),
        "finish",
        [sds(square, F32), sds(square, F32), sds((groups, width, width, taps), F32)],
        copies,
        [pltpu.VMEM((LANES * width, LANES), F32)],
    )
    kg = kg.transpose(3, 0, 1, 2)
    return (
        out.reshape(section_inputs.shape),
        exp_g[None],
        kg[None],
        red_g[None],
    )


def solution(mesh):
    placed = (
        P("section", "parts", "space", None, None, None),
        P("parts", "space", None, None, None),
        P("parts", "space", None, None),
        P("section", None, "chan"),
        P("section", None, "chan"),
        P("section", None, "chan", None, None),
        P("section", "chan", None),
    )
    return jax.shard_map(
        on_device,
        mesh=mesh,
        in_specs=placed,
        out_specs=(
            P("section", "parts", "space", None, None, None),
            P(("parts", "section"), None, "chan"),
            P(("parts", "section"), None, "chan", None, None),
            P(("parts", "section"), "chan", None),
        ),
        check_vma=False,
    )
```

time: 75.6 us -> 68.8 us (0.910)
  starting transfers between devices: 30.6 us -> 23.9 us
  local copies, waits for them, and re-layouts: 3.78 us -> 5.9 us
  Pallas kernels: 23.2 us -> 21.3 us
    ppermute x9 -> x4, starting transfers between devices: 16.4 us -> 9.62 us  [the longest x1 5.1 us: on_device(): a = lax.ppermute(packed[2 * n], ('space', 'chan'), route_a)]
    unnamed x19 -> x13, local copies, waits for them, and re-layouts: 3.75 us -> 5.88 us
    pallas_call x10 -> x14, Pallas kernels: 23.2 us -> 21.3 us  [call(): pl.pallas_call(kernel, in_specs=[vmem] * len(args) if in_specs is None el...]
    ppermute x18 -> x14, waiting for transfers between devices: 0.05 us -> 1.56 us  [swap(): return lax.ppermute(v, 'chan', [(0, 1), (1, 0)])]
    ppermute x3, waiting for transfers between devices: 1.19 us -> 0.01 us  [send_on(): st = lax.ppermute(out, 'section', route_s)]
    ppermute x9 -> x4, waiting for transfers between devices: 14.4 us -> 13.3 us  [the longest x1 6.42 us: on_device(): b = lax.ppermute(packed[2 * n + 1], ('space', 'chan'), route_b)]
    ppermute x18 -> x14, starting transfers between devices: 4.26 us -> 4.11 us  [swap(): return lax.ppermute(v, 'chan', [(0, 1), (1, 0)])]
  transfers between devices with their start and end apart: 33 -> 24, of which waited for: 7 -> 6; matrix products, arithmetic and copies ran while one was open for 0% -> 1% of each run, Pallas kernels for 25% -> 17%
where the time goes in v3:
time: 68.8 us; the launch traced here: 68.3 us
  starting transfers between devices  23.9 us (35%)
  Pallas kernels  21.3 us (31%)
  waiting for transfers between devices  16.2 us (24%)
  local copies, waits for them, and re-layouts  5.9 us (9%)
  between operations  0.87 us (1%)
    pallas_call x14, Pallas kernels, call(): pl.pallas_call(kernel, in_specs=[vmem] * len(args) if in_specs is None el...  21.3 us
    ppermute x1, waiting for transfers between devices, on_device(): b = lax.ppermute(packed[2 * n + 1], ('space', 'chan'), route_b)  6.42 us
    unnamed x13, local copies, waits for them, and re-layouts  5.88 us
    ppermute x3, starting transfers between devices, send_on(): dg = lax.ppermute(out, ('space', 'section', 'chan'), route_d)  5.58 us
    ppermute x1, starting transfers between devices, on_device(): a = lax.ppermute(packed[2 * n], ('space', 'chan'), route_a)  5.1 us
    ppermute x3, starting transfers between devices, send_on(): st = lax.ppermute(out, 'section', route_s)  4.6 us
    ppermute x1, waiting for transfers between devices, on_device(): grads = grads + lax.ppermute(grads, 'space', near)  4.51 us
    ppermute x1, starting transfers between devices, on_device(): copies = [grads, lax.ppermute(grads, 'space', far)]  4.44 us
  transfers between devices with their start and end apart: 24, of which 6 were waited for; matrix products, arithmetic and copies ran while one was open for 1% of the time, Pallas kernels for 17%

profile of v3, /device:TPU:0, one launch (start us, length us, event | category | flops | bytes accessed | tf_op | source)
XLA Modules:
  0.0 68.3 jit_solution(4487964639180745847)
XLA Ops:
  0.6 2.0 %pack.1 = (bf16[1584,128]{1,0:T(8,128)(2,1)}, bf16[816,128]{1,0:T(8,128)(2,1)}, bf16[3,2,16,128]{3,2,1,0:T(8,128)(2,1)}) custom-call(bf16[3,2,256,128]{3,2,1,0:T(8,128)(2,1)} %bitcast.16, bf16[3,2,256,128]{3,2,1,0:T(8,128)(2,1)} %bitcast.18, s32[3,2,16,16]{3,2,1,0:T(8,128)} %tag_ref.1), custom_call_target="tpu_custom_call" | custom-call | flops 1000 | bytes 1000 | tf_op jit(solution)/shard_map/pack/pallas_call | solution.py:334
  2.7 5.1 %collective-permute-start = (bf16[1584,128]{1,0:T(8,128)(2,1)}, bf16[1584,128]{1,0:T(8,128)(2,1)S(1)}, u32[]{:S(2)}, u32[]{:S(2)}) collective-permute-start(bf16[1584,128]{1,0:T(8,128)(2,1)} %get-tuple-element.76), channel_id=1, source_target_pairs={{0,12},{1,5},{4,0},{5,9},{8,4},{9,13},{12,8},{13,1},{2,14},{3,7},{... | collective-permute-start | bytes 1216520 | tf_op jit(solution)/shard_map/ppermute | solution.py:412
  7.8 0.9 %copy-done.2 = bf16[1,27,16,8,8]{1,4,3,2,0:T(8,128)(2,1)S(1)} copy-done((bf16[1,27,16,8,8]{1,4,3,2,0:T(8,128)(2,1)S(1)}, bf16[1,27,16,8,8]{1,4,3,2,0:T(8,128)(2,1)}, u32[]{:S(2)}) %copy-start.2) | copy-done | bytes 55320
  8.7 0.9 %weights.1 = (bf16[4608,256]{1,0:T(8,128)(2,1)S(1)}, bf16[4608,256]{1,0:T(8,128)(2,1)S(1)}) custom-call(bf16[16,8,8,27]{3,2,1,0:T(8,128)(2,1)S(1)} %bitcast.20), custom_call_target="tpu_custom_call" | custom-call | flops 1000 | bytes 1000 | tf_op jit(solution)/shard_map/weights/pallas_call | solution.py:334
  9.7 0.7 %copy.13 = f32[1,3,128]{2,1,0:T(4,128)S(1)} copy(f32[1,3,128]{2,0,1:T(1,128)} %param.11) | data formatting | bytes 3072
  10.4 1.0 %copy-done = bf16[1,3,2,16,16,128]{5,4,3,2,1,0:T(8,128)(2,1)S(1)} copy-done((bf16[1,3,2,16,16,128]{5,4,3,2,1,0:T(8,128)(2,1)S(1)}, bf16[1,3,2,16,16,128]{5,4,3,2,1,0:T(8,128)(2,1)}, u32[]{:S(2)}) %copy-start) | copy-done | bytes 393240
  11.4 1.0 %copy-done.1 = bf16[3,2,16,16,128]{4,3,2,1,0:T(8,128)(2,1)S(1)} copy-done((bf16[3,2,16,16,128]{4,3,2,1,0:T(8,128)(2,1)S(1)}, bf16[3,2,16,16,128]{4,3,2,1,0:T(8,128)(2,1)}, u32[]{:S(2)}) %copy-start.1) | copy-done | bytes 393240
  12.4 0.8 %copy-done.3 = bf16[1,128,128]{2,1,0:T(8,128)(2,1)S(1)} copy-done((bf16[1,128,128]{2,1,0:T(8,128)(2,1)S(1)}, bf16[1,128,128]{2,1,0:T(8,128)(2,1)}, u32[]{:S(2)}) %copy-start.3) | copy-done | bytes 32792
  13.1 0.8 %copy-done.4 = bf16[1,128,128]{2,1,0:T(8,128)(2,1)S(1)} copy-done((bf16[1,128,128]{2,1,0:T(8,128)(2,1)S(1)}, bf16[1,128,128]{2,1,0:T(8,128)(2,1)}, u32[]{:S(2)}) %copy-start.4) | copy-done | bytes 32792
  13.9 0.7 %copy-done.5 = bf16[3,2,16,128]{3,2,1,0:T(8,128)(2,1)S(1)} copy-done((bf16[3,2,16,128]{3,2,1,0:T(8,128)(2,1)S(1)}, bf16[3,2,16,128]{3,2,1,0:T(8,128)(2,1)}, u32[]{:S(2)}) %copy-start.5) | copy-done | bytes 24600
  14.6 0.8 %own.1 = (bf16[2,288,384]{2,1,0:T(8,128)(2,1)S(1)}, bf16[2,256,128]{2,1,0:T(8,128)(2,1)S(1)}, f32[2,256,128]{2,1,0:T(8,128)S(1)}, bf16[2,288,384]{2,1,0:T(8,128)...) custom-call(bf16[3,2,256,128]{3,2,1,0:T(8,128)(2,1)S(1)} %bitcast.17, ...), custom_call_target="tpu_custom_call" | custom-call | flops 1000 | bytes 1000 | tf_op jit(solution)/shard_map/own/pallas_call | solution.py:334
  15.4 6.4 %collective-permute-done.1.b_ref = bf16[816,128]{1,0:T(8,128)(2,1)S(1)} collective-permute-done((bf16[816,128]{1,0:T(8,128)(2,1)}, bf16[816,128]{1,0:T(8,128)(2,1)S(1)}, u32[]{:S(2)}, u32[]{:S(2)}) %collective-permute-start.1) | collective-permute-done | bytes 208928 | tf_op jit(solution)/shard_map/ppermute | solution.py:413
  21.8 0.5 collective-permute-start.3
  22.3 1.5 %collective-permute-done.3.b2_ref = bf16[816,128]{1,0:T(8,128)(2,1)S(1)} collective-permute-done((bf16[816,128]{1,0:T(8,128)(2,1)S(1)}, bf16[816,128]{1,0:T(8,128)(2,1)S(1)}, u32[]{:S(2)}, u32[]{:S(2)}) %collective-permute-start.3) | collective-permute-done | bytes 208928 | tf_op jit(solution)/shard_map/ppermute | solution.py:375
  23.9 0.0 collective-permute-done.2.a2_ref.cta2_ref
  23.9 1.9 %forward.3 = (f32[4,256,128]{2,1,0:T(8,128)S(1)}, bf16[2,256,128]{2,1,0:T(8,128)(2,1)S(1)}) custom-call(bf16[2,288,384]{2,1,0:T(8,128)(2,1)S(1)} %get-tuple-element.96.own_ref, bf16[1584,128]{1,0:T(8,128)(2,1)S(1)} %collective-permute-done.a_ref.cta_ref, bf16[816,128]{1,0:T(8,128)(2,1)S(1)} %collective-permute-done.1.b_ref, ...), custom_call_target="tpu_custom_call" | custom-call | flops 1000 | bytes 1000 | tf_op jit(solution)/shard_map/forward/pallas_call | solution.py:334
  25.8 1.2 %backward_first.3 = (f32[256,128]{1,0:T(8,128)S(1)}, bf16[256,128]{1,0:T(8,128)(2,1)S(1)}) custom-call(bf16[3,2,256,128]{3,2,1,0:T(8,128)(2,1)S(1)} %get-tuple-element.74.x_ref, bf16[3,2,256,128]{3,2,1,0:T(8,128)(2,1)S(1)} %get-tuple-element.75.ct_ref, bf16[1584,128]{1,0:T(8,128)(2,1)S(1)} %collective-permute-done.a_ref.cta_ref, ...), custom_call_target="tpu_custom_call" | custom-call | flops 1000 | bytes 1000 | tf_op jit(solution)/shard_map/backward_first/pallas_call | solution.py:334
  27.0 0.2 collective-permute-start.4
  27.2 1.9 %forward.4 = (f32[4,256,128]{2,1,0:T(8,128)S(1)}, bf16[2,256,128]{2,1,0:T(8,128)(2,1)S(1)}) custom-call(bf16[2,288,384]{2,1,0:T(8,128)(2,1)S(1)} %get-tuple-element.103.own_ref, bf16[1584,128]{1,0:T(8,128)(2,1)S(1)} %collective-permute-done.a_ref.cta_ref, bf16[816,128]{1,0:T(8,128)(2,1)S(1)} %collective-permute-done.1.b_ref, ...), custom_call_target="tpu_custom_call" | custom-call | flops 1000 | bytes 1000 | tf_op jit(solution)/shard_map/forward/pallas_call | solution.py:334
  29.1 1.2 %backward_first.4 = (f32[256,128]{1,0:T(8,128)S(1)}, bf16[256,128]{1,0:T(8,128)(2,1)S(1)}) custom-call(bf16[3,2,256,128]{3,2,1,0:T(8,128)(2,1)S(1)} %get-tuple-element.74.x_ref, bf16[3,2,256,128]{3,2,1,0:T(8,128)(2,1)S(1)} %get-tuple-element.75.ct_ref, bf16[1584,128]{1,0:T(8,128)(2,1)S(1)} %collective-permute-done.a_ref.cta_ref, ...), custom_call_target="tpu_custom_call" | custom-call | flops 1000 | bytes 1000 | tf_op jit(solution)/shard_map/backward_first/pallas_call | solution.py:334
  30.3 0.4 collective-permute-start.5
  30.8 1.9 %forward.5 = (f32[4,256,128]{2,1,0:T(8,128)S(1)}, bf16[2,256,128]{2,1,0:T(8,128)(2,1)S(1)}) custom-call(bf16[2,288,384]{2,1,0:T(8,128)(2,1)S(1)} %get-tuple-element.108.own_ref, bf16[1584,128]{1,0:T(8,128)(2,1)S(1)} %collective-permute-done.a_ref.cta_ref, bf16[816,128]{1,0:T(8,128)(2,1)S(1)} %collective-permute-done.1.b_ref, ...), custom_call_target="tpu_custom_call" | custom-call | flops 1000 | bytes 1000 | tf_op jit(solution)/shard_map/forward/pallas_call | solution.py:334
  32.7 1.6 %collective-permute-start.15 = (bf16[256,128]{1,0:T(8,128)(2,1)S(1)}, bf16[256,128]{1,0:T(8,128)(2,1)S(1)}, u32[]{:S(2)}, u32[]{:S(2)}) collective-permute-start(bf16[256,128]{1,0:T(8,128)(2,1)S(1)} %add_convert_fusion.2), channel_id=1, source_target_pairs={{0,2},{2,0},{1,3},{3,1},{4,6},{6,4},{5,7},{7,5},{8,10},{10,8},{9,1... | collective-permute-start | bytes 196616 | tf_op jit(solution)/shard_map/ppermute | solution.py:425
  34.2 1.2 %backward_first.5 = (f32[256,128]{1,0:T(8,128)S(1)}, bf16[256,128]{1,0:T(8,128)(2,1)S(1)}) custom-call(bf16[3,2,256,128]{3,2,1,0:T(8,128)(2,1)S(1)} %get-tuple-element.74.x_ref, bf16[3,2,256,128]{3,2,1,0:T(8,128)(2,1)S(1)} %get-tuple-element.75.ct_ref, bf16[1584,128]{1,0:T(8,128)(2,1)S(1)} %collective-permute-done.a_ref.cta_ref, ...), custom_call_target="tpu_custom_call" | custom-call | flops 1000 | bytes 1000 | tf_op jit(solution)/shard_map/backward_first/pallas_call | solution.py:334
  35.5 0.1 collective-permute-start.6
  35.6 1.3 %collective-permute-start.17 = (bf16[256,128]{1,0:T(8,128)(2,1)S(1)}, bf16[256,128]{1,0:T(8,128)(2,1)S(1)}, u32[]{:S(2)}, u32[]{:S(2)}) collective-permute-start(bf16[256,128]{1,0:T(8,128)(2,1)S(1)} %add_convert_fusion.2), channel_id=1, source_target_pairs={{0,14},{2,12},{1,7},{3,5},{4,2},{6,0},{5,11},{7,9},{8,6},{10,4},{9... | collective-permute-start | bytes 196616 | tf_op jit(solution)/shard_map/ppermute | solution.py:426
  36.9 1.5 %collective-permute-start.11 = (bf16[256,128]{1,0:T(8,128)(2,1)S(1)}, bf16[256,128]{1,0:T(8,128)(2,1)S(1)}, u32[]{:S(2)}, u32[]{:S(2)}) collective-permute-start(bf16[256,128]{1,0:T(8,128)(2,1)S(1)} %add_convert_fusion.1), channel_id=1, source_target_pairs={{0,2},{2,0},{1,3},{3,1},{4,6},{6,4},{5,7},{7,5},{8,10},{10,8},{9,1... | collective-permute-start | bytes 196616 | tf_op jit(solution)/shard_map/ppermute | solution.py:425
  38.4 0.4 collective-permute-start.13
  38.8 1.6 %collective-permute-start.7 = (bf16[256,128]{1,0:T(8,128)(2,1)S(1)}, bf16[256,128]{1,0:T(8,128)(2,1)S(1)}, u32[]{:S(2)}, u32[]{:S(2)}) collective-permute-start(bf16[256,128]{1,0:T(8,128)(2,1)S(1)} %add_convert_fusion), channel_id=1, source_target_pairs={{0,2},{2,0},{1,3},{3,1},{4,6},{6,4},{5,7},{7,5},{8,10},{10,8},{9,1... | collective-permute-start | bytes 196616 | tf_op jit(solution)/shard_map/ppermute | solution.py:425
  40.4 0.4 collective-permute-done.17.rest_2_
  40.8 3.9 %collective-permute-start.9 = (bf16[256,128]{1,0:T(8,128)(2,1)S(1)}, bf16[256,128]{1,0:T(8,128)(2,1)S(1)}, u32[]{:S(2)}, u32[]{:S(2)}) collective-permute-start(bf16[256,128]{1,0:T(8,128)(2,1)S(1)} %add_convert_fusion), channel_id=1, source_target_pairs={{0,14},{2,12},{1,7},{3,5},{4,2},{6,0},{5,11},{7,9},{8,6},{10,4},{9... | collective-permute-start | bytes 196616 | tf_op jit(solution)/shard_map/ppermute | solution.py:426
  44.7 0.5 collective-permute-start.12
  45.2 0.1 collective-permute-start.14
  45.3 0.4 collective-permute-start.8
  45.7 0.9 %collective-permute-done.9.rest_2_ = bf16[256,128]{1,0:T(8,128)(2,1)S(1)} collective-permute-done((bf16[256,128]{1,0:T(8,128)(2,1)S(1)}, bf16[256,128]{1,0:T(8,128)(2,1)S(1)}, u32[]{:S(2)}, u32[]{:S(2)}) %collective-permute-start.9) | collective-permute-done | bytes 65568 | tf_op jit(solution)/shard_map/ppermute | solution.py:426
  46.6 1.2 %collective-permute-start.10 = (bf16[256,128]{1,0:T(8,128)(2,1)S(1)}, bf16[256,128]{1,0:T(8,128)(2,1)S(1)}, u32[]{:S(2)}, u32[]{:S(2)}) collective-permute-start(bf16[256,128]{1,0:T(8,128)(2,1)S(1)} %collective-permute-done.9.rest_2_), channel_id=1, source_target_pairs={{0,1},{1,0},{2,3},{3,2},{4,5},{5,4},{6,7},{7,6},{8,9},{9,8},{10,11... | collective-permute-start | bytes 196616 | tf_op jit(solution)/shard_map/ppermute | solution.py:375
  47.8 2.2 %backward_full.3 = (bf16[2,256,128]{2,1,0:T(8,128)(2,1)S(1)}, bf16[2,256,128]{2,1,0:T(8,128)(2,1)S(1)}, f32[128,128]{1,0:T(8,128)S(1)}, f32[128,128]{1,0:T(8,128)S(1)}, f32[216,128]{1,0:T(8,128)S(1)}) custom-call(bf16[3,2,256,128]{3,2,1,0:T(8,128)(2,1)S(1)} %get-tuple-element.74.x_ref, bf16[3,2,256,128]{3,2,1,0:T(8,128)(2,1)S(1)} %get-tuple-element.75.ct_ref, ...), custom_call_target="tpu_custom_call" | custom-call | flops 1000 | bytes 1000 | tf_op jit(solution)/shard_map/backward_full/pallas_call | solution.py:334
  50.1 2.1 %backward_full.4 = (bf16[2,256,128]{2,1,0:T(8,128)(2,1)S(1)}, bf16[2,256,128]{2,1,0:T(8,128)(2,1)S(1)}, f32[128,128]{1,0:T(8,128)S(1)}, f32[128,128]{1,0:T(8,128)S(1)}, f32[216,128]{1,0:T(8,128)S(1)}) custom-call(bf16[3,2,256,128]{3,2,1,0:T(8,128)(2,1)S(1)} %get-tuple-element.74.x_ref, bf16[3,2,256,128]{3,2,1,0:T(8,128)(2,1)S(1)} %get-tuple-element.75.ct_ref, ...), custom_call_target="tpu_custom_call" | custom-call | flops 1000 | bytes 1000 | tf_op jit(solution)/shard_map/backward_full/pallas_call | solution.py:334
  52.2 2.1 %backward_full.5 = (bf16[2,256,128]{2,1,0:T(8,128)(2,1)S(1)}, bf16[2,256,128]{2,1,0:T(8,128)(2,1)S(1)}, f32[128,128]{1,0:T(8,128)S(1)}, f32[128,128]{1,0:T(8,128)S(1)}, f32[216,128]{1,0:T(8,128)S(1)}) custom-call(bf16[3,2,256,128]{3,2,1,0:T(8,128)(2,1)S(1)} %get-tuple-element.74.x_ref, bf16[3,2,256,128]{3,2,1,0:T(8,128)(2,1)S(1)} %get-tuple-element.75.ct_ref, ...), custom_call_target="tpu_custom_call" | custom-call | flops 1000 | bytes 1000 | tf_op jit(solution)/shard_map/backward_full/pallas_call | solution.py:334
  54.3 0.1 collective-permute-start.19
  54.4 0.1 collective-permute-start.21
  54.4 0.5 collective-permute-start.22
  54.9 0.1 collective-permute-start.23
  55.0 4.5 %collective-permute-done.19 = bf16[472,128]{1,0:T(8,128)(2,1)S(1)} collective-permute-done((bf16[472,128]{1,0:T(8,128)(2,1)S(1)}, bf16[472,128]{1,0:T(8,128)(2,1)S(1)}, u32[]{:S(2)}, u32[]{:S(2)}) %collective-permute-start.19) | collective-permute-done | bytes 120864 | tf_op jit(solution)/shard_map/ppermute | solution.py:483
  59.6 4.4 %collective-permute-start.20 = (bf16[472,128]{1,0:T(8,128)(2,1)S(1)}, bf16[472,128]{1,0:T(8,128)(2,1)S(1)}, u32[]{:S(2)}, u32[]{:S(2)}) collective-permute-start(bf16[472,128]{1,0:T(8,128)(2,1)S(1)} %fusion.refs_0_), channel_id=1, source_target_pairs={{0,12},{4,8},{8,4},{12,0},{1,13},{5,9},{9,5},{13,1},{2,14},{6,10},... | collective-permute-start | bytes 362504 | tf_op jit(solution)/shard_map/ppermute | solution.py:484
  64.0 0.9 %emit.1 = bf16[3,2,256,128]{3,2,1,0:T(8,128)(2,1)} custom-call(bf16[2,256,128]{2,1,0:T(8,128)(2,1)S(1)} %get-tuple-element.130.refs_0_, bf16[2,256,128]{2,1,0:T(8,128)(2,1)S(1)} %get-tuple-element.131.refs_1_, bf16[2,256,128]{2,1,0:T(8,128)(2,1)S(1)} %collective-permute-done.21.refs_2_, bf16[2,256,128]{2,1,0:T(8,128)(2,1)S(1)} %get-tuple-element.132.refs_3_, ...), custom_call_target="tpu_custom_call" | custom-call | flops 1000 | bytes 1000 | tf_op jit(solution)/shard_map/emit/pallas_call | solution.py:334
  64.9 2.4 %collective-permute-done.20.refs_1_ = bf16[472,128]{1,0:T(8,128)(2,1)S(1)} collective-permute-done((bf16[472,128]{1,0:T(8,128)(2,1)S(1)}, bf16[472,128]{1,0:T(8,128)(2,1)S(1)}, u32[]{:S(2)}, u32[]{:S(2)}) %collective-permute-start.20) | collective-permute-done | bytes 120864 | tf_op jit(solution)/shard_map/ppermute | solution.py:484
  67.3 1.0 %finish.1 = (f32[128,128]{1,0:T(8,128)}, f32[128,128]{1,0:T(8,128)}, f32[16,8,8,27]{3,2,1,0:T(8,128)}) custom-call(bf16[472,128]{1,0:T(8,128)(2,1)S(1)} %fusion.refs_0_, bf16[472,128]{1,0:T(8,128)(2,1)S(1)} %collective-permute-done.20.refs_1_), custom_call_target="tpu_custom_call" | custom-call | flops 1000 | bytes 1000 | tf_op jit(solution)/shard_map/finish/pallas_call | solution.py:334
  (38 shorter events, 0.2 us)
Async XLA Ops:
  2.7 19.2 %collective-permute-start = (bf16[1584,128]{1,0:T(8,128)(2,1)}, bf16[1584,128]{1,0:T(8,128)(2,1)S(1)}, u32[]{:S(2)}, u32[]{:S(2)}) collective-permute-start(bf16[1584,128]{1,0:T(8,128)(2,1)} %get-tuple-element.76), channel_id=1, source_target_pairs={{0,12},{1,5},{4,0},{5,9},{8,4},{9,13},{12,8},{13,1},{2,14},{3,7},{... | collective-permute-start | bytes 1216520 | tf_op jit(solution)/shard_map/ppermute | solution.py:412
  7.8 14.1 %collective-permute-start.1 = (bf16[816,128]{1,0:T(8,128)(2,1)}, bf16[816,128]{1,0:T(8,128)(2,1)S(1)}, u32[]{:S(2)}, u32[]{:S(2)}) collective-permute-start(bf16[816,128]{1,0:T(8,128)(2,1)} %get-tuple-element.77), channel_id=1, source_target_pairs={{0,4},{1,13},{4,8},{5,1},{8,12},{9,5},{12,0},{13,9},{2,6},{3,15},{... | collective-permute-start | bytes 626696 | tf_op jit(solution)/shard_map/ppermute | solution.py:413
  7.8 1.0 %copy-start.2 = (bf16[1,27,16,8,8]{1,4,3,2,0:T(8,128)(2,1)S(1)}, bf16[1,27,16,8,8]{1,4,3,2,0:T(8,128)(2,1)}, u32[]{:S(2)}) copy-start(bf16[1,27,16,8,8]{1,4,3,2,0:T(8,128)(2,1)} %param.12) | copy-start | bytes 165892
  10.4 1.0 %copy-start = (bf16[1,3,2,16,16,128]{5,4,3,2,1,0:T(8,128)(2,1)S(1)}, bf16[1,3,2,16,16,128]{5,4,3,2,1,0:T(8,128)(2,1)}, u32[]{:S(2)}) copy-start(bf16[1,3,2,16,16,128]{5,4,3,2,1,0:T(8,128)(2,1)} %param.7) | copy-start | bytes 1179652
  11.4 1.0 %copy-start.1 = (bf16[3,2,16,16,128]{4,3,2,1,0:T(8,128)(2,1)S(1)}, bf16[3,2,16,16,128]{4,3,2,1,0:T(8,128)(2,1)}, u32[]{:S(2)}) copy-start(bf16[3,2,16,16,128]{4,3,2,1,0:T(8,128)(2,1)} %param.8) | copy-start | bytes 1179652
  12.4 0.8 %copy-start.3 = (bf16[1,128,128]{2,1,0:T(8,128)(2,1)S(1)}, bf16[1,128,128]{2,1,0:T(8,128)(2,1)}, u32[]{:S(2)}) copy-start(bf16[1,128,128]{2,1,0:T(8,128)(2,1)} %param.10) | copy-start | bytes 98308
  13.1 0.8 %copy-start.4 = (bf16[1,128,128]{2,1,0:T(8,128)(2,1)S(1)}, bf16[1,128,128]{2,1,0:T(8,128)(2,1)}, u32[]{:S(2)}) copy-start(bf16[1,128,128]{2,1,0:T(8,128)(2,1)} %param.13) | copy-start | bytes 98308
  13.9 0.7 %copy-start.5 = (bf16[3,2,16,128]{3,2,1,0:T(8,128)(2,1)S(1)}, bf16[3,2,16,128]{3,2,1,0:T(8,128)(2,1)}, u32[]{:S(2)}) copy-start(bf16[3,2,16,128]{3,2,1,0:T(8,128)(2,1)} %get-tuple-element.73.lab_ref) | copy-start | bytes 73732
  21.8 2.0 %collective-permute-start.2 = (bf16[1584,128]{1,0:T(8,128)(2,1)S(1)}, bf16[1584,128]{1,0:T(8,128)(2,1)S(1)}, u32[]{:S(2)}, u32[]{:S(2)}) collective-permute-start(bf16[1584,128]{1,0:T(8,128)(2,1)S(1)} %collective-permute-done.a_ref.cta_ref), channel_id=1, source_target_pairs={{0,1},{1,0},{2,3},{3,2},{4,5},{5,4},{6,7},{7,6},{8,9},{9,8},{10,11... | collective-permute-start | bytes 1216520 | tf_op jit(solution)/shard_map/ppermute | solution.py:375
  21.8 2.0 %collective-permute-start.3 = (bf16[816,128]{1,0:T(8,128)(2,1)S(1)}, bf16[816,128]{1,0:T(8,128)(2,1)S(1)}, u32[]{:S(2)}, u32[]{:S(2)}) collective-permute-start(bf16[816,128]{1,0:T(8,128)(2,1)S(1)} %collective-permute-done.1.b_ref), channel_id=1, source_target_pairs={{0,1},{1,0},{2,3},{3,2},{4,5},{5,4},{6,7},{7,6},{8,9},{9,8},{10,11... | collective-permute-start | bytes 626696 | tf_op jit(solution)/shard_map/ppermute | solution.py:375
  27.0 2.1 %collective-permute-start.4 = (bf16[256,128]{1,0:T(8,128)(2,1)S(1)}, bf16[256,128]{1,0:T(8,128)(2,1)S(1)}, u32[]{:S(2)}, u32[]{:S(2)}) collective-permute-start(bf16[256,128]{1,0:T(8,128)(2,1)S(1)} %get-tuple-element.102), channel_id=1, source_target_pairs={{0,1},{1,0},{2,3},{3,2},{4,5},{5,4},{6,7},{7,6},{8,9},{9,8},{10,11... | collective-permute-start | bytes 196616 | tf_op jit(solution)/shard_map/ppermute | solution.py:375
  30.3 3.9 %collective-permute-start.5 = (bf16[256,128]{1,0:T(8,128)(2,1)S(1)}, bf16[256,128]{1,0:T(8,128)(2,1)S(1)}, u32[]{:S(2)}, u32[]{:S(2)}) collective-permute-start(bf16[256,128]{1,0:T(8,128)(2,1)S(1)} %get-tuple-element.107), channel_id=1, source_target_pairs={{0,1},{1,0},{2,3},{3,2},{4,5},{5,4},{6,7},{7,6},{8,9},{9,8},{10,11... | collective-permute-start | bytes 196616 | tf_op jit(solution)/shard_map/ppermute | solution.py:375
  32.7 6.1 %collective-permute-start.15 = (bf16[256,128]{1,0:T(8,128)(2,1)S(1)}, bf16[256,128]{1,0:T(8,128)(2,1)S(1)}, u32[]{:S(2)}, u32[]{:S(2)}) collective-permute-start(bf16[256,128]{1,0:T(8,128)(2,1)S(1)} %add_convert_fusion.2), channel_id=1, source_target_pairs={{0,2},{2,0},{1,3},{3,1},{4,6},{6,4},{5,7},{7,5},{8,10},{10,8},{9,1... | collective-permute-start | bytes 196616 | tf_op jit(solution)/shard_map/ppermute | solution.py:425
  35.5 3.3 %collective-permute-start.6 = (bf16[256,128]{1,0:T(8,128)(2,1)S(1)}, bf16[256,128]{1,0:T(8,128)(2,1)S(1)}, u32[]{:S(2)}, u32[]{:S(2)}) collective-permute-start(bf16[256,128]{1,0:T(8,128)(2,1)S(1)} %get-tuple-element.112), channel_id=1, source_target_pairs={{0,1},{1,0},{2,3},{3,2},{4,5},{5,4},{6,7},{7,6},{8,9},{9,8},{10,11... | collective-permute-start | bytes 196616 | tf_op jit(solution)/shard_map/ppermute | solution.py:375
  35.6 5.2 %collective-permute-start.17 = (bf16[256,128]{1,0:T(8,128)(2,1)S(1)}, bf16[256,128]{1,0:T(8,128)(2,1)S(1)}, u32[]{:S(2)}, u32[]{:S(2)}) collective-permute-start(bf16[256,128]{1,0:T(8,128)(2,1)S(1)} %add_convert_fusion.2), channel_id=1, source_target_pairs={{0,14},{2,12},{1,7},{3,5},{4,2},{6,0},{5,11},{7,9},{8,6},{10,4},{9... | collective-permute-start | bytes 196616 | tf_op jit(solution)/shard_map/ppermute | solution.py:426
  36.9 7.8 %collective-permute-start.11 = (bf16[256,128]{1,0:T(8,128)(2,1)S(1)}, bf16[256,128]{1,0:T(8,128)(2,1)S(1)}, u32[]{:S(2)}, u32[]{:S(2)}) collective-permute-start(bf16[256,128]{1,0:T(8,128)(2,1)S(1)} %add_convert_fusion.1), channel_id=1, source_target_pairs={{0,2},{2,0},{1,3},{3,1},{4,6},{6,4},{5,7},{7,5},{8,10},{10,8},{9,1... | collective-permute-start | bytes 196616 | tf_op jit(solution)/shard_map/ppermute | solution.py:425
  38.4 6.3 %collective-permute-start.13 = (bf16[256,128]{1,0:T(8,128)(2,1)S(1)}, bf16[256,128]{1,0:T(8,128)(2,1)S(1)}, u32[]{:S(2)}, u32[]{:S(2)}) collective-permute-start(bf16[256,128]{1,0:T(8,128)(2,1)S(1)} %add_convert_fusion.1), channel_id=1, source_target_pairs={{0,14},{2,12},{1,7},{3,5},{4,2},{6,0},{5,11},{7,9},{8,6},{10,4},{9... | collective-permute-start | bytes 196616 | tf_op jit(solution)/shard_map/ppermute | solution.py:426
  38.8 6.4 %collective-permute-start.16 = (bf16[256,128]{1,0:T(8,128)(2,1)S(1)}, bf16[256,128]{1,0:T(8,128)(2,1)S(1)}, u32[]{:S(2)}, u32[]{:S(2)}) collective-permute-start(bf16[256,128]{1,0:T(8,128)(2,1)S(1)} %collective-permute-done.15.rest_0_), channel_id=1, source_target_pairs={{0,1},{1,0},{2,3},{3,2},{4,5},{5,4},{6,7},{7,6},{8,9},{9,8},{10,11... | collective-permute-start | bytes 196616 | tf_op jit(solution)/shard_map/ppermute | solution.py:375
  38.8 6.4 %collective-permute-start.7 = (bf16[256,128]{1,0:T(8,128)(2,1)S(1)}, bf16[256,128]{1,0:T(8,128)(2,1)S(1)}, u32[]{:S(2)}, u32[]{:S(2)}) collective-permute-start(bf16[256,128]{1,0:T(8,128)(2,1)S(1)} %add_convert_fusion), channel_id=1, source_target_pairs={{0,2},{2,0},{1,3},{3,1},{4,6},{6,4},{5,7},{7,5},{8,10},{10,8},{9,1... | collective-permute-start | bytes 196616 | tf_op jit(solution)/shard_map/ppermute | solution.py:425
  40.8 5.8 %collective-permute-start.9 = (bf16[256,128]{1,0:T(8,128)(2,1)S(1)}, bf16[256,128]{1,0:T(8,128)(2,1)S(1)}, u32[]{:S(2)}, u32[]{:S(2)}) collective-permute-start(bf16[256,128]{1,0:T(8,128)(2,1)S(1)} %add_convert_fusion), channel_id=1, source_target_pairs={{0,14},{2,12},{1,7},{3,5},{4,2},{6,0},{5,11},{7,9},{8,6},{10,4},{9... | collective-permute-start | bytes 196616 | tf_op jit(solution)/shard_map/ppermute | solution.py:426
  44.7 3.1 %collective-permute-start.18 = (bf16[256,128]{1,0:T(8,128)(2,1)S(1)}, bf16[256,128]{1,0:T(8,128)(2,1)S(1)}, u32[]{:S(2)}, u32[]{:S(2)}) collective-permute-start(bf16[256,128]{1,0:T(8,128)(2,1)S(1)} %collective-permute-done.17.rest_2_), channel_id=1, source_target_pairs={{0,1},{1,0},{2,3},{3,2},{4,5},{5,4},{6,7},{7,6},{8,9},{9,8},{10,11... | collective-permute-start | bytes 196616 | tf_op jit(solution)/shard_map/ppermute | solution.py:375
  44.7 5.4 %collective-permute-start.12 = (bf16[256,128]{1,0:T(8,128)(2,1)S(1)}, bf16[256,128]{1,0:T(8,128)(2,1)S(1)}, u32[]{:S(2)}, u32[]{:S(2)}) collective-permute-start(bf16[256,128]{1,0:T(8,128)(2,1)S(1)} %collective-permute-done.11.rest_0_), channel_id=1, source_target_pairs={{0,1},{1,0},{2,3},{3,2},{4,5},{5,4},{6,7},{7,6},{8,9},{9,8},{10,11... | collective-permute-start | bytes 196616 | tf_op jit(solution)/shard_map/ppermute | solution.py:375
  45.2 4.9 %collective-permute-start.14 = (bf16[256,128]{1,0:T(8,128)(2,1)S(1)}, bf16[256,128]{1,0:T(8,128)(2,1)S(1)}, u32[]{:S(2)}, u32[]{:S(2)}) collective-permute-start(bf16[256,128]{1,0:T(8,128)(2,1)S(1)} %collective-permute-done.13.rest_2_), channel_id=1, source_target_pairs={{0,1},{1,0},{2,3},{3,2},{4,5},{5,4},{6,7},{7,6},{8,9},{9,8},{10,11... | collective-permute-start | bytes 196616 | tf_op jit(solution)/shard_map/ppermute | solution.py:375
  45.3 6.9 %collective-permute-start.8 = (bf16[256,128]{1,0:T(8,128)(2,1)S(1)}, bf16[256,128]{1,0:T(8,128)(2,1)S(1)}, u32[]{:S(2)}, u32[]{:S(2)}) collective-permute-start(bf16[256,128]{1,0:T(8,128)(2,1)S(1)} %collective-permute-done.7.rest_0_), channel_id=1, source_target_pairs={{0,1},{1,0},{2,3},{3,2},{4,5},{5,4},{6,7},{7,6},{8,9},{9,8},{10,11... | collective-permute-start | bytes 196616 | tf_op jit(solution)/shard_map/ppermute | solution.py:375
  46.6 5.6 %collective-permute-start.10 = (bf16[256,128]{1,0:T(8,128)(2,1)S(1)}, bf16[256,128]{1,0:T(8,128)(2,1)S(1)}, u32[]{:S(2)}, u32[]{:S(2)}) collective-permute-start(bf16[256,128]{1,0:T(8,128)(2,1)S(1)} %collective-permute-done.9.rest_2_), channel_id=1, source_target_pairs={{0,1},{1,0},{2,3},{3,2},{4,5},{5,4},{6,7},{7,6},{8,9},{9,8},{10,11... | collective-permute-start | bytes 196616 | tf_op jit(solution)/shard_map/ppermute | solution.py:375
  54.3 5.2 %collective-permute-start.19 = (bf16[472,128]{1,0:T(8,128)(2,1)S(1)}, bf16[472,128]{1,0:T(8,128)(2,1)S(1)}, u32[]{:S(2)}, u32[]{:S(2)}) collective-permute-start(bf16[472,128]{1,0:T(8,128)(2,1)S(1)} %pad_maximum_fusion), channel_id=1, source_target_pairs={{0,4},{4,0},{8,12},{12,8},{1,5},{5,1},{9,13},{13,9},{2,6},{6,2},{1... | collective-permute-start | bytes 362504 | tf_op jit(solution)/shard_map/ppermute | solution.py:483
  54.4 9.7 %collective-permute-start.21 = (bf16[2,256,128]{2,1,0:T(8,128)(2,1)S(1)}, bf16[2,256,128]{2,1,0:T(8,128)(2,1)S(1)}, u32[]{:S(2)}, u32[]{:S(2)}) collective-permute-start(bf16[2,256,128]{2,1,0:T(8,128)(2,1)S(1)} %get-tuple-element.131.refs_1_), channel_id=1, source_target_pairs={{0,1},{1,0},{2,3},{3,2},{4,5},{5,4},{6,7},{7,6},{8,9},{9,8},{10,11... | collective-permute-start | bytes 393224 | tf_op jit(solution)/shard_map/ppermute | solution.py:375
  54.4 9.6 %collective-permute-start.22 = (bf16[2,256,128]{2,1,0:T(8,128)(2,1)S(1)}, bf16[2,256,128]{2,1,0:T(8,128)(2,1)S(1)}, u32[]{:S(2)}, u32[]{:S(2)}) collective-permute-start(bf16[2,256,128]{2,1,0:T(8,128)(2,1)S(1)} %get-tuple-element.133.refs_4_), channel_id=1, source_target_pairs={{0,1},{1,0},{2,3},{3,2},{4,5},{5,4},{6,7},{7,6},{8,9},{9,8},{10,11... | collective-permute-start | bytes 393224 | tf_op jit(solution)/shard_map/ppermute | solution.py:375
  54.9 9.1 %collective-permute-start.23 = (bf16[2,256,128]{2,1,0:T(8,128)(2,1)S(1)}, bf16[2,256,128]{2,1,0:T(8,128)(2,1)S(1)}, u32[]{:S(2)}, u32[]{:S(2)}) collective-permute-start(bf16[2,256,128]{2,1,0:T(8,128)(2,1)S(1)} %get-tuple-element.135.refs_7_), channel_id=1, source_target_pairs={{0,1},{1,0},{2,3},{3,2},{4,5},{5,4},{6,7},{7,6},{8,9},{9,8},{10,11... | collective-permute-start | bytes 393224 | tf_op jit(solution)/shard_map/ppermute | solution.py:375
  59.6 7.7 %collective-permute-start.20 = (bf16[472,128]{1,0:T(8,128)(2,1)S(1)}, bf16[472,128]{1,0:T(8,128)(2,1)S(1)}, u32[]{:S(2)}, u32[]{:S(2)}) collective-permute-start(bf16[472,128]{1,0:T(8,128)(2,1)S(1)} %fusion.refs_0_), channel_id=1, source_target_pairs={{0,12},{4,8},{8,4},{12,0},{1,13},{5,9},{9,5},{13,1},{2,14},{6,10},... | collective-permute-start | bytes 362504 | tf_op jit(solution)/shard_map/ppermute | solution.py:484

commit v4 on v3

--- a/solution.py
+++ b/solution.py
@@ -57,30 +57,16 @@
     return outs
 
 
-def pack_kernel(groups, cells, wide, x_ref, ct_ref, tag_ref, *rest):
-    micro = sum(len(group) for group in groups)
-    outs, (own_ref, lab_ref, sem) = rest[: 2 * len(groups)], rest[2 * len(groups) :]
-    spots = []
-    for n, group in enumerate(groups):
-        for i in range(len(group)):
-            at = i * (cells + wide)
-            a_ref = outs[2 * n].at[pl.ds(at + i * cells, 2 * cells + wide)]
-            spots.append((a_ref, outs[2 * n + 1].at[pl.ds(at, cells + wide)]))
-    tags = pltpu.make_async_copy(tag_ref, lab_ref, sem.at[3 * micro])
+def pack_kernel(micro, cells, wide, x_ref, tag_ref, out_ref, own_ref, lab_ref, sem):
+    tags = pltpu.make_async_copy(tag_ref, lab_ref, sem.at[micro])
     tags.start()
     c = lax.axis_index("chan")
     copies = []
     for m in range(micro):
-        a_ref, b_ref = spots[m]
-        moves = (
-            (x_ref.at[m, c], a_ref.at[0:cells]),
-            (x_ref.at[m, c], b_ref.at[0:cells]),
-            (ct_ref.at[m, c], a_ref.at[cells + wide : 2 * cells + wide]),
-        )
-        for n, (src, dst) in enumerate(moves):
-            copy = pltpu.make_async_copy(src, dst, sem.at[3 * m + n])
-            copy.start()
-            copies.append(copy)
+        spot = out_ref.at[pl.ds(m * (cells + wide), cells)]
+        copy = pltpu.make_async_copy(x_ref.at[m, c], spot, sem.at[m])
+        copy.start()
+        copies.append(copy)
     deep = lab_ref.shape[3]
     tags.wait()
     row = lax.broadcasted_iota(jnp.int32, (LANES, LANES), 0)
@@ -91,9 +77,7 @@
             own_ref[m, p] = jnp.zeros((deep, LANES), BF)
             turned = nt_dot(eye, lab_ref[m, p].astype(F32).astype(BF))
             own_ref[m, p, :, 0:wide] = turned.astype(BF)
-        lab = own_ref[m, c]
-        spots[m][0][cells : cells + wide] = lab
-        spots[m][1][cells : cells + wide] = lab
+        out_ref[m * (cells + wide) + cells : (m + 1) * (cells + wide)] = own_ref[m, c]
     for copy in copies:
         copy.wait()
 
@@ -149,8 +133,13 @@
 def own_kernel(
     micro, wide, deep, x_ref, ct_ref, lab_ref, w_ref, rw_ref, code_ref, *outs
 ):
-    for src, dst in zip((x_ref, ct_ref, w_ref, rw_ref, code_ref), outs[3 * micro :]):
+    *kept, edge_ref = outs[3 * micro :]
+    for src, dst in zip((x_ref, ct_ref, w_ref, rw_ref, code_ref), kept):
         dst[...] = src[...]
+    c = lax.axis_index("chan")
+    cells = wide * deep
+    for m in range(micro):
+        edge_ref[m * cells : (m + 1) * cells] = ct_ref[m, c]
     codes = code_rows(code_ref, deep)
     for m in range(micro):
         hs_ref, hid_ref, spre_ref = outs[3 * m : 3 * m + 3]
@@ -182,11 +171,10 @@
     c = lax.axis_index("chan")
     cells = wide * deep
     codes = code_rows(code_ref, deep)
-    a_ref, a2_ref = [v.at[pl.ds(slot * (2 * cells + wide), 2 * cells + wide)] for v in (a_ref, a2_ref)]
-    b_ref, b2_ref = [v.at[pl.ds(slot * (cells + wide), cells + wide)] for v in (b_ref, b2_ref)]
+    start = slot * (cells + wide)
     for ref, plane in ((a_ref, 2 - c), (b_ref, 3 * c), (a2_ref, 1 + c), (b2_ref, 3 - 3 * c)):
-        lab = ref[cells : cells + wide]
-        pre = hidden_rows(ref[0:cells], lab, w_ref[...], codes, wide, deep)
+        lab = ref[start + cells : start + cells + wide]
+        pre = hidden_rows(ref[start : start + cells], lab, w_ref[...], codes, wide, deep)
         store_shifts(hs_ref, plane, pre * gate(pre), wide, deep)
     planes = [(hs_ref, 0), (hs_ref, 1), (own_ref, 0), (own_ref, 1), (hs_ref, 2), (hs_ref, 3)]
     for p, conv in enumerate(conv_pairs(planes, (1, 3), kf_ref, cells, deep)):
@@ -199,7 +187,7 @@
 def backward_kernel(
     mode,
     m,
-    slot,
+    sent_slot,
     wide,
     deep,
     taps,
@@ -217,7 +205,7 @@
 ):
     c = lax.axis_index("chan")
     cells = wide * deep
-    tail = pl.ds(slot * (2 * cells + wide) + cells + wide, cells)
+    tail = pl.ds(m * cells, cells)
     full = mode == "full"
     if mode == "first":
         base_ref, other_ref, gs_ref, br_ref = rest
@@ -230,6 +218,7 @@
             part_ref, up_ref, exp_ref, red_ref, kg_ref, gs_ref = rest
         else:
             base_ref, other_ref, gs_ref, br_ref, up_ref = rest
+        here = pl.ds(sent_slot * cells, cells)
         last = lax.axis_index("section") == lax.axis_size("section") - 1
 
         @pl.when(last)
@@ -239,11 +228,11 @@
 
         @pl.when(jnp.logical_not(last))
         def _():
-            up_ref[c] = st_ref[...]
-            up_ref[1 - c] = st2_ref[...]
-
-        halo = jnp.where(last, cta_ref[tail], dg_ref[...])
-        halo2 = jnp.where(last, cta2_ref[tail], dg2_ref[...])
+            up_ref[c] = st_ref[here]
+            up_ref[1 - c] = st2_ref[here]
+
+        halo = jnp.where(last, cta_ref[tail], dg_ref[here])
+        halo2 = jnp.where(last, cta2_ref[tail], dg2_ref[here])
     ups = ((up_ref[0], 1), (up_ref[1], 2), (halo, 3 - 3 * c), (halo2, 3 * c))
     for up, plane in ups:
         grad = nt_dot(up, rw_ref[...]) * sconv_ref[plane]
@@ -316,8 +305,8 @@
         outs[2][:, i] = turned[:, :taps].reshape(LANES // width, width, taps)
 
 
-def GROUPS(micro):
-    return [list(range(micro))]
+def SENDS(micro):
+    return [[m] for m in range(micro)]
 
 
 def sds(shape, dtype):
@@ -338,7 +327,7 @@
         out_shape=out_shape,
         scratch_shapes=list(scratch),
         name=name,
-        cost_estimate=pl.CostEstimate(flops=1000, bytes_accessed=1000, transcendentals=0),
+        cost_estimate=pl.CostEstimate(flops=2 * 10**9, bytes_accessed=4 * 2**20, transcendentals=0),
         compiler_params=params(room),
     )(*args)
 
@@ -374,20 +363,18 @@
     def swap(v):
         return lax.ppermute(v, "chan", [(0, 1), (1, 0)])
 
-    groups_m = GROUPS(micro)
-    rows_a, rows_b = 2 * cells + wide, cells + wide
+    rows = cells + wide
     hbm = pl.BlockSpec(memory_space=pltpu.HBM)
-    *packed, lab = call(
-        functools.partial(pack_kernel, groups_m, cells, wide),
+    packed, lab = call(
+        functools.partial(pack_kernel, micro, cells, wide),
         "pack",
-        [sds((len(g) * n, LANES), BF) for g in groups_m for n in (rows_a, rows_b)]
-        + [sds((micro, depth, deep, LANES), BF)],
-        (x, ct, phase_labels),
+        [sds((micro * rows, LANES), BF), sds((micro, depth, deep, LANES), BF)],
+        (x, phase_labels),
         [
             pltpu.VMEM(phase_labels.shape, jnp.int32),
-            pltpu.SemaphoreType.DMA((3 * micro + 1,)),
+            pltpu.SemaphoreType.DMA((micro + 1,)),
         ],
-        [hbm, hbm, hbm],
+        [hbm, hbm],
         60,
     )
     plane2, plane4, flat = (2, cells, LANES), (4, cells, LANES), (cells, LANES)
@@ -400,30 +387,34 @@
         (kern,),
         [pltpu.VMEM((LANES * width, LANES), F32), pltpu.VMEM((2,) + thin, F32)],
     )
-    *owned, x, ct, w, rw, code = call(
+    *owned, x, ct, w, rw, code, edge = call(
         functools.partial(own_kernel, micro, wide, deep),
         "own",
         [sds((2, pad_rows, 3 * LANES), BF), sds(plane2, BF), sds(plane2, F32)] * micro
-        + [sds(v.shape, v.dtype) for v in (x, ct, w, rw, code)],
+        + [sds(v.shape, v.dtype) for v in (x, ct, w, rw, code)]
+        + [sds((micro * cells, LANES), BF)],
         (x, ct, lab, w, rw, code),
     )
-    halos, slots = [], []
-    for n, group in enumerate(groups_m):
-        a = lax.ppermute(packed[2 * n], ("space", "chan"), route_a)
-        b = lax.ppermute(packed[2 * n + 1], ("space", "chan"), route_b)
-        if n == 0:
-            a, b, dense_f, dense_b, *owned = lax.optimization_barrier(
-                (a, b, dense_f, dense_b, *owned)
-            )
-        halos += [(a, b, swap(a), swap(b))] * len(group)
-        slots += list(range(len(group)))
-
-    def joined(base, other):
-        return (base + swap(other).astype(F32)).astype(BF)
+    a = lax.ppermute(packed, ("space", "chan"), route_a)
+    b = lax.ppermute(packed, ("space", "chan"), route_b)
+    a, b, dense_f, dense_b, *owned = lax.optimization_barrier((a, b, dense_f, dense_b, *owned))
+    halos = (a, b, swap(a), swap(b))
+    edge = lax.ppermute(edge, ("space", "chan"), route_a)
+
+    def joined(pairs):
+        outs = [(base + swap(other).astype(F32)).astype(BF) for base, other in pairs]
+        return outs[0] if len(outs) == 1 else jnp.concatenate(outs, axis=0)
 
     def send_on(out):
         st = lax.ppermute(out, "section", route_s)
         dg = lax.ppermute(out, ("space", "section", "chan"), route_d)
+        return st, dg
+
+    def after(arrays, first):
+        *arrays, _ = lax.optimization_barrier((*arrays, first))
+        return arrays
+
+    def shared(st, dg):
         return st, swap(st), dg, swap(dg)
 
     def back_pass(mode, m, extra, extra_out=()):
@@ -434,46 +425,64 @@
         if mode == "light":
             scratch.append(pltpu.VMEM(plane2, BF))
         return call(
-            functools.partial(backward_kernel, mode, m, slots[m], wide, deep, taps, width),
+            functools.partial(backward_kernel, mode, m, sent_slot[m], wide, deep, taps, width),
             "backward_" + mode,
             outs + list(extra_out),
-            (x, ct, halos[m][0], halos[m][2], w, rw, dense_b, spre[m], sconv[m], *extra),
+            (x, ct, *edges, w, rw, dense_b, spre[m], sconv[m], *extra),
             scratch,
         )
 
-    sconv, mixed, ups = [], [], []
+    sconv, mixed, sent = [], [], []
+    sends = SENDS(micro)
+    sender = [n for n, group in enumerate(sends) for _ in group]
+    sent_slot = [i for group in sends for i in range(len(group))]
     spre = [owned[3 * m + 2] for m in range(micro)]
-    pending = None
-    for m in range(micro):
-        a, b, a2, b2 = halos[m]
+    for m in range(micro):
+        if m:
+            (code,) = after((code,), sconv[-1])
         con, mix = call(
-            functools.partial(forward_kernel, slots[m], wide, deep),
+            functools.partial(forward_kernel, m, wide, deep),
             "forward",
             [sds(plane4, F32), sds(plane2, BF)],
-            (owned[3 * m], a, b, a2, b2, w, code, dense_f),
+            (owned[3 * m], *halos, w, code, dense_f),
             [pltpu.VMEM((4, pad_rows, 3 * LANES), BF)],
         )
         sconv.append(con)
         mixed.append(mix)
-        if pending is not None:
-            out, sconv[m] = lax.optimization_barrier((joined(*pending), sconv[m]))
-            ups.append(send_on(out))
-        pending = back_pass("first", m, ())
-    ups.append(send_on(joined(*pending)))
+    (edge,) = after((edge,), sconv[-1])
+    edges = (edge, swap(edge))
+    pending = []
+    for m in range(micro):
+        if m == 0:
+            (sconv[m],) = after((sconv[m],), sconv[-1])
+        if pending and len(pending) == len(sends[len(sent)]):
+            out, sconv[m] = lax.optimization_barrier((joined(pending), sconv[m]))
+            sent.append(send_on(out))
+            pending = []
+        pending.append(back_pass("first", m, ()))
+    out = joined(pending)
+    sent = [after(pair, pending[-1][1]) for pair in sent[:1]] + [after(pair, pending[-1][1]) for pair in sent[1:]]
+    sent.append(send_on(out))
+    ups = [shared(*pair) for pair in sent]
 
     rank = lax.axis_index("section")
     for stage in range(1, sections - 1):
-        fresh = [send_on(joined(*back_pass("light", m, ups[m]))) for m in range(micro)]
+        fresh = []
+        for group in sends:
+            out = joined([back_pass("light", m, ups[sender[m]]) for m in group])
+            fresh.append(shared(*send_on(out)))
         mine = rank == sections - 2 - stage
         ups = [
-            tuple(jnp.where(mine, n, o) for n, o in zip(fresh[m], ups[m])) for m in range(micro)
+            tuple(jnp.where(mine, n, o) for n, o in zip(new, old)) for new, old in zip(fresh, ups)
         ]
     sum_shapes = [sds(s, F32) for s in (square, square, thin)]
     sums = [jnp.zeros(s.shape, F32) for s in sum_shapes]
     pieces = []
     for m in range(micro):
-        extra = (*ups[m], owned[3 * m + 1], mixed[m], *sums)
+        extra = (*ups[sender[m]], owned[3 * m + 1], mixed[m], *sums)
         part, up, *sums = back_pass("full", m, extra, sum_shapes)
+        if m == 0 and sections == 2 and sender[-1] > 0:
+            ups[-1] = shared(*after(sent[-1], part))
         pieces += [up, part, swap(part)]
 
     grads = jnp.concatenate([s.astype(BF) for s in sums], axis=0)

time: 68.8 us -> 64.1 us (0.932)
  local copies, waits for them, and re-layouts: 5.9 us -> 0.14 us
  starting transfers between devices: 23.9 us -> 24.8 us
  waiting for transfers between devices: 16.2 us -> 16.9 us
    unnamed x13 -> x15, local copies, waits for them, and re-layouts: 5.88 us -> 0.12 us
    ppermute x2 -> x3, starting transfers between devices: 5.1 us -> 6.84 us  [the longest x1 5.1 us: on_device(): a = lax.ppermute(packed, ('space', 'chan'), route_a)]
    ppermute x2 -> x3, waiting for transfers between devices: 6.42 us -> 7.91 us  [the longest x1 3.96 us: on_device(): b = lax.ppermute(packed, ('space', 'chan'), route_b)]
    ppermute x3, waiting for transfers between devices: 1.31 us -> 0.01 us  [send_on(): dg = lax.ppermute(out, ('space', 'section', 'chan'), route_d)]
    ppermute x1, starting transfers between devices: 4.44 us -> 3.46 us  [on_device(): copies = [grads, lax.ppermute(grads, 'space', far)]]
    ppermute x14 -> x15, waiting for transfers between devices: 1.56 us -> 2.17 us  [swap(): return lax.ppermute(v, 'chan', [(0, 1), (1, 0)])]
    ppermute x14 -> x15, starting transfers between devices: 4.11 us -> 3.66 us  [swap(): return lax.ppermute(v, 'chan', [(0, 1), (1, 0)])]
  transfers between devices with their start and end apart: 24 -> 26, of which waited for: 6 -> 7; matrix products, arithmetic and copies ran while one was open for 1% -> 0% of each run, Pallas kernels for 17% -> 22%
where the time goes in v4:
time: 64.1 us; the launch traced here: 64 us
  starting transfers between devices  24.8 us (39%)
  Pallas kernels  21.1 us (33%)
  waiting for transfers between devices  16.9 us (26%)
  between operations  0.93 us (1%)
    pallas_call x14, Pallas kernels, call(): pl.pallas_call(kernel, in_specs=[vmem] * len(args) if in_specs is None el...  21.1 us
    ppermute x3, starting transfers between devices, send_on(): dg = lax.ppermute(out, ('space', 'section', 'chan'), route_d)  5.8 us
    ppermute x1, starting transfers between devices, on_device(): a = lax.ppermute(packed, ('space', 'chan'), route_a)  5.1 us
    ppermute x3, starting transfers between devices, send_on(): st = lax.ppermute(out, 'section', route_s)  4.52 us
    ppermute x1, waiting for transfers between devices, on_device(): grads = grads + lax.ppermute(grads, 'space', near)  4.28 us
    ppermute x1, waiting for transfers between devices, on_device(): b = lax.ppermute(packed, ('space', 'chan'), route_b)  3.96 us
    ppermute x1, waiting for transfers between devices, on_device(): a = lax.ppermute(packed, ('space', 'chan'), route_a)  3.95 us
    ppermute x15, starting transfers between devices, swap(): return lax.ppermute(v, 'chan', [(0, 1), (1, 0)])  3.66 us
  transfers between devices with their start and end apart: 26, of which 7 were waited for; matrix products, arithmetic and copies ran while one was open for 0% of the time, Pallas kernels for 22%

profile of v4, /device:TPU:0, one launch (start us, length us, event | category | flops | bytes accessed | tf_op | source)
XLA Modules:
  0.0 64.0 jit_solution(1467126832244943824)
XLA Ops:
  0.6 1.7 %pack.1 = (bf16[816,128]{1,0:T(8,128)(2,1)}, bf16[3,2,16,128]{3,2,1,0:T(8,128)(2,1)}) custom-call(bf16[3,2,256,128]{3,2,1,0:T(8,128)(2,1)} %bitcast.16, s32[3,2,16,16]{3,2,1,0:T(8,128)} %tag_ref.1), custom_call_target="tpu_custom_call" | custom-call | flops 2000000000 | bytes 4194304 | tf_op jit(solution)/shard_map/pack/pallas_call | solution.py:323
  2.4 5.1 %collective-permute-start.1 = (bf16[816,128]{1,0:T(8,128)(2,1)}, bf16[816,128]{1,0:T(8,128)(2,1)S(1)}, u32[]{:S(2)}, u32[]{:S(2)}) collective-permute-start(bf16[816,128]{1,0:T(8,128)(2,1)} %get-tuple-element.87), channel_id=1, source_target_pairs={{0,12},{1,5},{4,0},{5,9},{8,4},{9,13},{12,8},{13,1},{2,14},{3,7},{... | collective-permute-start | bytes 626696 | tf_op jit(solution)/shard_map/ppermute | solution.py:398
  7.5 0.0 collective-permute-start.2
  7.5 0.0 copy-start.1
  7.5 0.0 copy-start.3
  7.5 0.0 copy-start.4
  7.5 0.0 copy-start.5
  7.5 0.9 %weights.1 = (bf16[4608,256]{1,0:T(8,128)(2,1)S(1)}, bf16[4608,256]{1,0:T(8,128)(2,1)S(1)}) custom-call(bf16[16,8,8,27]{3,2,1,0:T(8,128)(2,1)S(1)} %bitcast.19), custom_call_target="tpu_custom_call" | custom-call | flops 2000000000 | bytes 4194304 | tf_op jit(solution)/shard_map/weights/pallas_call | solution.py:323
  8.5 0.1 copy-done.1
  8.6 0.8 %own.1 = (bf16[2,288,384]{2,1,0:T(8,128)(2,1)S(1)}, bf16[2,256,128]{2,1,0:T(8,128)(2,1)S(1)}, f32[2,256,128]{2,1,0:T(8,128)S(1)}, bf16[2,288,384]{2,1,0:T(8,128)...) custom-call(bf16[3,2,256,128]{3,2,1,0:T(8,128)(2,1)S(1)} %bitcast.17, ...), custom_call_target="tpu_custom_call" | custom-call | flops 2000000000 | bytes 4194304 | tf_op jit(solution)/shard_map/own/pallas_call | solution.py:323
  9.4 3.9 %collective-permute-done.1.a_ref = bf16[816,128]{1,0:T(8,128)(2,1)S(1)} collective-permute-done((bf16[816,128]{1,0:T(8,128)(2,1)}, bf16[816,128]{1,0:T(8,128)(2,1)S(1)}, u32[]{:S(2)}, u32[]{:S(2)}) %collective-permute-start.1) | collective-permute-done | bytes 208928 | tf_op jit(solution)/shard_map/ppermute | solution.py:398
  13.3 4.0 %collective-permute-done.2.b_ref = bf16[816,128]{1,0:T(8,128)(2,1)S(1)} collective-permute-done((bf16[816,128]{1,0:T(8,128)(2,1)}, bf16[816,128]{1,0:T(8,128)(2,1)S(1)}, u32[]{:S(2)}, u32[]{:S(2)}) %collective-permute-start.2) | collective-permute-done | bytes 208928 | tf_op jit(solution)/shard_map/ppermute | solution.py:399
  17.3 0.0 collective-permute-start.3
  17.3 0.5 collective-permute-start.4
  17.8 1.7 %collective-permute-start = (bf16[768,128]{1,0:T(8,128)(2,1)S(1)}, bf16[768,128]{1,0:T(8,128)(2,1)S(1)}, u32[]{:S(2)}, u32[]{:S(2)}) collective-permute-start(bf16[768,128]{1,0:T(8,128)(2,1)S(1)} %get-tuple-element.86), channel_id=1, source_target_pairs={{0,12},{1,5},{4,0},{5,9},{8,4},{9,13},{12,8},{13,1},{2,14},{3,7},{... | collective-permute-start | bytes 589832 | tf_op jit(solution)/shard_map/ppermute | solution.py:402
  19.6 1.9 %forward.3 = (f32[4,256,128]{2,1,0:T(8,128)S(1)}, bf16[2,256,128]{2,1,0:T(8,128)(2,1)S(1)}) custom-call(bf16[2,288,384]{2,1,0:T(8,128)(2,1)S(1)} %get-tuple-element.104.own_ref, bf16[816,128]{1,0:T(8,128)(2,1)S(1)} %collective-permute-done.1.a_ref, bf16[816,128]{1,0:T(8,128)(2,1)S(1)} %collective-permute-done.2.b_ref, ...), custom_call_target="tpu_custom_call" | custom-call | flops 2000000000 | bytes 4194304 | tf_op jit(solution)/shard_map/forward/pallas_call | solution.py:323
  21.5 1.9 %forward.4 = (f32[4,256,128]{2,1,0:T(8,128)S(1)}, bf16[2,256,128]{2,1,0:T(8,128)(2,1)S(1)}) custom-call(bf16[2,288,384]{2,1,0:T(8,128)(2,1)S(1)} %get-tuple-element.108.own_ref, bf16[816,128]{1,0:T(8,128)(2,1)S(1)} %collective-permute-done.1.a_ref, bf16[816,128]{1,0:T(8,128)(2,1)S(1)} %collective-permute-done.2.b_ref, ...), custom_call_target="tpu_custom_call" | custom-call | flops 2000000000 | bytes 4194304 | tf_op jit(solution)/shard_map/forward/pallas_call | solution.py:323
  23.3 1.9 %forward.5 = (f32[4,256,128]{2,1,0:T(8,128)S(1)}, bf16[2,256,128]{2,1,0:T(8,128)(2,1)S(1)}) custom-call(bf16[2,288,384]{2,1,0:T(8,128)(2,1)S(1)} %get-tuple-element.99.own_ref, bf16[816,128]{1,0:T(8,128)(2,1)S(1)} %collective-permute-done.1.a_ref, bf16[816,128]{1,0:T(8,128)(2,1)S(1)} %collective-permute-done.2.b_ref, ...), custom_call_target="tpu_custom_call" | custom-call | flops 2000000000 | bytes 4194304 | tf_op jit(solution)/shard_map/forward/pallas_call | solution.py:323
  25.2 0.3 collective-permute-start.5
  25.6 1.2 %collective-permute-done.5.cta2_ref = bf16[768,128]{1,0:T(8,128)(2,1)S(1)} collective-permute-done((bf16[768,128]{1,0:T(8,128)(2,1)S(1)}, bf16[768,128]{1,0:T(8,128)(2,1)S(1)}, u32[]{:S(2)}, u32[]{:S(2)}) %collective-permute-start.5) | collective-permute-done | bytes 196640 | tf_op jit(solution)/shard_map/ppermute | solution.py:364
  26.7 1.2 %backward_first.3 = (f32[256,128]{1,0:T(8,128)S(1)}, bf16[256,128]{1,0:T(8,128)(2,1)S(1)}) custom-call(bf16[3,2,256,128]{3,2,1,0:T(8,128)(2,1)S(1)} %get-tuple-element.84.x_ref, bf16[3,2,256,128]{3,2,1,0:T(8,128)(2,1)S(1)} %get-tuple-element.85.ct_ref, bf16[768,128]{1,0:T(8,128)(2,1)S(1)} %collective-permute-done.cta_ref, ...), custom_call_target="tpu_custom_call" | custom-call | flops 2000000000 | bytes 4194304 | tf_op jit(solution)/shard_map/backward_first/pallas_call | solution.py:323
  28.0 0.3 collective-permute-start.6
  28.3 1.0 %collective-permute-done.6 = bf16[256,128]{1,0:T(8,128)(2,1)S(1)} collective-permute-done((bf16[256,128]{1,0:T(8,128)(2,1)S(1)}, bf16[256,128]{1,0:T(8,128)(2,1)S(1)}, u32[]{:S(2)}, u32[]{:S(2)}) %collective-permute-start.6) | collective-permute-done | bytes 65568 | tf_op jit(solution)/shard_map/ppermute | solution.py:364
  29.3 1.2 %backward_first.4 = (f32[256,128]{1,0:T(8,128)S(1)}, bf16[256,128]{1,0:T(8,128)(2,1)S(1)}) custom-call(bf16[3,2,256,128]{3,2,1,0:T(8,128)(2,1)S(1)} %get-tuple-element.84.x_ref, bf16[3,2,256,128]{3,2,1,0:T(8,128)(2,1)S(1)} %get-tuple-element.85.ct_ref, bf16[768,128]{1,0:T(8,128)(2,1)S(1)} %collective-permute-done.cta_ref, ...), custom_call_target="tpu_custom_call" | custom-call | flops 2000000000 | bytes 4194304 | tf_op jit(solution)/shard_map/backward_first/pallas_call | solution.py:323
  30.6 0.3 collective-permute-start.7
  30.9 1.5 %collective-permute-start.11 = (bf16[256,128]{1,0:T(8,128)(2,1)S(1)}, bf16[256,128]{1,0:T(8,128)(2,1)S(1)}, u32[]{:S(2)}, u32[]{:S(2)}) collective-permute-start(bf16[256,128]{1,0:T(8,128)(2,1)S(1)} %add_convert_fusion.2), channel_id=1, source_target_pairs={{0,2},{2,0},{1,3},{3,1},{4,6},{6,4},{5,7},{7,5},{8,10},{10,8},{9,1... | collective-permute-start | bytes 196616 | tf_op jit(solution)/shard_map/ppermute | solution.py:409
  32.4 1.6 %collective-permute-start.12 = (bf16[256,128]{1,0:T(8,128)(2,1)S(1)}, bf16[256,128]{1,0:T(8,128)(2,1)S(1)}, u32[]{:S(2)}, u32[]{:S(2)}) collective-permute-start(bf16[256,128]{1,0:T(8,128)(2,1)S(1)} %add_convert_fusion.2), channel_id=1, source_target_pairs={{0,14},{2,12},{1,7},{3,5},{4,2},{6,0},{5,11},{7,9},{8,6},{10,4},{9... | collective-permute-start | bytes 196616 | tf_op jit(solution)/shard_map/ppermute | solution.py:410
  34.0 1.2 %backward_first.5 = (f32[256,128]{1,0:T(8,128)S(1)}, bf16[256,128]{1,0:T(8,128)(2,1)S(1)}) custom-call(bf16[3,2,256,128]{3,2,1,0:T(8,128)(2,1)S(1)} %get-tuple-element.84.x_ref, bf16[3,2,256,128]{3,2,1,0:T(8,128)(2,1)S(1)} %get-tuple-element.85.ct_ref, bf16[768,128]{1,0:T(8,128)(2,1)S(1)} %collective-permute-done.cta_ref, ...), custom_call_target="tpu_custom_call" | custom-call | flops 2000000000 | bytes 4194304 | tf_op jit(solution)/shard_map/backward_first/pallas_call | solution.py:323
  35.3 0.1 collective-permute-start.8
  35.4 1.6 %collective-permute-start.17 = (bf16[256,128]{1,0:T(8,128)(2,1)S(1)}, bf16[256,128]{1,0:T(8,128)(2,1)S(1)}, u32[]{:S(2)}, u32[]{:S(2)}) collective-permute-start(bf16[256,128]{1,0:T(8,128)(2,1)S(1)} %add_convert_fusion.1), channel_id=1, source_target_pairs={{0,2},{2,0},{1,3},{3,1},{4,6},{6,4},{5,7},{7,5},{8,10},{10,8},{9,1... | collective-permute-start | bytes 196616 | tf_op jit(solution)/shard_map/ppermute | solution.py:409
  36.9 1.8 %collective-permute-start.18 = (bf16[256,128]{1,0:T(8,128)(2,1)S(1)}, bf16[256,128]{1,0:T(8,128)(2,1)S(1)}, u32[]{:S(2)}, u32[]{:S(2)}) collective-permute-start(bf16[256,128]{1,0:T(8,128)(2,1)S(1)} %add_convert_fusion.1), channel_id=1, source_target_pairs={{0,14},{2,12},{1,7},{3,5},{4,2},{6,0},{5,11},{7,9},{8,6},{10,4},{9... | collective-permute-start | bytes 196616 | tf_op jit(solution)/shard_map/ppermute | solution.py:410
  38.7 0.5 collective-permute-start.14
  39.2 2.4 %collective-permute-start.10 = (bf16[256,128]{1,0:T(8,128)(2,1)S(1)}, bf16[256,128]{1,0:T(8,128)(2,1)S(1)}, u32[]{:S(2)}, u32[]{:S(2)}) collective-permute-start(bf16[256,128]{1,0:T(8,128)(2,1)S(1)} %add_convert_fusion), channel_id=1, source_target_pairs={{0,14},{2,12},{1,7},{3,5},{4,2},{6,0},{5,11},{7,9},{8,6},{10,4},{9... | collective-permute-start | bytes 196616 | tf_op jit(solution)/shard_map/ppermute | solution.py:410
  41.7 1.5 %collective-permute-start.9 = (bf16[256,128]{1,0:T(8,128)(2,1)S(1)}, bf16[256,128]{1,0:T(8,128)(2,1)S(1)}, u32[]{:S(2)}, u32[]{:S(2)}) collective-permute-start(bf16[256,128]{1,0:T(8,128)(2,1)S(1)} %add_convert_fusion), channel_id=1, source_target_pairs={{0,2},{2,0},{1,3},{3,1},{4,6},{6,4},{5,7},{7,5},{8,10},{10,8},{9,1... | collective-permute-start | bytes 196616 | tf_op jit(solution)/shard_map/ppermute | solution.py:409
  43.2 0.5 collective-permute-start.20
  43.7 2.3 %backward_full.3 = (bf16[2,256,128]{2,1,0:T(8,128)(2,1)S(1)}, bf16[2,256,128]{2,1,0:T(8,128)(2,1)S(1)}, f32[128,128]{1,0:T(8,128)S(1)}, f32[128,128]{1,0:T(8,128)S(1)}, f32[216,128]{1,0:T(8,128)S(1)}) custom-call(bf16[3,2,256,128]{3,2,1,0:T(8,128)(2,1)S(1)} %get-tuple-element.84.x_ref, bf16[3,2,256,128]{3,2,1,0:T(8,128)(2,1)S(1)} %get-tuple-element.85.ct_ref, ...), custom_call_target="tpu_custom_call" | custom-call | flops 2000000000 | bytes 4194304 | tf_op jit(solution)/shard_map/backward_full/pallas_call | solution.py:323
  46.0 0.1 collective-permute-done.9.rest_0_
  46.1 0.1 collective-permute-start.15
  46.1 0.4 collective-permute-start.16
  46.6 2.1 %backward_full.4 = (bf16[2,256,128]{2,1,0:T(8,128)(2,1)S(1)}, bf16[2,256,128]{2,1,0:T(8,128)(2,1)S(1)}, f32[128,128]{1,0:T(8,128)S(1)}, f32[128,128]{1,0:T(8,128)S(1)}, f32[216,128]{1,0:T(8,128)S(1)}) custom-call(bf16[3,2,256,128]{3,2,1,0:T(8,128)(2,1)S(1)} %get-tuple-element.84.x_ref, bf16[3,2,256,128]{3,2,1,0:T(8,128)(2,1)S(1)} %get-tuple-element.85.ct_ref, ...), custom_call_target="tpu_custom_call" | custom-call | flops 2000000000 | bytes 4194304 | tf_op jit(solution)/shard_map/backward_full/pallas_call | solution.py:323
  48.7 2.1 %backward_full.5 = (bf16[2,256,128]{2,1,0:T(8,128)(2,1)S(1)}, bf16[2,256,128]{2,1,0:T(8,128)(2,1)S(1)}, f32[128,128]{1,0:T(8,128)S(1)}, f32[128,128]{1,0:T(8,128)S(1)}, f32[216,128]{1,0:T(8,128)S(1)}) custom-call(bf16[3,2,256,128]{3,2,1,0:T(8,128)(2,1)S(1)} %get-tuple-element.84.x_ref, bf16[3,2,256,128]{3,2,1,0:T(8,128)(2,1)S(1)} %get-tuple-element.85.ct_ref, ...), custom_call_target="tpu_custom_call" | custom-call | flops 2000000000 | bytes 4194304 | tf_op jit(solution)/shard_map/backward_full/pallas_call | solution.py:323
  50.8 0.5 collective-permute-start.21
  51.3 0.5 collective-permute-start.24
  51.8 4.3 %collective-permute-done.21 = bf16[472,128]{1,0:T(8,128)(2,1)S(1)} collective-permute-done((bf16[472,128]{1,0:T(8,128)(2,1)S(1)}, bf16[472,128]{1,0:T(8,128)(2,1)S(1)}, u32[]{:S(2)}, u32[]{:S(2)}) %collective-permute-start.21) | collective-permute-done | bytes 120864 | tf_op jit(solution)/shard_map/ppermute | solution.py:492
  56.2 3.5 %collective-permute-start.22 = (bf16[472,128]{1,0:T(8,128)(2,1)S(1)}, bf16[472,128]{1,0:T(8,128)(2,1)S(1)}, u32[]{:S(2)}, u32[]{:S(2)}) collective-permute-start(bf16[472,128]{1,0:T(8,128)(2,1)S(1)} %fusion.refs_0_), channel_id=1, source_target_pairs={{0,12},{4,8},{8,4},{12,0},{1,13},{5,9},{9,5},{13,1},{2,14},{6,10},... | collective-permute-start | bytes 362504 | tf_op jit(solution)/shard_map/ppermute | solution.py:493
  59.6 0.9 %emit.1 = bf16[3,2,256,128]{3,2,1,0:T(8,128)(2,1)} custom-call(bf16[2,256,128]{2,1,0:T(8,128)(2,1)S(1)} %get-tuple-element.151.refs_0_, bf16[2,256,128]{2,1,0:T(8,128)(2,1)S(1)} %get-tuple-element.132.refs_1_, bf16[2,256,128]{2,1,0:T(8,128)(2,1)S(1)} %collective-permute-done.23.refs_2_, bf16[2,256,128]{2,1,0:T(8,128)(2,1)S(1)} %get-tuple-element.152.refs_3_, ...), custom_call_target="tpu_custom_call" | custom-call | flops 2000000000 | bytes 4194304 | tf_op jit(solution)/shard_map/emit/pallas_call | solution.py:323
  60.5 2.4 %collective-permute-done.22.refs_1_ = bf16[472,128]{1,0:T(8,128)(2,1)S(1)} collective-permute-done((bf16[472,128]{1,0:T(8,128)(2,1)S(1)}, bf16[472,128]{1,0:T(8,128)(2,1)S(1)}, u32[]{:S(2)}, u32[]{:S(2)}) %collective-permute-start.22) | collective-permute-done | bytes 120864 | tf_op jit(solution)/shard_map/ppermute | solution.py:493
  62.9 1.0 %finish.1 = (f32[128,128]{1,0:T(8,128)}, f32[128,128]{1,0:T(8,128)}, f32[16,8,8,27]{3,2,1,0:T(8,128)}) custom-call(bf16[472,128]{1,0:T(8,128)(2,1)S(1)} %fusion.refs_0_, bf16[472,128]{1,0:T(8,128)(2,1)S(1)} %collective-permute-done.22.refs_1_), custom_call_target="tpu_custom_call" | custom-call | flops 2000000000 | bytes 4194304 | tf_op jit(solution)/shard_map/finish/pallas_call | solution.py:323
  (44 shorter events, 0.2 us)
Async XLA Ops:
  0.6 6.8 %copy-start.2 = (bf16[1,27,16,8,8]{1,4,3,2,0:T(8,128)(2,1)S(1)}, bf16[1,27,16,8,8]{1,4,3,2,0:T(8,128)(2,1)}, u32[]{:S(2)}) copy-start(bf16[1,27,16,8,8]{1,4,3,2,0:T(8,128)(2,1)} %param.12) | copy-start | bytes 165892
  2.4 11.0 %collective-permute-start.1 = (bf16[816,128]{1,0:T(8,128)(2,1)}, bf16[816,128]{1,0:T(8,128)(2,1)S(1)}, u32[]{:S(2)}, u32[]{:S(2)}) collective-permute-start(bf16[816,128]{1,0:T(8,128)(2,1)} %get-tuple-element.87), channel_id=1, source_target_pairs={{0,12},{1,5},{4,0},{5,9},{8,4},{9,13},{12,8},{13,1},{2,14},{3,7},{... | collective-permute-start | bytes 626696 | tf_op jit(solution)/shard_map/ppermute | solution.py:398
  7.5 9.9 %collective-permute-start.2 = (bf16[816,128]{1,0:T(8,128)(2,1)}, bf16[816,128]{1,0:T(8,128)(2,1)S(1)}, u32[]{:S(2)}, u32[]{:S(2)}) collective-permute-start(bf16[816,128]{1,0:T(8,128)(2,1)} %get-tuple-element.87), channel_id=1, source_target_pairs={{0,4},{1,13},{4,8},{5,1},{8,12},{9,5},{12,0},{13,9},{2,6},{3,15},{... | collective-permute-start | bytes 626696 | tf_op jit(solution)/shard_map/ppermute | solution.py:399
  7.5 1.0 %copy-start.6 = (f32[1,3,128]{2,0,1:T(1,128)S(1)}, f32[1,3,128]{2,0,1:T(1,128)}, u32[]{:S(2)}) copy-start(f32[1,3,128]{2,0,1:T(1,128)} %param.11) | copy-start | bytes 4612
  7.5 1.0 %copy-start = (bf16[1,3,2,16,16,128]{5,4,3,2,1,0:T(8,128)(2,1)S(1)}, bf16[1,3,2,16,16,128]{5,4,3,2,1,0:T(8,128)(2,1)}, u32[]{:S(2)}) copy-start(bf16[1,3,2,16,16,128]{5,4,3,2,1,0:T(8,128)(2,1)} %param.7) | copy-start | bytes 1179652
  7.5 1.1 %copy-start.1 = (bf16[3,2,16,16,128]{4,3,2,1,0:T(8,128)(2,1)S(1)}, bf16[3,2,16,16,128]{4,3,2,1,0:T(8,128)(2,1)}, u32[]{:S(2)}) copy-start(bf16[3,2,16,16,128]{4,3,2,1,0:T(8,128)(2,1)} %param.8) | copy-start | bytes 1179652
  7.5 1.1 %copy-start.3 = (bf16[1,128,128]{2,1,0:T(8,128)(2,1)S(1)}, bf16[1,128,128]{2,1,0:T(8,128)(2,1)}, u32[]{:S(2)}) copy-start(bf16[1,128,128]{2,1,0:T(8,128)(2,1)} %param.10) | copy-start | bytes 98308
  7.5 1.1 %copy-start.4 = (bf16[1,128,128]{2,1,0:T(8,128)(2,1)S(1)}, bf16[1,128,128]{2,1,0:T(8,128)(2,1)}, u32[]{:S(2)}) copy-start(bf16[1,128,128]{2,1,0:T(8,128)(2,1)} %param.13) | copy-start | bytes 98308
  7.5 1.1 %copy-start.5 = (bf16[3,2,16,128]{3,2,1,0:T(8,128)(2,1)S(1)}, bf16[3,2,16,128]{3,2,1,0:T(8,128)(2,1)}, u32[]{:S(2)}) copy-start(bf16[3,2,16,128]{3,2,1,0:T(8,128)(2,1)} %get-tuple-element.83.lab_ref) | copy-start | bytes 73732
  17.3 2.3 %collective-permute-start.3 = (bf16[816,128]{1,0:T(8,128)(2,1)S(1)}, bf16[816,128]{1,0:T(8,128)(2,1)S(1)}, u32[]{:S(2)}, u32[]{:S(2)}) collective-permute-start(bf16[816,128]{1,0:T(8,128)(2,1)S(1)} %collective-permute-done.1.a_ref), channel_id=1, source_target_pairs={{0,1},{1,0},{2,3},{3,2},{4,5},{5,4},{6,7},{7,6},{8,9},{9,8},{10,11... | collective-permute-start | bytes 626696 | tf_op jit(solution)/shard_map/ppermute | solution.py:364
  17.3 2.3 %collective-permute-start.4 = (bf16[816,128]{1,0:T(8,128)(2,1)S(1)}, bf16[816,128]{1,0:T(8,128)(2,1)S(1)}, u32[]{:S(2)}, u32[]{:S(2)}) collective-permute-start(bf16[816,128]{1,0:T(8,128)(2,1)S(1)} %collective-permute-done.2.b_ref), channel_id=1, source_target_pairs={{0,1},{1,0},{2,3},{3,2},{4,5},{5,4},{6,7},{7,6},{8,9},{9,8},{10,11... | collective-permute-start | bytes 626696 | tf_op jit(solution)/shard_map/ppermute | solution.py:364
  17.8 7.4 %collective-permute-start = (bf16[768,128]{1,0:T(8,128)(2,1)S(1)}, bf16[768,128]{1,0:T(8,128)(2,1)S(1)}, u32[]{:S(2)}, u32[]{:S(2)}) collective-permute-start(bf16[768,128]{1,0:T(8,128)(2,1)S(1)} %get-tuple-element.86), channel_id=1, source_target_pairs={{0,12},{1,5},{4,0},{5,9},{8,4},{9,13},{12,8},{13,1},{2,14},{3,7},{... | collective-permute-start | bytes 589832 | tf_op jit(solution)/shard_map/ppermute | solution.py:402
  25.2 1.5 %collective-permute-start.5 = (bf16[768,128]{1,0:T(8,128)(2,1)S(1)}, bf16[768,128]{1,0:T(8,128)(2,1)S(1)}, u32[]{:S(2)}, u32[]{:S(2)}) collective-permute-start(bf16[768,128]{1,0:T(8,128)(2,1)S(1)} %collective-permute-done.cta_ref), channel_id=1, source_target_pairs={{0,1},{1,0},{2,3},{3,2},{4,5},{5,4},{6,7},{7,6},{8,9},{9,8},{10,11... | collective-permute-start | bytes 589832 | tf_op jit(solution)/shard_map/ppermute | solution.py:364
  28.0 1.3 %collective-permute-start.6 = (bf16[256,128]{1,0:T(8,128)(2,1)S(1)}, bf16[256,128]{1,0:T(8,128)(2,1)S(1)}, u32[]{:S(2)}, u32[]{:S(2)}) collective-permute-start(bf16[256,128]{1,0:T(8,128)(2,1)S(1)} %get-tuple-element.120), channel_id=1, source_target_pairs={{0,1},{1,0},{2,3},{3,2},{4,5},{5,4},{6,7},{7,6},{8,9},{9,8},{10,11... | collective-permute-start | bytes 196616 | tf_op jit(solution)/shard_map/ppermute | solution.py:364
  30.6 3.4 %collective-permute-start.7 = (bf16[256,128]{1,0:T(8,128)(2,1)S(1)}, bf16[256,128]{1,0:T(8,128)(2,1)S(1)}, u32[]{:S(2)}, u32[]{:S(2)}) collective-permute-start(bf16[256,128]{1,0:T(8,128)(2,1)S(1)} %get-tuple-element.123), channel_id=1, source_target_pairs={{0,1},{1,0},{2,3},{3,2},{4,5},{5,4},{6,7},{7,6},{8,9},{9,8},{10,11... | collective-permute-start | bytes 196616 | tf_op jit(solution)/shard_map/ppermute | solution.py:364
  30.9 7.8 %collective-permute-start.11 = (bf16[256,128]{1,0:T(8,128)(2,1)S(1)}, bf16[256,128]{1,0:T(8,128)(2,1)S(1)}, u32[]{:S(2)}, u32[]{:S(2)}) collective-permute-start(bf16[256,128]{1,0:T(8,128)(2,1)S(1)} %add_convert_fusion.2), channel_id=1, source_target_pairs={{0,2},{2,0},{1,3},{3,1},{4,6},{6,4},{5,7},{7,5},{8,10},{10,8},{9,1... | collective-permute-start | bytes 196616 | tf_op jit(solution)/shard_map/ppermute | solution.py:409
  32.4 6.3 %collective-permute-start.12 = (bf16[256,128]{1,0:T(8,128)(2,1)S(1)}, bf16[256,128]{1,0:T(8,128)(2,1)S(1)}, u32[]{:S(2)}, u32[]{:S(2)}) collective-permute-start(bf16[256,128]{1,0:T(8,128)(2,1)S(1)} %add_convert_fusion.2), channel_id=1, source_target_pairs={{0,14},{2,12},{1,7},{3,5},{4,2},{6,0},{5,11},{7,9},{8,6},{10,4},{9... | collective-permute-start | bytes 196616 | tf_op jit(solution)/shard_map/ppermute | solution.py:410
  35.3 3.9 %collective-permute-start.8 = (bf16[256,128]{1,0:T(8,128)(2,1)S(1)}, bf16[256,128]{1,0:T(8,128)(2,1)S(1)}, u32[]{:S(2)}, u32[]{:S(2)}) collective-permute-start(bf16[256,128]{1,0:T(8,128)(2,1)S(1)} %get-tuple-element.126), channel_id=1, source_target_pairs={{0,1},{1,0},{2,3},{3,2},{4,5},{5,4},{6,7},{7,6},{8,9},{9,8},{10,11... | collective-permute-start | bytes 196616 | tf_op jit(solution)/shard_map/ppermute | solution.py:364
  35.4 6.3 %collective-permute-start.17 = (bf16[256,128]{1,0:T(8,128)(2,1)S(1)}, bf16[256,128]{1,0:T(8,128)(2,1)S(1)}, u32[]{:S(2)}, u32[]{:S(2)}) collective-permute-start(bf16[256,128]{1,0:T(8,128)(2,1)S(1)} %add_convert_fusion.1), channel_id=1, source_target_pairs={{0,2},{2,0},{1,3},{3,1},{4,6},{6,4},{5,7},{7,5},{8,10},{10,8},{9,1... | collective-permute-start | bytes 196616 | tf_op jit(solution)/shard_map/ppermute | solution.py:409
  36.9 6.2 %collective-permute-start.18 = (bf16[256,128]{1,0:T(8,128)(2,1)S(1)}, bf16[256,128]{1,0:T(8,128)(2,1)S(1)}, u32[]{:S(2)}, u32[]{:S(2)}) collective-permute-start(bf16[256,128]{1,0:T(8,128)(2,1)S(1)} %add_convert_fusion.1), channel_id=1, source_target_pairs={{0,14},{2,12},{1,7},{3,5},{4,2},{6,0},{5,11},{7,9},{8,6},{10,4},{9... | collective-permute-start | bytes 196616 | tf_op jit(solution)/shard_map/ppermute | solution.py:410
  38.7 4.5 %collective-permute-start.13 = (bf16[256,128]{1,0:T(8,128)(2,1)S(1)}, bf16[256,128]{1,0:T(8,128)(2,1)S(1)}, u32[]{:S(2)}, u32[]{:S(2)}) collective-permute-start(bf16[256,128]{1,0:T(8,128)(2,1)S(1)} %collective-permute-done.11.rest_0_), channel_id=1, source_target_pairs={{0,1},{1,0},{2,3},{3,2},{4,5},{5,4},{6,7},{7,6},{8,9},{9,8},{10,11... | collective-permute-start | bytes 196616 | tf_op jit(solution)/shard_map/ppermute | solution.py:364
  38.7 5.0 %collective-permute-start.14 = (bf16[256,128]{1,0:T(8,128)(2,1)S(1)}, bf16[256,128]{1,0:T(8,128)(2,1)S(1)}, u32[]{:S(2)}, u32[]{:S(2)}) collective-permute-start(bf16[256,128]{1,0:T(8,128)(2,1)S(1)} %collective-permute-done.12.rest_2_), channel_id=1, source_target_pairs={{0,1},{1,0},{2,3},{3,2},{4,5},{5,4},{6,7},{7,6},{8,9},{9,8},{10,11... | collective-permute-start | bytes 196616 | tf_op jit(solution)/shard_map/ppermute | solution.py:364
  39.2 6.7 %collective-permute-start.10 = (bf16[256,128]{1,0:T(8,128)(2,1)S(1)}, bf16[256,128]{1,0:T(8,128)(2,1)S(1)}, u32[]{:S(2)}, u32[]{:S(2)}) collective-permute-start(bf16[256,128]{1,0:T(8,128)(2,1)S(1)} %add_convert_fusion), channel_id=1, source_target_pairs={{0,14},{2,12},{1,7},{3,5},{4,2},{6,0},{5,11},{7,9},{8,6},{10,4},{9... | collective-permute-start | bytes 196616 | tf_op jit(solution)/shard_map/ppermute | solution.py:410
  41.7 4.4 %collective-permute-start.9 = (bf16[256,128]{1,0:T(8,128)(2,1)S(1)}, bf16[256,128]{1,0:T(8,128)(2,1)S(1)}, u32[]{:S(2)}, u32[]{:S(2)}) collective-permute-start(bf16[256,128]{1,0:T(8,128)(2,1)S(1)} %add_convert_fusion), channel_id=1, source_target_pairs={{0,2},{2,0},{1,3},{3,1},{4,6},{6,4},{5,7},{7,5},{8,10},{10,8},{9,1... | collective-permute-start | bytes 196616 | tf_op jit(solution)/shard_map/ppermute | solution.py:409
  43.2 3.4 %collective-permute-start.19 = (bf16[256,128]{1,0:T(8,128)(2,1)S(1)}, bf16[256,128]{1,0:T(8,128)(2,1)S(1)}, u32[]{:S(2)}, u32[]{:S(2)}) collective-permute-start(bf16[256,128]{1,0:T(8,128)(2,1)S(1)} %collective-permute-done.17.rest_0_), channel_id=1, source_target_pairs={{0,1},{1,0},{2,3},{3,2},{4,5},{5,4},{6,7},{7,6},{8,9},{9,8},{10,11... | collective-permute-start | bytes 196616 | tf_op jit(solution)/shard_map/ppermute | solution.py:364
  43.2 3.4 %collective-permute-start.20 = (bf16[256,128]{1,0:T(8,128)(2,1)S(1)}, bf16[256,128]{1,0:T(8,128)(2,1)S(1)}, u32[]{:S(2)}, u32[]{:S(2)}) collective-permute-start(bf16[256,128]{1,0:T(8,128)(2,1)S(1)} %collective-permute-done.18.rest_2_), channel_id=1, source_target_pairs={{0,1},{1,0},{2,3},{3,2},{4,5},{5,4},{6,7},{7,6},{8,9},{9,8},{10,11... | collective-permute-start | bytes 196616 | tf_op jit(solution)/shard_map/ppermute | solution.py:364
  46.1 2.6 %collective-permute-start.15 = (bf16[256,128]{1,0:T(8,128)(2,1)S(1)}, bf16[256,128]{1,0:T(8,128)(2,1)S(1)}, u32[]{:S(2)}, u32[]{:S(2)}) collective-permute-start(bf16[256,128]{1,0:T(8,128)(2,1)S(1)} %collective-permute-done.9.rest_0_), channel_id=1, source_target_pairs={{0,1},{1,0},{2,3},{3,2},{4,5},{5,4},{6,7},{7,6},{8,9},{9,8},{10,11... | collective-permute-start | bytes 196616 | tf_op jit(solution)/shard_map/ppermute | solution.py:364
  46.1 2.5 %collective-permute-start.16 = (bf16[256,128]{1,0:T(8,128)(2,1)S(1)}, bf16[256,128]{1,0:T(8,128)(2,1)S(1)}, u32[]{:S(2)}, u32[]{:S(2)}) collective-permute-start(bf16[256,128]{1,0:T(8,128)(2,1)S(1)} %collective-permute-done.10.rest_2_), channel_id=1, source_target_pairs={{0,1},{1,0},{2,3},{3,2},{4,5},{5,4},{6,7},{7,6},{8,9},{9,8},{10,11... | collective-permute-start | bytes 196616 | tf_op jit(solution)/shard_map/ppermute | solution.py:364
  50.8 5.3 %collective-permute-start.21 = (bf16[472,128]{1,0:T(8,128)(2,1)S(1)}, bf16[472,128]{1,0:T(8,128)(2,1)S(1)}, u32[]{:S(2)}, u32[]{:S(2)}) collective-permute-start(bf16[472,128]{1,0:T(8,128)(2,1)S(1)} %pad_maximum_fusion), channel_id=1, source_target_pairs={{0,4},{4,0},{8,12},{12,8},{1,5},{5,1},{9,13},{13,9},{2,6},{6,2},{1... | collective-permute-start | bytes 362504 | tf_op jit(solution)/shard_map/ppermute | solution.py:492
  51.3 8.3 %collective-permute-start.23 = (bf16[2,256,128]{2,1,0:T(8,128)(2,1)S(1)}, bf16[2,256,128]{2,1,0:T(8,128)(2,1)S(1)}, u32[]{:S(2)}, u32[]{:S(2)}) collective-permute-start(bf16[2,256,128]{2,1,0:T(8,128)(2,1)S(1)} %get-tuple-element.132.refs_1_), channel_id=1, source_target_pairs={{0,1},{1,0},{2,3},{3,2},{4,5},{5,4},{6,7},{7,6},{8,9},{9,8},{10,11... | collective-permute-start | bytes 393224 | tf_op jit(solution)/shard_map/ppermute | solution.py:364
  51.3 8.3 %collective-permute-start.24 = (bf16[2,256,128]{2,1,0:T(8,128)(2,1)S(1)}, bf16[2,256,128]{2,1,0:T(8,128)(2,1)S(1)}, u32[]{:S(2)}, u32[]{:S(2)}) collective-permute-start(bf16[2,256,128]{2,1,0:T(8,128)(2,1)S(1)} %get-tuple-element.153.refs_4_), channel_id=1, source_target_pairs={{0,1},{1,0},{2,3},{3,2},{4,5},{5,4},{6,7},{7,6},{8,9},{9,8},{10,11... | collective-permute-start | bytes 393224 | tf_op jit(solution)/shard_map/ppermute | solution.py:364
  51.8 7.8 %collective-permute-start.25 = (bf16[2,256,128]{2,1,0:T(8,128)(2,1)S(1)}, bf16[2,256,128]{2,1,0:T(8,128)(2,1)S(1)}, u32[]{:S(2)}, u32[]{:S(2)}) collective-permute-start(bf16[2,256,128]{2,1,0:T(8,128)(2,1)S(1)} %get-tuple-element.155.refs_7_), channel_id=1, source_target_pairs={{0,1},{1,0},{2,3},{3,2},{4,5},{5,4},{6,7},{7,6},{8,9},{9,8},{10,11... | collective-permute-start | bytes 393224 | tf_op jit(solution)/shard_map/ppermute | solution.py:364
  56.2 6.8 %collective-permute-start.22 = (bf16[472,128]{1,0:T(8,128)(2,1)S(1)}, bf16[472,128]{1,0:T(8,128)(2,1)S(1)}, u32[]{:S(2)}, u32[]{:S(2)}) collective-permute-start(bf16[472,128]{1,0:T(8,128)(2,1)S(1)} %fusion.refs_0_), channel_id=1, source_target_pairs={{0,12},{4,8},{8,4},{12,0},{1,13},{5,9},{9,5},{13,1},{2,14},{6,10},... | collective-permute-start | bytes 362504 | tf_op jit(solution)/shard_map/ppermute | solution.py:493

commit v5 on v4

--- a/solution.py
+++ b/solution.py
@@ -57,16 +57,23 @@
     return outs
 
 
-def pack_kernel(micro, cells, wide, x_ref, tag_ref, out_ref, own_ref, lab_ref, sem):
-    tags = pltpu.make_async_copy(tag_ref, lab_ref, sem.at[micro])
+def pack_kernel(
+    micro, cells, wide, x_ref, ct_ref, tag_ref, a_ref, b_ref, own_ref, lab_ref, sem
+):
+    tags = pltpu.make_async_copy(tag_ref, lab_ref, sem.at[2 * micro + 1])
     tags.start()
     c = lax.axis_index("chan")
     copies = []
     for m in range(micro):
-        spot = out_ref.at[pl.ds(m * (cells + wide), cells)]
-        copy = pltpu.make_async_copy(x_ref.at[m, c], spot, sem.at[m])
-        copy.start()
-        copies.append(copy)
+        for n, out_ref in enumerate((a_ref, b_ref)):
+            spot = out_ref.at[pl.ds(m * (cells + wide), cells)]
+            copy = pltpu.make_async_copy(x_ref.at[m, c], spot, sem.at[2 * m + n])
+            copy.start()
+            copies.append(copy)
+    spot = a_ref.at[pl.ds(micro * (cells + wide), cells)]
+    copy = pltpu.make_async_copy(ct_ref.at[0, c], spot, sem.at[2 * micro])
+    copy.start()
+    copies.append(copy)
     deep = lab_ref.shape[3]
     tags.wait()
     row = lax.broadcasted_iota(jnp.int32, (LANES, LANES), 0)
@@ -77,7 +84,8 @@
             own_ref[m, p] = jnp.zeros((deep, LANES), BF)
             turned = nt_dot(eye, lab_ref[m, p].astype(F32).astype(BF))
             own_ref[m, p, :, 0:wide] = turned.astype(BF)
-        out_ref[m * (cells + wide) + cells : (m + 1) * (cells + wide)] = own_ref[m, c]
+        for out_ref in (a_ref, b_ref):
+            out_ref[m * (cells + wide) + cells : (m + 1) * (cells + wide)] = own_ref[m, c]
     for copy in copies:
         copy.wait()
 
@@ -138,8 +146,8 @@
         dst[...] = src[...]
     c = lax.axis_index("chan")
     cells = wide * deep
-    for m in range(micro):
-        edge_ref[m * cells : (m + 1) * cells] = ct_ref[m, c]
+    for m in range(1, micro):
+        edge_ref[(m - 1) * cells : m * cells] = ct_ref[m, c]
     codes = code_rows(code_ref, deep)
     for m in range(micro):
         hs_ref, hid_ref, spre_ref = outs[3 * m : 3 * m + 3]
@@ -172,9 +180,12 @@
     cells = wide * deep
     codes = code_rows(code_ref, deep)
     start = slot * (cells + wide)
-    for ref, plane in ((a_ref, 2 - c), (b_ref, 3 * c), (a2_ref, 1 + c), (b2_ref, 3 - 3 * c)):
-        lab = ref[start + cells : start + cells + wide]
-        pre = hidden_rows(ref[start : start + cells], lab, w_ref[...], codes, wide, deep)
+    first = c == 0
+    sources = ((b_ref, b2_ref), (a2_ref, a_ref), (a_ref, a2_ref), (b2_ref, b_ref))
+    for plane, (yes, no) in enumerate(sources):
+        rows = slice(start, start + cells + wide)
+        both = jnp.where(first, yes[rows], no[rows])
+        pre = hidden_rows(both[:cells], both[cells:], w_ref[...], codes, wide, deep)
         store_shifts(hs_ref, plane, pre * gate(pre), wide, deep)
     planes = [(hs_ref, 0), (hs_ref, 1), (own_ref, 0), (own_ref, 1), (hs_ref, 2), (hs_ref, 3)]
     for p, conv in enumerate(conv_pairs(planes, (1, 3), kf_ref, cells, deep)):
@@ -188,6 +199,7 @@
     mode,
     m,
     sent_slot,
+    tail_start,
     wide,
     deep,
     taps,
@@ -205,12 +217,13 @@
 ):
     c = lax.axis_index("chan")
     cells = wide * deep
-    tail = pl.ds(m * cells, cells)
+    tail = pl.ds(tail_start, cells)
     full = mode == "full"
     if mode == "first":
         base_ref, other_ref, gs_ref, br_ref = rest
         up_ref = ct_ref.at[m]
         halo, halo2 = cta_ref[tail], cta2_ref[tail]
+        own = (ct_ref[m, 0], ct_ref[m, 1])
     else:
         st_ref, st2_ref, dg_ref, dg2_ref, *rest = rest
         if full:
@@ -221,20 +234,18 @@
         here = pl.ds(sent_slot * cells, cells)
         last = lax.axis_index("section") == lax.axis_size("section") - 1
 
-        @pl.when(last)
-        def _():
-            up_ref[0] = ct_ref[m, 0]
-            up_ref[1] = ct_ref[m, 1]
-
-        @pl.when(jnp.logical_not(last))
-        def _():
-            up_ref[c] = st_ref[here]
-            up_ref[1 - c] = st2_ref[here]
-
+        mine, theirs = st_ref[here], st2_ref[here]
+        own = (
+            jnp.where(last, ct_ref[m, 0], jnp.where(c == 0, mine, theirs)),
+            jnp.where(last, ct_ref[m, 1], jnp.where(c == 0, theirs, mine)),
+        )
+        for p in (0, 1):
+            up_ref[p] = own[p]
         halo = jnp.where(last, cta_ref[tail], dg_ref[here])
         halo2 = jnp.where(last, cta2_ref[tail], dg2_ref[here])
-    ups = ((up_ref[0], 1), (up_ref[1], 2), (halo, 3 - 3 * c), (halo2, 3 * c))
-    for up, plane in ups:
+    below = jnp.where(c == 0, halo2, halo)
+    above = jnp.where(c == 0, halo, halo2)
+    for plane, up in enumerate((below, *own, above)):
         grad = nt_dot(up, rw_ref[...]) * sconv_ref[plane]
         store_shifts(gs_ref, plane, grad.astype(BF).astype(F32), wide, deep)
     if full:
@@ -365,16 +376,20 @@
 
     rows = cells + wide
     hbm = pl.BlockSpec(memory_space=pltpu.HBM)
-    packed, lab = call(
+    packed_a, packed_b, lab = call(
         functools.partial(pack_kernel, micro, cells, wide),
         "pack",
-        [sds((micro * rows, LANES), BF), sds((micro, depth, deep, LANES), BF)],
-        (x, phase_labels),
+        [
+            sds((micro * rows + cells, LANES), BF),
+            sds((micro * rows, LANES), BF),
+            sds((micro, depth, deep, LANES), BF),
+        ],
+        (x, ct, phase_labels),
         [
             pltpu.VMEM(phase_labels.shape, jnp.int32),
-            pltpu.SemaphoreType.DMA((micro + 1,)),
+            pltpu.SemaphoreType.DMA((2 * micro + 2,)),
         ],
-        [hbm, hbm],
+        [hbm, hbm, hbm],
         60,
     )
     plane2, plane4, flat = (2, cells, LANES), (4, cells, LANES), (cells, LANES)
@@ -392,11 +407,11 @@
         "own",
         [sds((2, pad_rows, 3 * LANES), BF), sds(plane2, BF), sds(plane2, F32)] * micro
         + [sds(v.shape, v.dtype) for v in (x, ct, w, rw, code)]
-        + [sds((micro * cells, LANES), BF)],
+        + [sds((max(1, micro - 1) * cells, LANES), BF)],
         (x, ct, lab, w, rw, code),
     )
-    a = lax.ppermute(packed, ("space", "chan"), route_a)
-    b = lax.ppermute(packed, ("space", "chan"), route_b)
+    a = lax.ppermute(packed_a, ("space", "chan"), route_a)
+    b = lax.ppermute(packed_b, ("space", "chan"), route_b)
     a, b, dense_f, dense_b, *owned = lax.optimization_barrier((a, b, dense_f, dense_b, *owned))
     halos = (a, b, swap(a), swap(b))
     edge = lax.ppermute(edge, ("space", "chan"), route_a)
@@ -425,10 +440,10 @@
         if mode == "light":
             scratch.append(pltpu.VMEM(plane2, BF))
         return call(
-            functools.partial(backward_kernel, mode, m, sent_slot[m], wide, deep, taps, width),
+            functools.partial(backward_kernel, mode, m, sent_slot[m], tails[m], wide, deep, taps, width),
             "backward_" + mode,
             outs + list(extra_out),
-            (x, ct, *edges, w, rw, dense_b, spre[m], sconv[m], *extra),
+            (x, ct, *edges[m], w, rw, dense_b, spre[m], sconv[m], *extra),
             scratch,
         )
 
@@ -437,9 +452,10 @@
     sender = [n for n, group in enumerate(sends) for _ in group]
     sent_slot = [i for group in sends for i in range(len(group))]
     spre = [owned[3 * m + 2] for m in range(micro)]
+    tails = [micro * rows] + [m * cells for m in range(micro - 1)]
+    edges = [(halos[0], halos[2])]
+    pending, previous = [], None
     for m in range(micro):
-        if m:
-            (code,) = after((code,), sconv[-1])
         con, mix = call(
             functools.partial(forward_kernel, m, wide, deep),
             "forward",
@@ -449,20 +465,18 @@
         )
         sconv.append(con)
         mixed.append(mix)
+        (code,) = after((code,), con)
+        if m == 0:
+            previous = back_pass("first", 0, ())
+            (code,) = after((code,), previous[1])
+            sent.append(send_on(joined([previous])))
     (edge,) = after((edge,), sconv[-1])
-    edges = (edge, swap(edge))
-    pending = []
-    for m in range(micro):
-        if m == 0:
-            (sconv[m],) = after((sconv[m],), sconv[-1])
-        if pending and len(pending) == len(sends[len(sent)]):
-            out, sconv[m] = lax.optimization_barrier((joined(pending), sconv[m]))
-            sent.append(send_on(out))
-            pending = []
-        pending.append(back_pass("first", m, ()))
-    out = joined(pending)
-    sent = [after(pair, pending[-1][1]) for pair in sent[:1]] + [after(pair, pending[-1][1]) for pair in sent[1:]]
-    sent.append(send_on(out))
+    edges += [(edge, swap(edge))] * (micro - 1)
+    for m in range(1, micro):
+        (sconv[m],) = after((sconv[m],), previous[1])
+        previous = back_pass("first", m, ())
+        sent.append(send_on(joined([previous])))
+    sent[0] = after(sent[0], previous[1])
     ups = [shared(*pair) for pair in sent]
 
     rank = lax.axis_index("section")

time: 64.1 us -> 63.7 us (level)
  waiting for transfers between devices: 16.9 us -> 20.1 us
  starting transfers between devices: 24.8 us -> 22 us
  Pallas kernels: 21.1 us -> 20.2 us
    ppermute x3, waiting for transfers between devices: 0.01 us -> 3.55 us  [send_on(): dg = lax.ppermute(out, ('space', 'section', 'chan'), route_d)]
    ppermute x15, waiting for transfers between devices: 2.17 us -> 0.04 us  [swap(): return lax.ppermute(v, 'chan', [(0, 1), (1, 0)])]
    ppermute x3, starting transfers between devices: 4.52 us -> 2.76 us  [send_on(): st = lax.ppermute(out, 'section', route_s)]
    ppermute x2, waiting for transfers between devices: 7.91 us -> 9.33 us  [the longest x1 9.33 us: on_device(): b = lax.ppermute(packed_b, ('space', 'chan'), route_b)]
    ppermute x3, starting transfers between devices: 5.8 us -> 4.67 us  [send_on(): dg = lax.ppermute(out, ('space', 'section', 'chan'), route_d)]
    pallas_call x14, Pallas kernels: 21.1 us -> 20.2 us  [call(): pl.pallas_call(kernel, in_specs=[vmem] * len(args) if in_specs is None el...]
  transfers between devices with their start and end apart: 26 -> 26, of which waited for: 7 -> 7; matrix products, arithmetic and copies ran while one was open for 0% -> 0% of each run, Pallas kernels for 22% -> 24%
where the time goes in v5:
time: 63.7 us; the launch traced here: 63.5 us
  starting transfers between devices  22 us (35%)
  Pallas kernels  20.2 us (32%)
  waiting for transfers between devices  20.1 us (32%)
  between operations  0.92 us (1%)
    pallas_call x14, Pallas kernels, call(): pl.pallas_call(kernel, in_specs=[vmem] * len(args) if in_specs is None el...  20.2 us
    ppermute x1, waiting for transfers between devices, on_device(): b = lax.ppermute(packed_b, ('space', 'chan'), route_b)  9.33 us
    ppermute x1, starting transfers between devices, on_device(): a = lax.ppermute(packed_a, ('space', 'chan'), route_a)  5.1 us
    ppermute x3, starting transfers between devices, send_on(): dg = lax.ppermute(out, ('space', 'section', 'chan'), route_d)  4.67 us
    ppermute x1, waiting for transfers between devices, on_device(): grads = grads + lax.ppermute(grads, 'space', near)  4.26 us
    ppermute x15, starting transfers between devices, swap(): return lax.ppermute(v, 'chan', [(0, 1), (1, 0)])  4.12 us
    ppermute x3, waiting for transfers between devices, send_on(): dg = lax.ppermute(out, ('space', 'section', 'chan'), route_d)  3.55 us
    ppermute x1, starting transfers between devices, on_device(): copies = [grads, lax.ppermute(grads, 'space', far)]  3.09 us
  transfers between devices with their start and end apart: 26, of which 7 were waited for; matrix products, arithmetic and copies ran while one was open for 0% of the time, Pallas kernels for 24%

profile of v5, /device:TPU:0, one launch (start us, length us, event | category | flops | bytes accessed | tf_op | source)
XLA Modules:
  0.0 63.5 jit_solution(17357435644425910079)
XLA Ops:
  0.6 1.9 %pack.1 = (bf16[1072,128]{1,0:T(8,128)(2,1)}, bf16[816,128]{1,0:T(8,128)(2,1)}, bf16[3,2,16,128]{3,2,1,0:T(8,128)(2,1)}) custom-call(bf16[3,2,256,128]{3,2,1,0:T(8,128)(2,1)} %bitcast.16, bf16[3,2,256,128]{3,2,1,0:T(8,128)(2,1)} %bitcast.18, s32[3,2,16,16]{3,2,1,0:T(8,128)} %tag_ref.1), custom_call_target="tpu_custom_call" | custom-call | flops 2000000000 | bytes 4194304 | tf_op jit(solution)/shard_map/pack/pallas_call | solution.py:334
  2.6 5.1 %collective-permute-start.1 = (bf16[1072,128]{1,0:T(8,128)(2,1)}, bf16[1072,128]{1,0:T(8,128)(2,1)S(1)}, u32[]{:S(2)}, u32[]{:S(2)}) collective-permute-start(bf16[1072,128]{1,0:T(8,128)(2,1)} %get-tuple-element.84), channel_id=1, source_target_pairs={{0,12},{1,5},{4,0},{5,9},{8,4},{9,13},{12,8},{13,1},{2,14},{3,7},{... | collective-permute-start | bytes 823304 | tf_op jit(solution)/shard_map/ppermute | solution.py:413
  7.7 0.0 collective-permute-start.2
  7.7 0.0 copy-start.1
  7.7 0.0 copy-start.3
  7.7 0.0 copy-start.4
  7.7 0.0 copy-start.5
  7.8 0.9 %weights.1 = (bf16[4608,256]{1,0:T(8,128)(2,1)S(1)}, bf16[4608,256]{1,0:T(8,128)(2,1)S(1)}) custom-call(bf16[16,8,8,27]{3,2,1,0:T(8,128)(2,1)S(1)} %bitcast.20), custom_call_target="tpu_custom_call" | custom-call | flops 2000000000 | bytes 4194304 | tf_op jit(solution)/shard_map/weights/pallas_call | solution.py:334
  8.7 0.1 copy-done.1
  8.8 0.8 %own.1 = (bf16[2,288,384]{2,1,0:T(8,128)(2,1)S(1)}, bf16[2,256,128]{2,1,0:T(8,128)(2,1)S(1)}, f32[2,256,128]{2,1,0:T(8,128)S(1)}, bf16[2,288,384]{2,1,0:T(8,128)...) custom-call(bf16[3,2,256,128]{3,2,1,0:T(8,128)(2,1)S(1)} %bitcast.17, ...), custom_call_target="tpu_custom_call" | custom-call | flops 2000000000 | bytes 4194304 | tf_op jit(solution)/shard_map/own/pallas_call | solution.py:334
  9.6 9.3 %collective-permute-done.2.b_ref = bf16[816,128]{1,0:T(8,128)(2,1)S(1)} collective-permute-done((bf16[816,128]{1,0:T(8,128)(2,1)}, bf16[816,128]{1,0:T(8,128)(2,1)S(1)}, u32[]{:S(2)}, u32[]{:S(2)}) %collective-permute-start.2) | collective-permute-done | bytes 208928 | tf_op jit(solution)/shard_map/ppermute | solution.py:414
  19.0 0.5 collective-permute-start.4
  19.5 1.7 %collective-permute-start = (bf16[512,128]{1,0:T(8,128)(2,1)S(1)}, bf16[512,128]{1,0:T(8,128)(2,1)S(1)}, u32[]{:S(2)}, u32[]{:S(2)}) collective-permute-start(bf16[512,128]{1,0:T(8,128)(2,1)S(1)} %get-tuple-element.83), channel_id=1, source_target_pairs={{0,12},{1,5},{4,0},{5,9},{8,4},{9,13},{12,8},{13,1},{2,14},{3,7},{... | collective-permute-start | bytes 393224 | tf_op jit(solution)/shard_map/ppermute | solution.py:417
  21.2 0.0 collective-permute-done.3.a2_ref.cta2_ref
  21.2 1.6 %forward.3 = (f32[4,256,128]{2,1,0:T(8,128)S(1)}, bf16[2,256,128]{2,1,0:T(8,128)(2,1)S(1)}) custom-call(bf16[2,288,384]{2,1,0:T(8,128)(2,1)S(1)} %get-tuple-element.102.own_ref, bf16[1072,128]{1,0:T(8,128)(2,1)S(1)} %collective-permute-done.1.a_ref.cta_ref, bf16[816,128]{1,0:T(8,128)(2,1)S(1)} %collective-permute-done.2.b_ref, ...), custom_call_target="tpu_custom_call" | custom-call | flops 2000000000 | bytes 4194304 | tf_op jit(solution)/shard_map/forward/pallas_call | solution.py:334
  22.9 1.2 %backward_first.3 = (f32[256,128]{1,0:T(8,128)S(1)}, bf16[256,128]{1,0:T(8,128)(2,1)S(1)}) custom-call(bf16[3,2,256,128]{3,2,1,0:T(8,128)(2,1)S(1)} %get-tuple-element.81.x_ref, bf16[3,2,256,128]{3,2,1,0:T(8,128)(2,1)S(1)} %get-tuple-element.82.ct_ref, bf16[1072,128]{1,0:T(8,128)(2,1)S(1)} %collective-permute-done.1.a_ref.cta_ref, ...), custom_call_target="tpu_custom_call" | custom-call | flops 2000000000 | bytes 4194304 | tf_op jit(solution)/shard_map/backward_first/pallas_call | solution.py:334
  24.1 0.1 collective-permute-start.9
  24.2 1.6 %forward.4 = (f32[4,256,128]{2,1,0:T(8,128)S(1)}, bf16[2,256,128]{2,1,0:T(8,128)(2,1)S(1)}) custom-call(bf16[2,288,384]{2,1,0:T(8,128)(2,1)S(1)} %get-tuple-element.111.own_ref, bf16[1072,128]{1,0:T(8,128)(2,1)S(1)} %collective-permute-done.1.a_ref.cta_ref, bf16[816,128]{1,0:T(8,128)(2,1)S(1)} %collective-permute-done.2.b_ref, ...), custom_call_target="tpu_custom_call" | custom-call | flops 2000000000 | bytes 4194304 | tf_op jit(solution)/shard_map/forward/pallas_call | solution.py:334
  25.8 1.7 %forward.5 = (f32[4,256,128]{2,1,0:T(8,128)S(1)}, bf16[2,256,128]{2,1,0:T(8,128)(2,1)S(1)}) custom-call(bf16[2,288,384]{2,1,0:T(8,128)(2,1)S(1)} %get-tuple-element.97.own_ref, bf16[1072,128]{1,0:T(8,128)(2,1)S(1)} %collective-permute-done.1.a_ref.cta_ref, bf16[816,128]{1,0:T(8,128)(2,1)S(1)} %collective-permute-done.2.b_ref, ...), custom_call_target="tpu_custom_call" | custom-call | flops 2000000000 | bytes 4194304 | tf_op jit(solution)/shard_map/forward/pallas_call | solution.py:334
  27.5 0.6 collective-permute-start.5
  28.1 0.0 collective-permute-done.9
  28.1 1.6 %collective-permute-start.10 = (bf16[256,128]{1,0:T(8,128)(2,1)S(1)}, bf16[256,128]{1,0:T(8,128)(2,1)S(1)}, u32[]{:S(2)}, u32[]{:S(2)}) collective-permute-start(bf16[256,128]{1,0:T(8,128)(2,1)S(1)} %add_convert_fusion.1), channel_id=1, source_target_pairs={{0,2},{2,0},{1,3},{3,1},{4,6},{6,4},{5,7},{7,5},{8,10},{10,8},{9,1... | collective-permute-start | bytes 196616 | tf_op jit(solution)/shard_map/ppermute | solution.py:424
  29.7 1.3 %collective-permute-start.11 = (bf16[256,128]{1,0:T(8,128)(2,1)S(1)}, bf16[256,128]{1,0:T(8,128)(2,1)S(1)}, u32[]{:S(2)}, u32[]{:S(2)}) collective-permute-start(bf16[256,128]{1,0:T(8,128)(2,1)S(1)} %add_convert_fusion.1), channel_id=1, source_target_pairs={{0,14},{2,12},{1,7},{3,5},{4,2},{6,0},{5,11},{7,9},{8,6},{10,4},{9... | collective-permute-start | bytes 196616 | tf_op jit(solution)/shard_map/ppermute | solution.py:425
  31.0 1.2 %backward_first.4 = (f32[256,128]{1,0:T(8,128)S(1)}, bf16[256,128]{1,0:T(8,128)(2,1)S(1)}) custom-call(bf16[3,2,256,128]{3,2,1,0:T(8,128)(2,1)S(1)} %get-tuple-element.81.x_ref, bf16[3,2,256,128]{3,2,1,0:T(8,128)(2,1)S(1)} %get-tuple-element.82.ct_ref, bf16[512,128]{1,0:T(8,128)(2,1)S(1)} %collective-permute-done.cta_ref, ...), custom_call_target="tpu_custom_call" | custom-call | flops 2000000000 | bytes 4194304 | tf_op jit(solution)/shard_map/backward_first/pallas_call | solution.py:334
  32.2 0.1 collective-permute-start.16
  32.3 1.2 %backward_first.5 = (f32[256,128]{1,0:T(8,128)S(1)}, bf16[256,128]{1,0:T(8,128)(2,1)S(1)}) custom-call(bf16[3,2,256,128]{3,2,1,0:T(8,128)(2,1)S(1)} %get-tuple-element.81.x_ref, bf16[3,2,256,128]{3,2,1,0:T(8,128)(2,1)S(1)} %get-tuple-element.82.ct_ref, bf16[512,128]{1,0:T(8,128)(2,1)S(1)} %collective-permute-done.cta_ref, ...), custom_call_target="tpu_custom_call" | custom-call | flops 2000000000 | bytes 4194304 | tf_op jit(solution)/shard_map/backward_first/pallas_call | solution.py:334
  33.5 0.6 collective-permute-start.6
  34.1 1.4 %collective-permute-done.11.rest_2_ = bf16[256,128]{1,0:T(8,128)(2,1)S(1)} collective-permute-done((bf16[256,128]{1,0:T(8,128)(2,1)S(1)}, bf16[256,128]{1,0:T(8,128)(2,1)S(1)}, u32[]{:S(2)}, u32[]{:S(2)}) %collective-permute-start.11) | collective-permute-done | bytes 65568 | tf_op jit(solution)/shard_map/ppermute | solution.py:425
  35.5 0.5 collective-permute-start.13
  36.1 0.6 collective-permute-start.17
  36.7 3.4 %collective-permute-start.19 = (bf16[256,128]{1,0:T(8,128)(2,1)S(1)}, bf16[256,128]{1,0:T(8,128)(2,1)S(1)}, u32[]{:S(2)}, u32[]{:S(2)}) collective-permute-start(bf16[256,128]{1,0:T(8,128)(2,1)S(1)} %add_convert_fusion), channel_id=1, source_target_pairs={{0,14},{2,12},{1,7},{3,5},{4,2},{6,0},{5,11},{7,9},{8,6},{10,4},{9... | collective-permute-start | bytes 196616 | tf_op jit(solution)/shard_map/ppermute | solution.py:425
  40.1 0.6 collective-permute-start.7
  40.7 0.0 collective-permute-start.8
  40.7 0.2 collective-permute-done.17.rest_0_
  40.8 1.1 %collective-permute-done.19.rest_2_ = bf16[256,128]{1,0:T(8,128)(2,1)S(1)} collective-permute-done((bf16[256,128]{1,0:T(8,128)(2,1)S(1)}, bf16[256,128]{1,0:T(8,128)(2,1)S(1)}, u32[]{:S(2)}, u32[]{:S(2)}) %collective-permute-start.19) | collective-permute-done | bytes 65568 | tf_op jit(solution)/shard_map/ppermute | solution.py:425
  42.0 0.8 %collective-permute-start.20 = (bf16[256,128]{1,0:T(8,128)(2,1)S(1)}, bf16[256,128]{1,0:T(8,128)(2,1)S(1)}, u32[]{:S(2)}, u32[]{:S(2)}) collective-permute-start(bf16[256,128]{1,0:T(8,128)(2,1)S(1)} %collective-permute-done.19.rest_2_), channel_id=1, source_target_pairs={{0,1},{1,0},{2,3},{3,2},{4,5},{5,4},{6,7},{7,6},{8,9},{9,8},{10,11... | collective-permute-start | bytes 196616 | tf_op jit(solution)/shard_map/ppermute | solution.py:375
  42.8 2.0 %backward_full.3 = (bf16[2,256,128]{2,1,0:T(8,128)(2,1)S(1)}, bf16[2,256,128]{2,1,0:T(8,128)(2,1)S(1)}, f32[128,128]{1,0:T(8,128)S(1)}, f32[128,128]{1,0:T(8,128)S(1)}, f32[216,128]{1,0:T(8,128)S(1)}) custom-call(bf16[3,2,256,128]{3,2,1,0:T(8,128)(2,1)S(1)} %get-tuple-element.81.x_ref, bf16[3,2,256,128]{3,2,1,0:T(8,128)(2,1)S(1)} %get-tuple-element.82.ct_ref, ...), custom_call_target="tpu_custom_call" | custom-call | flops 2000000000 | bytes 4194304 | tf_op jit(solution)/shard_map/backward_full/pallas_call | solution.py:334
  44.8 1.0 %collective-permute-done.8.rest_2_ = bf16[256,128]{1,0:T(8,128)(2,1)S(1)} collective-permute-done((bf16[256,128]{1,0:T(8,128)(2,1)S(1)}, bf16[256,128]{1,0:T(8,128)(2,1)S(1)}, u32[]{:S(2)}, u32[]{:S(2)}) %collective-permute-start.8) | collective-permute-done | bytes 65568 | tf_op jit(solution)/shard_map/ppermute | solution.py:425
  45.8 0.5 collective-permute-start.15
  46.3 2.0 %backward_full.4 = (bf16[2,256,128]{2,1,0:T(8,128)(2,1)S(1)}, bf16[2,256,128]{2,1,0:T(8,128)(2,1)S(1)}, f32[128,128]{1,0:T(8,128)S(1)}, f32[128,128]{1,0:T(8,128)S(1)}, f32[216,128]{1,0:T(8,128)S(1)}) custom-call(bf16[3,2,256,128]{3,2,1,0:T(8,128)(2,1)S(1)} %get-tuple-element.81.x_ref, bf16[3,2,256,128]{3,2,1,0:T(8,128)(2,1)S(1)} %get-tuple-element.82.ct_ref, ...), custom_call_target="tpu_custom_call" | custom-call | flops 2000000000 | bytes 4194304 | tf_op jit(solution)/shard_map/backward_full/pallas_call | solution.py:334
  48.4 2.0 %backward_full.5 = (bf16[2,256,128]{2,1,0:T(8,128)(2,1)S(1)}, bf16[2,256,128]{2,1,0:T(8,128)(2,1)S(1)}, f32[128,128]{1,0:T(8,128)S(1)}, f32[128,128]{1,0:T(8,128)S(1)}, f32[216,128]{1,0:T(8,128)S(1)}) custom-call(bf16[3,2,256,128]{3,2,1,0:T(8,128)(2,1)S(1)} %get-tuple-element.81.x_ref, bf16[3,2,256,128]{3,2,1,0:T(8,128)(2,1)S(1)} %get-tuple-element.82.ct_ref, ...), custom_call_target="tpu_custom_call" | custom-call | flops 2000000000 | bytes 4194304 | tf_op jit(solution)/shard_map/backward_full/pallas_call | solution.py:334
  50.4 0.5 collective-permute-start.21
  50.9 0.5 collective-permute-start.24
  51.4 4.3 %collective-permute-done.21 = bf16[472,128]{1,0:T(8,128)(2,1)S(1)} collective-permute-done((bf16[472,128]{1,0:T(8,128)(2,1)S(1)}, bf16[472,128]{1,0:T(8,128)(2,1)S(1)}, u32[]{:S(2)}, u32[]{:S(2)}) %collective-permute-start.21) | collective-permute-done | bytes 120864 | tf_op jit(solution)/shard_map/ppermute | solution.py:506
  55.7 3.1 %collective-permute-start.22 = (bf16[472,128]{1,0:T(8,128)(2,1)S(1)}, bf16[472,128]{1,0:T(8,128)(2,1)S(1)}, u32[]{:S(2)}, u32[]{:S(2)}) collective-permute-start(bf16[472,128]{1,0:T(8,128)(2,1)S(1)} %fusion.refs_0_), channel_id=1, source_target_pairs={{0,12},{4,8},{8,4},{12,0},{1,13},{5,9},{9,5},{13,1},{2,14},{6,10},... | collective-permute-start | bytes 362504 | tf_op jit(solution)/shard_map/ppermute | solution.py:507
  58.8 0.9 %emit.1 = bf16[3,2,256,128]{3,2,1,0:T(8,128)(2,1)} custom-call(bf16[2,256,128]{2,1,0:T(8,128)(2,1)S(1)} %get-tuple-element.145.refs_0_, bf16[2,256,128]{2,1,0:T(8,128)(2,1)S(1)} %get-tuple-element.128.refs_1_, bf16[2,256,128]{2,1,0:T(8,128)(2,1)S(1)} %collective-permute-done.23.refs_2_, bf16[2,256,128]{2,1,0:T(8,128)(2,1)S(1)} %get-tuple-element.146.refs_3_, ...), custom_call_target="tpu_custom_call" | custom-call | flops 2000000000 | bytes 4194304 | tf_op jit(solution)/shard_map/emit/pallas_call | solution.py:334
  59.7 2.8 %collective-permute-done.22.refs_1_ = bf16[472,128]{1,0:T(8,128)(2,1)S(1)} collective-permute-done((bf16[472,128]{1,0:T(8,128)(2,1)S(1)}, bf16[472,128]{1,0:T(8,128)(2,1)S(1)}, u32[]{:S(2)}, u32[]{:S(2)}) %collective-permute-start.22) | collective-permute-done | bytes 120864 | tf_op jit(solution)/shard_map/ppermute | solution.py:507
  62.5 1.0 %finish.1 = (f32[128,128]{1,0:T(8,128)}, f32[128,128]{1,0:T(8,128)}, f32[16,8,8,27]{3,2,1,0:T(8,128)}) custom-call(bf16[472,128]{1,0:T(8,128)(2,1)S(1)} %fusion.refs_0_, bf16[472,128]{1,0:T(8,128)(2,1)S(1)} %collective-permute-done.22.refs_1_), custom_call_target="tpu_custom_call" | custom-call | flops 2000000000 | bytes 4194304 | tf_op jit(solution)/shard_map/finish/pallas_call | solution.py:334
  (44 shorter events, 0.2 us)
Async XLA Ops:
  0.6 7.1 %copy-start.2 = (bf16[1,27,16,8,8]{1,4,3,2,0:T(8,128)(2,1)S(1)}, bf16[1,27,16,8,8]{1,4,3,2,0:T(8,128)(2,1)}, u32[]{:S(2)}) copy-start(bf16[1,27,16,8,8]{1,4,3,2,0:T(8,128)(2,1)} %param.12) | copy-start | bytes 165892
  2.6 16.4 %collective-permute-start.1 = (bf16[1072,128]{1,0:T(8,128)(2,1)}, bf16[1072,128]{1,0:T(8,128)(2,1)S(1)}, u32[]{:S(2)}, u32[]{:S(2)}) collective-permute-start(bf16[1072,128]{1,0:T(8,128)(2,1)} %get-tuple-element.84), channel_id=1, source_target_pairs={{0,12},{1,5},{4,0},{5,9},{8,4},{9,13},{12,8},{13,1},{2,14},{3,7},{... | collective-permute-start | bytes 823304 | tf_op jit(solution)/shard_map/ppermute | solution.py:413
  7.7 11.3 %collective-permute-start.2 = (bf16[816,128]{1,0:T(8,128)(2,1)}, bf16[816,128]{1,0:T(8,128)(2,1)S(1)}, u32[]{:S(2)}, u32[]{:S(2)}) collective-permute-start(bf16[816,128]{1,0:T(8,128)(2,1)} %get-tuple-element.85), channel_id=1, source_target_pairs={{0,4},{1,13},{4,8},{5,1},{8,12},{9,5},{12,0},{13,9},{2,6},{3,15},{... | collective-permute-start | bytes 626696 | tf_op jit(solution)/shard_map/ppermute | solution.py:414
  7.7 1.0 %copy-start.6 = (f32[1,3,128]{2,0,1:T(1,128)S(1)}, f32[1,3,128]{2,0,1:T(1,128)}, u32[]{:S(2)}) copy-start(f32[1,3,128]{2,0,1:T(1,128)} %param.11) | copy-start | bytes 4612
  7.7 1.0 %copy-start = (bf16[1,3,2,16,16,128]{5,4,3,2,1,0:T(8,128)(2,1)S(1)}, bf16[1,3,2,16,16,128]{5,4,3,2,1,0:T(8,128)(2,1)}, u32[]{:S(2)}) copy-start(bf16[1,3,2,16,16,128]{5,4,3,2,1,0:T(8,128)(2,1)} %param.7) | copy-start | bytes 1179652
  7.7 1.1 %copy-start.1 = (bf16[3,2,16,16,128]{4,3,2,1,0:T(8,128)(2,1)S(1)}, bf16[3,2,16,16,128]{4,3,2,1,0:T(8,128)(2,1)}, u32[]{:S(2)}) copy-start(bf16[3,2,16,16,128]{4,3,2,1,0:T(8,128)(2,1)} %param.8) | copy-start | bytes 1179652
  7.7 1.1 %copy-start.3 = (bf16[1,128,128]{2,1,0:T(8,128)(2,1)S(1)}, bf16[1,128,128]{2,1,0:T(8,128)(2,1)}, u32[]{:S(2)}) copy-start(bf16[1,128,128]{2,1,0:T(8,128)(2,1)} %param.10) | copy-start | bytes 98308
  7.7 1.1 %copy-start.4 = (bf16[1,128,128]{2,1,0:T(8,128)(2,1)S(1)}, bf16[1,128,128]{2,1,0:T(8,128)(2,1)}, u32[]{:S(2)}) copy-start(bf16[1,128,128]{2,1,0:T(8,128)(2,1)} %param.13) | copy-start | bytes 98308
  7.7 1.1 %copy-start.5 = (bf16[3,2,16,128]{3,2,1,0:T(8,128)(2,1)S(1)}, bf16[3,2,16,128]{3,2,1,0:T(8,128)(2,1)}, u32[]{:S(2)}) copy-start(bf16[3,2,16,128]{3,2,1,0:T(8,128)(2,1)} %get-tuple-element.80.lab_ref) | copy-start | bytes 73732
  19.0 2.3 %collective-permute-start.3 = (bf16[1072,128]{1,0:T(8,128)(2,1)S(1)}, bf16[1072,128]{1,0:T(8,128)(2,1)S(1)}, u32[]{:S(2)}, u32[]{:S(2)}) collective-permute-start(bf16[1072,128]{1,0:T(8,128)(2,1)S(1)} %collective-permute-done.1.a_ref.cta_ref), channel_id=1, source_target_pairs={{0,1},{1,0},{2,3},{3,2},{4,5},{5,4},{6,7},{7,6},{8,9},{9,8},{10,11... | collective-permute-start | bytes 823304 | tf_op jit(solution)/shard_map/ppermute | solution.py:375
  19.0 2.3 %collective-permute-start.4 = (bf16[816,128]{1,0:T(8,128)(2,1)S(1)}, bf16[816,128]{1,0:T(8,128)(2,1)S(1)}, u32[]{:S(2)}, u32[]{:S(2)}) collective-permute-start(bf16[816,128]{1,0:T(8,128)(2,1)S(1)} %collective-permute-done.2.b_ref), channel_id=1, source_target_pairs={{0,1},{1,0},{2,3},{3,2},{4,5},{5,4},{6,7},{7,6},{8,9},{9,8},{10,11... | collective-permute-start | bytes 626696 | tf_op jit(solution)/shard_map/ppermute | solution.py:375
  19.5 8.1 %collective-permute-start = (bf16[512,128]{1,0:T(8,128)(2,1)S(1)}, bf16[512,128]{1,0:T(8,128)(2,1)S(1)}, u32[]{:S(2)}, u32[]{:S(2)}) collective-permute-start(bf16[512,128]{1,0:T(8,128)(2,1)S(1)} %get-tuple-element.83), channel_id=1, source_target_pairs={{0,12},{1,5},{4,0},{5,9},{8,4},{9,13},{12,8},{13,1},{2,14},{3,7},{... | collective-permute-start | bytes 393224 | tf_op jit(solution)/shard_map/ppermute | solution.py:417
  24.1 4.0 %collective-permute-start.9 = (bf16[256,128]{1,0:T(8,128)(2,1)S(1)}, bf16[256,128]{1,0:T(8,128)(2,1)S(1)}, u32[]{:S(2)}, u32[]{:S(2)}) collective-permute-start(bf16[256,128]{1,0:T(8,128)(2,1)S(1)} %get-tuple-element.109), channel_id=1, source_target_pairs={{0,1},{1,0},{2,3},{3,2},{4,5},{5,4},{6,7},{7,6},{8,9},{9,8},{10,11... | collective-permute-start | bytes 196616 | tf_op jit(solution)/shard_map/ppermute | solution.py:375
  27.5 3.5 %collective-permute-start.5 = (bf16[512,128]{1,0:T(8,128)(2,1)S(1)}, bf16[512,128]{1,0:T(8,128)(2,1)S(1)}, u32[]{:S(2)}, u32[]{:S(2)}) collective-permute-start(bf16[512,128]{1,0:T(8,128)(2,1)S(1)} %collective-permute-done.cta_ref), channel_id=1, source_target_pairs={{0,1},{1,0},{2,3},{3,2},{4,5},{5,4},{6,7},{7,6},{8,9},{9,8},{10,11... | collective-permute-start | bytes 393224 | tf_op jit(solution)/shard_map/ppermute | solution.py:375
  28.1 6.0 %collective-permute-start.10 = (bf16[256,128]{1,0:T(8,128)(2,1)S(1)}, bf16[256,128]{1,0:T(8,128)(2,1)S(1)}, u32[]{:S(2)}, u32[]{:S(2)}) collective-permute-start(bf16[256,128]{1,0:T(8,128)(2,1)S(1)} %add_convert_fusion.1), channel_id=1, source_target_pairs={{0,2},{2,0},{1,3},{3,1},{4,6},{6,4},{5,7},{7,5},{8,10},{10,8},{9,1... | collective-permute-start | bytes 196616 | tf_op jit(solution)/shard_map/ppermute | solution.py:424
  29.7 5.9 %collective-permute-start.11 = (bf16[256,128]{1,0:T(8,128)(2,1)S(1)}, bf16[256,128]{1,0:T(8,128)(2,1)S(1)}, u32[]{:S(2)}, u32[]{:S(2)}) collective-permute-start(bf16[256,128]{1,0:T(8,128)(2,1)S(1)} %add_convert_fusion.1), channel_id=1, source_target_pairs={{0,14},{2,12},{1,7},{3,5},{4,2},{6,0},{5,11},{7,9},{8,6},{10,4},{9... | collective-permute-start | bytes 196616 | tf_op jit(solution)/shard_map/ppermute | solution.py:425
  32.2 3.8 %collective-permute-start.16 = (bf16[256,128]{1,0:T(8,128)(2,1)S(1)}, bf16[256,128]{1,0:T(8,128)(2,1)S(1)}, u32[]{:S(2)}, u32[]{:S(2)}) collective-permute-start(bf16[256,128]{1,0:T(8,128)(2,1)S(1)} %get-tuple-element.119), channel_id=1, source_target_pairs={{0,1},{1,0},{2,3},{3,2},{4,5},{5,4},{6,7},{7,6},{8,9},{9,8},{10,11... | collective-permute-start | bytes 196616 | tf_op jit(solution)/shard_map/ppermute | solution.py:375
  33.5 6.5 %collective-permute-start.6 = (bf16[256,128]{1,0:T(8,128)(2,1)S(1)}, bf16[256,128]{1,0:T(8,128)(2,1)S(1)}, u32[]{:S(2)}, u32[]{:S(2)}) collective-permute-start(bf16[256,128]{1,0:T(8,128)(2,1)S(1)} %get-tuple-element.122), channel_id=1, source_target_pairs={{0,1},{1,0},{2,3},{3,2},{4,5},{5,4},{6,7},{7,6},{8,9},{9,8},{10,11... | collective-permute-start | bytes 196616 | tf_op jit(solution)/shard_map/ppermute | solution.py:375
  35.5 5.1 %collective-permute-start.12 = (bf16[256,128]{1,0:T(8,128)(2,1)S(1)}, bf16[256,128]{1,0:T(8,128)(2,1)S(1)}, u32[]{:S(2)}, u32[]{:S(2)}) collective-permute-start(bf16[256,128]{1,0:T(8,128)(2,1)S(1)} %collective-permute-done.10.rest_0_), channel_id=1, source_target_pairs={{0,1},{1,0},{2,3},{3,2},{4,5},{5,4},{6,7},{7,6},{8,9},{9,8},{10,11... | collective-permute-start | bytes 196616 | tf_op jit(solution)/shard_map/ppermute | solution.py:375
  35.5 7.3 %collective-permute-start.13 = (bf16[256,128]{1,0:T(8,128)(2,1)S(1)}, bf16[256,128]{1,0:T(8,128)(2,1)S(1)}, u32[]{:S(2)}, u32[]{:S(2)}) collective-permute-start(bf16[256,128]{1,0:T(8,128)(2,1)S(1)} %collective-permute-done.11.rest_2_), channel_id=1, source_target_pairs={{0,1},{1,0},{2,3},{3,2},{4,5},{5,4},{6,7},{7,6},{8,9},{9,8},{10,11... | collective-permute-start | bytes 196616 | tf_op jit(solution)/shard_map/ppermute | solution.py:375
  36.1 4.8 %collective-permute-start.17 = (bf16[256,128]{1,0:T(8,128)(2,1)S(1)}, bf16[256,128]{1,0:T(8,128)(2,1)S(1)}, u32[]{:S(2)}, u32[]{:S(2)}) collective-permute-start(bf16[256,128]{1,0:T(8,128)(2,1)S(1)} %add_convert_fusion), channel_id=1, source_target_pairs={{0,2},{2,0},{1,3},{3,1},{4,6},{6,4},{5,7},{7,5},{8,10},{10,8},{9,1... | collective-permute-start | bytes 196616 | tf_op jit(solution)/shard_map/ppermute | solution.py:424
  36.7 5.3 %collective-permute-start.19 = (bf16[256,128]{1,0:T(8,128)(2,1)S(1)}, bf16[256,128]{1,0:T(8,128)(2,1)S(1)}, u32[]{:S(2)}, u32[]{:S(2)}) collective-permute-start(bf16[256,128]{1,0:T(8,128)(2,1)S(1)} %add_convert_fusion), channel_id=1, source_target_pairs={{0,14},{2,12},{1,7},{3,5},{4,2},{6,0},{5,11},{7,9},{8,6},{10,4},{9... | collective-permute-start | bytes 196616 | tf_op jit(solution)/shard_map/ppermute | solution.py:425
  40.1 4.8 %collective-permute-start.7 = (bf16[256,128]{1,0:T(8,128)(2,1)S(1)}, bf16[256,128]{1,0:T(8,128)(2,1)S(1)}, u32[]{:S(2)}, u32[]{:S(2)}) collective-permute-start(bf16[256,128]{1,0:T(8,128)(2,1)S(1)} %add_convert_fusion.2), channel_id=1, source_target_pairs={{0,2},{2,0},{1,3},{3,1},{4,6},{6,4},{5,7},{7,5},{8,10},{10,8},{9,1... | collective-permute-start | bytes 196616 | tf_op jit(solution)/shard_map/ppermute | solution.py:424
  40.7 5.2 %collective-permute-start.8 = (bf16[256,128]{1,0:T(8,128)(2,1)S(1)}, bf16[256,128]{1,0:T(8,128)(2,1)S(1)}, u32[]{:S(2)}, u32[]{:S(2)}) collective-permute-start(bf16[256,128]{1,0:T(8,128)(2,1)S(1)} %add_convert_fusion.2), channel_id=1, source_target_pairs={{0,14},{2,12},{1,7},{3,5},{4,2},{6,0},{5,11},{7,9},{8,6},{10,4},{9... | collective-permute-start | bytes 196616 | tf_op jit(solution)/shard_map/ppermute | solution.py:425
  40.8 5.5 %collective-permute-start.18 = (bf16[256,128]{1,0:T(8,128)(2,1)S(1)}, bf16[256,128]{1,0:T(8,128)(2,1)S(1)}, u32[]{:S(2)}, u32[]{:S(2)}) collective-permute-start(bf16[256,128]{1,0:T(8,128)(2,1)S(1)} %collective-permute-done.17.rest_0_), channel_id=1, source_target_pairs={{0,1},{1,0},{2,3},{3,2},{4,5},{5,4},{6,7},{7,6},{8,9},{9,8},{10,11... | collective-permute-start | bytes 196616 | tf_op jit(solution)/shard_map/ppermute | solution.py:375
  42.0 4.4 %collective-permute-start.20 = (bf16[256,128]{1,0:T(8,128)(2,1)S(1)}, bf16[256,128]{1,0:T(8,128)(2,1)S(1)}, u32[]{:S(2)}, u32[]{:S(2)}) collective-permute-start(bf16[256,128]{1,0:T(8,128)(2,1)S(1)} %collective-permute-done.19.rest_2_), channel_id=1, source_target_pairs={{0,1},{1,0},{2,3},{3,2},{4,5},{5,4},{6,7},{7,6},{8,9},{9,8},{10,11... | collective-permute-start | bytes 196616 | tf_op jit(solution)/shard_map/ppermute | solution.py:375
  45.8 2.5 %collective-permute-start.14 = (bf16[256,128]{1,0:T(8,128)(2,1)S(1)}, bf16[256,128]{1,0:T(8,128)(2,1)S(1)}, u32[]{:S(2)}, u32[]{:S(2)}) collective-permute-start(bf16[256,128]{1,0:T(8,128)(2,1)S(1)} %collective-permute-done.7.rest_0_), channel_id=1, source_target_pairs={{0,1},{1,0},{2,3},{3,2},{4,5},{5,4},{6,7},{7,6},{8,9},{9,8},{10,11... | collective-permute-start | bytes 196616 | tf_op jit(solution)/shard_map/ppermute | solution.py:375
  45.8 2.5 %collective-permute-start.15 = (bf16[256,128]{1,0:T(8,128)(2,1)S(1)}, bf16[256,128]{1,0:T(8,128)(2,1)S(1)}, u32[]{:S(2)}, u32[]{:S(2)}) collective-permute-start(bf16[256,128]{1,0:T(8,128)(2,1)S(1)} %collective-permute-done.8.rest_2_), channel_id=1, source_target_pairs={{0,1},{1,0},{2,3},{3,2},{4,5},{5,4},{6,7},{7,6},{8,9},{9,8},{10,11... | collective-permute-start | bytes 196616 | tf_op jit(solution)/shard_map/ppermute | solution.py:375
  50.4 5.3 %collective-permute-start.21 = (bf16[472,128]{1,0:T(8,128)(2,1)S(1)}, bf16[472,128]{1,0:T(8,128)(2,1)S(1)}, u32[]{:S(2)}, u32[]{:S(2)}) collective-permute-start(bf16[472,128]{1,0:T(8,128)(2,1)S(1)} %pad_maximum_fusion), channel_id=1, source_target_pairs={{0,4},{4,0},{8,12},{12,8},{1,5},{5,1},{9,13},{13,9},{2,6},{6,2},{1... | collective-permute-start | bytes 362504 | tf_op jit(solution)/shard_map/ppermute | solution.py:506
  50.9 7.9 %collective-permute-start.23 = (bf16[2,256,128]{2,1,0:T(8,128)(2,1)S(1)}, bf16[2,256,128]{2,1,0:T(8,128)(2,1)S(1)}, u32[]{:S(2)}, u32[]{:S(2)}) collective-permute-start(bf16[2,256,128]{2,1,0:T(8,128)(2,1)S(1)} %get-tuple-element.128.refs_1_), channel_id=1, source_target_pairs={{0,1},{1,0},{2,3},{3,2},{4,5},{5,4},{6,7},{7,6},{8,9},{9,8},{10,11... | collective-permute-start | bytes 393224 | tf_op jit(solution)/shard_map/ppermute | solution.py:375
  50.9 7.9 %collective-permute-start.24 = (bf16[2,256,128]{2,1,0:T(8,128)(2,1)S(1)}, bf16[2,256,128]{2,1,0:T(8,128)(2,1)S(1)}, u32[]{:S(2)}, u32[]{:S(2)}) collective-permute-start(bf16[2,256,128]{2,1,0:T(8,128)(2,1)S(1)} %get-tuple-element.147.refs_4_), channel_id=1, source_target_pairs={{0,1},{1,0},{2,3},{3,2},{4,5},{5,4},{6,7},{7,6},{8,9},{9,8},{10,11... | collective-permute-start | bytes 393224 | tf_op jit(solution)/shard_map/ppermute | solution.py:375
  51.4 7.4 %collective-permute-start.25 = (bf16[2,256,128]{2,1,0:T(8,128)(2,1)S(1)}, bf16[2,256,128]{2,1,0:T(8,128)(2,1)S(1)}, u32[]{:S(2)}, u32[]{:S(2)}) collective-permute-start(bf16[2,256,128]{2,1,0:T(8,128)(2,1)S(1)} %get-tuple-element.149.refs_7_), channel_id=1, source_target_pairs={{0,1},{1,0},{2,3},{3,2},{4,5},{5,4},{6,7},{7,6},{8,9},{9,8},{10,11... | collective-permute-start | bytes 393224 | tf_op jit(solution)/shard_map/ppermute | solution.py:375
  55.7 6.8 %collective-permute-start.22 = (bf16[472,128]{1,0:T(8,128)(2,1)S(1)}, bf16[472,128]{1,0:T(8,128)(2,1)S(1)}, u32[]{:S(2)}, u32[]{:S(2)}) collective-permute-start(bf16[472,128]{1,0:T(8,128)(2,1)S(1)} %fusion.refs_0_), channel_id=1, source_target_pairs={{0,12},{4,8},{8,4},{12,0},{1,13},{5,9},{9,5},{13,1},{2,14},{6,10},... | collective-permute-start | bytes 362504 | tf_op jit(solution)/shard_map/ppermute | solution.py:507

commit v6 on v5

--- a/solution.py
+++ b/solution.py
@@ -141,7 +141,7 @@
 def own_kernel(
     micro, wide, deep, x_ref, ct_ref, lab_ref, w_ref, rw_ref, code_ref, *outs
 ):
-    *kept, edge_ref = outs[3 * micro :]
+    *kept, edge_ref, flip_ref = outs[3 * micro :]
     for src, dst in zip((x_ref, ct_ref, w_ref, rw_ref, code_ref), kept):
         dst[...] = src[...]
     c = lax.axis_index("chan")
@@ -151,11 +151,12 @@
     codes = code_rows(code_ref, deep)
     for m in range(micro):
         hs_ref, hid_ref, spre_ref = outs[3 * m : 3 * m + 3]
+        flip_ref[m] = x_ref[m].reshape(2 * cells, LANES).T
         for p in range(2):
             pre = hidden_rows(x_ref[m, p], lab_ref[m, p], w_ref[...], codes, wide, deep)
             q = gate(pre)
             h = pre * q
-            hid_ref[p] = h.astype(BF)
+            hid_ref[:, p * cells : (p + 1) * cells] = h.astype(BF).T
             spre_ref[p] = slope(pre, q)
             store_shifts(hs_ref, p, h, wide, deep)
 
@@ -192,7 +193,7 @@
         q = gate(conv)
         sconv_ref[p] = slope(conv, q)
         if p in (1, 2):
-            mixed_ref[p - 1] = (conv * q).astype(BF)
+            mixed_ref[:, (p - 1) * cells : p * cells] = (conv * q).astype(BF).T
 
 
 def backward_kernel(
@@ -250,28 +251,25 @@
         store_shifts(gs_ref, plane, grad.astype(BF).astype(F32), wide, deep)
     if full:
         ups2 = up_ref[...].reshape(2 * cells, LANES)
-        red = lax.dot_general(
-            mixed_ref[...].reshape(2 * cells, LANES),
-            ups2,
-            (((0,), (0,)), ((), ())),
-            preferred_element_type=F32,
-        )
+        red = jnp.dot(mixed_ref[...], ups2, preferred_element_type=F32)
         red_ref[...] = red_in[...] + red
         groups = LANES // width
         keep = diagonal_mask(width)
-        turned = [hid_ref[p].T for p in (0, 1)]
-        left = jnp.concatenate(turned, axis=1)
-        for dx in (-1, 0, 1):
-            for dy in (-1, 0, 1):
-                rows = slice((1 + dy) * deep, (1 + dy) * deep + cells)
-                right = jnp.concatenate([gs_ref[1 + dx, rows, :], gs_ref[2 + dx, rows, :]], axis=0)
-                dense = jnp.dot(left, right, preferred_element_type=F32)
-                for j in range(3):
-                    tap = 9 * (dx + 1) + 3 * (dy + 1) + j
-                    block = dense[:, j * LANES : (j + 1) * LANES].reshape(groups, width, LANES)
-                    thin = jnp.sum(jnp.where(keep, block, 0.0), axis=0)
-                    at = slice((taps - 1 - tap) * width, (taps - tap) * width)
-                    kg_ref[at] = kg_in[at] + thin
+        left = hid_ref[...]
+        right = []
+        for p in (0, 1):
+            parts = [
+                gs_ref[p + dx, dy * deep : dy * deep + cells, :]
+                for dx in range(3)
+                for dy in range(3)
+            ]
+            right.append(jnp.concatenate(parts, axis=1))
+        dense = jnp.dot(left, jnp.concatenate(right, axis=0), preferred_element_type=F32)
+        for tap in range(taps):
+            block = dense[:, tap * LANES : (tap + 1) * LANES].reshape(groups, width, LANES)
+            thin = jnp.sum(jnp.where(keep, block, 0.0), axis=0)
+            at = slice((taps - 1 - tap) * width, (taps - tap) * width)
+            kg_ref[at] = kg_in[at] + thin
     planes = [(gs_ref, p) for p in range(4)]
     grads = []
     for p, grad_hidden in enumerate(conv_pairs(planes, (1,), kb_ref, cells, deep)):
@@ -283,11 +281,8 @@
         else:
             br_ref[p] = branch
     if full:
-        exp_ref[...] = exp_in[...] + lax.dot_general(
-            x_ref[m].reshape(2 * cells, LANES),
-            jnp.concatenate(grads, axis=0),
-            (((0,), (0,)), ((), ())),
-            preferred_element_type=F32,
+        exp_ref[...] = exp_in[...] + jnp.dot(
+            x_ref[m], jnp.concatenate(grads, axis=0), preferred_element_type=F32
         )
     else:
         base_ref[...] = up_ref[c].astype(F32) + br_ref[c]
@@ -402,12 +397,13 @@
         (kern,),
         [pltpu.VMEM((LANES * width, LANES), F32), pltpu.VMEM((2,) + thin, F32)],
     )
-    *owned, x, ct, w, rw, code, edge = call(
+    *owned, x, ct, w, rw, code, edge, flip = call(
         functools.partial(own_kernel, micro, wide, deep),
         "own",
-        [sds((2, pad_rows, 3 * LANES), BF), sds(plane2, BF), sds(plane2, F32)] * micro
+        [sds((2, pad_rows, 3 * LANES), BF), sds((LANES, 2 * cells), BF), sds(plane2, F32)]
+        * micro
         + [sds(v.shape, v.dtype) for v in (x, ct, w, rw, code)]
-        + [sds((max(1, micro - 1) * cells, LANES), BF)],
+        + [sds((max(1, micro - 1) * cells, LANES), BF), sds((micro, LANES, 2 * cells), BF)],
         (x, ct, lab, w, rw, code),
     )
     a = lax.ppermute(packed_a, ("space", "chan"), route_a)
@@ -443,7 +439,7 @@
             functools.partial(backward_kernel, mode, m, sent_slot[m], tails[m], wide, deep, taps, width),
             "backward_" + mode,
             outs + list(extra_out),
-            (x, ct, *edges[m], w, rw, dense_b, spre[m], sconv[m], *extra),
+            (flip, ct, *edges[m], w, rw, dense_b, spre[m], sconv[m], *extra),
             scratch,
         )
 
@@ -459,7 +455,7 @@
         con, mix = call(
             functools.partial(forward_kernel, m, wide, deep),
             "forward",
-            [sds(plane4, F32), sds(plane2, BF)],
+            [sds(plane4, F32), sds((LANES, 2 * cells), BF)],
             (owned[3 * m], *halos, w, code, dense_f),
             [pltpu.VMEM((4, pad_rows, 3 * LANES), BF)],
         )

time: 63.7 us -> 63.5 us (level)
  Pallas kernels: 20.2 us -> 20.9 us
    ppermute x1, waiting for transfers between devices: 9.33 us -> 8.32 us  [on_device(): b = lax.ppermute(packed_b, ('space', 'chan'), route_b)]
    pallas_call x14, Pallas kernels: 20.2 us -> 20.9 us  [call(): pl.pallas_call(kernel, in_specs=[vmem] * len(args) if in_specs is None el...]
  transfers between devices with their start and end apart: 26 -> 26, of which waited for: 7 -> 7; matrix products, arithmetic and copies ran while one was open for 0% -> 0% of each run, Pallas kernels for 24% -> 25%
where the time goes in v6:
time: 63.5 us; the launch traced here: 63.3 us
  starting transfers between devices  21.7 us (34%)
  Pallas kernels  20.9 us (33%)
  waiting for transfers between devices  19.5 us (31%)
  between operations  0.92 us (1%)
    pallas_call x14, Pallas kernels, call(): pl.pallas_call(kernel, in_specs=[vmem] * len(args) if in_specs is None el...  20.9 us
    ppermute x1, waiting for transfers between devices, on_device(): b = lax.ppermute(packed_b, ('space', 'chan'), route_b)  8.32 us
    ppermute x1, starting transfers between devices, on_device(): a = lax.ppermute(packed_a, ('space', 'chan'), route_a)  5.1 us
    ppermute x3, starting transfers between devices, send_on(): dg = lax.ppermute(out, ('space', 'section', 'chan'), route_d)  4.68 us
    ppermute x1, waiting for transfers between devices, on_device(): grads = grads + lax.ppermute(grads, 'space', near)  4.4 us
    ppermute x15, starting transfers between devices, swap(): return lax.ppermute(v, 'chan', [(0, 1), (1, 0)])  4.12 us
    ppermute x3, waiting for transfers between devices, send_on(): dg = lax.ppermute(out, ('space', 'section', 'chan'), route_d)  3.68 us
    ppermute x1, starting transfers between devices, on_device(): copies = [grads, lax.ppermute(grads, 'space', far)]  2.95 us
  transfers between devices with their start and end apart: 26, of which 7 were waited for; matrix products, arithmetic and copies ran while one was open for 0% of the time, Pallas kernels for 25%

profile of v6, /device:TPU:0, one launch (start us, length us, event | category | flops | bytes accessed | tf_op | source)
XLA Modules:
  0.0 63.3 jit_solution(8756300622775057947)
XLA Ops:
  0.6 1.9 %pack.1 = (bf16[1072,128]{1,0:T(8,128)(2,1)}, bf16[816,128]{1,0:T(8,128)(2,1)}, bf16[3,2,16,128]{3,2,1,0:T(8,128)(2,1)}) custom-call(bf16[3,2,256,128]{3,2,1,0:T(8,128)(2,1)} %bitcast.16, bf16[3,2,256,128]{3,2,1,0:T(8,128)(2,1)} %bitcast.18, s32[3,2,16,16]{3,2,1,0:T(8,128)} %tag_ref.1), custom_call_target="tpu_custom_call" | custom-call | flops 2000000000 | bytes 4194304 | tf_op jit(solution)/shard_map/pack/pallas_call | solution.py:329
  2.6 5.1 %collective-permute-start.1 = (bf16[1072,128]{1,0:T(8,128)(2,1)}, bf16[1072,128]{1,0:T(8,128)(2,1)S(1)}, u32[]{:S(2)}, u32[]{:S(2)}) collective-permute-start(bf16[1072,128]{1,0:T(8,128)(2,1)} %get-tuple-element.84), channel_id=1, source_target_pairs={{0,12},{1,5},{4,0},{5,9},{8,4},{9,13},{12,8},{13,1},{2,14},{3,7},{... | collective-permute-start | bytes 823304 | tf_op jit(solution)/shard_map/ppermute | solution.py:409
  7.7 0.0 collective-permute-start.2
  7.7 0.0 copy-start.1
  7.7 0.0 copy-start.3
  7.7 0.0 copy-start.4
  7.7 0.0 copy-start.5
  7.8 0.9 %weights.1 = (bf16[4608,256]{1,0:T(8,128)(2,1)S(1)}, bf16[4608,256]{1,0:T(8,128)(2,1)S(1)}) custom-call(bf16[16,8,8,27]{3,2,1,0:T(8,128)(2,1)S(1)} %bitcast.20), custom_call_target="tpu_custom_call" | custom-call | flops 2000000000 | bytes 4194304 | tf_op jit(solution)/shard_map/weights/pallas_call | solution.py:329
  8.7 0.1 copy-done.1
  8.8 1.8 %own.1 = (bf16[2,288,384]{2,1,0:T(8,128)(2,1)S(1)}, bf16[128,512]{1,0:T(8,128)(2,1)S(1)}, f32[2,256,128]{2,1,0:T(8,128)S(1)}, bf16[2,288,384]{2,1,0:T(8,128)(2,1...) custom-call(bf16[3,2,256,128]{3,2,1,0:T(8,128)(2,1)S(1)} %bitcast.17, ...), custom_call_target="tpu_custom_call" | custom-call | flops 2000000000 | bytes 4194304 | tf_op jit(solution)/shard_map/own/pallas_call | solution.py:329
  10.6 8.3 %collective-permute-done.2.b_ref = bf16[816,128]{1,0:T(8,128)(2,1)S(1)} collective-permute-done((bf16[816,128]{1,0:T(8,128)(2,1)}, bf16[816,128]{1,0:T(8,128)(2,1)S(1)}, u32[]{:S(2)}, u32[]{:S(2)}) %collective-permute-start.2) | collective-permute-done | bytes 208928 | tf_op jit(solution)/shard_map/ppermute | solution.py:410
  19.0 0.5 collective-permute-start.4
  19.5 1.7 %collective-permute-start = (bf16[512,128]{1,0:T(8,128)(2,1)S(1)}, bf16[512,128]{1,0:T(8,128)(2,1)S(1)}, u32[]{:S(2)}, u32[]{:S(2)}) collective-permute-start(bf16[512,128]{1,0:T(8,128)(2,1)S(1)} %get-tuple-element.83), channel_id=1, source_target_pairs={{0,12},{1,5},{4,0},{5,9},{8,4},{9,13},{12,8},{13,1},{2,14},{3,7},{... | collective-permute-start | bytes 393224 | tf_op jit(solution)/shard_map/ppermute | solution.py:413
  21.2 1.7 %forward.3 = (f32[4,256,128]{2,1,0:T(8,128)S(1)}, bf16[128,512]{1,0:T(8,128)(2,1)S(1)}) custom-call(bf16[2,288,384]{2,1,0:T(8,128)(2,1)S(1)} %get-tuple-element.102.own_ref, bf16[1072,128]{1,0:T(8,128)(2,1)S(1)} %collective-permute-done.1.a_ref.cta_ref, bf16[816,128]{1,0:T(8,128)(2,1)S(1)} %collective-permute-done.2.b_ref, ...), custom_call_target="tpu_custom_call" | custom-call | flops 2000000000 | bytes 4194304 | tf_op jit(solution)/shard_map/forward/pallas_call | solution.py:329
  22.9 1.2 %backward_first.3 = (f32[256,128]{1,0:T(8,128)S(1)}, bf16[256,128]{1,0:T(8,128)(2,1)S(1)}) custom-call(bf16[3,128,512]{2,1,0:T(8,128)(2,1)S(1)} %get-tuple-element.81.x_ref, bf16[3,2,256,128]{3,2,1,0:T(8,128)(2,1)S(1)} %get-tuple-element.82.ct_ref, bf16[1072,128]{1,0:T(8,128)(2,1)S(1)} %collective-permute-done.1.a_ref.cta_ref, ...), custom_call_target="tpu_custom_call" | custom-call | flops 2000000000 | bytes 4194304 | tf_op jit(solution)/shard_map/backward_first/pallas_call | solution.py:329
  24.2 0.1 collective-permute-start.9
  24.2 1.7 %forward.4 = (f32[4,256,128]{2,1,0:T(8,128)S(1)}, bf16[128,512]{1,0:T(8,128)(2,1)S(1)}) custom-call(bf16[2,288,384]{2,1,0:T(8,128)(2,1)S(1)} %get-tuple-element.111.own_ref, bf16[1072,128]{1,0:T(8,128)(2,1)S(1)} %collective-permute-done.1.a_ref.cta_ref, bf16[816,128]{1,0:T(8,128)(2,1)S(1)} %collective-permute-done.2.b_ref, ...), custom_call_target="tpu_custom_call" | custom-call | flops 2000000000 | bytes 4194304 | tf_op jit(solution)/shard_map/forward/pallas_call | solution.py:329
  25.9 1.7 %forward.5 = (f32[4,256,128]{2,1,0:T(8,128)S(1)}, bf16[128,512]{1,0:T(8,128)(2,1)S(1)}) custom-call(bf16[2,288,384]{2,1,0:T(8,128)(2,1)S(1)} %get-tuple-element.97.own_ref, bf16[1072,128]{1,0:T(8,128)(2,1)S(1)} %collective-permute-done.1.a_ref.cta_ref, bf16[816,128]{1,0:T(8,128)(2,1)S(1)} %collective-permute-done.2.b_ref, ...), custom_call_target="tpu_custom_call" | custom-call | flops 2000000000 | bytes 4194304 | tf_op jit(solution)/shard_map/forward/pallas_call | solution.py:329
  27.7 0.0 collective-permute-done.cta_ref
  27.7 0.6 collective-permute-start.5
  28.2 0.0 collective-permute-done.9
  28.3 1.6 %collective-permute-start.10 = (bf16[256,128]{1,0:T(8,128)(2,1)S(1)}, bf16[256,128]{1,0:T(8,128)(2,1)S(1)}, u32[]{:S(2)}, u32[]{:S(2)}) collective-permute-start(bf16[256,128]{1,0:T(8,128)(2,1)S(1)} %add_convert_fusion.1), channel_id=1, source_target_pairs={{0,2},{2,0},{1,3},{3,1},{4,6},{6,4},{5,7},{7,5},{8,10},{10,8},{9,1... | collective-permute-start | bytes 196616 | tf_op jit(solution)/shard_map/ppermute | solution.py:420
  29.8 1.3 %collective-permute-start.11 = (bf16[256,128]{1,0:T(8,128)(2,1)S(1)}, bf16[256,128]{1,0:T(8,128)(2,1)S(1)}, u32[]{:S(2)}, u32[]{:S(2)}) collective-permute-start(bf16[256,128]{1,0:T(8,128)(2,1)S(1)} %add_convert_fusion.1), channel_id=1, source_target_pairs={{0,14},{2,12},{1,7},{3,5},{4,2},{6,0},{5,11},{7,9},{8,6},{10,4},{9... | collective-permute-start | bytes 196616 | tf_op jit(solution)/shard_map/ppermute | solution.py:421
  31.1 1.2 %backward_first.4 = (f32[256,128]{1,0:T(8,128)S(1)}, bf16[256,128]{1,0:T(8,128)(2,1)S(1)}) custom-call(bf16[3,128,512]{2,1,0:T(8,128)(2,1)S(1)} %get-tuple-element.81.x_ref, bf16[3,2,256,128]{3,2,1,0:T(8,128)(2,1)S(1)} %get-tuple-element.82.ct_ref, bf16[512,128]{1,0:T(8,128)(2,1)S(1)} %collective-permute-done.cta_ref, ...), custom_call_target="tpu_custom_call" | custom-call | flops 2000000000 | bytes 4194304 | tf_op jit(solution)/shard_map/backward_first/pallas_call | solution.py:329
  32.4 0.1 collective-permute-start.16
  32.5 1.2 %backward_first.5 = (f32[256,128]{1,0:T(8,128)S(1)}, bf16[256,128]{1,0:T(8,128)(2,1)S(1)}) custom-call(bf16[3,128,512]{2,1,0:T(8,128)(2,1)S(1)} %get-tuple-element.81.x_ref, bf16[3,2,256,128]{3,2,1,0:T(8,128)(2,1)S(1)} %get-tuple-element.82.ct_ref, bf16[512,128]{1,0:T(8,128)(2,1)S(1)} %collective-permute-done.cta_ref, ...), custom_call_target="tpu_custom_call" | custom-call | flops 2000000000 | bytes 4194304 | tf_op jit(solution)/shard_map/backward_first/pallas_call | solution.py:329
  33.7 0.6 collective-permute-start.6
  34.3 1.4 %collective-permute-done.11.rest_2_ = bf16[256,128]{1,0:T(8,128)(2,1)S(1)} collective-permute-done((bf16[256,128]{1,0:T(8,128)(2,1)S(1)}, bf16[256,128]{1,0:T(8,128)(2,1)S(1)}, u32[]{:S(2)}, u32[]{:S(2)}) %collective-permute-start.11) | collective-permute-done | bytes 65568 | tf_op jit(solution)/shard_map/ppermute | solution.py:421
  35.7 0.5 collective-permute-start.13
  36.2 0.6 collective-permute-start.17
  36.8 3.4 %collective-permute-start.19 = (bf16[256,128]{1,0:T(8,128)(2,1)S(1)}, bf16[256,128]{1,0:T(8,128)(2,1)S(1)}, u32[]{:S(2)}, u32[]{:S(2)}) collective-permute-start(bf16[256,128]{1,0:T(8,128)(2,1)S(1)} %add_convert_fusion), channel_id=1, source_target_pairs={{0,14},{2,12},{1,7},{3,5},{4,2},{6,0},{5,11},{7,9},{8,6},{10,4},{9... | collective-permute-start | bytes 196616 | tf_op jit(solution)/shard_map/ppermute | solution.py:421
  40.2 0.6 collective-permute-start.7
  40.8 0.0 collective-permute-start.8
  40.8 0.2 collective-permute-done.17.rest_0_
  41.0 1.1 %collective-permute-done.19.rest_2_ = bf16[256,128]{1,0:T(8,128)(2,1)S(1)} collective-permute-done((bf16[256,128]{1,0:T(8,128)(2,1)S(1)}, bf16[256,128]{1,0:T(8,128)(2,1)S(1)}, u32[]{:S(2)}, u32[]{:S(2)}) %collective-permute-start.19) | collective-permute-done | bytes 65568 | tf_op jit(solution)/shard_map/ppermute | solution.py:421
  42.1 0.8 %collective-permute-start.20 = (bf16[256,128]{1,0:T(8,128)(2,1)S(1)}, bf16[256,128]{1,0:T(8,128)(2,1)S(1)}, u32[]{:S(2)}, u32[]{:S(2)}) collective-permute-start(bf16[256,128]{1,0:T(8,128)(2,1)S(1)} %collective-permute-done.19.rest_2_), channel_id=1, source_target_pairs={{0,1},{1,0},{2,3},{3,2},{4,5},{5,4},{6,7},{7,6},{8,9},{9,8},{10,11... | collective-permute-start | bytes 196616 | tf_op jit(solution)/shard_map/ppermute | solution.py:370
  43.0 1.9 %backward_full.3 = (bf16[2,256,128]{2,1,0:T(8,128)(2,1)S(1)}, bf16[2,256,128]{2,1,0:T(8,128)(2,1)S(1)}, f32[128,128]{1,0:T(8,128)S(1)}, f32[128,128]{1,0:T(8,128)S(1)}, f32[216,128]{1,0:T(8,128)S(1)}) custom-call(bf16[3,128,512]{2,1,0:T(8,128)(2,1)S(1)} %get-tuple-element.81.x_ref, bf16[3,2,256,128]{3,2,1,0:T(8,128)(2,1)S(1)} %get-tuple-element.82.ct_ref, ...), custom_call_target="tpu_custom_call" | custom-call | flops 2000000000 | bytes 4194304 | tf_op jit(solution)/shard_map/backward_full/pallas_call | solution.py:329
  44.8 1.1 %collective-permute-done.8.rest_2_ = bf16[256,128]{1,0:T(8,128)(2,1)S(1)} collective-permute-done((bf16[256,128]{1,0:T(8,128)(2,1)S(1)}, bf16[256,128]{1,0:T(8,128)(2,1)S(1)}, u32[]{:S(2)}, u32[]{:S(2)}) %collective-permute-start.8) | collective-permute-done | bytes 65568 | tf_op jit(solution)/shard_map/ppermute | solution.py:421
  46.0 0.5 collective-permute-start.15
  46.5 1.8 %backward_full.4 = (bf16[2,256,128]{2,1,0:T(8,128)(2,1)S(1)}, bf16[2,256,128]{2,1,0:T(8,128)(2,1)S(1)}, f32[128,128]{1,0:T(8,128)S(1)}, f32[128,128]{1,0:T(8,128)S(1)}, f32[216,128]{1,0:T(8,128)S(1)}) custom-call(bf16[3,128,512]{2,1,0:T(8,128)(2,1)S(1)} %get-tuple-element.81.x_ref, bf16[3,2,256,128]{3,2,1,0:T(8,128)(2,1)S(1)} %get-tuple-element.82.ct_ref, ...), custom_call_target="tpu_custom_call" | custom-call | flops 2000000000 | bytes 4194304 | tf_op jit(solution)/shard_map/backward_full/pallas_call | solution.py:329
  48.3 1.8 %backward_full.5 = (bf16[2,256,128]{2,1,0:T(8,128)(2,1)S(1)}, bf16[2,256,128]{2,1,0:T(8,128)(2,1)S(1)}, f32[128,128]{1,0:T(8,128)S(1)}, f32[128,128]{1,0:T(8,128)S(1)}, f32[216,128]{1,0:T(8,128)S(1)}) custom-call(bf16[3,128,512]{2,1,0:T(8,128)(2,1)S(1)} %get-tuple-element.81.x_ref, bf16[3,2,256,128]{3,2,1,0:T(8,128)(2,1)S(1)} %get-tuple-element.82.ct_ref, ...), custom_call_target="tpu_custom_call" | custom-call | flops 2000000000 | bytes 4194304 | tf_op jit(solution)/shard_map/backward_full/pallas_call | solution.py:329
  50.2 0.3 collective-permute-start.21
  50.6 0.5 collective-permute-start.24
  51.1 4.4 %collective-permute-done.21 = bf16[472,128]{1,0:T(8,128)(2,1)S(1)} collective-permute-done((bf16[472,128]{1,0:T(8,128)(2,1)S(1)}, bf16[472,128]{1,0:T(8,128)(2,1)S(1)}, u32[]{:S(2)}, u32[]{:S(2)}) %collective-permute-start.21) | collective-permute-done | bytes 120864 | tf_op jit(solution)/shard_map/ppermute | solution.py:502
  55.5 3.0 %collective-permute-start.22 = (bf16[472,128]{1,0:T(8,128)(2,1)S(1)}, bf16[472,128]{1,0:T(8,128)(2,1)S(1)}, u32[]{:S(2)}, u32[]{:S(2)}) collective-permute-start(bf16[472,128]{1,0:T(8,128)(2,1)S(1)} %fusion.refs_0_), channel_id=1, source_target_pairs={{0,12},{4,8},{8,4},{12,0},{1,13},{5,9},{9,5},{13,1},{2,14},{6,10},... | collective-permute-start | bytes 362504 | tf_op jit(solution)/shard_map/ppermute | solution.py:503
  58.5 0.9 %emit.1 = bf16[3,2,256,128]{3,2,1,0:T(8,128)(2,1)} custom-call(bf16[2,256,128]{2,1,0:T(8,128)(2,1)S(1)} %get-tuple-element.145.refs_0_, bf16[2,256,128]{2,1,0:T(8,128)(2,1)S(1)} %get-tuple-element.128.refs_1_, bf16[2,256,128]{2,1,0:T(8,128)(2,1)S(1)} %collective-permute-done.23.refs_2_, bf16[2,256,128]{2,1,0:T(8,128)(2,1)S(1)} %get-tuple-element.146.refs_3_, ...), custom_call_target="tpu_custom_call" | custom-call | flops 2000000000 | bytes 4194304 | tf_op jit(solution)/shard_map/emit/pallas_call | solution.py:329
  59.4 2.9 %collective-permute-done.22.refs_1_ = bf16[472,128]{1,0:T(8,128)(2,1)S(1)} collective-permute-done((bf16[472,128]{1,0:T(8,128)(2,1)S(1)}, bf16[472,128]{1,0:T(8,128)(2,1)S(1)}, u32[]{:S(2)}, u32[]{:S(2)}) %collective-permute-start.22) | collective-permute-done | bytes 120864 | tf_op jit(solution)/shard_map/ppermute | solution.py:503
  62.3 1.0 %finish.1 = (f32[128,128]{1,0:T(8,128)}, f32[128,128]{1,0:T(8,128)}, f32[16,8,8,27]{3,2,1,0:T(8,128)}) custom-call(bf16[472,128]{1,0:T(8,128)(2,1)S(1)} %fusion.refs_0_, bf16[472,128]{1,0:T(8,128)(2,1)S(1)} %collective-permute-done.22.refs_1_), custom_call_target="tpu_custom_call" | custom-call | flops 2000000000 | bytes 4194304 | tf_op jit(solution)/shard_map/finish/pallas_call | solution.py:329
  (44 shorter events, 0.2 us)
Async XLA Ops:
  0.6 7.1 %copy-start.2 = (bf16[1,27,16,8,8]{1,4,3,2,0:T(8,128)(2,1)S(1)}, bf16[1,27,16,8,8]{1,4,3,2,0:T(8,128)(2,1)}, u32[]{:S(2)}) copy-start(bf16[1,27,16,8,8]{1,4,3,2,0:T(8,128)(2,1)} %param.12) | copy-start | bytes 165892
  2.6 16.4 %collective-permute-start.1 = (bf16[1072,128]{1,0:T(8,128)(2,1)}, bf16[1072,128]{1,0:T(8,128)(2,1)S(1)}, u32[]{:S(2)}, u32[]{:S(2)}) collective-permute-start(bf16[1072,128]{1,0:T(8,128)(2,1)} %get-tuple-element.84), channel_id=1, source_target_pairs={{0,12},{1,5},{4,0},{5,9},{8,4},{9,13},{12,8},{13,1},{2,14},{3,7},{... | collective-permute-start | bytes 823304 | tf_op jit(solution)/shard_map/ppermute | solution.py:409
  7.7 11.3 %collective-permute-start.2 = (bf16[816,128]{1,0:T(8,128)(2,1)}, bf16[816,128]{1,0:T(8,128)(2,1)S(1)}, u32[]{:S(2)}, u32[]{:S(2)}) collective-permute-start(bf16[816,128]{1,0:T(8,128)(2,1)} %get-tuple-element.85), channel_id=1, source_target_pairs={{0,4},{1,13},{4,8},{5,1},{8,12},{9,5},{12,0},{13,9},{2,6},{3,15},{... | collective-permute-start | bytes 626696 | tf_op jit(solution)/shard_map/ppermute | solution.py:410
  7.7 1.0 %copy-start.6 = (f32[1,3,128]{2,0,1:T(1,128)S(1)}, f32[1,3,128]{2,0,1:T(1,128)}, u32[]{:S(2)}) copy-start(f32[1,3,128]{2,0,1:T(1,128)} %param.11) | copy-start | bytes 4612
  7.7 1.0 %copy-start = (bf16[1,3,2,16,16,128]{5,4,3,2,1,0:T(8,128)(2,1)S(1)}, bf16[1,3,2,16,16,128]{5,4,3,2,1,0:T(8,128)(2,1)}, u32[]{:S(2)}) copy-start(bf16[1,3,2,16,16,128]{5,4,3,2,1,0:T(8,128)(2,1)} %param.7) | copy-start | bytes 1179652
  7.7 1.1 %copy-start.1 = (bf16[3,2,16,16,128]{4,3,2,1,0:T(8,128)(2,1)S(1)}, bf16[3,2,16,16,128]{4,3,2,1,0:T(8,128)(2,1)}, u32[]{:S(2)}) copy-start(bf16[3,2,16,16,128]{4,3,2,1,0:T(8,128)(2,1)} %param.8) | copy-start | bytes 1179652
  7.7 1.1 %copy-start.3 = (bf16[1,128,128]{2,1,0:T(8,128)(2,1)S(1)}, bf16[1,128,128]{2,1,0:T(8,128)(2,1)}, u32[]{:S(2)}) copy-start(bf16[1,128,128]{2,1,0:T(8,128)(2,1)} %param.10) | copy-start | bytes 98308
  7.7 1.1 %copy-start.4 = (bf16[1,128,128]{2,1,0:T(8,128)(2,1)S(1)}, bf16[1,128,128]{2,1,0:T(8,128)(2,1)}, u32[]{:S(2)}) copy-start(bf16[1,128,128]{2,1,0:T(8,128)(2,1)} %param.13) | copy-start | bytes 98308
  7.7 1.1 %copy-start.5 = (bf16[3,2,16,128]{3,2,1,0:T(8,128)(2,1)S(1)}, bf16[3,2,16,128]{3,2,1,0:T(8,128)(2,1)}, u32[]{:S(2)}) copy-start(bf16[3,2,16,128]{3,2,1,0:T(8,128)(2,1)} %get-tuple-element.80.lab_ref) | copy-start | bytes 73732
  19.0 2.3 %collective-permute-start.3 = (bf16[1072,128]{1,0:T(8,128)(2,1)S(1)}, bf16[1072,128]{1,0:T(8,128)(2,1)S(1)}, u32[]{:S(2)}, u32[]{:S(2)}) collective-permute-start(bf16[1072,128]{1,0:T(8,128)(2,1)S(1)} %collective-permute-done.1.a_ref.cta_ref), channel_id=1, source_target_pairs={{0,1},{1,0},{2,3},{3,2},{4,5},{5,4},{6,7},{7,6},{8,9},{9,8},{10,11... | collective-permute-start | bytes 823304 | tf_op jit(solution)/shard_map/ppermute | solution.py:370
  19.0 2.3 %collective-permute-start.4 = (bf16[816,128]{1,0:T(8,128)(2,1)S(1)}, bf16[816,128]{1,0:T(8,128)(2,1)S(1)}, u32[]{:S(2)}, u32[]{:S(2)}) collective-permute-start(bf16[816,128]{1,0:T(8,128)(2,1)S(1)} %collective-permute-done.2.b_ref), channel_id=1, source_target_pairs={{0,1},{1,0},{2,3},{3,2},{4,5},{5,4},{6,7},{7,6},{8,9},{9,8},{10,11... | collective-permute-start | bytes 626696 | tf_op jit(solution)/shard_map/ppermute | solution.py:370
  19.5 8.2 %collective-permute-start = (bf16[512,128]{1,0:T(8,128)(2,1)S(1)}, bf16[512,128]{1,0:T(8,128)(2,1)S(1)}, u32[]{:S(2)}, u32[]{:S(2)}) collective-permute-start(bf16[512,128]{1,0:T(8,128)(2,1)S(1)} %get-tuple-element.83), channel_id=1, source_target_pairs={{0,12},{1,5},{4,0},{5,9},{8,4},{9,13},{12,8},{13,1},{2,14},{3,7},{... | collective-permute-start | bytes 393224 | tf_op jit(solution)/shard_map/ppermute | solution.py:413
  24.2 4.1 %collective-permute-start.9 = (bf16[256,128]{1,0:T(8,128)(2,1)S(1)}, bf16[256,128]{1,0:T(8,128)(2,1)S(1)}, u32[]{:S(2)}, u32[]{:S(2)}) collective-permute-start(bf16[256,128]{1,0:T(8,128)(2,1)S(1)} %get-tuple-element.109), channel_id=1, source_target_pairs={{0,1},{1,0},{2,3},{3,2},{4,5},{5,4},{6,7},{7,6},{8,9},{9,8},{10,11... | collective-permute-start | bytes 196616 | tf_op jit(solution)/shard_map/ppermute | solution.py:370
  27.7 3.5 %collective-permute-start.5 = (bf16[512,128]{1,0:T(8,128)(2,1)S(1)}, bf16[512,128]{1,0:T(8,128)(2,1)S(1)}, u32[]{:S(2)}, u32[]{:S(2)}) collective-permute-start(bf16[512,128]{1,0:T(8,128)(2,1)S(1)} %collective-permute-done.cta_ref), channel_id=1, source_target_pairs={{0,1},{1,0},{2,3},{3,2},{4,5},{5,4},{6,7},{7,6},{8,9},{9,8},{10,11... | collective-permute-start | bytes 393224 | tf_op jit(solution)/shard_map/ppermute | solution.py:370
  28.3 6.0 %collective-permute-start.10 = (bf16[256,128]{1,0:T(8,128)(2,1)S(1)}, bf16[256,128]{1,0:T(8,128)(2,1)S(1)}, u32[]{:S(2)}, u32[]{:S(2)}) collective-permute-start(bf16[256,128]{1,0:T(8,128)(2,1)S(1)} %add_convert_fusion.1), channel_id=1, source_target_pairs={{0,2},{2,0},{1,3},{3,1},{4,6},{6,4},{5,7},{7,5},{8,10},{10,8},{9,1... | collective-permute-start | bytes 196616 | tf_op jit(solution)/shard_map/ppermute | solution.py:420
  29.8 5.9 %collective-permute-start.11 = (bf16[256,128]{1,0:T(8,128)(2,1)S(1)}, bf16[256,128]{1,0:T(8,128)(2,1)S(1)}, u32[]{:S(2)}, u32[]{:S(2)}) collective-permute-start(bf16[256,128]{1,0:T(8,128)(2,1)S(1)} %add_convert_fusion.1), channel_id=1, source_target_pairs={{0,14},{2,12},{1,7},{3,5},{4,2},{6,0},{5,11},{7,9},{8,6},{10,4},{9... | collective-permute-start | bytes 196616 | tf_op jit(solution)/shard_map/ppermute | solution.py:421
  32.4 3.8 %collective-permute-start.16 = (bf16[256,128]{1,0:T(8,128)(2,1)S(1)}, bf16[256,128]{1,0:T(8,128)(2,1)S(1)}, u32[]{:S(2)}, u32[]{:S(2)}) collective-permute-start(bf16[256,128]{1,0:T(8,128)(2,1)S(1)} %get-tuple-element.119), channel_id=1, source_target_pairs={{0,1},{1,0},{2,3},{3,2},{4,5},{5,4},{6,7},{7,6},{8,9},{9,8},{10,11... | collective-permute-start | bytes 196616 | tf_op jit(solution)/shard_map/ppermute | solution.py:370
  33.7 6.5 %collective-permute-start.6 = (bf16[256,128]{1,0:T(8,128)(2,1)S(1)}, bf16[256,128]{1,0:T(8,128)(2,1)S(1)}, u32[]{:S(2)}, u32[]{:S(2)}) collective-permute-start(bf16[256,128]{1,0:T(8,128)(2,1)S(1)} %get-tuple-element.122), channel_id=1, source_target_pairs={{0,1},{1,0},{2,3},{3,2},{4,5},{5,4},{6,7},{7,6},{8,9},{9,8},{10,11... | collective-permute-start | bytes 196616 | tf_op jit(solution)/shard_map/ppermute | solution.py:370
  35.7 5.1 %collective-permute-start.12 = (bf16[256,128]{1,0:T(8,128)(2,1)S(1)}, bf16[256,128]{1,0:T(8,128)(2,1)S(1)}, u32[]{:S(2)}, u32[]{:S(2)}) collective-permute-start(bf16[256,128]{1,0:T(8,128)(2,1)S(1)} %collective-permute-done.10.rest_0_), channel_id=1, source_target_pairs={{0,1},{1,0},{2,3},{3,2},{4,5},{5,4},{6,7},{7,6},{8,9},{9,8},{10,11... | collective-permute-start | bytes 196616 | tf_op jit(solution)/shard_map/ppermute | solution.py:370
  35.7 7.3 %collective-permute-start.13 = (bf16[256,128]{1,0:T(8,128)(2,1)S(1)}, bf16[256,128]{1,0:T(8,128)(2,1)S(1)}, u32[]{:S(2)}, u32[]{:S(2)}) collective-permute-start(bf16[256,128]{1,0:T(8,128)(2,1)S(1)} %collective-permute-done.11.rest_2_), channel_id=1, source_target_pairs={{0,1},{1,0},{2,3},{3,2},{4,5},{5,4},{6,7},{7,6},{8,9},{9,8},{10,11... | collective-permute-start | bytes 196616 | tf_op jit(solution)/shard_map/ppermute | solution.py:370
  36.2 4.8 %collective-permute-start.17 = (bf16[256,128]{1,0:T(8,128)(2,1)S(1)}, bf16[256,128]{1,0:T(8,128)(2,1)S(1)}, u32[]{:S(2)}, u32[]{:S(2)}) collective-permute-start(bf16[256,128]{1,0:T(8,128)(2,1)S(1)} %add_convert_fusion), channel_id=1, source_target_pairs={{0,2},{2,0},{1,3},{3,1},{4,6},{6,4},{5,7},{7,5},{8,10},{10,8},{9,1... | collective-permute-start | bytes 196616 | tf_op jit(solution)/shard_map/ppermute | solution.py:420
  36.8 5.3 %collective-permute-start.19 = (bf16[256,128]{1,0:T(8,128)(2,1)S(1)}, bf16[256,128]{1,0:T(8,128)(2,1)S(1)}, u32[]{:S(2)}, u32[]{:S(2)}) collective-permute-start(bf16[256,128]{1,0:T(8,128)(2,1)S(1)} %add_convert_fusion), channel_id=1, source_target_pairs={{0,14},{2,12},{1,7},{3,5},{4,2},{6,0},{5,11},{7,9},{8,6},{10,4},{9... | collective-permute-start | bytes 196616 | tf_op jit(solution)/shard_map/ppermute | solution.py:421
  40.2 4.6 %collective-permute-start.7 = (bf16[256,128]{1,0:T(8,128)(2,1)S(1)}, bf16[256,128]{1,0:T(8,128)(2,1)S(1)}, u32[]{:S(2)}, u32[]{:S(2)}) collective-permute-start(bf16[256,128]{1,0:T(8,128)(2,1)S(1)} %add_convert_fusion.2), channel_id=1, source_target_pairs={{0,2},{2,0},{1,3},{3,1},{4,6},{6,4},{5,7},{7,5},{8,10},{10,8},{9,1... | collective-permute-start | bytes 196616 | tf_op jit(solution)/shard_map/ppermute | solution.py:420
  40.8 5.2 %collective-permute-start.8 = (bf16[256,128]{1,0:T(8,128)(2,1)S(1)}, bf16[256,128]{1,0:T(8,128)(2,1)S(1)}, u32[]{:S(2)}, u32[]{:S(2)}) collective-permute-start(bf16[256,128]{1,0:T(8,128)(2,1)S(1)} %add_convert_fusion.2), channel_id=1, source_target_pairs={{0,14},{2,12},{1,7},{3,5},{4,2},{6,0},{5,11},{7,9},{8,6},{10,4},{9... | collective-permute-start | bytes 196616 | tf_op jit(solution)/shard_map/ppermute | solution.py:421
  41.0 5.5 %collective-permute-start.18 = (bf16[256,128]{1,0:T(8,128)(2,1)S(1)}, bf16[256,128]{1,0:T(8,128)(2,1)S(1)}, u32[]{:S(2)}, u32[]{:S(2)}) collective-permute-start(bf16[256,128]{1,0:T(8,128)(2,1)S(1)} %collective-permute-done.17.rest_0_), channel_id=1, source_target_pairs={{0,1},{1,0},{2,3},{3,2},{4,5},{5,4},{6,7},{7,6},{8,9},{9,8},{10,11... | collective-permute-start | bytes 196616 | tf_op jit(solution)/shard_map/ppermute | solution.py:370
  42.1 4.4 %collective-permute-start.20 = (bf16[256,128]{1,0:T(8,128)(2,1)S(1)}, bf16[256,128]{1,0:T(8,128)(2,1)S(1)}, u32[]{:S(2)}, u32[]{:S(2)}) collective-permute-start(bf16[256,128]{1,0:T(8,128)(2,1)S(1)} %collective-permute-done.19.rest_2_), channel_id=1, source_target_pairs={{0,1},{1,0},{2,3},{3,2},{4,5},{5,4},{6,7},{7,6},{8,9},{9,8},{10,11... | collective-permute-start | bytes 196616 | tf_op jit(solution)/shard_map/ppermute | solution.py:370
  46.0 2.4 %collective-permute-start.14 = (bf16[256,128]{1,0:T(8,128)(2,1)S(1)}, bf16[256,128]{1,0:T(8,128)(2,1)S(1)}, u32[]{:S(2)}, u32[]{:S(2)}) collective-permute-start(bf16[256,128]{1,0:T(8,128)(2,1)S(1)} %collective-permute-done.7.rest_0_), channel_id=1, source_target_pairs={{0,1},{1,0},{2,3},{3,2},{4,5},{5,4},{6,7},{7,6},{8,9},{9,8},{10,11... | collective-permute-start | bytes 196616 | tf_op jit(solution)/shard_map/ppermute | solution.py:370
  46.0 2.4 %collective-permute-start.15 = (bf16[256,128]{1,0:T(8,128)(2,1)S(1)}, bf16[256,128]{1,0:T(8,128)(2,1)S(1)}, u32[]{:S(2)}, u32[]{:S(2)}) collective-permute-start(bf16[256,128]{1,0:T(8,128)(2,1)S(1)} %collective-permute-done.8.rest_2_), channel_id=1, source_target_pairs={{0,1},{1,0},{2,3},{3,2},{4,5},{5,4},{6,7},{7,6},{8,9},{9,8},{10,11... | collective-permute-start | bytes 196616 | tf_op jit(solution)/shard_map/ppermute | solution.py:370
  50.2 5.3 %collective-permute-start.21 = (bf16[472,128]{1,0:T(8,128)(2,1)S(1)}, bf16[472,128]{1,0:T(8,128)(2,1)S(1)}, u32[]{:S(2)}, u32[]{:S(2)}) collective-permute-start(bf16[472,128]{1,0:T(8,128)(2,1)S(1)} %pad_maximum_fusion), channel_id=1, source_target_pairs={{0,4},{4,0},{8,12},{12,8},{1,5},{5,1},{9,13},{13,9},{2,6},{6,2},{1... | collective-permute-start | bytes 362504 | tf_op jit(solution)/shard_map/ppermute | solution.py:502
  50.6 7.9 %collective-permute-start.23 = (bf16[2,256,128]{2,1,0:T(8,128)(2,1)S(1)}, bf16[2,256,128]{2,1,0:T(8,128)(2,1)S(1)}, u32[]{:S(2)}, u32[]{:S(2)}) collective-permute-start(bf16[2,256,128]{2,1,0:T(8,128)(2,1)S(1)} %get-tuple-element.128.refs_1_), channel_id=1, source_target_pairs={{0,1},{1,0},{2,3},{3,2},{4,5},{5,4},{6,7},{7,6},{8,9},{9,8},{10,11... | collective-permute-start | bytes 393224 | tf_op jit(solution)/shard_map/ppermute | solution.py:370
  50.6 7.9 %collective-permute-start.24 = (bf16[2,256,128]{2,1,0:T(8,128)(2,1)S(1)}, bf16[2,256,128]{2,1,0:T(8,128)(2,1)S(1)}, u32[]{:S(2)}, u32[]{:S(2)}) collective-permute-start(bf16[2,256,128]{2,1,0:T(8,128)(2,1)S(1)} %get-tuple-element.147.refs_4_), channel_id=1, source_target_pairs={{0,1},{1,0},{2,3},{3,2},{4,5},{5,4},{6,7},{7,6},{8,9},{9,8},{10,11... | collective-permute-start | bytes 393224 | tf_op jit(solution)/shard_map/ppermute | solution.py:370
  51.1 7.4 %collective-permute-start.25 = (bf16[2,256,128]{2,1,0:T(8,128)(2,1)S(1)}, bf16[2,256,128]{2,1,0:T(8,128)(2,1)S(1)}, u32[]{:S(2)}, u32[]{:S(2)}) collective-permute-start(bf16[2,256,128]{2,1,0:T(8,128)(2,1)S(1)} %get-tuple-element.149.refs_7_), channel_id=1, source_target_pairs={{0,1},{1,0},{2,3},{3,2},{4,5},{5,4},{6,7},{7,6},{8,9},{9,8},{10,11... | collective-permute-start | bytes 393224 | tf_op jit(solution)/shard_map/ppermute | solution.py:370
  55.5 6.8 %collective-permute-start.22 = (bf16[472,128]{1,0:T(8,128)(2,1)S(1)}, bf16[472,128]{1,0:T(8,128)(2,1)S(1)}, u32[]{:S(2)}, u32[]{:S(2)}) collective-permute-start(bf16[472,128]{1,0:T(8,128)(2,1)S(1)} %fusion.refs_0_), channel_id=1, source_target_pairs={{0,12},{4,8},{8,4},{12,0},{1,13},{5,9},{9,5},{13,1},{2,14},{6,10},... | collective-permute-start | bytes 362504 | tf_op jit(solution)/shard_map/ppermute | solution.py:503

commit v7 on v6

--- a/solution.py
+++ b/solution.py
@@ -312,7 +312,7 @@
 
 
 def SENDS(micro):
-    return [[m] for m in range(micro)]
+    return [[0], list(range(1, micro))] if micro > 1 else [[0]]
 
 
 def sds(shape, dtype):
@@ -468,10 +468,12 @@
             sent.append(send_on(joined([previous])))
     (edge,) = after((edge,), sconv[-1])
     edges += [(edge, swap(edge))] * (micro - 1)
+    waiting = []
     for m in range(1, micro):
         (sconv[m],) = after((sconv[m],), previous[1])
         previous = back_pass("first", m, ())
-        sent.append(send_on(joined([previous])))
+        waiting.append(previous)
+    sent.append(send_on(joined(waiting)))
     sent[0] = after(sent[0], previous[1])
     ups = [shared(*pair) for pair in sent]
 

time: 63.5 us -> 63.1 us (level)
  starting transfers between devices: 21.7 us -> 20.2 us
  waiting for transfers between devices: 19.5 us -> 20.6 us
    ppermute x3 -> x2, waiting for transfers between devices: 3.68 us -> 1.42 us  [send_on(): dg = lax.ppermute(out, ('space', 'section', 'chan'), route_d)]
    ppermute x3 -> x2, waiting for transfers between devices: 0.18 us -> 2.14 us  [send_on(): st = lax.ppermute(out, 'section', route_s)]
    ppermute x15 -> x13, waiting for transfers between devices: 0.04 us -> 1.05 us  [swap(): return lax.ppermute(v, 'chan', [(0, 1), (1, 0)])]
    ppermute x15 -> x13, starting transfers between devices: 4.12 us -> 3.45 us  [swap(): return lax.ppermute(v, 'chan', [(0, 1), (1, 0)])]
    ppermute x3 -> x2, starting transfers between devices: 2.76 us -> 2.16 us  [send_on(): st = lax.ppermute(out, 'section', route_s)]
    ppermute x3 -> x2, starting transfers between devices: 4.68 us -> 4.67 us  [send_on(): dg = lax.ppermute(out, ('space', 'section', 'chan'), route_d)]
  transfers between devices with their start and end apart: 26 -> 22, of which waited for: 7 -> 7; matrix products, arithmetic and copies ran while one was open for 0% -> 0% of each run, Pallas kernels for 25% -> 23%
where the time goes in v7:
time: 63.1 us; the launch traced here: 63 us
  Pallas kernels  20.9 us (33%)
  waiting for transfers between devices  20.6 us (33%)
  starting transfers between devices  20.2 us (32%)
  between operations  0.91 us (1%)
    pallas_call x14, Pallas kernels, call(): pl.pallas_call(kernel, in_specs=[vmem] * len(args) if in_specs is None el...  20.9 us
    ppermute x1, waiting for transfers between devices, on_device(): b = lax.ppermute(packed_b, ('space', 'chan'), route_b)  8.32 us
    ppermute x1, starting transfers between devices, on_device(): a = lax.ppermute(packed_a, ('space', 'chan'), route_a)  5.1 us
    ppermute x2, starting transfers between devices, send_on(): dg = lax.ppermute(out, ('space', 'section', 'chan'), route_d)  4.67 us
    ppermute x1, waiting for transfers between devices, on_device(): grads = grads + lax.ppermute(grads, 'space', near)  4.59 us
    ppermute x13, starting transfers between devices, swap(): return lax.ppermute(v, 'chan', [(0, 1), (1, 0)])  3.45 us
    ppermute x1, waiting for transfers between devices, on_device(): copies = [grads, lax.ppermute(grads, 'space', far)]  3.1 us
    ppermute x1, starting transfers between devices, on_device(): copies = [grads, lax.ppermute(grads, 'space', far)]  2.78 us
  transfers between devices with their start and end apart: 22, of which 7 were waited for; matrix products, arithmetic and copies ran while one was open for 0% of the time, Pallas kernels for 23%

profile of v7, /device:TPU:0, one launch (start us, length us, event | category | flops | bytes accessed | tf_op | source)
XLA Modules:
  0.0 63.0 jit_solution(4809321282893816338)
XLA Ops:
  0.6 1.9 %pack.1 = (bf16[1072,128]{1,0:T(8,128)(2,1)}, bf16[816,128]{1,0:T(8,128)(2,1)}, bf16[3,2,16,128]{3,2,1,0:T(8,128)(2,1)}) custom-call(bf16[3,2,256,128]{3,2,1,0:T(8,128)(2,1)} %bitcast.16, bf16[3,2,256,128]{3,2,1,0:T(8,128)(2,1)} %bitcast.18, s32[3,2,16,16]{3,2,1,0:T(8,128)} %tag_ref.1), custom_call_target="tpu_custom_call" | custom-call | flops 2000000000 | bytes 4194304 | tf_op jit(solution)/shard_map/pack/pallas_call | solution.py:329
  2.6 5.1 %collective-permute-start.1 = (bf16[1072,128]{1,0:T(8,128)(2,1)}, bf16[1072,128]{1,0:T(8,128)(2,1)S(1)}, u32[]{:S(2)}, u32[]{:S(2)}) collective-permute-start(bf16[1072,128]{1,0:T(8,128)(2,1)} %get-tuple-element.84), channel_id=1, source_target_pairs={{0,12},{1,5},{4,0},{5,9},{8,4},{9,13},{12,8},{13,1},{2,14},{3,7},{... | collective-permute-start | bytes 823304 | tf_op jit(solution)/shard_map/ppermute | solution.py:409
  7.7 0.0 copy-start.1
  7.7 0.0 copy-start.3
  7.7 0.0 copy-start.4
  7.7 0.0 copy-start.5
  7.8 0.9 %weights.1 = (bf16[4608,256]{1,0:T(8,128)(2,1)S(1)}, bf16[4608,256]{1,0:T(8,128)(2,1)S(1)}) custom-call(bf16[16,8,8,27]{3,2,1,0:T(8,128)(2,1)S(1)} %bitcast.20), custom_call_target="tpu_custom_call" | custom-call | flops 2000000000 | bytes 4194304 | tf_op jit(solution)/shard_map/weights/pallas_call | solution.py:329
  8.7 0.1 copy-done.1
  8.8 1.8 %own.1 = (bf16[2,288,384]{2,1,0:T(8,128)(2,1)S(1)}, bf16[128,512]{1,0:T(8,128)(2,1)S(1)}, f32[2,256,128]{2,1,0:T(8,128)S(1)}, bf16[2,288,384]{2,1,0:T(8,128)(2,1...) custom-call(bf16[3,2,256,128]{3,2,1,0:T(8,128)(2,1)S(1)} %bitcast.17, ...), custom_call_target="tpu_custom_call" | custom-call | flops 2000000000 | bytes 4194304 | tf_op jit(solution)/shard_map/own/pallas_call | solution.py:329
  10.6 8.3 %collective-permute-done.2.b_ref = bf16[816,128]{1,0:T(8,128)(2,1)S(1)} collective-permute-done((bf16[816,128]{1,0:T(8,128)(2,1)}, bf16[816,128]{1,0:T(8,128)(2,1)S(1)}, u32[]{:S(2)}, u32[]{:S(2)}) %collective-permute-start.2) | collective-permute-done | bytes 208928 | tf_op jit(solution)/shard_map/ppermute | solution.py:410
  18.9 0.0 collective-permute-done.1.a_ref.cta_ref
  19.0 0.0 collective-permute-start.3
  19.0 0.5 collective-permute-start.4
  19.5 1.7 %collective-permute-start = (bf16[512,128]{1,0:T(8,128)(2,1)S(1)}, bf16[512,128]{1,0:T(8,128)(2,1)S(1)}, u32[]{:S(2)}, u32[]{:S(2)}) collective-permute-start(bf16[512,128]{1,0:T(8,128)(2,1)S(1)} %get-tuple-element.83), channel_id=1, source_target_pairs={{0,12},{1,5},{4,0},{5,9},{8,4},{9,13},{12,8},{13,1},{2,14},{3,7},{... | collective-permute-start | bytes 393224 | tf_op jit(solution)/shard_map/ppermute | solution.py:413
  21.2 1.7 %forward.3 = (f32[4,256,128]{2,1,0:T(8,128)S(1)}, bf16[128,512]{1,0:T(8,128)(2,1)S(1)}) custom-call(bf16[2,288,384]{2,1,0:T(8,128)(2,1)S(1)} %get-tuple-element.102.own_ref, bf16[1072,128]{1,0:T(8,128)(2,1)S(1)} %collective-permute-done.1.a_ref.cta_ref, bf16[816,128]{1,0:T(8,128)(2,1)S(1)} %collective-permute-done.2.b_ref, ...), custom_call_target="tpu_custom_call" | custom-call | flops 2000000000 | bytes 4194304 | tf_op jit(solution)/shard_map/forward/pallas_call | solution.py:329
  22.9 1.2 %backward_first.3 = (f32[256,128]{1,0:T(8,128)S(1)}, bf16[256,128]{1,0:T(8,128)(2,1)S(1)}) custom-call(bf16[3,128,512]{2,1,0:T(8,128)(2,1)S(1)} %get-tuple-element.81.x_ref, bf16[3,2,256,128]{3,2,1,0:T(8,128)(2,1)S(1)} %get-tuple-element.82.ct_ref, bf16[1072,128]{1,0:T(8,128)(2,1)S(1)} %collective-permute-done.1.a_ref.cta_ref, ...), custom_call_target="tpu_custom_call" | custom-call | flops 2000000000 | bytes 4194304 | tf_op jit(solution)/shard_map/backward_first/pallas_call | solution.py:329
  24.2 0.1 collective-permute-start.10
  24.2 1.7 %forward.4 = (f32[4,256,128]{2,1,0:T(8,128)S(1)}, bf16[128,512]{1,0:T(8,128)(2,1)S(1)}) custom-call(bf16[2,288,384]{2,1,0:T(8,128)(2,1)S(1)} %get-tuple-element.111.own_ref, bf16[1072,128]{1,0:T(8,128)(2,1)S(1)} %collective-permute-done.1.a_ref.cta_ref, bf16[816,128]{1,0:T(8,128)(2,1)S(1)} %collective-permute-done.2.b_ref, ...), custom_call_target="tpu_custom_call" | custom-call | flops 2000000000 | bytes 4194304 | tf_op jit(solution)/shard_map/forward/pallas_call | solution.py:329
  25.9 1.7 %forward.5 = (f32[4,256,128]{2,1,0:T(8,128)S(1)}, bf16[128,512]{1,0:T(8,128)(2,1)S(1)}) custom-call(bf16[2,288,384]{2,1,0:T(8,128)(2,1)S(1)} %get-tuple-element.97.own_ref, bf16[1072,128]{1,0:T(8,128)(2,1)S(1)} %collective-permute-done.1.a_ref.cta_ref, bf16[816,128]{1,0:T(8,128)(2,1)S(1)} %collective-permute-done.2.b_ref, ...), custom_call_target="tpu_custom_call" | custom-call | flops 2000000000 | bytes 4194304 | tf_op jit(solution)/shard_map/forward/pallas_call | solution.py:329
  27.7 0.0 collective-permute-done.cta_ref
  27.7 0.6 collective-permute-start.5
  28.3 1.6 %collective-permute-start.11 = (bf16[256,128]{1,0:T(8,128)(2,1)S(1)}, bf16[256,128]{1,0:T(8,128)(2,1)S(1)}, u32[]{:S(2)}, u32[]{:S(2)}) collective-permute-start(bf16[256,128]{1,0:T(8,128)(2,1)S(1)} %add_convert_fusion), channel_id=1, source_target_pairs={{0,2},{2,0},{1,3},{3,1},{4,6},{6,4},{5,7},{7,5},{8,10},{10,8},{9,1... | collective-permute-start | bytes 196616 | tf_op jit(solution)/shard_map/ppermute | solution.py:420
  29.8 1.3 %collective-permute-start.12 = (bf16[256,128]{1,0:T(8,128)(2,1)S(1)}, bf16[256,128]{1,0:T(8,128)(2,1)S(1)}, u32[]{:S(2)}, u32[]{:S(2)}) collective-permute-start(bf16[256,128]{1,0:T(8,128)(2,1)S(1)} %add_convert_fusion), channel_id=1, source_target_pairs={{0,14},{2,12},{1,7},{3,5},{4,2},{6,0},{5,11},{7,9},{8,6},{10,4},{9... | collective-permute-start | bytes 196616 | tf_op jit(solution)/shard_map/ppermute | solution.py:421
  31.1 1.2 %backward_first.4 = (f32[256,128]{1,0:T(8,128)S(1)}, bf16[256,128]{1,0:T(8,128)(2,1)S(1)}) custom-call(bf16[3,128,512]{2,1,0:T(8,128)(2,1)S(1)} %get-tuple-element.81.x_ref, bf16[3,2,256,128]{3,2,1,0:T(8,128)(2,1)S(1)} %get-tuple-element.82.ct_ref, bf16[512,128]{1,0:T(8,128)(2,1)S(1)} %collective-permute-done.cta_ref, ...), custom_call_target="tpu_custom_call" | custom-call | flops 2000000000 | bytes 4194304 | tf_op jit(solution)/shard_map/backward_first/pallas_call | solution.py:329
  32.4 0.1 collective-permute-start.6
  32.5 1.2 %backward_first.5 = (f32[256,128]{1,0:T(8,128)S(1)}, bf16[256,128]{1,0:T(8,128)(2,1)S(1)}) custom-call(bf16[3,128,512]{2,1,0:T(8,128)(2,1)S(1)} %get-tuple-element.81.x_ref, bf16[3,2,256,128]{3,2,1,0:T(8,128)(2,1)S(1)} %get-tuple-element.82.ct_ref, bf16[512,128]{1,0:T(8,128)(2,1)S(1)} %collective-permute-done.cta_ref, ...), custom_call_target="tpu_custom_call" | custom-call | flops 2000000000 | bytes 4194304 | tf_op jit(solution)/shard_map/backward_first/pallas_call | solution.py:329
  33.7 0.6 collective-permute-start.7
  34.3 1.4 %collective-permute-done.12.rest_2_ = bf16[256,128]{1,0:T(8,128)(2,1)S(1)} collective-permute-done((bf16[256,128]{1,0:T(8,128)(2,1)S(1)}, bf16[256,128]{1,0:T(8,128)(2,1)S(1)}, u32[]{:S(2)}, u32[]{:S(2)}) %collective-permute-start.12) | collective-permute-done | bytes 65568 | tf_op jit(solution)/shard_map/ppermute | solution.py:421
  35.7 0.5 collective-permute-start.14
  36.3 0.6 collective-permute-start.8
  36.9 3.4 %collective-permute-start.9 = (bf16[512,128]{1,0:T(8,128)(2,1)S(1)}, bf16[512,128]{1,0:T(8,128)(2,1)S(1)}, u32[]{:S(2)}, u32[]{:S(2)}) collective-permute-start(bf16[512,128]{1,0:T(8,128)(2,1)S(1)} %pad_maximum_fusion), channel_id=1, source_target_pairs={{0,14},{2,12},{1,7},{3,5},{4,2},{6,0},{5,11},{7,9},{8,6},{10,4},{9... | collective-permute-start | bytes 393224 | tf_op jit(solution)/shard_map/ppermute | solution.py:421
  40.3 1.8 %backward_full.3 = (bf16[2,256,128]{2,1,0:T(8,128)(2,1)S(1)}, bf16[2,256,128]{2,1,0:T(8,128)(2,1)S(1)}, f32[128,128]{1,0:T(8,128)S(1)}, f32[128,128]{1,0:T(8,128)S(1)}, f32[216,128]{1,0:T(8,128)S(1)}) custom-call(bf16[3,128,512]{2,1,0:T(8,128)(2,1)S(1)} %get-tuple-element.81.x_ref, bf16[3,2,256,128]{3,2,1,0:T(8,128)(2,1)S(1)} %get-tuple-element.82.ct_ref, ...), custom_call_target="tpu_custom_call" | custom-call | flops 2000000000 | bytes 4194304 | tf_op jit(solution)/shard_map/backward_full/pallas_call | solution.py:329
  42.1 2.1 %collective-permute-done.8.rest_0_ = bf16[512,128]{1,0:T(8,128)(2,1)S(1)} collective-permute-done((bf16[512,128]{1,0:T(8,128)(2,1)S(1)}, bf16[512,128]{1,0:T(8,128)(2,1)S(1)}, u32[]{:S(2)}, u32[]{:S(2)}) %collective-permute-start.8) | collective-permute-done | bytes 131104 | tf_op jit(solution)/shard_map/ppermute | solution.py:420
  44.3 0.1 collective-permute-start.15
  44.4 0.4 collective-permute-start.16
  44.8 0.8 %collective-permute-done.15.rest_1_ = bf16[512,128]{1,0:T(8,128)(2,1)S(1)} collective-permute-done((bf16[512,128]{1,0:T(8,128)(2,1)S(1)}, bf16[512,128]{1,0:T(8,128)(2,1)S(1)}, u32[]{:S(2)}, u32[]{:S(2)}) %collective-permute-start.15) | collective-permute-done | bytes 131104 | tf_op jit(solution)/shard_map/ppermute | solution.py:370
  45.6 0.2 collective-permute-done.16.rest_3_
  45.8 1.8 %backward_full.4 = (bf16[2,256,128]{2,1,0:T(8,128)(2,1)S(1)}, bf16[2,256,128]{2,1,0:T(8,128)(2,1)S(1)}, f32[128,128]{1,0:T(8,128)S(1)}, f32[128,128]{1,0:T(8,128)S(1)}, f32[216,128]{1,0:T(8,128)S(1)}) custom-call(bf16[3,128,512]{2,1,0:T(8,128)(2,1)S(1)} %get-tuple-element.81.x_ref, bf16[3,2,256,128]{3,2,1,0:T(8,128)(2,1)S(1)} %get-tuple-element.82.ct_ref, ...), custom_call_target="tpu_custom_call" | custom-call | flops 2000000000 | bytes 4194304 | tf_op jit(solution)/shard_map/backward_full/pallas_call | solution.py:329
  47.6 1.8 %backward_full.5 = (bf16[2,256,128]{2,1,0:T(8,128)(2,1)S(1)}, bf16[2,256,128]{2,1,0:T(8,128)(2,1)S(1)}, f32[128,128]{1,0:T(8,128)S(1)}, f32[128,128]{1,0:T(8,128)S(1)}, f32[216,128]{1,0:T(8,128)S(1)}) custom-call(bf16[3,128,512]{2,1,0:T(8,128)(2,1)S(1)} %get-tuple-element.81.x_ref, bf16[3,2,256,128]{3,2,1,0:T(8,128)(2,1)S(1)} %get-tuple-element.82.ct_ref, ...), custom_call_target="tpu_custom_call" | custom-call | flops 2000000000 | bytes 4194304 | tf_op jit(solution)/shard_map/backward_full/pallas_call | solution.py:329
  49.5 0.3 collective-permute-start.17
  49.9 0.1 collective-permute-start.19
  50.0 0.4 collective-permute-start.21
  50.4 0.1 collective-permute-start.20
  50.5 4.6 %collective-permute-done.17 = bf16[472,128]{1,0:T(8,128)(2,1)S(1)} collective-permute-done((bf16[472,128]{1,0:T(8,128)(2,1)S(1)}, bf16[472,128]{1,0:T(8,128)(2,1)S(1)}, u32[]{:S(2)}, u32[]{:S(2)}) %collective-permute-start.17) | collective-permute-done | bytes 120864 | tf_op jit(solution)/shard_map/ppermute | solution.py:504
  55.2 2.8 %collective-permute-start.18 = (bf16[472,128]{1,0:T(8,128)(2,1)S(1)}, bf16[472,128]{1,0:T(8,128)(2,1)S(1)}, u32[]{:S(2)}, u32[]{:S(2)}) collective-permute-start(bf16[472,128]{1,0:T(8,128)(2,1)S(1)} %fusion.refs_0_), channel_id=1, source_target_pairs={{0,12},{4,8},{8,4},{12,0},{1,13},{5,9},{9,5},{13,1},{2,14},{6,10},... | collective-permute-start | bytes 362504 | tf_op jit(solution)/shard_map/ppermute | solution.py:505
  58.0 0.9 %emit.1 = bf16[3,2,256,128]{3,2,1,0:T(8,128)(2,1)} custom-call(bf16[2,256,128]{2,1,0:T(8,128)(2,1)S(1)} %get-tuple-element.145.refs_0_, bf16[2,256,128]{2,1,0:T(8,128)(2,1)S(1)} %get-tuple-element.129.refs_1_, bf16[2,256,128]{2,1,0:T(8,128)(2,1)S(1)} %collective-permute-done.19.refs_2_, bf16[2,256,128]{2,1,0:T(8,128)(2,1)S(1)} %get-tuple-element.146.refs_3_, ...), custom_call_target="tpu_custom_call" | custom-call | flops 2000000000 | bytes 4194304 | tf_op jit(solution)/shard_map/emit/pallas_call | solution.py:329
  58.8 3.1 %collective-permute-done.18.refs_1_ = bf16[472,128]{1,0:T(8,128)(2,1)S(1)} collective-permute-done((bf16[472,128]{1,0:T(8,128)(2,1)S(1)}, bf16[472,128]{1,0:T(8,128)(2,1)S(1)}, u32[]{:S(2)}, u32[]{:S(2)}) %collective-permute-start.18) | collective-permute-done | bytes 120864 | tf_op jit(solution)/shard_map/ppermute | solution.py:505
  61.9 1.0 %finish.1 = (f32[128,128]{1,0:T(8,128)}, f32[128,128]{1,0:T(8,128)}, f32[16,8,8,27]{3,2,1,0:T(8,128)}) custom-call(bf16[472,128]{1,0:T(8,128)(2,1)S(1)} %fusion.refs_0_, bf16[472,128]{1,0:T(8,128)(2,1)S(1)} %collective-permute-done.18.refs_1_), custom_call_target="tpu_custom_call" | custom-call | flops 2000000000 | bytes 4194304 | tf_op jit(solution)/shard_map/finish/pallas_call | solution.py:329
  (37 shorter events, 0.2 us)
Async XLA Ops:
  0.6 7.1 %copy-start.2 = (bf16[1,27,16,8,8]{1,4,3,2,0:T(8,128)(2,1)S(1)}, bf16[1,27,16,8,8]{1,4,3,2,0:T(8,128)(2,1)}, u32[]{:S(2)}) copy-start(bf16[1,27,16,8,8]{1,4,3,2,0:T(8,128)(2,1)} %param.12) | copy-start | bytes 165892
  2.6 16.4 %collective-permute-start.1 = (bf16[1072,128]{1,0:T(8,128)(2,1)}, bf16[1072,128]{1,0:T(8,128)(2,1)S(1)}, u32[]{:S(2)}, u32[]{:S(2)}) collective-permute-start(bf16[1072,128]{1,0:T(8,128)(2,1)} %get-tuple-element.84), channel_id=1, source_target_pairs={{0,12},{1,5},{4,0},{5,9},{8,4},{9,13},{12,8},{13,1},{2,14},{3,7},{... | collective-permute-start | bytes 823304 | tf_op jit(solution)/shard_map/ppermute | solution.py:409
  7.7 11.3 %collective-permute-start.2 = (bf16[816,128]{1,0:T(8,128)(2,1)}, bf16[816,128]{1,0:T(8,128)(2,1)S(1)}, u32[]{:S(2)}, u32[]{:S(2)}) collective-permute-start(bf16[816,128]{1,0:T(8,128)(2,1)} %get-tuple-element.85), channel_id=1, source_target_pairs={{0,4},{1,13},{4,8},{5,1},{8,12},{9,5},{12,0},{13,9},{2,6},{3,15},{... | collective-permute-start | bytes 626696 | tf_op jit(solution)/shard_map/ppermute | solution.py:410
  7.7 1.0 %copy-start.6 = (f32[1,3,128]{2,0,1:T(1,128)S(1)}, f32[1,3,128]{2,0,1:T(1,128)}, u32[]{:S(2)}) copy-start(f32[1,3,128]{2,0,1:T(1,128)} %param.11) | copy-start | bytes 4612
  7.7 1.0 %copy-start = (bf16[1,3,2,16,16,128]{5,4,3,2,1,0:T(8,128)(2,1)S(1)}, bf16[1,3,2,16,16,128]{5,4,3,2,1,0:T(8,128)(2,1)}, u32[]{:S(2)}) copy-start(bf16[1,3,2,16,16,128]{5,4,3,2,1,0:T(8,128)(2,1)} %param.7) | copy-start | bytes 1179652
  7.7 1.1 %copy-start.1 = (bf16[3,2,16,16,128]{4,3,2,1,0:T(8,128)(2,1)S(1)}, bf16[3,2,16,16,128]{4,3,2,1,0:T(8,128)(2,1)}, u32[]{:S(2)}) copy-start(bf16[3,2,16,16,128]{4,3,2,1,0:T(8,128)(2,1)} %param.8) | copy-start | bytes 1179652
  7.7 1.1 %copy-start.3 = (bf16[1,128,128]{2,1,0:T(8,128)(2,1)S(1)}, bf16[1,128,128]{2,1,0:T(8,128)(2,1)}, u32[]{:S(2)}) copy-start(bf16[1,128,128]{2,1,0:T(8,128)(2,1)} %param.10) | copy-start | bytes 98308
  7.7 1.1 %copy-start.4 = (bf16[1,128,128]{2,1,0:T(8,128)(2,1)S(1)}, bf16[1,128,128]{2,1,0:T(8,128)(2,1)}, u32[]{:S(2)}) copy-start(bf16[1,128,128]{2,1,0:T(8,128)(2,1)} %param.13) | copy-start | bytes 98308
  7.7 1.1 %copy-start.5 = (bf16[3,2,16,128]{3,2,1,0:T(8,128)(2,1)S(1)}, bf16[3,2,16,128]{3,2,1,0:T(8,128)(2,1)}, u32[]{:S(2)}) copy-start(bf16[3,2,16,128]{3,2,1,0:T(8,128)(2,1)} %get-tuple-element.80.lab_ref) | copy-start | bytes 73732
  19.0 2.3 %collective-permute-start.3 = (bf16[1072,128]{1,0:T(8,128)(2,1)S(1)}, bf16[1072,128]{1,0:T(8,128)(2,1)S(1)}, u32[]{:S(2)}, u32[]{:S(2)}) collective-permute-start(bf16[1072,128]{1,0:T(8,128)(2,1)S(1)} %collective-permute-done.1.a_ref.cta_ref), channel_id=1, source_target_pairs={{0,1},{1,0},{2,3},{3,2},{4,5},{5,4},{6,7},{7,6},{8,9},{9,8},{10,11... | collective-permute-start | bytes 823304 | tf_op jit(solution)/shard_map/ppermute | solution.py:370
  19.0 2.3 %collective-permute-start.4 = (bf16[816,128]{1,0:T(8,128)(2,1)S(1)}, bf16[816,128]{1,0:T(8,128)(2,1)S(1)}, u32[]{:S(2)}, u32[]{:S(2)}) collective-permute-start(bf16[816,128]{1,0:T(8,128)(2,1)S(1)} %collective-permute-done.2.b_ref), channel_id=1, source_target_pairs={{0,1},{1,0},{2,3},{3,2},{4,5},{5,4},{6,7},{7,6},{8,9},{9,8},{10,11... | collective-permute-start | bytes 626696 | tf_op jit(solution)/shard_map/ppermute | solution.py:370
  19.5 8.2 %collective-permute-start = (bf16[512,128]{1,0:T(8,128)(2,1)S(1)}, bf16[512,128]{1,0:T(8,128)(2,1)S(1)}, u32[]{:S(2)}, u32[]{:S(2)}) collective-permute-start(bf16[512,128]{1,0:T(8,128)(2,1)S(1)} %get-tuple-element.83), channel_id=1, source_target_pairs={{0,12},{1,5},{4,0},{5,9},{8,4},{9,13},{12,8},{13,1},{2,14},{3,7},{... | collective-permute-start | bytes 393224 | tf_op jit(solution)/shard_map/ppermute | solution.py:413
  24.2 4.1 %collective-permute-start.10 = (bf16[256,128]{1,0:T(8,128)(2,1)S(1)}, bf16[256,128]{1,0:T(8,128)(2,1)S(1)}, u32[]{:S(2)}, u32[]{:S(2)}) collective-permute-start(bf16[256,128]{1,0:T(8,128)(2,1)S(1)} %get-tuple-element.109), channel_id=1, source_target_pairs={{0,1},{1,0},{2,3},{3,2},{4,5},{5,4},{6,7},{7,6},{8,9},{9,8},{10,11... | collective-permute-start | bytes 196616 | tf_op jit(solution)/shard_map/ppermute | solution.py:370
  27.7 3.5 %collective-permute-start.5 = (bf16[512,128]{1,0:T(8,128)(2,1)S(1)}, bf16[512,128]{1,0:T(8,128)(2,1)S(1)}, u32[]{:S(2)}, u32[]{:S(2)}) collective-permute-start(bf16[512,128]{1,0:T(8,128)(2,1)S(1)} %collective-permute-done.cta_ref), channel_id=1, source_target_pairs={{0,1},{1,0},{2,3},{3,2},{4,5},{5,4},{6,7},{7,6},{8,9},{9,8},{10,11... | collective-permute-start | bytes 393224 | tf_op jit(solution)/shard_map/ppermute | solution.py:370
  28.3 6.0 %collective-permute-start.11 = (bf16[256,128]{1,0:T(8,128)(2,1)S(1)}, bf16[256,128]{1,0:T(8,128)(2,1)S(1)}, u32[]{:S(2)}, u32[]{:S(2)}) collective-permute-start(bf16[256,128]{1,0:T(8,128)(2,1)S(1)} %add_convert_fusion), channel_id=1, source_target_pairs={{0,2},{2,0},{1,3},{3,1},{4,6},{6,4},{5,7},{7,5},{8,10},{10,8},{9,1... | collective-permute-start | bytes 196616 | tf_op jit(solution)/shard_map/ppermute | solution.py:420
  29.8 5.9 %collective-permute-start.12 = (bf16[256,128]{1,0:T(8,128)(2,1)S(1)}, bf16[256,128]{1,0:T(8,128)(2,1)S(1)}, u32[]{:S(2)}, u32[]{:S(2)}) collective-permute-start(bf16[256,128]{1,0:T(8,128)(2,1)S(1)} %add_convert_fusion), channel_id=1, source_target_pairs={{0,14},{2,12},{1,7},{3,5},{4,2},{6,0},{5,11},{7,9},{8,6},{10,4},{9... | collective-permute-start | bytes 196616 | tf_op jit(solution)/shard_map/ppermute | solution.py:421
  32.4 3.8 %collective-permute-start.6 = (bf16[256,128]{1,0:T(8,128)(2,1)S(1)}, bf16[256,128]{1,0:T(8,128)(2,1)S(1)}, u32[]{:S(2)}, u32[]{:S(2)}) collective-permute-start(bf16[256,128]{1,0:T(8,128)(2,1)S(1)} %get-tuple-element.119), channel_id=1, source_target_pairs={{0,1},{1,0},{2,3},{3,2},{4,5},{5,4},{6,7},{7,6},{8,9},{9,8},{10,11... | collective-permute-start | bytes 196616 | tf_op jit(solution)/shard_map/ppermute | solution.py:370
  33.7 2.5 %collective-permute-start.7 = (bf16[256,128]{1,0:T(8,128)(2,1)S(1)}, bf16[256,128]{1,0:T(8,128)(2,1)S(1)}, u32[]{:S(2)}, u32[]{:S(2)}) collective-permute-start(bf16[256,128]{1,0:T(8,128)(2,1)S(1)} %get-tuple-element.123), channel_id=1, source_target_pairs={{0,1},{1,0},{2,3},{3,2},{4,5},{5,4},{6,7},{7,6},{8,9},{9,8},{10,11... | collective-permute-start | bytes 196616 | tf_op jit(solution)/shard_map/ppermute | solution.py:370
  35.7 4.6 %collective-permute-start.13 = (bf16[256,128]{1,0:T(8,128)(2,1)S(1)}, bf16[256,128]{1,0:T(8,128)(2,1)S(1)}, u32[]{:S(2)}, u32[]{:S(2)}) collective-permute-start(bf16[256,128]{1,0:T(8,128)(2,1)S(1)} %collective-permute-done.11.rest_0_), channel_id=1, source_target_pairs={{0,1},{1,0},{2,3},{3,2},{4,5},{5,4},{6,7},{7,6},{8,9},{9,8},{10,11... | collective-permute-start | bytes 196616 | tf_op jit(solution)/shard_map/ppermute | solution.py:370
  35.7 4.6 %collective-permute-start.14 = (bf16[256,128]{1,0:T(8,128)(2,1)S(1)}, bf16[256,128]{1,0:T(8,128)(2,1)S(1)}, u32[]{:S(2)}, u32[]{:S(2)}) collective-permute-start(bf16[256,128]{1,0:T(8,128)(2,1)S(1)} %collective-permute-done.12.rest_2_), channel_id=1, source_target_pairs={{0,1},{1,0},{2,3},{3,2},{4,5},{5,4},{6,7},{7,6},{8,9},{9,8},{10,11... | collective-permute-start | bytes 196616 | tf_op jit(solution)/shard_map/ppermute | solution.py:370
  36.3 8.0 %collective-permute-start.8 = (bf16[512,128]{1,0:T(8,128)(2,1)S(1)}, bf16[512,128]{1,0:T(8,128)(2,1)S(1)}, u32[]{:S(2)}, u32[]{:S(2)}) collective-permute-start(bf16[512,128]{1,0:T(8,128)(2,1)S(1)} %pad_maximum_fusion), channel_id=1, source_target_pairs={{0,2},{2,0},{1,3},{3,1},{4,6},{6,4},{5,7},{7,5},{8,10},{10,8},{9,1... | collective-permute-start | bytes 393224 | tf_op jit(solution)/shard_map/ppermute | solution.py:420
  36.9 7.4 %collective-permute-start.9 = (bf16[512,128]{1,0:T(8,128)(2,1)S(1)}, bf16[512,128]{1,0:T(8,128)(2,1)S(1)}, u32[]{:S(2)}, u32[]{:S(2)}) collective-permute-start(bf16[512,128]{1,0:T(8,128)(2,1)S(1)} %pad_maximum_fusion), channel_id=1, source_target_pairs={{0,14},{2,12},{1,7},{3,5},{4,2},{6,0},{5,11},{7,9},{8,6},{10,4},{9... | collective-permute-start | bytes 393224 | tf_op jit(solution)/shard_map/ppermute | solution.py:421
  44.3 1.3 %collective-permute-start.15 = (bf16[512,128]{1,0:T(8,128)(2,1)S(1)}, bf16[512,128]{1,0:T(8,128)(2,1)S(1)}, u32[]{:S(2)}, u32[]{:S(2)}) collective-permute-start(bf16[512,128]{1,0:T(8,128)(2,1)S(1)} %collective-permute-done.8.rest_0_), channel_id=1, source_target_pairs={{0,1},{1,0},{2,3},{3,2},{4,5},{5,4},{6,7},{7,6},{8,9},{9,8},{10,11... | collective-permute-start | bytes 393224 | tf_op jit(solution)/shard_map/ppermute | solution.py:370
  44.4 1.4 %collective-permute-start.16 = (bf16[512,128]{1,0:T(8,128)(2,1)S(1)}, bf16[512,128]{1,0:T(8,128)(2,1)S(1)}, u32[]{:S(2)}, u32[]{:S(2)}) collective-permute-start(bf16[512,128]{1,0:T(8,128)(2,1)S(1)} %collective-permute-done.9.rest_2_), channel_id=1, source_target_pairs={{0,1},{1,0},{2,3},{3,2},{4,5},{5,4},{6,7},{7,6},{8,9},{9,8},{10,11... | collective-permute-start | bytes 393224 | tf_op jit(solution)/shard_map/ppermute | solution.py:370
  49.5 5.6 %collective-permute-start.17 = (bf16[472,128]{1,0:T(8,128)(2,1)S(1)}, bf16[472,128]{1,0:T(8,128)(2,1)S(1)}, u32[]{:S(2)}, u32[]{:S(2)}) collective-permute-start(bf16[472,128]{1,0:T(8,128)(2,1)S(1)} %pad_maximum_fusion.1), channel_id=1, source_target_pairs={{0,4},{4,0},{8,12},{12,8},{1,5},{5,1},{9,13},{13,9},{2,6},{6,2},{1... | collective-permute-start | bytes 362504 | tf_op jit(solution)/shard_map/ppermute | solution.py:504
  49.9 8.1 %collective-permute-start.19 = (bf16[2,256,128]{2,1,0:T(8,128)(2,1)S(1)}, bf16[2,256,128]{2,1,0:T(8,128)(2,1)S(1)}, u32[]{:S(2)}, u32[]{:S(2)}) collective-permute-start(bf16[2,256,128]{2,1,0:T(8,128)(2,1)S(1)} %get-tuple-element.129.refs_1_), channel_id=1, source_target_pairs={{0,1},{1,0},{2,3},{3,2},{4,5},{5,4},{6,7},{7,6},{8,9},{9,8},{10,11... | collective-permute-start | bytes 393224 | tf_op jit(solution)/shard_map/ppermute | solution.py:370
  50.0 7.9 %collective-permute-start.21 = (bf16[2,256,128]{2,1,0:T(8,128)(2,1)S(1)}, bf16[2,256,128]{2,1,0:T(8,128)(2,1)S(1)}, u32[]{:S(2)}, u32[]{:S(2)}) collective-permute-start(bf16[2,256,128]{2,1,0:T(8,128)(2,1)S(1)} %get-tuple-element.149.refs_7_), channel_id=1, source_target_pairs={{0,1},{1,0},{2,3},{3,2},{4,5},{5,4},{6,7},{7,6},{8,9},{9,8},{10,11... | collective-permute-start | bytes 393224 | tf_op jit(solution)/shard_map/ppermute | solution.py:370
  50.4 7.6 %collective-permute-start.20 = (bf16[2,256,128]{2,1,0:T(8,128)(2,1)S(1)}, bf16[2,256,128]{2,1,0:T(8,128)(2,1)S(1)}, u32[]{:S(2)}, u32[]{:S(2)}) collective-permute-start(bf16[2,256,128]{2,1,0:T(8,128)(2,1)S(1)} %get-tuple-element.147.refs_4_), channel_id=1, source_target_pairs={{0,1},{1,0},{2,3},{3,2},{4,5},{5,4},{6,7},{7,6},{8,9},{9,8},{10,11... | collective-permute-start | bytes 393224 | tf_op jit(solution)/shard_map/ppermute | solution.py:370
  55.2 6.8 %collective-permute-start.18 = (bf16[472,128]{1,0:T(8,128)(2,1)S(1)}, bf16[472,128]{1,0:T(8,128)(2,1)S(1)}, u32[]{:S(2)}, u32[]{:S(2)}) collective-permute-start(bf16[472,128]{1,0:T(8,128)(2,1)S(1)} %fusion.refs_0_), channel_id=1, source_target_pairs={{0,12},{4,8},{8,4},{12,0},{1,13},{5,9},{9,5},{13,1},{2,14},{6,10},... | collective-permute-start | bytes 362504 | tf_op jit(solution)/shard_map/ppermute | solution.py:505

commit v8 on v7

--- a/solution.py
+++ b/solution.py
@@ -65,11 +65,10 @@
     c = lax.axis_index("chan")
     copies = []
     for m in range(micro):
-        for n, out_ref in enumerate((a_ref, b_ref)):
-            spot = out_ref.at[pl.ds(m * (cells + wide), cells)]
-            copy = pltpu.make_async_copy(x_ref.at[m, c], spot, sem.at[2 * m + n])
-            copy.start()
-            copies.append(copy)
+        spot = a_ref.at[pl.ds(m * (cells + wide), cells)]
+        copy = pltpu.make_async_copy(x_ref.at[m, c], spot, sem.at[m])
+        copy.start()
+        copies.append(copy)
     spot = a_ref.at[pl.ds(micro * (cells + wide), cells)]
     copy = pltpu.make_async_copy(ct_ref.at[0, c], spot, sem.at[2 * micro])
     copy.start()
@@ -88,6 +87,9 @@
             out_ref[m * (cells + wide) + cells : (m + 1) * (cells + wide)] = own_ref[m, c]
     for copy in copies:
         copy.wait()
+    for m in range(micro):
+        rows = slice(m * (cells + wide), m * (cells + wide) + cells)
+        b_ref[rows] = a_ref[rows]
 
 
 def diagonal_mask(width):

time: 63.1 us -> 63 us (level)
  no operation moved by 1% of the time
where the time goes in v8:
time: 63 us; the launch traced here: 62.9 us
  Pallas kernels  20.8 us (33%)
  waiting for transfers between devices  20.6 us (33%)
  starting transfers between devices  20.2 us (32%)
  between operations  0.91 us (1%)
    pallas_call x14, Pallas kernels, call(): pl.pallas_call(kernel, in_specs=[vmem] * len(args) if in_specs is None el...  20.8 us
    ppermute x1, waiting for transfers between devices, on_device(): b = lax.ppermute(packed_b, ('space', 'chan'), route_b)  8.33 us
    ppermute x1, starting transfers between devices, on_device(): a = lax.ppermute(packed_a, ('space', 'chan'), route_a)  5.1 us
    ppermute x2, starting transfers between devices, send_on(): dg = lax.ppermute(out, ('space', 'section', 'chan'), route_d)  4.67 us
    ppermute x1, waiting for transfers between devices, on_device(): grads = grads + lax.ppermute(grads, 'space', near)  4.59 us
    ppermute x13, starting transfers between devices, swap(): return lax.ppermute(v, 'chan', [(0, 1), (1, 0)])  3.45 us
    ppermute x1, waiting for transfers between devices, on_device(): copies = [grads, lax.ppermute(grads, 'space', far)]  3.09 us
    ppermute x1, starting transfers between devices, on_device(): copies = [grads, lax.ppermute(grads, 'space', far)]  2.78 us
  transfers between devices with their start and end apart: 22, of which 7 were waited for; matrix products, arithmetic and copies ran while one was open for 0% of the time, Pallas kernels for 23%

profile of v8, /device:TPU:0, one launch (start us, length us, event | category | flops | bytes accessed | tf_op | source)
XLA Modules:
  0.0 62.9 jit_solution(1386349380467816356)
XLA Ops:
  0.6 1.8 %pack.1 = (bf16[1072,128]{1,0:T(8,128)(2,1)}, bf16[816,128]{1,0:T(8,128)(2,1)}, bf16[3,2,16,128]{3,2,1,0:T(8,128)(2,1)}) custom-call(bf16[3,2,256,128]{3,2,1,0:T(8,128)(2,1)} %bitcast.16, bf16[3,2,256,128]{3,2,1,0:T(8,128)(2,1)} %bitcast.18, s32[3,2,16,16]{3,2,1,0:T(8,128)} %tag_ref.1), custom_call_target="tpu_custom_call" | custom-call | flops 2000000000 | bytes 4194304 | tf_op jit(solution)/shard_map/pack/pallas_call | solution.py:331
  2.5 5.1 %collective-permute-start.1 = (bf16[1072,128]{1,0:T(8,128)(2,1)}, bf16[1072,128]{1,0:T(8,128)(2,1)S(1)}, u32[]{:S(2)}, u32[]{:S(2)}) collective-permute-start(bf16[1072,128]{1,0:T(8,128)(2,1)} %get-tuple-element.84), channel_id=1, source_target_pairs={{0,12},{1,5},{4,0},{5,9},{8,4},{9,13},{12,8},{13,1},{2,14},{3,7},{... | collective-permute-start | bytes 823304 | tf_op jit(solution)/shard_map/ppermute | solution.py:411
  7.6 0.0 collective-permute-start.2
  7.6 0.0 copy-start.1
  7.6 0.0 copy-start.3
  7.6 0.0 copy-start.4
  7.6 0.0 copy-start.5
  7.7 0.9 %weights.1 = (bf16[4608,256]{1,0:T(8,128)(2,1)S(1)}, bf16[4608,256]{1,0:T(8,128)(2,1)S(1)}) custom-call(bf16[16,8,8,27]{3,2,1,0:T(8,128)(2,1)S(1)} %bitcast.20), custom_call_target="tpu_custom_call" | custom-call | flops 2000000000 | bytes 4194304 | tf_op jit(solution)/shard_map/weights/pallas_call | solution.py:331
  8.6 0.1 copy-done.1
  8.7 1.8 %own.1 = (bf16[2,288,384]{2,1,0:T(8,128)(2,1)S(1)}, bf16[128,512]{1,0:T(8,128)(2,1)S(1)}, f32[2,256,128]{2,1,0:T(8,128)S(1)}, bf16[2,288,384]{2,1,0:T(8,128)(2,1...) custom-call(bf16[3,2,256,128]{3,2,1,0:T(8,128)(2,1)S(1)} %bitcast.17, ...), custom_call_target="tpu_custom_call" | custom-call | flops 2000000000 | bytes 4194304 | tf_op jit(solution)/shard_map/own/pallas_call | solution.py:331
  10.5 8.3 %collective-permute-done.2.b_ref = bf16[816,128]{1,0:T(8,128)(2,1)S(1)} collective-permute-done((bf16[816,128]{1,0:T(8,128)(2,1)}, bf16[816,128]{1,0:T(8,128)(2,1)S(1)}, u32[]{:S(2)}, u32[]{:S(2)}) %collective-permute-start.2) | collective-permute-done | bytes 208928 | tf_op jit(solution)/shard_map/ppermute | solution.py:412
  18.9 0.5 collective-permute-start.4
  19.4 1.7 %collective-permute-start = (bf16[512,128]{1,0:T(8,128)(2,1)S(1)}, bf16[512,128]{1,0:T(8,128)(2,1)S(1)}, u32[]{:S(2)}, u32[]{:S(2)}) collective-permute-start(bf16[512,128]{1,0:T(8,128)(2,1)S(1)} %get-tuple-element.83), channel_id=1, source_target_pairs={{0,12},{1,5},{4,0},{5,9},{8,4},{9,13},{12,8},{13,1},{2,14},{3,7},{... | collective-permute-start | bytes 393224 | tf_op jit(solution)/shard_map/ppermute | solution.py:415
  21.1 0.0 collective-permute-done.4.b2_ref
  21.1 0.0 collective-permute-done.3.a2_ref.cta2_ref
  21.1 1.7 %forward.3 = (f32[4,256,128]{2,1,0:T(8,128)S(1)}, bf16[128,512]{1,0:T(8,128)(2,1)S(1)}) custom-call(bf16[2,288,384]{2,1,0:T(8,128)(2,1)S(1)} %get-tuple-element.102.own_ref, bf16[1072,128]{1,0:T(8,128)(2,1)S(1)} %collective-permute-done.1.a_ref.cta_ref, bf16[816,128]{1,0:T(8,128)(2,1)S(1)} %collective-permute-done.2.b_ref, ...), custom_call_target="tpu_custom_call" | custom-call | flops 2000000000 | bytes 4194304 | tf_op jit(solution)/shard_map/forward/pallas_call | solution.py:331
  22.8 1.2 %backward_first.3 = (f32[256,128]{1,0:T(8,128)S(1)}, bf16[256,128]{1,0:T(8,128)(2,1)S(1)}) custom-call(bf16[3,128,512]{2,1,0:T(8,128)(2,1)S(1)} %get-tuple-element.81.x_ref, bf16[3,2,256,128]{3,2,1,0:T(8,128)(2,1)S(1)} %get-tuple-element.82.ct_ref, bf16[1072,128]{1,0:T(8,128)(2,1)S(1)} %collective-permute-done.1.a_ref.cta_ref, ...), custom_call_target="tpu_custom_call" | custom-call | flops 2000000000 | bytes 4194304 | tf_op jit(solution)/shard_map/backward_first/pallas_call | solution.py:331
  24.1 0.1 collective-permute-start.10
  24.1 1.7 %forward.4 = (f32[4,256,128]{2,1,0:T(8,128)S(1)}, bf16[128,512]{1,0:T(8,128)(2,1)S(1)}) custom-call(bf16[2,288,384]{2,1,0:T(8,128)(2,1)S(1)} %get-tuple-element.111.own_ref, bf16[1072,128]{1,0:T(8,128)(2,1)S(1)} %collective-permute-done.1.a_ref.cta_ref, bf16[816,128]{1,0:T(8,128)(2,1)S(1)} %collective-permute-done.2.b_ref, ...), custom_call_target="tpu_custom_call" | custom-call | flops 2000000000 | bytes 4194304 | tf_op jit(solution)/shard_map/forward/pallas_call | solution.py:331
  25.8 1.7 %forward.5 = (f32[4,256,128]{2,1,0:T(8,128)S(1)}, bf16[128,512]{1,0:T(8,128)(2,1)S(1)}) custom-call(bf16[2,288,384]{2,1,0:T(8,128)(2,1)S(1)} %get-tuple-element.97.own_ref, bf16[1072,128]{1,0:T(8,128)(2,1)S(1)} %collective-permute-done.1.a_ref.cta_ref, bf16[816,128]{1,0:T(8,128)(2,1)S(1)} %collective-permute-done.2.b_ref, ...), custom_call_target="tpu_custom_call" | custom-call | flops 2000000000 | bytes 4194304 | tf_op jit(solution)/shard_map/forward/pallas_call | solution.py:331
  27.6 0.6 collective-permute-start.5
  28.2 1.6 %collective-permute-start.11 = (bf16[256,128]{1,0:T(8,128)(2,1)S(1)}, bf16[256,128]{1,0:T(8,128)(2,1)S(1)}, u32[]{:S(2)}, u32[]{:S(2)}) collective-permute-start(bf16[256,128]{1,0:T(8,128)(2,1)S(1)} %add_convert_fusion), channel_id=1, source_target_pairs={{0,2},{2,0},{1,3},{3,1},{4,6},{6,4},{5,7},{7,5},{8,10},{10,8},{9,1... | collective-permute-start | bytes 196616 | tf_op jit(solution)/shard_map/ppermute | solution.py:422
  29.7 1.3 %collective-permute-start.12 = (bf16[256,128]{1,0:T(8,128)(2,1)S(1)}, bf16[256,128]{1,0:T(8,128)(2,1)S(1)}, u32[]{:S(2)}, u32[]{:S(2)}) collective-permute-start(bf16[256,128]{1,0:T(8,128)(2,1)S(1)} %add_convert_fusion), channel_id=1, source_target_pairs={{0,14},{2,12},{1,7},{3,5},{4,2},{6,0},{5,11},{7,9},{8,6},{10,4},{9... | collective-permute-start | bytes 196616 | tf_op jit(solution)/shard_map/ppermute | solution.py:423
  31.0 1.2 %backward_first.4 = (f32[256,128]{1,0:T(8,128)S(1)}, bf16[256,128]{1,0:T(8,128)(2,1)S(1)}) custom-call(bf16[3,128,512]{2,1,0:T(8,128)(2,1)S(1)} %get-tuple-element.81.x_ref, bf16[3,2,256,128]{3,2,1,0:T(8,128)(2,1)S(1)} %get-tuple-element.82.ct_ref, bf16[512,128]{1,0:T(8,128)(2,1)S(1)} %collective-permute-done.cta_ref, ...), custom_call_target="tpu_custom_call" | custom-call | flops 2000000000 | bytes 4194304 | tf_op jit(solution)/shard_map/backward_first/pallas_call | solution.py:331
  32.3 0.1 collective-permute-start.6
  32.4 1.2 %backward_first.5 = (f32[256,128]{1,0:T(8,128)S(1)}, bf16[256,128]{1,0:T(8,128)(2,1)S(1)}) custom-call(bf16[3,128,512]{2,1,0:T(8,128)(2,1)S(1)} %get-tuple-element.81.x_ref, bf16[3,2,256,128]{3,2,1,0:T(8,128)(2,1)S(1)} %get-tuple-element.82.ct_ref, bf16[512,128]{1,0:T(8,128)(2,1)S(1)} %collective-permute-done.cta_ref, ...), custom_call_target="tpu_custom_call" | custom-call | flops 2000000000 | bytes 4194304 | tf_op jit(solution)/shard_map/backward_first/pallas_call | solution.py:331
  33.6 0.6 collective-permute-start.7
  34.2 1.4 %collective-permute-done.12.rest_2_ = bf16[256,128]{1,0:T(8,128)(2,1)S(1)} collective-permute-done((bf16[256,128]{1,0:T(8,128)(2,1)S(1)}, bf16[256,128]{1,0:T(8,128)(2,1)S(1)}, u32[]{:S(2)}, u32[]{:S(2)}) %collective-permute-start.12) | collective-permute-done | bytes 65568 | tf_op jit(solution)/shard_map/ppermute | solution.py:423
  35.6 0.5 collective-permute-start.14
  36.2 0.6 collective-permute-start.8
  36.8 3.4 %collective-permute-start.9 = (bf16[512,128]{1,0:T(8,128)(2,1)S(1)}, bf16[512,128]{1,0:T(8,128)(2,1)S(1)}, u32[]{:S(2)}, u32[]{:S(2)}) collective-permute-start(bf16[512,128]{1,0:T(8,128)(2,1)S(1)} %pad_maximum_fusion), channel_id=1, source_target_pairs={{0,14},{2,12},{1,7},{3,5},{4,2},{6,0},{5,11},{7,9},{8,6},{10,4},{9... | collective-permute-start | bytes 393224 | tf_op jit(solution)/shard_map/ppermute | solution.py:423
  40.2 1.8 %backward_full.3 = (bf16[2,256,128]{2,1,0:T(8,128)(2,1)S(1)}, bf16[2,256,128]{2,1,0:T(8,128)(2,1)S(1)}, f32[128,128]{1,0:T(8,128)S(1)}, f32[128,128]{1,0:T(8,128)S(1)}, f32[216,128]{1,0:T(8,128)S(1)}) custom-call(bf16[3,128,512]{2,1,0:T(8,128)(2,1)S(1)} %get-tuple-element.81.x_ref, bf16[3,2,256,128]{3,2,1,0:T(8,128)(2,1)S(1)} %get-tuple-element.82.ct_ref, ...), custom_call_target="tpu_custom_call" | custom-call | flops 2000000000 | bytes 4194304 | tf_op jit(solution)/shard_map/backward_full/pallas_call | solution.py:331
  42.0 2.1 %collective-permute-done.8.rest_0_ = bf16[512,128]{1,0:T(8,128)(2,1)S(1)} collective-permute-done((bf16[512,128]{1,0:T(8,128)(2,1)S(1)}, bf16[512,128]{1,0:T(8,128)(2,1)S(1)}, u32[]{:S(2)}, u32[]{:S(2)}) %collective-permute-start.8) | collective-permute-done | bytes 131104 | tf_op jit(solution)/shard_map/ppermute | solution.py:422
  44.2 0.1 collective-permute-start.15
  44.3 0.4 collective-permute-start.16
  44.7 0.8 %collective-permute-done.15.rest_1_ = bf16[512,128]{1,0:T(8,128)(2,1)S(1)} collective-permute-done((bf16[512,128]{1,0:T(8,128)(2,1)S(1)}, bf16[512,128]{1,0:T(8,128)(2,1)S(1)}, u32[]{:S(2)}, u32[]{:S(2)}) %collective-permute-start.15) | collective-permute-done | bytes 131104 | tf_op jit(solution)/shard_map/ppermute | solution.py:372
  45.5 0.2 collective-permute-done.16.rest_3_
  45.7 1.8 %backward_full.4 = (bf16[2,256,128]{2,1,0:T(8,128)(2,1)S(1)}, bf16[2,256,128]{2,1,0:T(8,128)(2,1)S(1)}, f32[128,128]{1,0:T(8,128)S(1)}, f32[128,128]{1,0:T(8,128)S(1)}, f32[216,128]{1,0:T(8,128)S(1)}) custom-call(bf16[3,128,512]{2,1,0:T(8,128)(2,1)S(1)} %get-tuple-element.81.x_ref, bf16[3,2,256,128]{3,2,1,0:T(8,128)(2,1)S(1)} %get-tuple-element.82.ct_ref, ...), custom_call_target="tpu_custom_call" | custom-call | flops 2000000000 | bytes 4194304 | tf_op jit(solution)/shard_map/backward_full/pallas_call | solution.py:331
  47.5 1.8 %backward_full.5 = (bf16[2,256,128]{2,1,0:T(8,128)(2,1)S(1)}, bf16[2,256,128]{2,1,0:T(8,128)(2,1)S(1)}, f32[128,128]{1,0:T(8,128)S(1)}, f32[128,128]{1,0:T(8,128)S(1)}, f32[216,128]{1,0:T(8,128)S(1)}) custom-call(bf16[3,128,512]{2,1,0:T(8,128)(2,1)S(1)} %get-tuple-element.81.x_ref, bf16[3,2,256,128]{3,2,1,0:T(8,128)(2,1)S(1)} %get-tuple-element.82.ct_ref, ...), custom_call_target="tpu_custom_call" | custom-call | flops 2000000000 | bytes 4194304 | tf_op jit(solution)/shard_map/backward_full/pallas_call | solution.py:331
  49.4 0.3 collective-permute-start.17
  49.8 0.1 collective-permute-start.19
  49.9 0.4 collective-permute-start.21
  50.3 0.1 collective-permute-start.20
  50.4 4.6 %collective-permute-done.17 = bf16[472,128]{1,0:T(8,128)(2,1)S(1)} collective-permute-done((bf16[472,128]{1,0:T(8,128)(2,1)S(1)}, bf16[472,128]{1,0:T(8,128)(2,1)S(1)}, u32[]{:S(2)}, u32[]{:S(2)}) %collective-permute-start.17) | collective-permute-done | bytes 120864 | tf_op jit(solution)/shard_map/ppermute | solution.py:506
  55.1 2.8 %collective-permute-start.18 = (bf16[472,128]{1,0:T(8,128)(2,1)S(1)}, bf16[472,128]{1,0:T(8,128)(2,1)S(1)}, u32[]{:S(2)}, u32[]{:S(2)}) collective-permute-start(bf16[472,128]{1,0:T(8,128)(2,1)S(1)} %fusion.refs_0_), channel_id=1, source_target_pairs={{0,12},{4,8},{8,4},{12,0},{1,13},{5,9},{9,5},{13,1},{2,14},{6,10},... | collective-permute-start | bytes 362504 | tf_op jit(solution)/shard_map/ppermute | solution.py:507
  57.9 0.9 %emit.1 = bf16[3,2,256,128]{3,2,1,0:T(8,128)(2,1)} custom-call(bf16[2,256,128]{2,1,0:T(8,128)(2,1)S(1)} %get-tuple-element.145.refs_0_, bf16[2,256,128]{2,1,0:T(8,128)(2,1)S(1)} %get-tuple-element.129.refs_1_, bf16[2,256,128]{2,1,0:T(8,128)(2,1)S(1)} %collective-permute-done.19.refs_2_, bf16[2,256,128]{2,1,0:T(8,128)(2,1)S(1)} %get-tuple-element.146.refs_3_, ...), custom_call_target="tpu_custom_call" | custom-call | flops 2000000000 | bytes 4194304 | tf_op jit(solution)/shard_map/emit/pallas_call | solution.py:331
  58.7 3.1 %collective-permute-done.18.refs_1_ = bf16[472,128]{1,0:T(8,128)(2,1)S(1)} collective-permute-done((bf16[472,128]{1,0:T(8,128)(2,1)S(1)}, bf16[472,128]{1,0:T(8,128)(2,1)S(1)}, u32[]{:S(2)}, u32[]{:S(2)}) %collective-permute-start.18) | collective-permute-done | bytes 120864 | tf_op jit(solution)/shard_map/ppermute | solution.py:507
  61.8 1.0 %finish.1 = (f32[128,128]{1,0:T(8,128)}, f32[128,128]{1,0:T(8,128)}, f32[16,8,8,27]{3,2,1,0:T(8,128)}) custom-call(bf16[472,128]{1,0:T(8,128)(2,1)S(1)} %fusion.refs_0_, bf16[472,128]{1,0:T(8,128)(2,1)S(1)} %collective-permute-done.18.refs_1_), custom_call_target="tpu_custom_call" | custom-call | flops 2000000000 | bytes 4194304 | tf_op jit(solution)/shard_map/finish/pallas_call | solution.py:331
  (37 shorter events, 0.2 us)
Async XLA Ops:
  0.6 7.0 %copy-start.2 = (bf16[1,27,16,8,8]{1,4,3,2,0:T(8,128)(2,1)S(1)}, bf16[1,27,16,8,8]{1,4,3,2,0:T(8,128)(2,1)}, u32[]{:S(2)}) copy-start(bf16[1,27,16,8,8]{1,4,3,2,0:T(8,128)(2,1)} %param.12) | copy-start | bytes 165892
  2.5 16.4 %collective-permute-start.1 = (bf16[1072,128]{1,0:T(8,128)(2,1)}, bf16[1072,128]{1,0:T(8,128)(2,1)S(1)}, u32[]{:S(2)}, u32[]{:S(2)}) collective-permute-start(bf16[1072,128]{1,0:T(8,128)(2,1)} %get-tuple-element.84), channel_id=1, source_target_pairs={{0,12},{1,5},{4,0},{5,9},{8,4},{9,13},{12,8},{13,1},{2,14},{3,7},{... | collective-permute-start | bytes 823304 | tf_op jit(solution)/shard_map/ppermute | solution.py:411
  7.6 11.3 %collective-permute-start.2 = (bf16[816,128]{1,0:T(8,128)(2,1)}, bf16[816,128]{1,0:T(8,128)(2,1)S(1)}, u32[]{:S(2)}, u32[]{:S(2)}) collective-permute-start(bf16[816,128]{1,0:T(8,128)(2,1)} %get-tuple-element.85), channel_id=1, source_target_pairs={{0,4},{1,13},{4,8},{5,1},{8,12},{9,5},{12,0},{13,9},{2,6},{3,15},{... | collective-permute-start | bytes 626696 | tf_op jit(solution)/shard_map/ppermute | solution.py:412
  7.6 1.0 %copy-start.6 = (f32[1,3,128]{2,0,1:T(1,128)S(1)}, f32[1,3,128]{2,0,1:T(1,128)}, u32[]{:S(2)}) copy-start(f32[1,3,128]{2,0,1:T(1,128)} %param.11) | copy-start | bytes 4612
  7.6 1.0 %copy-start = (bf16[1,3,2,16,16,128]{5,4,3,2,1,0:T(8,128)(2,1)S(1)}, bf16[1,3,2,16,16,128]{5,4,3,2,1,0:T(8,128)(2,1)}, u32[]{:S(2)}) copy-start(bf16[1,3,2,16,16,128]{5,4,3,2,1,0:T(8,128)(2,1)} %param.7) | copy-start | bytes 1179652
  7.6 1.1 %copy-start.1 = (bf16[3,2,16,16,128]{4,3,2,1,0:T(8,128)(2,1)S(1)}, bf16[3,2,16,16,128]{4,3,2,1,0:T(8,128)(2,1)}, u32[]{:S(2)}) copy-start(bf16[3,2,16,16,128]{4,3,2,1,0:T(8,128)(2,1)} %param.8) | copy-start | bytes 1179652
  7.6 1.1 %copy-start.3 = (bf16[1,128,128]{2,1,0:T(8,128)(2,1)S(1)}, bf16[1,128,128]{2,1,0:T(8,128)(2,1)}, u32[]{:S(2)}) copy-start(bf16[1,128,128]{2,1,0:T(8,128)(2,1)} %param.10) | copy-start | bytes 98308
  7.6 1.1 %copy-start.4 = (bf16[1,128,128]{2,1,0:T(8,128)(2,1)S(1)}, bf16[1,128,128]{2,1,0:T(8,128)(2,1)}, u32[]{:S(2)}) copy-start(bf16[1,128,128]{2,1,0:T(8,128)(2,1)} %param.13) | copy-start | bytes 98308
  7.6 1.1 %copy-start.5 = (bf16[3,2,16,128]{3,2,1,0:T(8,128)(2,1)S(1)}, bf16[3,2,16,128]{3,2,1,0:T(8,128)(2,1)}, u32[]{:S(2)}) copy-start(bf16[3,2,16,128]{3,2,1,0:T(8,128)(2,1)} %get-tuple-element.80.lab_ref) | copy-start | bytes 73732
  18.9 2.3 %collective-permute-start.3 = (bf16[1072,128]{1,0:T(8,128)(2,1)S(1)}, bf16[1072,128]{1,0:T(8,128)(2,1)S(1)}, u32[]{:S(2)}, u32[]{:S(2)}) collective-permute-start(bf16[1072,128]{1,0:T(8,128)(2,1)S(1)} %collective-permute-done.1.a_ref.cta_ref), channel_id=1, source_target_pairs={{0,1},{1,0},{2,3},{3,2},{4,5},{5,4},{6,7},{7,6},{8,9},{9,8},{10,11... | collective-permute-start | bytes 823304 | tf_op jit(solution)/shard_map/ppermute | solution.py:372
  18.9 2.3 %collective-permute-start.4 = (bf16[816,128]{1,0:T(8,128)(2,1)S(1)}, bf16[816,128]{1,0:T(8,128)(2,1)S(1)}, u32[]{:S(2)}, u32[]{:S(2)}) collective-permute-start(bf16[816,128]{1,0:T(8,128)(2,1)S(1)} %collective-permute-done.2.b_ref), channel_id=1, source_target_pairs={{0,1},{1,0},{2,3},{3,2},{4,5},{5,4},{6,7},{7,6},{8,9},{9,8},{10,11... | collective-permute-start | bytes 626696 | tf_op jit(solution)/shard_map/ppermute | solution.py:372
  19.4 8.2 %collective-permute-start = (bf16[512,128]{1,0:T(8,128)(2,1)S(1)}, bf16[512,128]{1,0:T(8,128)(2,1)S(1)}, u32[]{:S(2)}, u32[]{:S(2)}) collective-permute-start(bf16[512,128]{1,0:T(8,128)(2,1)S(1)} %get-tuple-element.83), channel_id=1, source_target_pairs={{0,12},{1,5},{4,0},{5,9},{8,4},{9,13},{12,8},{13,1},{2,14},{3,7},{... | collective-permute-start | bytes 393224 | tf_op jit(solution)/shard_map/ppermute | solution.py:415
  24.1 4.1 %collective-permute-start.10 = (bf16[256,128]{1,0:T(8,128)(2,1)S(1)}, bf16[256,128]{1,0:T(8,128)(2,1)S(1)}, u32[]{:S(2)}, u32[]{:S(2)}) collective-permute-start(bf16[256,128]{1,0:T(8,128)(2,1)S(1)} %get-tuple-element.109), channel_id=1, source_target_pairs={{0,1},{1,0},{2,3},{3,2},{4,5},{5,4},{6,7},{7,6},{8,9},{9,8},{10,11... | collective-permute-start | bytes 196616 | tf_op jit(solution)/shard_map/ppermute | solution.py:372
  27.6 3.5 %collective-permute-start.5 = (bf16[512,128]{1,0:T(8,128)(2,1)S(1)}, bf16[512,128]{1,0:T(8,128)(2,1)S(1)}, u32[]{:S(2)}, u32[]{:S(2)}) collective-permute-start(bf16[512,128]{1,0:T(8,128)(2,1)S(1)} %collective-permute-done.cta_ref), channel_id=1, source_target_pairs={{0,1},{1,0},{2,3},{3,2},{4,5},{5,4},{6,7},{7,6},{8,9},{9,8},{10,11... | collective-permute-start | bytes 393224 | tf_op jit(solution)/shard_map/ppermute | solution.py:372
  28.2 6.0 %collective-permute-start.11 = (bf16[256,128]{1,0:T(8,128)(2,1)S(1)}, bf16[256,128]{1,0:T(8,128)(2,1)S(1)}, u32[]{:S(2)}, u32[]{:S(2)}) collective-permute-start(bf16[256,128]{1,0:T(8,128)(2,1)S(1)} %add_convert_fusion), channel_id=1, source_target_pairs={{0,2},{2,0},{1,3},{3,1},{4,6},{6,4},{5,7},{7,5},{8,10},{10,8},{9,1... | collective-permute-start | bytes 196616 | tf_op jit(solution)/shard_map/ppermute | solution.py:422
  29.7 5.9 %collective-permute-start.12 = (bf16[256,128]{1,0:T(8,128)(2,1)S(1)}, bf16[256,128]{1,0:T(8,128)(2,1)S(1)}, u32[]{:S(2)}, u32[]{:S(2)}) collective-permute-start(bf16[256,128]{1,0:T(8,128)(2,1)S(1)} %add_convert_fusion), channel_id=1, source_target_pairs={{0,14},{2,12},{1,7},{3,5},{4,2},{6,0},{5,11},{7,9},{8,6},{10,4},{9... | collective-permute-start | bytes 196616 | tf_op jit(solution)/shard_map/ppermute | solution.py:423
  32.3 3.8 %collective-permute-start.6 = (bf16[256,128]{1,0:T(8,128)(2,1)S(1)}, bf16[256,128]{1,0:T(8,128)(2,1)S(1)}, u32[]{:S(2)}, u32[]{:S(2)}) collective-permute-start(bf16[256,128]{1,0:T(8,128)(2,1)S(1)} %get-tuple-element.119), channel_id=1, source_target_pairs={{0,1},{1,0},{2,3},{3,2},{4,5},{5,4},{6,7},{7,6},{8,9},{9,8},{10,11... | collective-permute-start | bytes 196616 | tf_op jit(solution)/shard_map/ppermute | solution.py:372
  33.6 2.5 %collective-permute-start.7 = (bf16[256,128]{1,0:T(8,128)(2,1)S(1)}, bf16[256,128]{1,0:T(8,128)(2,1)S(1)}, u32[]{:S(2)}, u32[]{:S(2)}) collective-permute-start(bf16[256,128]{1,0:T(8,128)(2,1)S(1)} %get-tuple-element.123), channel_id=1, source_target_pairs={{0,1},{1,0},{2,3},{3,2},{4,5},{5,4},{6,7},{7,6},{8,9},{9,8},{10,11... | collective-permute-start | bytes 196616 | tf_op jit(solution)/shard_map/ppermute | solution.py:372
  35.6 4.6 %collective-permute-start.13 = (bf16[256,128]{1,0:T(8,128)(2,1)S(1)}, bf16[256,128]{1,0:T(8,128)(2,1)S(1)}, u32[]{:S(2)}, u32[]{:S(2)}) collective-permute-start(bf16[256,128]{1,0:T(8,128)(2,1)S(1)} %collective-permute-done.11.rest_0_), channel_id=1, source_target_pairs={{0,1},{1,0},{2,3},{3,2},{4,5},{5,4},{6,7},{7,6},{8,9},{9,8},{10,11... | collective-permute-start | bytes 196616 | tf_op jit(solution)/shard_map/ppermute | solution.py:372
  35.6 4.6 %collective-permute-start.14 = (bf16[256,128]{1,0:T(8,128)(2,1)S(1)}, bf16[256,128]{1,0:T(8,128)(2,1)S(1)}, u32[]{:S(2)}, u32[]{:S(2)}) collective-permute-start(bf16[256,128]{1,0:T(8,128)(2,1)S(1)} %collective-permute-done.12.rest_2_), channel_id=1, source_target_pairs={{0,1},{1,0},{2,3},{3,2},{4,5},{5,4},{6,7},{7,6},{8,9},{9,8},{10,11... | collective-permute-start | bytes 196616 | tf_op jit(solution)/shard_map/ppermute | solution.py:372
  36.2 8.0 %collective-permute-start.8 = (bf16[512,128]{1,0:T(8,128)(2,1)S(1)}, bf16[512,128]{1,0:T(8,128)(2,1)S(1)}, u32[]{:S(2)}, u32[]{:S(2)}) collective-permute-start(bf16[512,128]{1,0:T(8,128)(2,1)S(1)} %pad_maximum_fusion), channel_id=1, source_target_pairs={{0,2},{2,0},{1,3},{3,1},{4,6},{6,4},{5,7},{7,5},{8,10},{10,8},{9,1... | collective-permute-start | bytes 393224 | tf_op jit(solution)/shard_map/ppermute | solution.py:422
  36.8 7.4 %collective-permute-start.9 = (bf16[512,128]{1,0:T(8,128)(2,1)S(1)}, bf16[512,128]{1,0:T(8,128)(2,1)S(1)}, u32[]{:S(2)}, u32[]{:S(2)}) collective-permute-start(bf16[512,128]{1,0:T(8,128)(2,1)S(1)} %pad_maximum_fusion), channel_id=1, source_target_pairs={{0,14},{2,12},{1,7},{3,5},{4,2},{6,0},{5,11},{7,9},{8,6},{10,4},{9... | collective-permute-start | bytes 393224 | tf_op jit(solution)/shard_map/ppermute | solution.py:423
  44.2 1.3 %collective-permute-start.15 = (bf16[512,128]{1,0:T(8,128)(2,1)S(1)}, bf16[512,128]{1,0:T(8,128)(2,1)S(1)}, u32[]{:S(2)}, u32[]{:S(2)}) collective-permute-start(bf16[512,128]{1,0:T(8,128)(2,1)S(1)} %collective-permute-done.8.rest_0_), channel_id=1, source_target_pairs={{0,1},{1,0},{2,3},{3,2},{4,5},{5,4},{6,7},{7,6},{8,9},{9,8},{10,11... | collective-permute-start | bytes 393224 | tf_op jit(solution)/shard_map/ppermute | solution.py:372
  44.3 1.4 %collective-permute-start.16 = (bf16[512,128]{1,0:T(8,128)(2,1)S(1)}, bf16[512,128]{1,0:T(8,128)(2,1)S(1)}, u32[]{:S(2)}, u32[]{:S(2)}) collective-permute-start(bf16[512,128]{1,0:T(8,128)(2,1)S(1)} %collective-permute-done.9.rest_2_), channel_id=1, source_target_pairs={{0,1},{1,0},{2,3},{3,2},{4,5},{5,4},{6,7},{7,6},{8,9},{9,8},{10,11... | collective-permute-start | bytes 393224 | tf_op jit(solution)/shard_map/ppermute | solution.py:372
  49.4 5.6 %collective-permute-start.17 = (bf16[472,128]{1,0:T(8,128)(2,1)S(1)}, bf16[472,128]{1,0:T(8,128)(2,1)S(1)}, u32[]{:S(2)}, u32[]{:S(2)}) collective-permute-start(bf16[472,128]{1,0:T(8,128)(2,1)S(1)} %pad_maximum_fusion.1), channel_id=1, source_target_pairs={{0,4},{4,0},{8,12},{12,8},{1,5},{5,1},{9,13},{13,9},{2,6},{6,2},{1... | collective-permute-start | bytes 362504 | tf_op jit(solution)/shard_map/ppermute | solution.py:506
  49.8 8.1 %collective-permute-start.19 = (bf16[2,256,128]{2,1,0:T(8,128)(2,1)S(1)}, bf16[2,256,128]{2,1,0:T(8,128)(2,1)S(1)}, u32[]{:S(2)}, u32[]{:S(2)}) collective-permute-start(bf16[2,256,128]{2,1,0:T(8,128)(2,1)S(1)} %get-tuple-element.129.refs_1_), channel_id=1, source_target_pairs={{0,1},{1,0},{2,3},{3,2},{4,5},{5,4},{6,7},{7,6},{8,9},{9,8},{10,11... | collective-permute-start | bytes 393224 | tf_op jit(solution)/shard_map/ppermute | solution.py:372
  49.9 7.9 %collective-permute-start.21 = (bf16[2,256,128]{2,1,0:T(8,128)(2,1)S(1)}, bf16[2,256,128]{2,1,0:T(8,128)(2,1)S(1)}, u32[]{:S(2)}, u32[]{:S(2)}) collective-permute-start(bf16[2,256,128]{2,1,0:T(8,128)(2,1)S(1)} %get-tuple-element.149.refs_7_), channel_id=1, source_target_pairs={{0,1},{1,0},{2,3},{3,2},{4,5},{5,4},{6,7},{7,6},{8,9},{9,8},{10,11... | collective-permute-start | bytes 393224 | tf_op jit(solution)/shard_map/ppermute | solution.py:372
  50.3 7.6 %collective-permute-start.20 = (bf16[2,256,128]{2,1,0:T(8,128)(2,1)S(1)}, bf16[2,256,128]{2,1,0:T(8,128)(2,1)S(1)}, u32[]{:S(2)}, u32[]{:S(2)}) collective-permute-start(bf16[2,256,128]{2,1,0:T(8,128)(2,1)S(1)} %get-tuple-element.147.refs_4_), channel_id=1, source_target_pairs={{0,1},{1,0},{2,3},{3,2},{4,5},{5,4},{6,7},{7,6},{8,9},{9,8},{10,11... | collective-permute-start | bytes 393224 | tf_op jit(solution)/shard_map/ppermute | solution.py:372
  55.1 6.8 %collective-permute-start.18 = (bf16[472,128]{1,0:T(8,128)(2,1)S(1)}, bf16[472,128]{1,0:T(8,128)(2,1)S(1)}, u32[]{:S(2)}, u32[]{:S(2)}) collective-permute-start(bf16[472,128]{1,0:T(8,128)(2,1)S(1)} %fusion.refs_0_), channel_id=1, source_target_pairs={{0,12},{4,8},{8,4},{12,0},{1,13},{5,9},{9,5},{13,1},{2,14},{6,10},... | collective-permute-start | bytes 362504 | tf_op jit(solution)/shard_map/ppermute | solution.py:507
